TPU v7x, 256 devices: a whole 4x4x8 slice. The times are simulated.
256 devices in a mesh: dp: 8 (over x, core), mp: 32 (over y, z).
Axes of the slice: x: 4, y: 4, z: 8, core: 2. Of those that a mesh axis runs over, the one named last changes fastest.
Arguments:
- hidden: bfloat16 [4096, 4096], P('dp'), may hold values from -170 to 170
- encoded: bfloat16 [64, 114688], P('dp'), may hold values from -4 to 4
- neighbours: int32 [64, 2], P('dp'), may hold values from 0 to 63, as said below
- w_query: bfloat16 [4096, 4096], P(None, 'mp'), as said below
- w_key: bfloat16 [896, 4096], P(None, 'mp'), as said below
- w_value: bfloat16 [896, 4096], P(None, 'mp'), may hold values from -0.1875 to 0.1875
- w_out: bfloat16 [4096, 4096], P('mp'), may hold values from -0.1875 to 0.1875
- cotangent: bfloat16 [4096, 4096], P('dp'), may hold values from -16 to 16
Outputs:
- attended: bfloat16 [4096, 4096], P('dp', 'mp')
- grad_hidden: bfloat16 [4096, 4096], P('dp', 'mp')
- grad_encoded: bfloat16 [64, 114688], P('dp', 'mp')
Inputs may be any that keep to these rules, and one draw needn't show every extreme that they name: `neighbours`: an id is owner * 8 + slot: the neighbour is row slot of the rows of encoded held by dp index owner. Of the 16 ids of one index of dp, at most 4 name one owner; one owner, the same for every index, is named exactly 4 times by every index of dp. `w_query`: entries scaled by the inverse square root of 4096. `w_key`: entries scaled by the inverse square root of 896, or smaller.
All inputs are finite; a program needn't handle non-finite values.
Results may differ from a plain program's by a relative error of at most 0.0065.
The roundings to bfloat16 on the way count: a program that leaves them out, or rounds other values in their place, can miss the bound.
Values may be sent and summed in bfloat16 or wider, within the bound.
No kernel may reach another device: no remote copies, remote signals or barrier semaphores. Data moves between devices by JAX's collectives and lax.ppermute only.
A program may use at most 128 MiB of HBM per device.

v0:
```python
import functools
import math

import jax
import jax.numpy as jnp
from jax import lax
from jax.experimental import pallas as pl
from jax.experimental.pallas import tpu as pltpu
from jax.sharding import Mesh, PartitionSpec as P

DH = 128
BF = jnp.bfloat16
F32 = jnp.float32
NT = (((1,), (1,)), ((), ()))
TN = (((0,), (0,)), ((), ()))
HEAD = 16
VMEM_LIMIT = 60 * 1024 * 1024


def params():
    return pltpu.CompilerParams(vmem_limit_bytes=VMEM_LIMIT)


def call(body, out_shape, in_spaces, flops, moved, scratch=(), out_space="v"):
    spaces = {"s": pltpu.SMEM, "v": pltpu.VMEM, "a": pl.ANY}
    single = not isinstance(out_shape, (tuple, list))
    out = pl.BlockSpec(memory_space=spaces[out_space])
    return pl.pallas_call(
        body,
        out_shape=out_shape,
        in_specs=[pl.BlockSpec(memory_space=spaces[k]) for k in in_spaces],
        out_specs=out if single else (out,) * len(out_shape),
        scratch_shapes=list(scratch),
        compiler_params=params(),
        cost_estimate=pl.CostEstimate(flops=flops, bytes_accessed=moved, transcendentals=0),
    )


def keys_values_body(stored, ids_ref, x_ref, wk_ref, wv_ref, out_ref, pair_ref, kv_ref):
    pair = jnp.concatenate([wk_ref[...], wv_ref[...]], axis=1)
    pair_ref[...] = pair
    seg = x_ref.shape[0] // stored
    both = jnp.dot(x_ref[...], pair, preferred_element_type=F32)
    for n in range(kv_ref.shape[0]):
        kv_ref[n] = both[:, n * DH : (n + 1) * DH]
        for s in range(stored):
            rows = slice(HEAD + s * seg, HEAD + (s + 1) * seg)
            out_ref[rows, n * DH : (n + 1) * DH] = kv_ref[n, pl.ds(s, seg, stride=stored), :].astype(BF)
    lane = lax.broadcasted_iota(jnp.int32, (HEAD, 2 * DH), 1)
    row = jnp.zeros((HEAD, 2 * DH), F32)
    for r in range(2 * ids_ref.shape[0]):
        row = jnp.where(lane == r, ids_ref[r // 2, r % 2].astype(F32), row)
    out_ref[:HEAD, :] = row.astype(BF)


def halves_body(cut, after_ref, before_ref, lo_ref, hi_ref, sem):
    copies = [
        pltpu.make_async_copy(after_ref.at[:cut], lo_ref, sem.at[0]),
        pltpu.make_async_copy(before_ref.at[cut:], hi_ref, sem.at[1]),
    ]
    for copy in copies:
        copy.start()
    for copy in copies:
        copy.wait()


def weights_body(n_z, pos_ref, wo_ref, wq_ref, out_ref, sem):
    first = 2 * lax.rem(pos_ref[0], 2) * n_z

    def move(block):
        copies = [
            pltpu.make_async_copy(block(i * n_z + z), out_ref.at[z, i], sem.at[i * n_z + z])
            for i in range(2)
            for z in range(n_z)
        ]
        for copy in copies:
            copy.start()
        for copy in copies:
            copy.wait()

    @pl.when(pos_ref[1] == 0)
    def _():
        move(lambda k: wo_ref.at[:, pl.ds(pl.multiple_of((first + k) * DH, DH), DH)])

    @pl.when(pos_ref[1] != 0)
    def _():
        move(lambda k: wq_ref.at[pl.ds(pl.multiple_of((first + k) * DH, DH), DH), :])


def attention_body(geom, pos_ref, ids_ref, q_ref, g_ref, *refs):
    blocks, block_len, n_x, n_y, cap, stored, seg = geom
    kv_refs, (attn_ref, gq_ref, out_ref, all_ids_ref, kv_ref, sem) = refs[:-6], refs[-6:]
    inv_root = 1.0 / math.sqrt(DH)
    piece = seg // n_y
    my_x, my_c = pos_ref[0], pos_ref[1]
    copies = []
    for i, ref in enumerate(kv_refs):
        c, k = i // 5, i % 5
        cut = HEAD + stored // 2 * seg
        if k < 2:
            to = kv_ref.at[c * n_x + k]
        elif k == 4:
            to = kv_ref.at[c * n_x + 3]
        else:
            to = kv_ref.at[c * n_x + 2, :cut] if k == 2 else kv_ref.at[c * n_x + 2, cut:]
        copies.append(pltpu.make_async_copy(ref, to, sem.at[i]))
        copies[-1].start()
    out_ref[...] = jnp.zeros_like(out_ref)
    for copy in copies:
        copy.wait()
    for c in range(2):
        for d in range(n_x):
            owner = lax.rem(my_x + d, n_x) * 2 + lax.rem(my_c + c, 2)
            row = kv_ref[c * n_x + d, :HEAD, :DH].astype(F32).astype(jnp.int32)
            all_ids_ref[pl.ds(owner, 1), :] = row[:1, :]

    def place(r):
        i = ids_ref[r // 2, r % 2]
        owner, slot = i // stored, lax.rem(i, stored)
        dx = lax.rem(owner // 2 - my_x + n_x, n_x)
        dc = lax.rem(lax.rem(owner, 2) + my_c, 2)
        return owner, dc * n_x + dx, pl.multiple_of(HEAD + slot * seg, HEAD)

    spots = [place(r) for r in range(2 * blocks)]
    for c in range(blocks):
        both = [kv_ref[spots[r][1], pl.ds(spots[r][2], seg), :] for r in (2 * c, 2 * c + 1)]
        k = jnp.concatenate([b[:, :DH] for b in both], axis=0)
        v = jnp.concatenate([b[:, DH:] for b in both], axis=0)
        rows = slice(c * block_len, (c + 1) * block_len)
        q = q_ref[rows, :]
        g = g_ref[rows, :]
        s = lax.dot_general(q, k, NT, preferred_element_type=F32) * inv_root
        e = jnp.exp(s - jnp.max(s, axis=-1, keepdims=True))
        p = e / jnp.sum(e, axis=-1, keepdims=True)
        ph = p.astype(BF)
        gp = lax.dot_general(g, v, NT, preferred_element_type=F32)
        attn_ref[rows, :] = jnp.dot(ph, v, preferred_element_type=F32).astype(BF)
        gs = (p * (gp - jnp.sum(p * gp, axis=-1, keepdims=True))).astype(BF)
        gq_ref[rows, :] = (jnp.dot(gs, k, preferred_element_type=F32) * inv_root).astype(BF)
        gv = lax.dot_general(ph, g, TN, preferred_element_type=F32).astype(BF)
        gk = (lax.dot_general(gs, q, TN, preferred_element_type=F32) * inv_root).astype(BF)
        for j in range(2):
            r = 2 * c + j
            owner = spots[r][0]
            pos = sum([(spots[i][0] == owner).astype(jnp.int32) for i in range(r)], jnp.int32(0))
            for y in range(n_y):
                part = slice(j * seg + y * piece, j * seg + (y + 1) * piece)
                out_ref[owner, y, pos, :, :DH] = gk[part, :]
                out_ref[owner, y, pos, :, DH:] = gv[part, :]


def encoded_body(stored, pos_ref, ids_ref, ret_ref, *refs):
    owners, n_y, cap, piece, _ = ret_ref.shape
    w_refs, (out_ref, got_ref, w_ref, acc_ref, prod_ref, sem) = refs[:n_y], refs[n_y:]
    me = pos_ref[0] * 2 + pos_ref[1]
    my_y = pos_ref[2]
    for d in range(owners):
        pltpu.make_async_copy(ret_ref.at[d], got_ref.at[d], sem.at[d]).start()
    weights = [pltpu.make_async_copy(w_refs[y], w_ref.at[y], sem.at[owners + y]) for y in range(n_y)]
    for copy in weights:
        copy.start()
    acc_ref[...] = jnp.zeros_like(acc_ref)

    def from_device(d, carry):
        pltpu.make_async_copy(ret_ref.at[d], got_ref.at[d], sem.at[d]).wait()
        count = jnp.int32(0)
        for r in range(owners * 2):
            at = ids_ref[d, r]
            named = at // stored == me

            @pl.when(named)
            def _(at=at, count=count):
                slot = lax.rem(at, stored)
                for y in range(n_y):
                    acc_ref[y, slot] += got_ref[d, y, count].astype(F32)

            count = count + named.astype(jnp.int32)
        return carry

    lax.fori_loop(0, owners, from_device, 0)
    lanes = prod_ref.shape[0]
    for copy in weights:
        copy.wait()
    both = [acc_ref[lax.rem(my_y + y, n_y)].astype(BF).reshape(stored * piece, 2 * DH) for y in range(n_y)]
    both = jnp.concatenate(both, axis=1)
    for n in range(0, lanes, 2):
        wide = min(2, lanes - n)
        w = jnp.concatenate([w_ref[y, n * DH : (n + wide) * DH, :] for y in range(n_y)], axis=1)
        term = lax.dot_general(both, w, NT, preferred_element_type=F32)
        for i in range(wide):
            prod_ref[n + i] = term[:, i * DH : (i + 1) * DH]
    for t in range(0, piece, 2):
        for n in range(lanes):
            two = [prod_ref[n, pl.ds(t + k, stored, stride=piece), :] for k in range(2)]
            out_ref[pl.ds(t * stored, 2 * stored), n * DH : (n + 1) * DH] = jnp.concatenate(two, axis=0).astype(BF)


def head_sum_body(n_z, n_y, second, pos_ref, *refs):
    pieces, mine, other = refs[:n_z], refs[n_z : n_z + 2], refs[n_z + 2 : n_z + 4]
    *outs, a_ref, w_ref, sem = refs[n_z + 4 :]
    my_x, my_c, my_y, my_z = (pos_ref[i] for i in range(4))

    def weight_copies(refs):
        own = lax.rem(my_x, 2)
        return [pltpu.make_async_copy(refs[i], w_ref.at[own if i == 0 else 1 - own], sem.at[n_z + i]) for i in range(2)]

    @pl.when(my_c == second)
    def _():
        for copy in weight_copies(mine):
            copy.start()

    @pl.when(my_c != second)
    def _():
        for copy in weight_copies(other):
            copy.start()

    copies = [
        pltpu.make_async_copy(pieces[j], a_ref.at[:, j * DH : (j + 1) * DH], sem.at[j]) for j in range(n_z)
    ]
    for copy in copies:
        copy.start()
    for copy in weight_copies(mine) + copies:
        copy.wait()
    heads = [lax.rem(my_z + j, n_z) for j in range(n_z)]
    for k in range(0, n_y, 2):
        at = [lax.rem(my_y + k + i, n_y) for i in range(2)]
        if second:
            w = [jnp.concatenate([w_ref[at[i] // 2, h, lax.rem(at[i], 2)] for h in heads], axis=1) for i in range(2)]
            total = lax.dot_general(a_ref[...], jnp.concatenate(w, axis=0), NT, preferred_element_type=F32)
        else:
            w = [jnp.concatenate([w_ref[at[i] // 2, h, lax.rem(at[i], 2)] for h in heads], axis=0) for i in range(2)]
            total = jnp.dot(a_ref[...], jnp.concatenate(w, axis=1), preferred_element_type=F32)
        for i in range(2):
            outs[k + i][...] = total[:, i * DH : (i + 1) * DH].astype(outs[k + i].dtype)


def shards(hidden, encoded, neighbours, w_query, w_key, w_value, w_out, cotangent):
    n_x, n_c, n_y, n_z = (lax.axis_size(a) for a in ("x", "c", "y", "z"))
    dp = ("x", "c")
    owners = n_x * n_c
    rows, width = hidden.shape
    blocks, per_block = neighbours.shape
    cap = blocks * per_block // 4
    stored = encoded.shape[0]
    enc_width = w_key.shape[0]
    seg = encoded.shape[1] // enc_width
    block_len = rows // blocks
    piece = seg // n_y
    core = lax.axis_index("c")
    place = jnp.stack([lax.axis_index(a) for a in ("x", "c", "y", "z")]).astype(jnp.int32)

    def shift(axis, n, k):
        return lambda a: lax.ppermute(a, axis, [(i, (i + k) % n) for i in range(n)])

    swap = shift("c", n_c, 1)
    x_up, x_down = shift("x", n_x, -1), shift("x", n_x, 1)
    z_up, z_down = shift("z", n_z, -1), shift("z", n_z, 1)
    tie = lax.optimization_barrier

    enc_rows = encoded.reshape(stored, seg, enc_width).transpose(1, 0, 2).reshape(seg * stored, enc_width)
    kv, pair = call(
        functools.partial(keys_values_body, stored),
        (jax.ShapeDtypeStruct((HEAD + stored * seg, 2 * DH), BF), jax.ShapeDtypeStruct((enc_width, 2 * DH), BF)),
        "svvv", 470_000_000, 3 << 20,
        scratch=(pltpu.VMEM((2, seg * stored, DH), F32),),
    )(neighbours, enc_rows, w_key, w_value)
    after, before, kv_other = x_up(kv), x_down(kv), swap(kv)
    cut = HEAD + stored // 2 * seg
    next_lo, next_hi = call(
        functools.partial(halves_body, cut),
        (jax.ShapeDtypeStruct((cut, 2 * DH), BF), jax.ShapeDtypeStruct((kv.shape[0] - cut, 2 * DH), BF)),
        "aa", 0, 1 << 20, scratch=(pltpu.SemaphoreType.DMA((2,)),), out_space="a",
    )(after, before)
    far_lo, far_hi = x_up(next_lo), x_down(next_hi)
    w_query_, w_out_, _ = tie((w_query, w_out, next_lo))
    mine = call(
        functools.partial(weights_body, n_z),
        jax.ShapeDtypeStruct((n_z, 2, DH, DH), BF), "saa", 0, 1 << 20,
        scratch=(pltpu.SemaphoreType.DMA((2 * n_z,)),), out_space="a",
    )(place, w_out_, w_query_)
    kv_all = [kv, after, far_lo, far_hi, before, kv_other] + [swap(a) for a in (after, far_lo, far_hi, before)]

    mine = lax.all_to_all(mine, "z", 0, 0, tiled=True)
    y_up, y_down = shift("y", n_y, -1), shift("y", n_y, 1)
    pair_up, pair_down = y_up(pair), y_down(pair)
    pairs = [pair, pair_up, y_up(pair_up), pair_down]

    queries = jnp.dot(hidden, w_query, preferred_element_type=F32).astype(BF)
    grad_attn = lax.dot_general(cotangent, w_out, NT, preferred_element_type=F32).astype(BF)

    queries, grad_attn, pairs = tie((queries, grad_attn, pairs))
    mine = [mine, lax.ppermute(mine, "x", [(i, i ^ 1) for i in range(n_x)])]
    other = [swap(a) for a in mine]

    slab = jax.ShapeDtypeStruct((rows, DH), BF)
    attn, gq, outgoing, ids_all = call(
        functools.partial(attention_body, (blocks, block_len, n_x, n_y, cap, stored, seg)),
        (
            slab,
            slab,
            jax.ShapeDtypeStruct((owners, n_y, cap, piece, 2 * DH), BF),
            jax.ShapeDtypeStruct((owners, DH), jnp.int32),
        ),
        "ssvv" + "a" * len(kv_all), 500_000_000, 7 << 20,
        scratch=(
            pltpu.VMEM((owners, kv.shape[0], 2 * DH), BF),
            pltpu.SemaphoreType.DMA((len(kv_all),)),
        ),
    )(place, neighbours, queries, grad_attn, *kv_all)

    def ring(own):
        pieces = {0: own}
        for k in range(1, n_z // 2 + 1):
            pieces[k] = z_up(pieces[k - 1])
        last = own
        for k in range(1, n_z - n_z // 2):
            last = z_down(last)
            pieces[n_z - k] = last
        return [pieces[k] for k in range(n_z)]

    returned = lax.all_to_all(
        outgoing.reshape(owners * n_y, cap, piece, 2 * DH), dp + ("y",), 0, 0, tiled=True
    ).reshape(owners, n_y, cap, piece, 2 * DH)
    attn_all, gq_all = ring(attn), ring(gq)
    attn_all, gq_all, returned = tie((attn_all, gq_all, returned))
    enc_part = call(
        functools.partial(encoded_body, stored),
        jax.ShapeDtypeStruct((piece * stored, enc_width), BF), "ssa" + "a" * n_y, 500_000_000, 5 << 20,
        scratch=(
            pltpu.VMEM((owners, n_y, cap, piece, 2 * DH), BF),
            pltpu.VMEM((n_y, enc_width, 2 * DH), BF),
            pltpu.VMEM((n_y, stored, piece, 2 * DH), F32),
            pltpu.VMEM((enc_width // DH, stored * piece, DH), F32),
            pltpu.SemaphoreType.DMA((owners + n_y,)),
        ),
    )(place, ids_all, returned, *pairs)
    attn_all, gq_all, enc_part = tie((attn_all, gq_all, enc_part))
    enc_parts = lax.all_to_all(enc_part.reshape(n_z, -1, enc_width), "z", 0, 0, tiled=True)
    enc_rows_sum = jnp.sum(enc_parts.astype(F32), axis=0).astype(BF)
    grad_encoded = enc_rows_sum.reshape(seg // (n_y * n_z), stored, enc_width).transpose(1, 0, 2).reshape(stored, -1)

    def summed(pieces, second):
        parts = call(
            functools.partial(head_sum_body, n_z, n_y, second),
            (jax.ShapeDtypeStruct((rows, DH), F32),) + (slab,) * (n_y - 1),
            "s" + "a" * (n_z + 4), 540_000_000, 3 << 20,
            scratch=(
                pltpu.VMEM((rows, n_z * DH), BF),
                pltpu.VMEM((2, n_z, 2, DH, DH), BF),
                pltpu.SemaphoreType.DMA((n_z + 2,)),
            ),
        )(place, *pieces, *mine, *other)
        total = parts[0]
        for k in range(1, n_y):
            total = total + shift("y", n_y, k)(parts[k]).astype(F32)
        return total.astype(BF)

    return summed(attn_all, 0), summed(gq_all, 1), grad_encoded


def solution(mesh):
    n_y = 4
    dp, mp = mesh.shape["dp"], mesh.shape["mp"]
    split = Mesh(mesh.devices.reshape(dp // 2, 2, n_y, mp // n_y), ("x", "c", "y", "z"))
    d, m = ("x", "c"), ("y", "z")
    return jax.shard_map(
        shards,
        mesh=split,
        in_specs=(P(d, None), P(d, None), P(d, None), P(None, m), P(None, m), P(None, m), P(m, None), P(d, None)),
        out_specs=(P(d, m), P(d, m), P(d, m)),
        check_vma=False,
    )
```

profile of v0, /device:TPU:32, one launch (start us, length us, event | category | flops | bytes accessed | tf_op | source)
XLA Modules:
  0.0 192.6 jit_solution(9070425016343729529)
XLA Ops:
  2.1 3.2 %shard_map.103 = (bf16[1040,256]{1,0:T(8,128)(2,1)}, bf16[896,256]{1,0:T(8,128)(2,1)}) custom-call(s32[8,2]{1,0:T(8,128)} %copy.12.ids_ref, bf16[1024,896]{1,0:T(8,128)(2,1)} %bitcast.23, bf16[896,128]{1,0:T(8,128)(2,1)} %wk_ref.1, bf16[896,128]{1,0:T(8,128)(2,1)} %wv_ref.1), custom_call_target="tpu_custom_call" | custom-call | flops 470000000 | bytes 3145728 | tf_op jit(solution)/shard_map/pallas_call | solution.py:261
  5.3 2.8 %collective-permute-start.3 = (bf16[1040,256]{1,0:T(8,128)(2,1)}, bf16[1040,256]{1,0:T(8,128)(2,1)S(1)}, u32[]{:S(2)}, u32[]{:S(2)}) collective-permute-start(bf16[1040,256]{1,0:T(8,128)(2,1)} %get-tuple-element.64.refs_0_), channel_id=1, source_target_pairs={{0,192},{64,0},{128,64},{192,128},{1,193},{65,1},{129,65},{193,129... | collective-permute-start | bytes 1597448 | tf_op jit(solution)/shard_map/ppermute | solution.py:253
  8.1 3.0 %collective-permute-start = (bf16[896,256]{1,0:T(8,128)(2,1)}, bf16[896,256]{1,0:T(8,128)(2,1)}, u32[]{:S(2)}, u32[]{:S(2)}) collective-permute-start(bf16[896,256]{1,0:T(8,128)(2,1)} %get-tuple-element.88.refs_0_), channel_id=1, source_target_pairs={{0,24},{8,0},{16,8},{24,16},{1,25},{9,1},{17,9},{25,17},{2,26},{10... | collective-permute-start | bytes 1376264 | tf_op jit(solution)/shard_map/ppermute | solution.py:253
  11.1 8.7 %collective-permute-done.3.after_ref.refs_1_ = bf16[1040,256]{1,0:T(8,128)(2,1)S(1)} collective-permute-done((bf16[1040,256]{1,0:T(8,128)(2,1)}, bf16[1040,256]{1,0:T(8,128)(2,1)S(1)}, u32[]{:S(2)}, u32[]{:S(2)}) %collective-permute-start.3) | collective-permute-done | bytes 532512 | tf_op jit(solution)/shard_map/ppermute | solution.py:253
  19.7 3.3 %collective-permute-done.4.before_ref.refs_4_ = bf16[1040,256]{1,0:T(8,128)(2,1)S(1)} collective-permute-done((bf16[1040,256]{1,0:T(8,128)(2,1)}, bf16[1040,256]{1,0:T(8,128)(2,1)S(1)}, u32[]{:S(2)}, u32[]{:S(2)}) %collective-permute-start.4) | collective-permute-done | bytes 532512 | tf_op jit(solution)/shard_map/ppermute | solution.py:253
  23.9 17.2 %shard_map.104 = (bf16[528,256]{1,0:T(8,128)(2,1)}, bf16[512,256]{1,0:T(8,128)(2,1)}) custom-call(bf16[1040,256]{1,0:T(8,128)(2,1)} %copy-done.2, bf16[1040,256]{1,0:T(8,128)(2,1)} %copy-done.3), custom_call_target="tpu_custom_call" | custom-call | bytes 1048576 | tf_op jit(solution)/shard_map/pallas_call | solution.py:269
  41.8 17.9 %shard_map.107 = bf16[8,2,128,128]{3,2,1,0:T(8,128)(2,1)} custom-call(s32[4]{0:T(128)} %pad_add_fusion.pos_ref, bf16[128,4096]{1,0:T(8,128)(2,1)} %wo_ref, bf16[4096,128]{1,0:T(8,128)(2,1)} %wq_ref), custom_call_target="tpu_custom_call" | custom-call | bytes 1048576 | tf_op jit(solution)/shard_map/pallas_call | solution.py:276
  59.8 8.6 %all-to-all-start.1 = ((bf16[8,2,128,128]{3,2,1,0:T(8,128)(2,1)}), bf16[8,2,128,128]{3,2,1,0:T(8,128)(2,1)S(1)}, u32[]{:S(2)}, u32[]{:S(2)}) async-start(bf16[8,2,128,128]{3,2,1,0:T(8,128)(2,1)} %shard_map.107), calls=%async_computation.1 | async-start | bytes 1048576 | tf_op jit(solution)/shard_map/all_to_all | solution.py:283
  68.3 3.1 %collective-permute-start.1 = (bf16[896,256]{1,0:T(8,128)(2,1)}, bf16[896,256]{1,0:T(8,128)(2,1)S(1)}, u32[]{:S(2)}, u32[]{:S(2)}) collective-permute-start(bf16[896,256]{1,0:T(8,128)(2,1)} %collective-permute-done.refs_1_), channel_id=1, source_target_pairs={{0,24},{8,0},{16,8},{24,16},{1,25},{9,1},{17,9},{25,17},{2,26},{10... | collective-permute-start | bytes 1376264 | tf_op jit(solution)/shard_map/ppermute | solution.py:253
  71.4 3.2 %collective-permute-start.5 = (bf16[528,256]{1,0:T(8,128)(2,1)}, bf16[528,256]{1,0:T(8,128)(2,1)S(1)}, u32[]{:S(2)}, u32[]{:S(2)}) collective-permute-start(bf16[528,256]{1,0:T(8,128)(2,1)} %get-tuple-element.65), channel_id=1, source_target_pairs={{0,192},{64,0},{128,64},{192,128},{1,193},{65,1},{129,65},{193,129... | collective-permute-start | bytes 811016 | tf_op jit(solution)/shard_map/ppermute | solution.py:253
  75.2 4.1 %convolution_convert_fusion.g_ref = bf16[512,128]{1,0:T(8,128)(2,1)} fusion(bf16[512,4096]{1,0:T(8,128)(2,1)} %param.15, bf16[128,4096]{1,0:T(8,128)(2,1)S(1)} %copy-done.5), kind=kOutput, calls=%fused_computation | convolution fusion | flops 536936448 | bytes 5373952 | tf_op jit(solution)/shard_map/dot_general | solution.py:289
  79.3 2.1 %collective-permute-done.5.refs_2_ = bf16[528,256]{1,0:T(8,128)(2,1)S(1)} collective-permute-done((bf16[528,256]{1,0:T(8,128)(2,1)}, bf16[528,256]{1,0:T(8,128)(2,1)S(1)}, u32[]{:S(2)}, u32[]{:S(2)}) %collective-permute-start.5) | collective-permute-done | bytes 270368 | tf_op jit(solution)/shard_map/ppermute | solution.py:253
  81.9 1.9 %convolution_convert_fusion.1.q_ref = bf16[512,128]{1,0:T(8,128)(2,1)} fusion(bf16[512,4096]{1,0:T(8,128)(2,1)S(1)} %copy-done.28, bf16[4096,128]{1,0:T(8,128)(2,1)S(1)} %copy-done.6), kind=kOutput, calls=%fused_computation.1 | convolution fusion | flops 536936448 | bytes 5373952 | tf_op jit(solution)/shard_map/dot_general | solution.py:288
  85.5 8.0 %shard_map.105 = (bf16[512,128]{1,0:T(8,128)(2,1)}, bf16[512,128]{1,0:T(8,128)(2,1)}, bf16[8,4,4,32,256]{4,3,2,1,0:T(8,128)(2,1)}, s32[8,128]{1,0:T(8,128)}) custom-call(s32[4]{0:T(128)} %pad_add_fusion.pos_ref, s32[8,2]{1,0:T(8,128)} %copy.12.ids_ref, bf16[512,128]{1,0:T(8,128)(2,1)} %convolution_convert_fusion.1.q_ref, ...), custom_call_target="tpu_custom_call" | custom-call | flops 500000000 | bytes 7340032 | tf_op jit(solution)/shard_map/pallas_call | solution.py:296
  93.5 5.8 %all-to-all-start = ((bf16[32,4,32,256]{3,2,1,0:T(8,128)(2,1)}), bf16[32,4,32,256]{3,2,1,0:T(8,128)(2,1)S(1)}, u32[]{:S(2)}, u32[]{:S(2)}) async-start(bf16[32,4,32,256]{3,2,1,0:T(8,128)(2,1)} %bitcast.22), calls=%async_computation | async-start | bytes 4194304 | tf_op jit(solution)/shard_map/all_to_all | solution.py:321
  99.3 1.9 collective-permute-start.26
  101.4 2.9 %collective-permute-start.19 = (bf16[512,128]{1,0:T(8,128)(2,1)S(1)}, bf16[512,128]{1,0:T(8,128)(2,1)S(1)}, u32[]{:S(2)}, u32[]{:S(2)}) collective-permute-start(bf16[512,128]{1,0:T(8,128)(2,1)S(1)} %copy-done.14), channel_id=1, source_target_pairs={{0,7},{1,0},{2,1},{3,2},{4,3},{5,4},{6,5},{7,6},{8,15},{9,8},{10,9... | collective-permute-start | bytes 393224 | tf_op jit(solution)/shard_map/ppermute | solution.py:253
  105.2 2.3 %collective-permute-done.12.refs_1_ = bf16[512,128]{1,0:T(8,128)(2,1)S(1)} collective-permute-done((bf16[512,128]{1,0:T(8,128)(2,1)S(1)}, bf16[512,128]{1,0:T(8,128)(2,1)S(1)}, u32[]{:S(2)}, u32[]{:S(2)}) %collective-permute-start.12) | collective-permute-done | bytes 131104 | tf_op jit(solution)/shard_map/ppermute | solution.py:253
  108.3 2.1 %collective-permute-done.19.refs_1_ = bf16[512,128]{1,0:T(8,128)(2,1)S(1)} collective-permute-done((bf16[512,128]{1,0:T(8,128)(2,1)S(1)}, bf16[512,128]{1,0:T(8,128)(2,1)S(1)}, u32[]{:S(2)}, u32[]{:S(2)}) %collective-permute-start.19) | collective-permute-done | bytes 131104 | tf_op jit(solution)/shard_map/ppermute | solution.py:253
  113.6 24.2 %collective-permute-done.26.refs_9_ = bf16[8,2,128,128]{3,2,1,0:T(8,128)(2,1)S(1)} collective-permute-done((bf16[8,2,128,128]{3,2,1,0:T(8,128)(2,1)S(1)}, bf16[8,2,128,128]{3,2,1,0:T(8,128)(2,1)S(1)}, u32[]{:S(2)}, u32[]{:S(2)}) %collective-permute-start.26) | collective-permute-done | bytes 524320 | tf_op jit(solution)/shard_map/ppermute | solution.py:292
  138.2 2.9 %collective-permute-start.21 = (bf16[512,128]{1,0:T(8,128)(2,1)S(1)}, bf16[512,128]{1,0:T(8,128)(2,1)S(1)}, u32[]{:S(2)}, u32[]{:S(2)}) collective-permute-start(bf16[512,128]{1,0:T(8,128)(2,1)S(1)} %collective-permute-done.20.refs_2_), channel_id=1, source_target_pairs={{0,7},{1,0},{2,1},{3,2},{4,3},{5,4},{6,5},{7,6},{8,15},{9,8},{10,9... | collective-permute-start | bytes 393224 | tf_op jit(solution)/shard_map/ppermute | solution.py:253
  141.2 3.1 %collective-permute-done.14.refs_3_ = bf16[512,128]{1,0:T(8,128)(2,1)S(1)} collective-permute-done((bf16[512,128]{1,0:T(8,128)(2,1)S(1)}, bf16[512,128]{1,0:T(8,128)(2,1)S(1)}, u32[]{:S(2)}, u32[]{:S(2)}) %collective-permute-start.14) | collective-permute-done | bytes 131104 | tf_op jit(solution)/shard_map/ppermute | solution.py:253
  147.3 3.7 %collective-permute-start.22 = (bf16[512,128]{1,0:T(8,128)(2,1)S(1)}, bf16[512,128]{1,0:T(8,128)(2,1)}, u32[]{:S(2)}, u32[]{:S(2)}) collective-permute-start(bf16[512,128]{1,0:T(8,128)(2,1)S(1)} %collective-permute-done.21.refs_3_), channel_id=1, source_target_pairs={{0,7},{1,0},{2,1},{3,2},{4,3},{5,4},{6,5},{7,6},{8,15},{9,8},{10,9... | collective-permute-start | bytes 393224 | tf_op jit(solution)/shard_map/ppermute | solution.py:253
  151.0 2.0 %collective-permute-done.15.refs_4_ = bf16[512,128]{1,0:T(8,128)(2,1)S(1)} collective-permute-done((bf16[512,128]{1,0:T(8,128)(2,1)S(1)}, bf16[512,128]{1,0:T(8,128)(2,1)S(1)}, u32[]{:S(2)}, u32[]{:S(2)}) %collective-permute-start.15) | collective-permute-done | bytes 131104 | tf_op jit(solution)/shard_map/ppermute | solution.py:253
  155.8 6.2 %shard_map.106 = bf16[256,896]{1,0:T(8,128)(2,1)} custom-call(s32[4]{0:T(128)} %pad_add_fusion.pos_ref, s32[8,128]{1,0:T(8,128)} %get-tuple-element.86.ids_ref, bf16[8,4,4,32,256]{4,3,2,1,0:T(8,128)(2,1)} %bitcast.21, bf16[896,256]{1,0:T(8,128)(2,1)} %get-tuple-element.88.refs_0_, bf16[896,256]{1,0:T(8,128)(2,1)} %collective-permute-done.refs_1_, ...), custom_call_target="tpu_custom_call" | custom-call | flops 500000000 | bytes 5242880 | tf_op jit(solution)/shard_map/pallas_call | solution.py:326
  162.0 7.5 %all-to-all-start.2 = ((bf16[8,32,896]{2,1,0:T(8,128)(2,1)}), bf16[8,32,896]{2,1,0:T(8,128)(2,1)S(1)}, u32[]{:S(2)}, u32[]{:S(2)}) async-start(bf16[8,32,896]{2,1,0:T(8,128)(2,1)} %bitcast.24), calls=%async_computation.2 | async-start | bytes 917504 | tf_op jit(solution)/shard_map/all_to_all | solution.py:338
  169.6 3.9 %shard_map.109 = (f32[512,128]{1,0:T(8,128)}, bf16[512,128]{1,0:T(8,128)(2,1)}, bf16[512,128]{1,0:T(8,128)(2,1)}, bf16[512,128]{1,0:T(8,128)(2,1)}) custom-call(s32[4]{0:T(128)} %pad_add_fusion.pos_ref, bf16[512,128]{1,0:T(8,128)(2,1)} %get-tuple-element.106.refs_0_, bf16[512,128]{1,0:T(8,128)(2,1)} %copy-done.19, bf16[512,128]{1,0:T(8,128)(2,1)} %copy-done.21, ...), custom_call_target="tpu_custom_call" | custom-call | flops 540000000 | bytes 3145728 | tf_op jit(solution)/shard_map/pallas_call | solution.py:343
  174.0 2.7 %collective-permute-start.33 = (bf16[512,128]{1,0:T(8,128)(2,1)}, bf16[512,128]{1,0:T(8,128)(2,1)S(1)}, u32[]{:S(2)}, u32[]{:S(2)}) collective-permute-start(bf16[512,128]{1,0:T(8,128)(2,1)} %get-tuple-element.116), channel_id=1, source_target_pairs={{0,16},{8,24},{16,0},{24,8},{1,17},{9,25},{17,1},{25,9},{2,18},{10... | collective-permute-start | bytes 393224 | tf_op jit(solution)/shard_map/ppermute | solution.py:253
  177.7 3.8 %shard_map.108 = (f32[512,128]{1,0:T(8,128)}, bf16[512,128]{1,0:T(8,128)(2,1)}, bf16[512,128]{1,0:T(8,128)(2,1)}, bf16[512,128]{1,0:T(8,128)(2,1)}) custom-call(s32[4]{0:T(128)} %pad_add_fusion.pos_ref, bf16[512,128]{1,0:T(8,128)(2,1)} %get-tuple-element.92.refs_0_, bf16[512,128]{1,0:T(8,128)(2,1)} %copy-done.15, bf16[512,128]{1,0:T(8,128)(2,1)} %copy-done.17, ...), custom_call_target="tpu_custom_call" | custom-call | flops 540000000 | bytes 3145728 | tf_op jit(solution)/shard_map/pallas_call | solution.py:343
  183.7 2.5 %collective-permute-start.31 = (bf16[512,128]{1,0:T(8,128)(2,1)}, bf16[512,128]{1,0:T(8,128)(2,1)S(1)}, u32[]{:S(2)}, u32[]{:S(2)}) collective-permute-start(bf16[512,128]{1,0:T(8,128)(2,1)} %get-tuple-element.105), channel_id=1, source_target_pairs={{0,24},{8,0},{16,8},{24,16},{1,25},{9,1},{17,9},{25,17},{2,26},{10... | collective-permute-start | bytes 393224 | tf_op jit(solution)/shard_map/ppermute | solution.py:253
  186.2 1.7 add_convert_fusion
  190.3 1.7 add_convert_fusion.1
  (116 shorter events, 23.8 us)
Async XLA Ops:
  5.3 14.4 %collective-permute-start.3 = (bf16[1040,256]{1,0:T(8,128)(2,1)}, bf16[1040,256]{1,0:T(8,128)(2,1)S(1)}, u32[]{:S(2)}, u32[]{:S(2)}) collective-permute-start(bf16[1040,256]{1,0:T(8,128)(2,1)} %get-tuple-element.64.refs_0_), channel_id=1, source_target_pairs={{0,192},{64,0},{128,64},{192,128},{1,193},{65,1},{129,65},{193,129... | collective-permute-start | bytes 1597448 | tf_op jit(solution)/shard_map/ppermute | solution.py:253
  8.1 15.0 %collective-permute-start.4 = (bf16[1040,256]{1,0:T(8,128)(2,1)}, bf16[1040,256]{1,0:T(8,128)(2,1)S(1)}, u32[]{:S(2)}, u32[]{:S(2)}) collective-permute-start(bf16[1040,256]{1,0:T(8,128)(2,1)} %get-tuple-element.64.refs_0_), channel_id=1, source_target_pairs={{0,64},{64,128},{128,192},{192,0},{1,65},{65,129},{129,193},{193,1... | collective-permute-start | bytes 1597448 | tf_op jit(solution)/shard_map/ppermute | solution.py:253
  8.1 60.3 %collective-permute-start = (bf16[896,256]{1,0:T(8,128)(2,1)}, bf16[896,256]{1,0:T(8,128)(2,1)}, u32[]{:S(2)}, u32[]{:S(2)}) collective-permute-start(bf16[896,256]{1,0:T(8,128)(2,1)} %get-tuple-element.88.refs_0_), channel_id=1, source_target_pairs={{0,24},{8,0},{16,8},{24,16},{1,25},{9,1},{17,9},{25,17},{2,26},{10... | collective-permute-start | bytes 1376264 | tf_op jit(solution)/shard_map/ppermute | solution.py:253
  11.1 63.6 %collective-permute-start.2 = (bf16[896,256]{1,0:T(8,128)(2,1)}, bf16[896,256]{1,0:T(8,128)(2,1)}, u32[]{:S(2)}, u32[]{:S(2)}) collective-permute-start(bf16[896,256]{1,0:T(8,128)(2,1)} %get-tuple-element.88.refs_0_), channel_id=1, source_target_pairs={{0,8},{8,16},{16,24},{24,0},{1,9},{9,17},{17,25},{25,1},{2,10},{10... | collective-permute-start | bytes 1376264 | tf_op jit(solution)/shard_map/ppermute | solution.py:253
  41.1 33.8 %collective-permute-start.6 = (bf16[512,256]{1,0:T(8,128)(2,1)}, bf16[512,256]{1,0:T(8,128)(2,1)}, u32[]{:S(2)}, u32[]{:S(2)}) collective-permute-start(bf16[512,256]{1,0:T(8,128)(2,1)} %get-tuple-element.66), channel_id=1, source_target_pairs={{0,64},{64,128},{128,192},{192,0},{1,65},{65,129},{129,193},{193,1... | collective-permute-start | bytes 786440 | tf_op jit(solution)/shard_map/ppermute | solution.py:253
  59.8 33.7 %all-to-all-start.1 = ((bf16[8,2,128,128]{3,2,1,0:T(8,128)(2,1)}), bf16[8,2,128,128]{3,2,1,0:T(8,128)(2,1)S(1)}, u32[]{:S(2)}, u32[]{:S(2)}) async-start(bf16[8,2,128,128]{3,2,1,0:T(8,128)(2,1)} %shard_map.107), calls=%async_computation.1 | async-start | bytes 1048576 | tf_op jit(solution)/shard_map/all_to_all | solution.py:283
  68.3 13.1 %collective-permute-start.1 = (bf16[896,256]{1,0:T(8,128)(2,1)}, bf16[896,256]{1,0:T(8,128)(2,1)S(1)}, u32[]{:S(2)}, u32[]{:S(2)}) collective-permute-start(bf16[896,256]{1,0:T(8,128)(2,1)} %collective-permute-done.refs_1_), channel_id=1, source_target_pairs={{0,24},{8,0},{16,8},{24,16},{1,25},{9,1},{17,9},{25,17},{2,26},{10... | collective-permute-start | bytes 1376264 | tf_op jit(solution)/shard_map/ppermute | solution.py:253
  71.4 12.4 %collective-permute-start.7 = (bf16[1040,256]{1,0:T(8,128)(2,1)S(1)}, bf16[1040,256]{1,0:T(8,128)(2,1)S(1)}, u32[]{:S(2)}, u32[]{:S(2)}) collective-permute-start(bf16[1040,256]{1,0:T(8,128)(2,1)S(1)} %copy-done.7), channel_id=1, source_target_pairs={{0,32},{32,0},{1,33},{33,1},{2,34},{34,2},{3,35},{35,3},{4,36},{36... | collective-permute-start | bytes 1597448 | tf_op jit(solution)/shard_map/ppermute | solution.py:253
  71.4 9.9 %collective-permute-start.5 = (bf16[528,256]{1,0:T(8,128)(2,1)}, bf16[528,256]{1,0:T(8,128)(2,1)S(1)}, u32[]{:S(2)}, u32[]{:S(2)}) collective-permute-start(bf16[528,256]{1,0:T(8,128)(2,1)} %get-tuple-element.65), channel_id=1, source_target_pairs={{0,192},{64,0},{128,64},{192,128},{1,193},{65,1},{129,65},{193,129... | collective-permute-start | bytes 811016 | tf_op jit(solution)/shard_map/ppermute | solution.py:253
  74.7 9.2 %collective-permute-start.11 = (bf16[1040,256]{1,0:T(8,128)(2,1)}, bf16[1040,256]{1,0:T(8,128)(2,1)}, u32[]{:S(2)}, u32[]{:S(2)}) collective-permute-start(bf16[1040,256]{1,0:T(8,128)(2,1)} %copy-done.3), channel_id=1, source_target_pairs={{0,32},{32,0},{1,33},{33,1},{2,34},{34,2},{3,35},{35,3},{4,36},{36... | collective-permute-start | bytes 1597448 | tf_op jit(solution)/shard_map/ppermute | solution.py:253
  74.9 9.0 %collective-permute-start.8 = (bf16[1040,256]{1,0:T(8,128)(2,1)}, bf16[1040,256]{1,0:T(8,128)(2,1)}, u32[]{:S(2)}, u32[]{:S(2)}) collective-permute-start(bf16[1040,256]{1,0:T(8,128)(2,1)} %copy-done.2), channel_id=1, source_target_pairs={{0,32},{32,0},{1,33},{33,1},{2,34},{34,2},{3,35},{35,3},{4,36},{36... | collective-permute-start | bytes 1597448 | tf_op jit(solution)/shard_map/ppermute | solution.py:253
  93.5 61.0 %all-to-all-start = ((bf16[32,4,32,256]{3,2,1,0:T(8,128)(2,1)}), bf16[32,4,32,256]{3,2,1,0:T(8,128)(2,1)S(1)}, u32[]{:S(2)}, u32[]{:S(2)}) async-start(bf16[32,4,32,256]{3,2,1,0:T(8,128)(2,1)} %bitcast.22), calls=%async_computation | async-start | bytes 4194304 | tf_op jit(solution)/shard_map/all_to_all | solution.py:321
  99.3 38.6 %collective-permute-start.26 = (bf16[8,2,128,128]{3,2,1,0:T(8,128)(2,1)S(1)}, bf16[8,2,128,128]{3,2,1,0:T(8,128)(2,1)S(1)}, u32[]{:S(2)}, u32[]{:S(2)}) collective-permute-start(bf16[8,2,128,128]{3,2,1,0:T(8,128)(2,1)S(1)} %all-to-all-done.1.refs_8_), channel_id=1, source_target_pairs={{0,64},{64,0},{128,192},{192,128},{1,65},{65,1},{129,193},{193,129... | collective-permute-start | bytes 1572872 | tf_op jit(solution)/shard_map/ppermute | solution.py:292
  101.4 8.9 %collective-permute-start.19 = (bf16[512,128]{1,0:T(8,128)(2,1)S(1)}, bf16[512,128]{1,0:T(8,128)(2,1)S(1)}, u32[]{:S(2)}, u32[]{:S(2)}) collective-permute-start(bf16[512,128]{1,0:T(8,128)(2,1)S(1)} %copy-done.14), channel_id=1, source_target_pairs={{0,7},{1,0},{2,1},{3,2},{4,3},{5,4},{6,5},{7,6},{8,15},{9,8},{10,9... | collective-permute-start | bytes 393224 | tf_op jit(solution)/shard_map/ppermute | solution.py:253
  104.4 7.6 %collective-permute-start.16 = (bf16[512,128]{1,0:T(8,128)(2,1)S(1)}, bf16[512,128]{1,0:T(8,128)(2,1)S(1)}, u32[]{:S(2)}, u32[]{:S(2)}) collective-permute-start(bf16[512,128]{1,0:T(8,128)(2,1)S(1)} %copy-done.13), channel_id=1, source_target_pairs={{0,1},{1,2},{2,3},{3,4},{4,5},{5,6},{6,7},{7,0},{8,9},{9,10},{10,1... | collective-permute-start | bytes 393224 | tf_op jit(solution)/shard_map/ppermute | solution.py:253
  104.4 8.0 %collective-permute-start.23 = (bf16[512,128]{1,0:T(8,128)(2,1)S(1)}, bf16[512,128]{1,0:T(8,128)(2,1)S(1)}, u32[]{:S(2)}, u32[]{:S(2)}) collective-permute-start(bf16[512,128]{1,0:T(8,128)(2,1)S(1)} %copy-done.14), channel_id=1, source_target_pairs={{0,1},{1,2},{2,3},{3,4},{4,5},{5,6},{6,7},{7,0},{8,9},{9,10},{10,1... | collective-permute-start | bytes 393224 | tf_op jit(solution)/shard_map/ppermute | solution.py:253
  110.3 27.5 %collective-permute-start.20 = (bf16[512,128]{1,0:T(8,128)(2,1)S(1)}, bf16[512,128]{1,0:T(8,128)(2,1)S(1)}, u32[]{:S(2)}, u32[]{:S(2)}) collective-permute-start(bf16[512,128]{1,0:T(8,128)(2,1)S(1)} %collective-permute-done.19.refs_1_), channel_id=1, source_target_pairs={{0,7},{1,0},{2,1},{3,2},{4,3},{5,4},{6,5},{7,6},{8,15},{9,8},{10,9... | collective-permute-start | bytes 393224 | tf_op jit(solution)/shard_map/ppermute | solution.py:253
  112.0 26.2 %collective-permute-start.17 = (bf16[512,128]{1,0:T(8,128)(2,1)S(1)}, bf16[512,128]{1,0:T(8,128)(2,1)S(1)}, u32[]{:S(2)}, u32[]{:S(2)}) collective-permute-start(bf16[512,128]{1,0:T(8,128)(2,1)S(1)} %collective-permute-done.16.refs_7_), channel_id=1, source_target_pairs={{0,1},{1,2},{2,3},{3,4},{4,5},{5,6},{6,7},{7,0},{8,9},{9,10},{10,1... | collective-permute-start | bytes 393224 | tf_op jit(solution)/shard_map/ppermute | solution.py:253
  112.4 28.8 %collective-permute-start.24 = (bf16[512,128]{1,0:T(8,128)(2,1)S(1)}, bf16[512,128]{1,0:T(8,128)(2,1)S(1)}, u32[]{:S(2)}, u32[]{:S(2)}) collective-permute-start(bf16[512,128]{1,0:T(8,128)(2,1)S(1)} %collective-permute-done.23.refs_7_), channel_id=1, source_target_pairs={{0,1},{1,2},{2,3},{3,4},{4,5},{5,6},{6,7},{7,0},{8,9},{9,10},{10,1... | collective-permute-start | bytes 393224 | tf_op jit(solution)/shard_map/ppermute | solution.py:253
  113.6 55.9 %collective-permute-start.27 = (bf16[8,2,128,128]{3,2,1,0:T(8,128)(2,1)S(1)}, bf16[8,2,128,128]{3,2,1,0:T(8,128)(2,1)}, u32[]{:S(2)}, u32[]{:S(2)}) collective-permute-start(bf16[8,2,128,128]{3,2,1,0:T(8,128)(2,1)S(1)} %all-to-all-done.1.refs_8_), channel_id=1, source_target_pairs={{0,32},{32,0},{1,33},{33,1},{2,34},{34,2},{3,35},{35,3},{4,36},{36... | collective-permute-start | bytes 1572872 | tf_op jit(solution)/shard_map/ppermute | solution.py:253
  137.8 31.7 %collective-permute-start.28 = (bf16[8,2,128,128]{3,2,1,0:T(8,128)(2,1)S(1)}, bf16[8,2,128,128]{3,2,1,0:T(8,128)(2,1)}, u32[]{:S(2)}, u32[]{:S(2)}) collective-permute-start(bf16[8,2,128,128]{3,2,1,0:T(8,128)(2,1)S(1)} %collective-permute-done.26.refs_9_), channel_id=1, source_target_pairs={{0,32},{32,0},{1,33},{33,1},{2,34},{34,2},{3,35},{35,3},{4,36},{36... | collective-permute-start | bytes 1572872 | tf_op jit(solution)/shard_map/ppermute | solution.py:253
  138.2 8.3 %collective-permute-start.21 = (bf16[512,128]{1,0:T(8,128)(2,1)S(1)}, bf16[512,128]{1,0:T(8,128)(2,1)S(1)}, u32[]{:S(2)}, u32[]{:S(2)}) collective-permute-start(bf16[512,128]{1,0:T(8,128)(2,1)S(1)} %collective-permute-done.20.refs_2_), channel_id=1, source_target_pairs={{0,7},{1,0},{2,1},{3,2},{4,3},{5,4},{6,5},{7,6},{8,15},{9,8},{10,9... | collective-permute-start | bytes 393224 | tf_op jit(solution)/shard_map/ppermute | solution.py:253
  144.2 6.8 %collective-permute-start.25 = (bf16[512,128]{1,0:T(8,128)(2,1)S(1)}, bf16[512,128]{1,0:T(8,128)(2,1)S(1)}, u32[]{:S(2)}, u32[]{:S(2)}) collective-permute-start(bf16[512,128]{1,0:T(8,128)(2,1)S(1)} %collective-permute-done.24.refs_6_), channel_id=1, source_target_pairs={{0,1},{1,2},{2,3},{3,4},{4,5},{5,6},{6,7},{7,0},{8,9},{9,10},{10,1... | collective-permute-start | bytes 393224 | tf_op jit(solution)/shard_map/ppermute | solution.py:253
  146.6 6.4 %collective-permute-start.15 = (bf16[512,128]{1,0:T(8,128)(2,1)S(1)}, bf16[512,128]{1,0:T(8,128)(2,1)S(1)}, u32[]{:S(2)}, u32[]{:S(2)}) collective-permute-start(bf16[512,128]{1,0:T(8,128)(2,1)S(1)} %collective-permute-done.14.refs_3_), channel_id=1, source_target_pairs={{0,7},{1,0},{2,1},{3,2},{4,3},{5,4},{6,5},{7,6},{8,15},{9,8},{10,9... | collective-permute-start | bytes 393224 | tf_op jit(solution)/shard_map/ppermute | solution.py:253
  147.3 7.2 %collective-permute-start.22 = (bf16[512,128]{1,0:T(8,128)(2,1)S(1)}, bf16[512,128]{1,0:T(8,128)(2,1)}, u32[]{:S(2)}, u32[]{:S(2)}) collective-permute-start(bf16[512,128]{1,0:T(8,128)(2,1)S(1)} %collective-permute-done.21.refs_3_), channel_id=1, source_target_pairs={{0,7},{1,0},{2,1},{3,2},{4,3},{5,4},{6,5},{7,6},{8,15},{9,8},{10,9... | collective-permute-start | bytes 393224 | tf_op jit(solution)/shard_map/ppermute | solution.py:253
  162.0 29.9 %all-to-all-start.2 = ((bf16[8,32,896]{2,1,0:T(8,128)(2,1)}), bf16[8,32,896]{2,1,0:T(8,128)(2,1)S(1)}, u32[]{:S(2)}, u32[]{:S(2)}) async-start(bf16[8,32,896]{2,1,0:T(8,128)(2,1)} %bitcast.24), calls=%async_computation.2 | async-start | bytes 917504 | tf_op jit(solution)/shard_map/all_to_all | solution.py:338
  173.4 10.3 %collective-permute-start.32 = (bf16[512,128]{1,0:T(8,128)(2,1)}, bf16[512,128]{1,0:T(8,128)(2,1)S(1)}, u32[]{:S(2)}, u32[]{:S(2)}) collective-permute-start(bf16[512,128]{1,0:T(8,128)(2,1)} %get-tuple-element.115), channel_id=1, source_target_pairs={{0,8},{8,16},{16,24},{24,0},{1,9},{9,17},{17,25},{25,1},{2,10},{10... | collective-permute-start | bytes 393224 | tf_op jit(solution)/shard_map/ppermute | solution.py:253
  174.0 12.2 %collective-permute-start.33 = (bf16[512,128]{1,0:T(8,128)(2,1)}, bf16[512,128]{1,0:T(8,128)(2,1)S(1)}, u32[]{:S(2)}, u32[]{:S(2)}) collective-permute-start(bf16[512,128]{1,0:T(8,128)(2,1)} %get-tuple-element.116), channel_id=1, source_target_pairs={{0,16},{8,24},{16,0},{24,8},{1,17},{9,25},{17,1},{25,9},{2,18},{10... | collective-permute-start | bytes 393224 | tf_op jit(solution)/shard_map/ppermute | solution.py:253
  176.7 9.5 %collective-permute-start.34 = (bf16[512,128]{1,0:T(8,128)(2,1)}, bf16[512,128]{1,0:T(8,128)(2,1)S(1)}, u32[]{:S(2)}, u32[]{:S(2)}) collective-permute-start(bf16[512,128]{1,0:T(8,128)(2,1)} %get-tuple-element.117), channel_id=1, source_target_pairs={{0,24},{8,0},{16,8},{24,16},{1,25},{9,1},{17,9},{25,17},{2,26},{10... | collective-permute-start | bytes 393224 | tf_op jit(solution)/shard_map/ppermute | solution.py:253
  181.5 6.5 %collective-permute-start.29 = (bf16[512,128]{1,0:T(8,128)(2,1)}, bf16[512,128]{1,0:T(8,128)(2,1)S(1)}, u32[]{:S(2)}, u32[]{:S(2)}) collective-permute-start(bf16[512,128]{1,0:T(8,128)(2,1)} %get-tuple-element.103), channel_id=1, source_target_pairs={{0,8},{8,16},{16,24},{24,0},{1,9},{9,17},{17,25},{25,1},{2,10},{10... | collective-permute-start | bytes 393224 | tf_op jit(solution)/shard_map/ppermute | solution.py:253
  182.7 6.7 %collective-permute-start.30 = (bf16[512,128]{1,0:T(8,128)(2,1)}, bf16[512,128]{1,0:T(8,128)(2,1)S(1)}, u32[]{:S(2)}, u32[]{:S(2)}) collective-permute-start(bf16[512,128]{1,0:T(8,128)(2,1)} %get-tuple-element.104), channel_id=1, source_target_pairs={{0,16},{8,24},{16,0},{24,8},{1,17},{9,25},{17,1},{25,9},{2,18},{10... | collective-permute-start | bytes 393224 | tf_op jit(solution)/shard_map/ppermute | solution.py:253
  183.7 6.6 %collective-permute-start.31 = (bf16[512,128]{1,0:T(8,128)(2,1)}, bf16[512,128]{1,0:T(8,128)(2,1)S(1)}, u32[]{:S(2)}, u32[]{:S(2)}) collective-permute-start(bf16[512,128]{1,0:T(8,128)(2,1)} %get-tuple-element.105), channel_id=1, source_target_pairs={{0,24},{8,0},{16,8},{24,16},{1,25},{9,1},{17,9},{25,17},{2,26},{10... | collective-permute-start | bytes 393224 | tf_op jit(solution)/shard_map/ppermute | solution.py:253
  (35 other events, 701.8 us)
where the time goes:
time: 193 us
  starting transfers between devices  63 us (33%)
  Pallas kernels  60.2 us (31%)
  waiting for transfers between devices  51.9 us (27%)
  matrix products  6.03 us (3%)
  local copies, waits for them, and re-layouts  5.87 us (3%)
  other arithmetic  4.63 us (2%)
    ppermute x34, starting transfers between devices, shift(): return lambda a: lax.ppermute(a, axis, [(i, (i + k) % n) for i in range(n)])  39.3 us
    ppermute x34, waiting for transfers between devices, shift(): return lambda a: lax.ppermute(a, axis, [(i, (i + k) % n) for i in range(n)])  27.7 us
    ppermute x1, waiting for transfers between devices, shards(): mine = [mine, lax.ppermute(mine, 'x', [(i, i ^ 1) for i in range(n_x)])]  24.2 us
    pallas_call x1, Pallas kernels, shards(): call(functools.partial(weights_body, n_z), jax.ShapeDtypeStruct((n_z, 2,...  17.9 us
    pallas_call x1, Pallas kernels, shards(): call(functools.partial(halves_body, cut), (jax.ShapeDtypeStruct((cut, 2 *...  17.2 us
    all_to_all x1, starting transfers between devices, shards(): mine = lax.all_to_all(mine, 'z', 0, 0, tiled=True)  8.58 us
    pallas_call x1, Pallas kernels, shards(): call(functools.partial(attention_body, (blocks, block_len, n_x, n_y, cap,...  7.96 us
    pallas_call x2, Pallas kernels, summed(): call(functools.partial(head_sum_body, n_z, n_y, second), (jax.ShapeDtypeS...  7.69 us
  transfers between devices with their start and end apart: 38, of which 14 were waited for; matrix products, arithmetic and copies ran while one was open for 5% of the time, Pallas kernels for 30%

commit v1 on v0

--- a/solution.py
+++ b/solution.py
@@ -22,7 +22,7 @@
 
 
 def call(body, out_shape, in_spaces, flops, moved, scratch=(), out_space="v"):
-    spaces = {"s": pltpu.SMEM, "v": pltpu.VMEM, "a": pl.ANY}
+    spaces = {"s": pltpu.SMEM, "v": pltpu.VMEM, "a": pltpu.HBM}
     single = not isinstance(out_shape, (tuple, list))
     out = pl.BlockSpec(memory_space=spaces[out_space])
     return pl.pallas_call(
@@ -64,13 +64,11 @@
         copy.wait()
 
 
-def weights_body(n_z, pos_ref, wo_ref, wq_ref, out_ref, sem):
-    first = 2 * lax.rem(pos_ref[0], 2) * n_z
-
+def weights_body(n_z, n_y, pos_ref, wo_ref, wq_ref, out_ref, sem):
     def move(block):
         copies = [
-            pltpu.make_async_copy(block(i * n_z + z), out_ref.at[z, i], sem.at[i * n_z + z])
-            for i in range(2)
+            pltpu.make_async_copy(block((y * n_z + z) * DH), out_ref.at[z, y], sem.at[y * n_z + z])
+            for y in range(n_y)
             for z in range(n_z)
         ]
         for copy in copies:
@@ -80,11 +78,11 @@
 
     @pl.when(pos_ref[1] == 0)
     def _():
-        move(lambda k: wo_ref.at[:, pl.ds(pl.multiple_of((first + k) * DH, DH), DH)])
+        move(lambda at: wo_ref.at[:, at : at + DH])
 
     @pl.when(pos_ref[1] != 0)
     def _():
-        move(lambda k: wq_ref.at[pl.ds(pl.multiple_of((first + k) * DH, DH), DH), :])
+        move(lambda at: wq_ref.at[at : at + DH, :])
 
 
 def attention_body(geom, pos_ref, ids_ref, q_ref, g_ref, *refs):
@@ -196,39 +194,34 @@
 
 
 def head_sum_body(n_z, n_y, second, pos_ref, *refs):
-    pieces, mine, other = refs[:n_z], refs[n_z : n_z + 2], refs[n_z + 2 : n_z + 4]
-    *outs, a_ref, w_ref, sem = refs[n_z + 4 :]
-    my_x, my_c, my_y, my_z = (pos_ref[i] for i in range(4))
-
-    def weight_copies(refs):
-        own = lax.rem(my_x, 2)
-        return [pltpu.make_async_copy(refs[i], w_ref.at[own if i == 0 else 1 - own], sem.at[n_z + i]) for i in range(2)]
+    pieces, mine, other = refs[:n_z], refs[n_z], refs[n_z + 1]
+    *outs, a_ref, w_ref, sem = refs[n_z + 2 :]
+    my_c, my_y, my_z = (pos_ref[i] for i in range(1, 4))
 
     @pl.when(my_c == second)
     def _():
-        for copy in weight_copies(mine):
-            copy.start()
+        pltpu.make_async_copy(mine, w_ref, sem.at[n_z]).start()
 
     @pl.when(my_c != second)
     def _():
-        for copy in weight_copies(other):
-            copy.start()
+        pltpu.make_async_copy(other, w_ref, sem.at[n_z]).start()
 
     copies = [
         pltpu.make_async_copy(pieces[j], a_ref.at[:, j * DH : (j + 1) * DH], sem.at[j]) for j in range(n_z)
     ]
     for copy in copies:
         copy.start()
-    for copy in weight_copies(mine) + copies:
+    pltpu.make_async_copy(mine, w_ref, sem.at[n_z]).wait()
+    for copy in copies:
         copy.wait()
     heads = [lax.rem(my_z + j, n_z) for j in range(n_z)]
     for k in range(0, n_y, 2):
         at = [lax.rem(my_y + k + i, n_y) for i in range(2)]
         if second:
-            w = [jnp.concatenate([w_ref[at[i] // 2, h, lax.rem(at[i], 2)] for h in heads], axis=1) for i in range(2)]
+            w = [jnp.concatenate([w_ref[h, at[i]] for h in heads], axis=1) for i in range(2)]
             total = lax.dot_general(a_ref[...], jnp.concatenate(w, axis=0), NT, preferred_element_type=F32)
         else:
-            w = [jnp.concatenate([w_ref[at[i] // 2, h, lax.rem(at[i], 2)] for h in heads], axis=0) for i in range(2)]
+            w = [jnp.concatenate([w_ref[h, at[i]] for h in heads], axis=0) for i in range(2)]
             total = jnp.dot(a_ref[...], jnp.concatenate(w, axis=1), preferred_element_type=F32)
         for i in range(2):
             outs[k + i][...] = total[:, i * DH : (i + 1) * DH].astype(outs[k + i].dtype)
@@ -265,32 +258,34 @@
         scratch=(pltpu.VMEM((2, seg * stored, DH), F32),),
     )(neighbours, enc_rows, w_key, w_value)
     after, before, kv_other = x_up(kv), x_down(kv), swap(kv)
+
+    w_query_, w_out_, kv_other = tie((w_query, w_out, kv_other))
+    mine = call(
+        functools.partial(weights_body, n_z, n_y),
+        jax.ShapeDtypeStruct((n_z, n_y, DH, DH), BF), "saa", 0, 2 << 20,
+        scratch=(pltpu.SemaphoreType.DMA((n_z * n_y,)),),
+    )(place, w_out_, w_query_)
+    after, before, mine = tie((after, before, mine))
+    mine = lax.all_to_all(mine, "z", 0, 0, tiled=True)
+
     cut = HEAD + stored // 2 * seg
     next_lo, next_hi = call(
         functools.partial(halves_body, cut),
         (jax.ShapeDtypeStruct((cut, 2 * DH), BF), jax.ShapeDtypeStruct((kv.shape[0] - cut, 2 * DH), BF)),
-        "aa", 0, 1 << 20, scratch=(pltpu.SemaphoreType.DMA((2,)),), out_space="a",
+        "aa", 0, 1 << 20, scratch=(pltpu.SemaphoreType.DMA((2,)),),
     )(after, before)
     far_lo, far_hi = x_up(next_lo), x_down(next_hi)
-    w_query_, w_out_, _ = tie((w_query, w_out, next_lo))
-    mine = call(
-        functools.partial(weights_body, n_z),
-        jax.ShapeDtypeStruct((n_z, 2, DH, DH), BF), "saa", 0, 1 << 20,
-        scratch=(pltpu.SemaphoreType.DMA((2 * n_z,)),), out_space="a",
-    )(place, w_out_, w_query_)
+    pair_, far_lo, far_hi = tie((pair, far_lo, far_hi))
     kv_all = [kv, after, far_lo, far_hi, before, kv_other] + [swap(a) for a in (after, far_lo, far_hi, before)]
 
-    mine = lax.all_to_all(mine, "z", 0, 0, tiled=True)
     y_up, y_down = shift("y", n_y, -1), shift("y", n_y, 1)
-    pair_up, pair_down = y_up(pair), y_down(pair)
+    pair_up, pair_down = y_up(pair_), y_down(pair_)
     pairs = [pair, pair_up, y_up(pair_up), pair_down]
 
     queries = jnp.dot(hidden, w_query, preferred_element_type=F32).astype(BF)
     grad_attn = lax.dot_general(cotangent, w_out, NT, preferred_element_type=F32).astype(BF)
 
-    queries, grad_attn, pairs = tie((queries, grad_attn, pairs))
-    mine = [mine, lax.ppermute(mine, "x", [(i, i ^ 1) for i in range(n_x)])]
-    other = [swap(a) for a in mine]
+    other = swap(mine)
 
     slab = jax.ShapeDtypeStruct((rows, DH), BF)
     attn, gq, outgoing, ids_all = call(
@@ -343,13 +338,13 @@
         parts = call(
             functools.partial(head_sum_body, n_z, n_y, second),
             (jax.ShapeDtypeStruct((rows, DH), F32),) + (slab,) * (n_y - 1),
-            "s" + "a" * (n_z + 4), 540_000_000, 3 << 20,
+            "s" + "a" * (n_z + 2), 540_000_000, 3 << 20,
             scratch=(
                 pltpu.VMEM((rows, n_z * DH), BF),
-                pltpu.VMEM((2, n_z, 2, DH, DH), BF),
-                pltpu.SemaphoreType.DMA((n_z + 2,)),
+                pltpu.VMEM((n_z, n_y, DH, DH), BF),
+                pltpu.SemaphoreType.DMA((n_z + 1,)),
             ),
-        )(place, *pieces, *mine, *other)
+        )(place, *pieces, mine, other)
         total = parts[0]
         for k in range(1, n_y):
             total = total + shift("y", n_y, k)(parts[k]).astype(F32)

time: 193 us -> 162 us (0.84)
  Pallas kernels: 60.2 us -> 30 us
  waiting for transfers between devices: 51.9 us -> 48.1 us
    ppermute x1 -> x0, waiting for transfers between devices: 24.2 us -> none  [shards(): mine = [mine, lax.ppermute(mine, 'x', [(i, i ^ 1) for i in range(n_x)])]]
    ppermute x34 -> x33, waiting for transfers between devices: 27.7 us -> 47.1 us  [shift(): return lambda a: lax.ppermute(a, axis, [(i, (i + k) % n) for i in range(n)])]
    pallas_call x1, Pallas kernels: 17.2 us -> 1.88 us  [shards(): call(functools.partial(halves_body, cut), (jax.ShapeDtypeStruct((cut, 2 *...]
    pallas_call x1, Pallas kernels: 17.9 us -> 3.12 us  [shards(): call(functools.partial(weights_body, n_z, n_y), jax.ShapeDtypeStruct((n_z...]
    ppermute x34 -> x33, starting transfers between devices: 39.3 us -> 43.8 us  [shift(): return lambda a: lax.ppermute(a, axis, [(i, (i + k) % n) for i in range(n)])]
    unnamed x59 -> x55, local copies, waits for them, and re-layouts: 5.87 us -> 5.16 us
  transfers between devices with their start and end apart: 38 -> 36, of which waited for: 14 -> 13; matrix products, arithmetic and copies ran while one was open for 5% -> 7% of each run, Pallas kernels for 30% -> 17%
where the time goes in v1:
time: 162 us; the launch traced here: 160 us
  starting transfers between devices  63.7 us (39%)
  waiting for transfers between devices  48.1 us (30%)
  Pallas kernels  30 us (19%)
  matrix products  7.53 us (5%)
  local copies, waits for them, and re-layouts  5.16 us (3%)
  other arithmetic  4.65 us (3%)
    ppermute x33, waiting for transfers between devices, shift(): return lambda a: lax.ppermute(a, axis, [(i, (i + k) % n) for i in range(n)])  47.1 us
    ppermute x33, starting transfers between devices, shift(): return lambda a: lax.ppermute(a, axis, [(i, (i + k) % n) for i in range(n)])  43.8 us
    all_to_all x1, starting transfers between devices, shards(): mine = lax.all_to_all(mine, 'z', 0, 0, tiled=True)  8.57 us
    pallas_call x1, Pallas kernels, shards(): call(functools.partial(attention_body, (blocks, block_len, n_x, n_y, cap,...  7.91 us
    pallas_call x2, Pallas kernels, summed(): call(functools.partial(head_sum_body, n_z, n_y, second), (jax.ShapeDtypeS...  7.69 us
    all_to_all x1, starting transfers between devices, shards(): lax.all_to_all(enc_part.reshape(n_z, -1, enc_width), 'z', 0, 0, tiled=True)  6.46 us
    pallas_call x1, Pallas kernels, shards(): call(functools.partial(encoded_body, stored), jax.ShapeDtypeStruct((piece...  6.13 us
    unnamed x55, local copies, waits for them, and re-layouts  5.16 us
  transfers between devices with their start and end apart: 36, of which 13 were waited for; matrix products, arithmetic and copies ran while one was open for 7% of the time, Pallas kernels for 17%

profile of v1, /device:TPU:32, one launch (start us, length us, event | category | flops | bytes accessed | tf_op | source)
XLA Modules:
  0.0 160.0 jit_solution(5765163389976757647)
XLA Ops:
  2.0 3.3 %shard_map.103 = (bf16[1040,256]{1,0:T(8,128)(2,1)}, bf16[896,256]{1,0:T(8,128)(2,1)}) custom-call(s32[8,2]{1,0:T(8,128)} %copy.12.ids_ref, bf16[1024,896]{1,0:T(8,128)(2,1)} %bitcast.23, bf16[896,128]{1,0:T(8,128)(2,1)} %wk_ref.1, bf16[896,128]{1,0:T(8,128)(2,1)} %wv_ref.1), custom_call_target="tpu_custom_call" | custom-call | flops 470000000 | bytes 3145728 | tf_op jit(solution)/shard_map/pallas_call | solution.py:254
  5.2 2.8 %collective-permute-start = (bf16[1040,256]{1,0:T(8,128)(2,1)}, bf16[1040,256]{1,0:T(8,128)(2,1)S(1)}, u32[]{:S(2)}, u32[]{:S(2)}) collective-permute-start(bf16[1040,256]{1,0:T(8,128)(2,1)} %get-tuple-element.62.refs_0_), channel_id=1, source_target_pairs={{0,192},{64,0},{128,64},{192,128},{1,193},{65,1},{129,65},{193,129... | collective-permute-start | bytes 1597448 | tf_op jit(solution)/shard_map/ppermute | solution.py:246
  8.6 3.1 %shard_map.104 = bf16[8,4,128,128]{3,2,1,0:T(8,128)(2,1)} custom-call(s32[4]{0:T(128)} %pad_add_fusion.pos_ref, bf16[128,4096]{1,0:T(8,128)(2,1)} %wo_ref, bf16[4096,128]{1,0:T(8,128)(2,1)} %wq_ref), custom_call_target="tpu_custom_call" | custom-call | bytes 2097152 | tf_op jit(solution)/shard_map/pallas_call | solution.py:263
  11.8 8.6 %collective-permute-done.after_ref.refs_1_ = bf16[1040,256]{1,0:T(8,128)(2,1)S(1)} collective-permute-done((bf16[1040,256]{1,0:T(8,128)(2,1)}, bf16[1040,256]{1,0:T(8,128)(2,1)S(1)}, u32[]{:S(2)}, u32[]{:S(2)}) %collective-permute-start) | collective-permute-done | bytes 532512 | tf_op jit(solution)/shard_map/ppermute | solution.py:246
  20.3 3.3 %collective-permute-done.1.before_ref.refs_4_ = bf16[1040,256]{1,0:T(8,128)(2,1)S(1)} collective-permute-done((bf16[1040,256]{1,0:T(8,128)(2,1)}, bf16[1040,256]{1,0:T(8,128)(2,1)S(1)}, u32[]{:S(2)}, u32[]{:S(2)}) %collective-permute-start.1) | collective-permute-done | bytes 532512 | tf_op jit(solution)/shard_map/ppermute | solution.py:246
  23.7 8.6 %all-to-all-start.1 = ((bf16[8,4,128,128]{3,2,1,0:T(8,128)(2,1)}), bf16[8,4,128,128]{3,2,1,0:T(8,128)(2,1)S(1)}, u32[]{:S(2)}, u32[]{:S(2)}) async-start(bf16[8,4,128,128]{3,2,1,0:T(8,128)(2,1)} %shard_map.104), calls=%async_computation.1 | async-start | bytes 2097152 | tf_op jit(solution)/shard_map/all_to_all | solution.py:269
  32.2 1.9 %shard_map.105 = (bf16[528,256]{1,0:T(8,128)(2,1)}, bf16[512,256]{1,0:T(8,128)(2,1)}) custom-call(bf16[1040,256]{1,0:T(8,128)(2,1)} %copy-done.2, bf16[1040,256]{1,0:T(8,128)(2,1)} %copy-done.3), custom_call_target="tpu_custom_call" | custom-call | bytes 1048576 | tf_op jit(solution)/shard_map/pallas_call | solution.py:272
  35.0 1.7 %collective-permute-start.4 = (bf16[512,256]{1,0:T(8,128)(2,1)}, bf16[512,256]{1,0:T(8,128)(2,1)S(1)}, u32[]{:S(2)}, u32[]{:S(2)}) collective-permute-start(bf16[512,256]{1,0:T(8,128)(2,1)} %get-tuple-element.69), channel_id=1, source_target_pairs={{0,64},{64,128},{128,192},{192,0},{1,65},{65,129},{129,193},{193,1... | collective-permute-start | bytes 786440 | tf_op jit(solution)/shard_map/ppermute | solution.py:246
  36.7 4.4 %convolution_convert_fusion.g_ref = bf16[512,128]{1,0:T(8,128)(2,1)} fusion(bf16[512,4096]{1,0:T(8,128)(2,1)} %param.15, bf16[128,4096]{1,0:T(8,128)(2,1)} %wo_ref), kind=kOutput, calls=%fused_computation | convolution fusion | flops 536936448 | bytes 5373952 | tf_op jit(solution)/shard_map/dot_general | solution.py:286
  41.1 3.4 %collective-permute-done.4.refs_3_ = bf16[512,256]{1,0:T(8,128)(2,1)S(1)} collective-permute-done((bf16[512,256]{1,0:T(8,128)(2,1)}, bf16[512,256]{1,0:T(8,128)(2,1)S(1)}, u32[]{:S(2)}, u32[]{:S(2)}) %collective-permute-start.4) | collective-permute-done | bytes 262176 | tf_op jit(solution)/shard_map/ppermute | solution.py:246
  45.1 3.1 %convolution_convert_fusion.1.q_ref = bf16[512,128]{1,0:T(8,128)(2,1)} fusion(bf16[512,4096]{1,0:T(8,128)(2,1)S(1)} %copy-done.26, bf16[4096,128]{1,0:T(8,128)(2,1)} %wq_ref), kind=kOutput, calls=%fused_computation.1 | convolution fusion | flops 536936448 | bytes 5373952 | tf_op jit(solution)/shard_map/dot_general | solution.py:285
  50.1 7.9 %shard_map.106 = (bf16[512,128]{1,0:T(8,128)(2,1)}, bf16[512,128]{1,0:T(8,128)(2,1)}, bf16[8,4,4,32,256]{4,3,2,1,0:T(8,128)(2,1)}, s32[8,128]{1,0:T(8,128)}) custom-call(s32[4]{0:T(128)} %pad_add_fusion.pos_ref, s32[8,2]{1,0:T(8,128)} %copy.12.ids_ref, bf16[512,128]{1,0:T(8,128)(2,1)} %convolution_convert_fusion.1.q_ref, ...), custom_call_target="tpu_custom_call" | custom-call | flops 500000000 | bytes 7340032 | tf_op jit(solution)/shard_map/pallas_call | solution.py:291
  59.1 4.9 %all-to-all-start = ((bf16[32,4,32,256]{3,2,1,0:T(8,128)(2,1)}), bf16[32,4,32,256]{3,2,1,0:T(8,128)(2,1)S(1)}, u32[]{:S(2)}, u32[]{:S(2)}) async-start(bf16[32,4,32,256]{3,2,1,0:T(8,128)(2,1)} %bitcast.22), calls=%async_computation | async-start | bytes 4194304 | tf_op jit(solution)/shard_map/all_to_all | solution.py:316
  64.0 3.3 %collective-permute-start.23 = (bf16[896,256]{1,0:T(8,128)(2,1)}, bf16[896,256]{1,0:T(8,128)(2,1)}, u32[]{:S(2)}, u32[]{:S(2)}) collective-permute-start(bf16[896,256]{1,0:T(8,128)(2,1)} %get-tuple-element.94.refs_0_), channel_id=1, source_target_pairs={{0,24},{8,0},{16,8},{24,16},{1,25},{9,1},{17,9},{25,17},{2,26},{10... | collective-permute-start | bytes 1376264 | tf_op jit(solution)/shard_map/ppermute | solution.py:246
  70.7 2.8 %collective-permute-done.9.refs_1_ = bf16[512,128]{1,0:T(8,128)(2,1)S(1)} collective-permute-done((bf16[512,128]{1,0:T(8,128)(2,1)S(1)}, bf16[512,128]{1,0:T(8,128)(2,1)S(1)}, u32[]{:S(2)}, u32[]{:S(2)}) %collective-permute-start.9) | collective-permute-done | bytes 131104 | tf_op jit(solution)/shard_map/ppermute | solution.py:246
  74.3 1.7 %collective-permute-done.16.refs_1_ = bf16[512,128]{1,0:T(8,128)(2,1)S(1)} collective-permute-done((bf16[512,128]{1,0:T(8,128)(2,1)S(1)}, bf16[512,128]{1,0:T(8,128)(2,1)S(1)}, u32[]{:S(2)}, u32[]{:S(2)}) %collective-permute-start.16) | collective-permute-done | bytes 131104 | tf_op jit(solution)/shard_map/ppermute | solution.py:246
  77.4 2.3 %collective-permute-start.17 = (bf16[512,128]{1,0:T(8,128)(2,1)S(1)}, bf16[512,128]{1,0:T(8,128)(2,1)S(1)}, u32[]{:S(2)}, u32[]{:S(2)}) collective-permute-start(bf16[512,128]{1,0:T(8,128)(2,1)S(1)} %collective-permute-done.16.refs_1_), channel_id=1, source_target_pairs={{0,7},{1,0},{2,1},{3,2},{4,3},{5,4},{6,5},{7,6},{8,15},{9,8},{10,9... | collective-permute-start | bytes 393224 | tf_op jit(solution)/shard_map/ppermute | solution.py:246
  79.7 20.4 %collective-permute-done.23.refs_1_ = bf16[896,256]{1,0:T(8,128)(2,1)} collective-permute-done((bf16[896,256]{1,0:T(8,128)(2,1)}, bf16[896,256]{1,0:T(8,128)(2,1)}, u32[]{:S(2)}, u32[]{:S(2)}) %collective-permute-start.23) | collective-permute-done | bytes 458784 | tf_op jit(solution)/shard_map/ppermute | solution.py:246
  101.5 2.6 %collective-permute-start.24 = (bf16[896,256]{1,0:T(8,128)(2,1)}, bf16[896,256]{1,0:T(8,128)(2,1)}, u32[]{:S(2)}, u32[]{:S(2)}) collective-permute-start(bf16[896,256]{1,0:T(8,128)(2,1)} %collective-permute-done.23.refs_1_), channel_id=1, source_target_pairs={{0,24},{8,0},{16,8},{24,16},{1,25},{9,1},{17,9},{25,17},{2,26},{10... | collective-permute-start | bytes 1376264 | tf_op jit(solution)/shard_map/ppermute | solution.py:246
  105.4 2.7 %collective-permute-start.18 = (bf16[512,128]{1,0:T(8,128)(2,1)S(1)}, bf16[512,128]{1,0:T(8,128)(2,1)S(1)}, u32[]{:S(2)}, u32[]{:S(2)}) collective-permute-start(bf16[512,128]{1,0:T(8,128)(2,1)S(1)} %collective-permute-done.17.refs_2_), channel_id=1, source_target_pairs={{0,7},{1,0},{2,1},{3,2},{4,3},{5,4},{6,5},{7,6},{8,15},{9,8},{10,9... | collective-permute-start | bytes 393224 | tf_op jit(solution)/shard_map/ppermute | solution.py:246
  109.7 2.4 %collective-permute-start.15 = (bf16[512,128]{1,0:T(8,128)(2,1)S(1)}, bf16[512,128]{1,0:T(8,128)(2,1)S(1)}, u32[]{:S(2)}, u32[]{:S(2)}) collective-permute-start(bf16[512,128]{1,0:T(8,128)(2,1)S(1)} %collective-permute-done.14.refs_6_), channel_id=1, source_target_pairs={{0,1},{1,2},{2,3},{3,4},{4,5},{5,6},{6,7},{7,0},{8,9},{9,10},{10,1... | collective-permute-start | bytes 393224 | tf_op jit(solution)/shard_map/ppermute | solution.py:246
  112.1 3.0 %collective-permute-start.22 = (bf16[512,128]{1,0:T(8,128)(2,1)S(1)}, bf16[512,128]{1,0:T(8,128)(2,1)S(1)}, u32[]{:S(2)}, u32[]{:S(2)}) collective-permute-start(bf16[512,128]{1,0:T(8,128)(2,1)S(1)} %collective-permute-done.21.refs_6_), channel_id=1, source_target_pairs={{0,1},{1,2},{2,3},{3,4},{4,5},{5,6},{6,7},{7,0},{8,9},{9,10},{10,1... | collective-permute-start | bytes 393224 | tf_op jit(solution)/shard_map/ppermute | solution.py:246
  115.7 3.0 %collective-permute-start.12 = (bf16[512,128]{1,0:T(8,128)(2,1)S(1)}, bf16[512,128]{1,0:T(8,128)(2,1)S(1)}, u32[]{:S(2)}, u32[]{:S(2)}) collective-permute-start(bf16[512,128]{1,0:T(8,128)(2,1)S(1)} %collective-permute-done.11.refs_3_), channel_id=1, source_target_pairs={{0,7},{1,0},{2,1},{3,2},{4,3},{5,4},{6,5},{7,6},{8,15},{9,8},{10,9... | collective-permute-start | bytes 393224 | tf_op jit(solution)/shard_map/ppermute | solution.py:246
  121.9 1.8 %collective-permute-done.19.refs_4_ = bf16[512,128]{1,0:T(8,128)(2,1)} collective-permute-done((bf16[512,128]{1,0:T(8,128)(2,1)S(1)}, bf16[512,128]{1,0:T(8,128)(2,1)}, u32[]{:S(2)}, u32[]{:S(2)}) %collective-permute-start.19) | collective-permute-done | bytes 131104 | tf_op jit(solution)/shard_map/ppermute | solution.py:246
  125.1 6.1 %shard_map.107 = bf16[256,896]{1,0:T(8,128)(2,1)} custom-call(s32[4]{0:T(128)} %pad_add_fusion.pos_ref, s32[8,128]{1,0:T(8,128)} %get-tuple-element.92.ids_ref, bf16[8,4,4,32,256]{4,3,2,1,0:T(8,128)(2,1)} %bitcast.21, bf16[896,256]{1,0:T(8,128)(2,1)} %get-tuple-element.94.refs_0_, bf16[896,256]{1,0:T(8,128)(2,1)} %collective-permute-done.23.refs_1_, ...), custom_call_target="tpu_custom_call" | custom-call | flops 500000000 | bytes 5242880 | tf_op jit(solution)/shard_map/pallas_call | solution.py:321
  131.2 6.5 %all-to-all-start.2 = ((bf16[8,32,896]{2,1,0:T(8,128)(2,1)}), bf16[8,32,896]{2,1,0:T(8,128)(2,1)S(1)}, u32[]{:S(2)}, u32[]{:S(2)}) async-start(bf16[8,32,896]{2,1,0:T(8,128)(2,1)} %bitcast.24), calls=%async_computation.2 | async-start | bytes 917504 | tf_op jit(solution)/shard_map/all_to_all | solution.py:333
  137.7 3.8 %shard_map.109 = (f32[512,128]{1,0:T(8,128)}, bf16[512,128]{1,0:T(8,128)(2,1)}, bf16[512,128]{1,0:T(8,128)(2,1)}, bf16[512,128]{1,0:T(8,128)(2,1)}) custom-call(s32[4]{0:T(128)} %pad_add_fusion.pos_ref, bf16[512,128]{1,0:T(8,128)(2,1)} %get-tuple-element.108.refs_0_, bf16[512,128]{1,0:T(8,128)(2,1)} %copy-done.16, bf16[512,128]{1,0:T(8,128)(2,1)} %copy-done.19, ...), custom_call_target="tpu_custom_call" | custom-call | flops 540000000 | bytes 3145728 | tf_op jit(solution)/shard_map/pallas_call | solution.py:338
  141.6 1.7 %collective-permute-start.31 = (bf16[512,128]{1,0:T(8,128)(2,1)}, bf16[512,128]{1,0:T(8,128)(2,1)S(1)}, u32[]{:S(2)}, u32[]{:S(2)}) collective-permute-start(bf16[512,128]{1,0:T(8,128)(2,1)} %get-tuple-element.118), channel_id=1, source_target_pairs={{0,16},{8,24},{16,0},{24,8},{1,17},{9,25},{17,1},{25,9},{2,18},{10... | collective-permute-start | bytes 393224 | tf_op jit(solution)/shard_map/ppermute | solution.py:246
  143.3 1.8 %collective-permute-start.32 = (bf16[512,128]{1,0:T(8,128)(2,1)}, bf16[512,128]{1,0:T(8,128)(2,1)S(1)}, u32[]{:S(2)}, u32[]{:S(2)}) collective-permute-start(bf16[512,128]{1,0:T(8,128)(2,1)} %get-tuple-element.119), channel_id=1, source_target_pairs={{0,24},{8,0},{16,8},{24,16},{1,25},{9,1},{17,9},{25,17},{2,26},{10... | collective-permute-start | bytes 393224 | tf_op jit(solution)/shard_map/ppermute | solution.py:246
  145.1 3.8 %shard_map.108 = (f32[512,128]{1,0:T(8,128)}, bf16[512,128]{1,0:T(8,128)(2,1)}, bf16[512,128]{1,0:T(8,128)(2,1)}, bf16[512,128]{1,0:T(8,128)(2,1)}) custom-call(s32[4]{0:T(128)} %pad_add_fusion.pos_ref, bf16[512,128]{1,0:T(8,128)(2,1)} %get-tuple-element.95.refs_0_, bf16[512,128]{1,0:T(8,128)(2,1)} %copy-done.13, bf16[512,128]{1,0:T(8,128)(2,1)} %copy-done.15, ...), custom_call_target="tpu_custom_call" | custom-call | flops 540000000 | bytes 3145728 | tf_op jit(solution)/shard_map/pallas_call | solution.py:338
  149.7 2.1 %collective-permute-start.28 = (bf16[512,128]{1,0:T(8,128)(2,1)}, bf16[512,128]{1,0:T(8,128)(2,1)S(1)}, u32[]{:S(2)}, u32[]{:S(2)}) collective-permute-start(bf16[512,128]{1,0:T(8,128)(2,1)} %get-tuple-element.106), channel_id=1, source_target_pairs={{0,16},{8,24},{16,0},{24,8},{1,17},{9,25},{17,1},{25,9},{2,18},{10... | collective-permute-start | bytes 393224 | tf_op jit(solution)/shard_map/ppermute | solution.py:246
  151.8 2.5 %collective-permute-start.29 = (bf16[512,128]{1,0:T(8,128)(2,1)}, bf16[512,128]{1,0:T(8,128)(2,1)S(1)}, u32[]{:S(2)}, u32[]{:S(2)}) collective-permute-start(bf16[512,128]{1,0:T(8,128)(2,1)} %get-tuple-element.107), channel_id=1, source_target_pairs={{0,24},{8,0},{16,8},{24,16},{1,25},{9,1},{17,9},{25,17},{2,26},{10... | collective-permute-start | bytes 393224 | tf_op jit(solution)/shard_map/ppermute | solution.py:246
  (108 shorter events, 28.0 us)
Async XLA Ops:
  5.2 15.1 %collective-permute-start = (bf16[1040,256]{1,0:T(8,128)(2,1)}, bf16[1040,256]{1,0:T(8,128)(2,1)S(1)}, u32[]{:S(2)}, u32[]{:S(2)}) collective-permute-start(bf16[1040,256]{1,0:T(8,128)(2,1)} %get-tuple-element.62.refs_0_), channel_id=1, source_target_pairs={{0,192},{64,0},{128,64},{192,128},{1,193},{65,1},{129,65},{193,129... | collective-permute-start | bytes 1597448 | tf_op jit(solution)/shard_map/ppermute | solution.py:246
  8.0 15.7 %collective-permute-start.1 = (bf16[1040,256]{1,0:T(8,128)(2,1)}, bf16[1040,256]{1,0:T(8,128)(2,1)S(1)}, u32[]{:S(2)}, u32[]{:S(2)}) collective-permute-start(bf16[1040,256]{1,0:T(8,128)(2,1)} %get-tuple-element.62.refs_0_), channel_id=1, source_target_pairs={{0,64},{64,128},{128,192},{192,0},{1,65},{65,129},{129,193},{193,1... | collective-permute-start | bytes 1597448 | tf_op jit(solution)/shard_map/ppermute | solution.py:246
  23.7 35.4 %all-to-all-start.1 = ((bf16[8,4,128,128]{3,2,1,0:T(8,128)(2,1)}), bf16[8,4,128,128]{3,2,1,0:T(8,128)(2,1)S(1)}, u32[]{:S(2)}, u32[]{:S(2)}) async-start(bf16[8,4,128,128]{3,2,1,0:T(8,128)(2,1)} %shard_map.104), calls=%async_computation.1 | async-start | bytes 2097152 | tf_op jit(solution)/shard_map/all_to_all | solution.py:269
  32.2 16.1 %collective-permute-start.5 = (bf16[1040,256]{1,0:T(8,128)(2,1)S(1)}, bf16[1040,256]{1,0:T(8,128)(2,1)S(1)}, u32[]{:S(2)}, u32[]{:S(2)}) collective-permute-start(bf16[1040,256]{1,0:T(8,128)(2,1)S(1)} %collective-permute-done.after_ref.refs_1_), channel_id=1, source_target_pairs={{0,32},{32,0},{1,33},{33,1},{2,34},{34,2},{3,35},{35,3},{4,36},{36... | collective-permute-start | bytes 1597448 | tf_op jit(solution)/shard_map/ppermute | solution.py:246
  34.1 14.2 %collective-permute-start.8 = (bf16[1040,256]{1,0:T(8,128)(2,1)}, bf16[1040,256]{1,0:T(8,128)(2,1)S(1)}, u32[]{:S(2)}, u32[]{:S(2)}) collective-permute-start(bf16[1040,256]{1,0:T(8,128)(2,1)} %copy-done.3), channel_id=1, source_target_pairs={{0,32},{32,0},{1,33},{33,1},{2,34},{34,2},{3,35},{35,3},{4,36},{36... | collective-permute-start | bytes 1597448 | tf_op jit(solution)/shard_map/ppermute | solution.py:246
  34.7 9.8 %collective-permute-start.3 = (bf16[528,256]{1,0:T(8,128)(2,1)}, bf16[528,256]{1,0:T(8,128)(2,1)S(1)}, u32[]{:S(2)}, u32[]{:S(2)}) collective-permute-start(bf16[528,256]{1,0:T(8,128)(2,1)} %get-tuple-element.68), channel_id=1, source_target_pairs={{0,192},{64,0},{128,64},{192,128},{1,193},{65,1},{129,65},{193,129... | collective-permute-start | bytes 811016 | tf_op jit(solution)/shard_map/ppermute | solution.py:246
  35.0 9.5 %collective-permute-start.4 = (bf16[512,256]{1,0:T(8,128)(2,1)}, bf16[512,256]{1,0:T(8,128)(2,1)S(1)}, u32[]{:S(2)}, u32[]{:S(2)}) collective-permute-start(bf16[512,256]{1,0:T(8,128)(2,1)} %get-tuple-element.69), channel_id=1, source_target_pairs={{0,64},{64,128},{128,192},{192,0},{1,65},{65,129},{129,193},{193,1... | collective-permute-start | bytes 786440 | tf_op jit(solution)/shard_map/ppermute | solution.py:246
  59.1 64.7 %all-to-all-start = ((bf16[32,4,32,256]{3,2,1,0:T(8,128)(2,1)}), bf16[32,4,32,256]{3,2,1,0:T(8,128)(2,1)S(1)}, u32[]{:S(2)}, u32[]{:S(2)}) async-start(bf16[32,4,32,256]{3,2,1,0:T(8,128)(2,1)} %bitcast.22), calls=%async_computation | async-start | bytes 4194304 | tf_op jit(solution)/shard_map/all_to_all | solution.py:316
  64.0 36.1 %collective-permute-start.23 = (bf16[896,256]{1,0:T(8,128)(2,1)}, bf16[896,256]{1,0:T(8,128)(2,1)}, u32[]{:S(2)}, u32[]{:S(2)}) collective-permute-start(bf16[896,256]{1,0:T(8,128)(2,1)} %get-tuple-element.94.refs_0_), channel_id=1, source_target_pairs={{0,24},{8,0},{16,8},{24,16},{1,25},{9,1},{17,9},{25,17},{2,26},{10... | collective-permute-start | bytes 1376264 | tf_op jit(solution)/shard_map/ppermute | solution.py:246
  67.2 70.4 %collective-permute-start.26 = (bf16[8,4,128,128]{3,2,1,0:T(8,128)(2,1)S(1)}, bf16[8,4,128,128]{3,2,1,0:T(8,128)(2,1)}, u32[]{:S(2)}, u32[]{:S(2)}) collective-permute-start(bf16[8,4,128,128]{3,2,1,0:T(8,128)(2,1)S(1)} %all-to-all-done.1.refs_8_), channel_id=1, source_target_pairs={{0,32},{32,0},{1,33},{33,1},{2,34},{34,2},{3,35},{35,3},{4,36},{36... | collective-permute-start | bytes 3145736 | tf_op jit(solution)/shard_map/ppermute | solution.py:246
  67.2 6.3 %collective-permute-start.9 = (bf16[512,128]{1,0:T(8,128)(2,1)S(1)}, bf16[512,128]{1,0:T(8,128)(2,1)S(1)}, u32[]{:S(2)}, u32[]{:S(2)}) collective-permute-start(bf16[512,128]{1,0:T(8,128)(2,1)S(1)} %copy-done.11), channel_id=1, source_target_pairs={{0,7},{1,0},{2,1},{3,2},{4,3},{5,4},{6,5},{7,6},{8,15},{9,8},{10,9... | collective-permute-start | bytes 393224 | tf_op jit(solution)/shard_map/ppermute | solution.py:246
  68.7 7.3 %collective-permute-start.16 = (bf16[512,128]{1,0:T(8,128)(2,1)S(1)}, bf16[512,128]{1,0:T(8,128)(2,1)S(1)}, u32[]{:S(2)}, u32[]{:S(2)}) collective-permute-start(bf16[512,128]{1,0:T(8,128)(2,1)S(1)} %copy-done.12), channel_id=1, source_target_pairs={{0,7},{1,0},{2,1},{3,2},{4,3},{5,4},{6,5},{7,6},{8,15},{9,8},{10,9... | collective-permute-start | bytes 393224 | tf_op jit(solution)/shard_map/ppermute | solution.py:246
  69.8 7.7 %collective-permute-start.13 = (bf16[512,128]{1,0:T(8,128)(2,1)S(1)}, bf16[512,128]{1,0:T(8,128)(2,1)S(1)}, u32[]{:S(2)}, u32[]{:S(2)}) collective-permute-start(bf16[512,128]{1,0:T(8,128)(2,1)S(1)} %copy-done.11), channel_id=1, source_target_pairs={{0,1},{1,2},{2,3},{3,4},{4,5},{5,6},{6,7},{7,0},{8,9},{9,10},{10,1... | collective-permute-start | bytes 393224 | tf_op jit(solution)/shard_map/ppermute | solution.py:246
  73.5 6.2 %collective-permute-start.20 = (bf16[512,128]{1,0:T(8,128)(2,1)S(1)}, bf16[512,128]{1,0:T(8,128)(2,1)S(1)}, u32[]{:S(2)}, u32[]{:S(2)}) collective-permute-start(bf16[512,128]{1,0:T(8,128)(2,1)S(1)} %copy-done.12), channel_id=1, source_target_pairs={{0,1},{1,2},{2,3},{3,4},{4,5},{5,6},{6,7},{7,0},{8,9},{9,10},{10,1... | collective-permute-start | bytes 393224 | tf_op jit(solution)/shard_map/ppermute | solution.py:246
  76.0 24.9 %collective-permute-start.10 = (bf16[512,128]{1,0:T(8,128)(2,1)S(1)}, bf16[512,128]{1,0:T(8,128)(2,1)S(1)}, u32[]{:S(2)}, u32[]{:S(2)}) collective-permute-start(bf16[512,128]{1,0:T(8,128)(2,1)S(1)} %collective-permute-done.9.refs_1_), channel_id=1, source_target_pairs={{0,7},{1,0},{2,1},{3,2},{4,3},{5,4},{6,5},{7,6},{8,15},{9,8},{10,9... | collective-permute-start | bytes 393224 | tf_op jit(solution)/shard_map/ppermute | solution.py:246
  77.4 24.1 %collective-permute-start.17 = (bf16[512,128]{1,0:T(8,128)(2,1)S(1)}, bf16[512,128]{1,0:T(8,128)(2,1)S(1)}, u32[]{:S(2)}, u32[]{:S(2)}) collective-permute-start(bf16[512,128]{1,0:T(8,128)(2,1)S(1)} %collective-permute-done.16.refs_1_), channel_id=1, source_target_pairs={{0,7},{1,0},{2,1},{3,2},{4,3},{5,4},{6,5},{7,6},{8,15},{9,8},{10,9... | collective-permute-start | bytes 393224 | tf_op jit(solution)/shard_map/ppermute | solution.py:246
  79.7 24.4 %collective-permute-start.14 = (bf16[512,128]{1,0:T(8,128)(2,1)S(1)}, bf16[512,128]{1,0:T(8,128)(2,1)S(1)}, u32[]{:S(2)}, u32[]{:S(2)}) collective-permute-start(bf16[512,128]{1,0:T(8,128)(2,1)S(1)} %collective-permute-done.13.refs_7_), channel_id=1, source_target_pairs={{0,1},{1,2},{2,3},{3,4},{4,5},{5,6},{6,7},{7,0},{8,9},{9,10},{10,1... | collective-permute-start | bytes 393224 | tf_op jit(solution)/shard_map/ppermute | solution.py:246
  100.1 5.3 %collective-permute-start.21 = (bf16[512,128]{1,0:T(8,128)(2,1)S(1)}, bf16[512,128]{1,0:T(8,128)(2,1)S(1)}, u32[]{:S(2)}, u32[]{:S(2)}) collective-permute-start(bf16[512,128]{1,0:T(8,128)(2,1)S(1)} %collective-permute-done.20.refs_7_), channel_id=1, source_target_pairs={{0,1},{1,2},{2,3},{3,4},{4,5},{5,6},{6,7},{7,0},{8,9},{9,10},{10,1... | collective-permute-start | bytes 393224 | tf_op jit(solution)/shard_map/ppermute | solution.py:246
  100.8 22.9 %collective-permute-start.25 = (bf16[896,256]{1,0:T(8,128)(2,1)}, bf16[896,256]{1,0:T(8,128)(2,1)}, u32[]{:S(2)}, u32[]{:S(2)}) collective-permute-start(bf16[896,256]{1,0:T(8,128)(2,1)} %get-tuple-element.94.refs_0_), channel_id=1, source_target_pairs={{0,8},{8,16},{16,24},{24,0},{1,9},{9,17},{17,25},{25,1},{2,10},{10... | collective-permute-start | bytes 1376264 | tf_op jit(solution)/shard_map/ppermute | solution.py:246
  101.5 22.2 %collective-permute-start.24 = (bf16[896,256]{1,0:T(8,128)(2,1)}, bf16[896,256]{1,0:T(8,128)(2,1)}, u32[]{:S(2)}, u32[]{:S(2)}) collective-permute-start(bf16[896,256]{1,0:T(8,128)(2,1)} %collective-permute-done.23.refs_1_), channel_id=1, source_target_pairs={{0,24},{8,0},{16,8},{24,16},{1,25},{9,1},{17,9},{25,17},{2,26},{10... | collective-permute-start | bytes 1376264 | tf_op jit(solution)/shard_map/ppermute | solution.py:246
  104.1 5.6 %collective-permute-start.11 = (bf16[512,128]{1,0:T(8,128)(2,1)S(1)}, bf16[512,128]{1,0:T(8,128)(2,1)S(1)}, u32[]{:S(2)}, u32[]{:S(2)}) collective-permute-start(bf16[512,128]{1,0:T(8,128)(2,1)S(1)} %collective-permute-done.10.refs_2_), channel_id=1, source_target_pairs={{0,7},{1,0},{2,1},{3,2},{4,3},{5,4},{6,5},{7,6},{8,15},{9,8},{10,9... | collective-permute-start | bytes 393224 | tf_op jit(solution)/shard_map/ppermute | solution.py:246
  105.4 6.7 %collective-permute-start.18 = (bf16[512,128]{1,0:T(8,128)(2,1)S(1)}, bf16[512,128]{1,0:T(8,128)(2,1)S(1)}, u32[]{:S(2)}, u32[]{:S(2)}) collective-permute-start(bf16[512,128]{1,0:T(8,128)(2,1)S(1)} %collective-permute-done.17.refs_2_), channel_id=1, source_target_pairs={{0,7},{1,0},{2,1},{3,2},{4,3},{5,4},{6,5},{7,6},{8,15},{9,8},{10,9... | collective-permute-start | bytes 393224 | tf_op jit(solution)/shard_map/ppermute | solution.py:246
  109.7 6.0 %collective-permute-start.15 = (bf16[512,128]{1,0:T(8,128)(2,1)S(1)}, bf16[512,128]{1,0:T(8,128)(2,1)S(1)}, u32[]{:S(2)}, u32[]{:S(2)}) collective-permute-start(bf16[512,128]{1,0:T(8,128)(2,1)S(1)} %collective-permute-done.14.refs_6_), channel_id=1, source_target_pairs={{0,1},{1,2},{2,3},{3,4},{4,5},{5,6},{6,7},{7,0},{8,9},{9,10},{10,1... | collective-permute-start | bytes 393224 | tf_op jit(solution)/shard_map/ppermute | solution.py:246
  112.1 6.5 %collective-permute-start.22 = (bf16[512,128]{1,0:T(8,128)(2,1)S(1)}, bf16[512,128]{1,0:T(8,128)(2,1)S(1)}, u32[]{:S(2)}, u32[]{:S(2)}) collective-permute-start(bf16[512,128]{1,0:T(8,128)(2,1)S(1)} %collective-permute-done.21.refs_6_), channel_id=1, source_target_pairs={{0,1},{1,2},{2,3},{3,4},{4,5},{5,6},{6,7},{7,0},{8,9},{9,10},{10,1... | collective-permute-start | bytes 393224 | tf_op jit(solution)/shard_map/ppermute | solution.py:246
  115.7 5.5 %collective-permute-start.12 = (bf16[512,128]{1,0:T(8,128)(2,1)S(1)}, bf16[512,128]{1,0:T(8,128)(2,1)S(1)}, u32[]{:S(2)}, u32[]{:S(2)}) collective-permute-start(bf16[512,128]{1,0:T(8,128)(2,1)S(1)} %collective-permute-done.11.refs_3_), channel_id=1, source_target_pairs={{0,7},{1,0},{2,1},{3,2},{4,3},{5,4},{6,5},{7,6},{8,15},{9,8},{10,9... | collective-permute-start | bytes 393224 | tf_op jit(solution)/shard_map/ppermute | solution.py:246
  131.2 28.1 %all-to-all-start.2 = ((bf16[8,32,896]{2,1,0:T(8,128)(2,1)}), bf16[8,32,896]{2,1,0:T(8,128)(2,1)S(1)}, u32[]{:S(2)}, u32[]{:S(2)}) async-start(bf16[8,32,896]{2,1,0:T(8,128)(2,1)} %bitcast.24), calls=%async_computation.2 | async-start | bytes 917504 | tf_op jit(solution)/shard_map/all_to_all | solution.py:333
  141.5 10.3 %collective-permute-start.30 = (bf16[512,128]{1,0:T(8,128)(2,1)}, bf16[512,128]{1,0:T(8,128)(2,1)S(1)}, u32[]{:S(2)}, u32[]{:S(2)}) collective-permute-start(bf16[512,128]{1,0:T(8,128)(2,1)} %get-tuple-element.117), channel_id=1, source_target_pairs={{0,8},{8,16},{16,24},{24,0},{1,9},{9,17},{17,25},{25,1},{2,10},{10... | collective-permute-start | bytes 393224 | tf_op jit(solution)/shard_map/ppermute | solution.py:246
  141.6 12.7 %collective-permute-start.31 = (bf16[512,128]{1,0:T(8,128)(2,1)}, bf16[512,128]{1,0:T(8,128)(2,1)S(1)}, u32[]{:S(2)}, u32[]{:S(2)}) collective-permute-start(bf16[512,128]{1,0:T(8,128)(2,1)} %get-tuple-element.118), channel_id=1, source_target_pairs={{0,16},{8,24},{16,0},{24,8},{1,17},{9,25},{17,1},{25,9},{2,18},{10... | collective-permute-start | bytes 393224 | tf_op jit(solution)/shard_map/ppermute | solution.py:246
  143.3 11.0 %collective-permute-start.32 = (bf16[512,128]{1,0:T(8,128)(2,1)}, bf16[512,128]{1,0:T(8,128)(2,1)S(1)}, u32[]{:S(2)}, u32[]{:S(2)}) collective-permute-start(bf16[512,128]{1,0:T(8,128)(2,1)} %get-tuple-element.119), channel_id=1, source_target_pairs={{0,24},{8,0},{16,8},{24,16},{1,25},{9,1},{17,9},{25,17},{2,26},{10... | collective-permute-start | bytes 393224 | tf_op jit(solution)/shard_map/ppermute | solution.py:246
  148.9 7.9 %collective-permute-start.27 = (bf16[512,128]{1,0:T(8,128)(2,1)}, bf16[512,128]{1,0:T(8,128)(2,1)S(1)}, u32[]{:S(2)}, u32[]{:S(2)}) collective-permute-start(bf16[512,128]{1,0:T(8,128)(2,1)} %get-tuple-element.105), channel_id=1, source_target_pairs={{0,8},{8,16},{16,24},{24,0},{1,9},{9,17},{17,25},{25,1},{2,10},{10... | collective-permute-start | bytes 393224 | tf_op jit(solution)/shard_map/ppermute | solution.py:246
  149.7 7.2 %collective-permute-start.28 = (bf16[512,128]{1,0:T(8,128)(2,1)}, bf16[512,128]{1,0:T(8,128)(2,1)S(1)}, u32[]{:S(2)}, u32[]{:S(2)}) collective-permute-start(bf16[512,128]{1,0:T(8,128)(2,1)} %get-tuple-element.106), channel_id=1, source_target_pairs={{0,16},{8,24},{16,0},{24,8},{1,17},{9,25},{17,1},{25,9},{2,18},{10... | collective-permute-start | bytes 393224 | tf_op jit(solution)/shard_map/ppermute | solution.py:246
  151.8 5.9 %collective-permute-start.29 = (bf16[512,128]{1,0:T(8,128)(2,1)}, bf16[512,128]{1,0:T(8,128)(2,1)S(1)}, u32[]{:S(2)}, u32[]{:S(2)}) collective-permute-start(bf16[512,128]{1,0:T(8,128)(2,1)} %get-tuple-element.107), channel_id=1, source_target_pairs={{0,24},{8,0},{16,8},{24,16},{1,25},{9,1},{17,9},{25,17},{2,26},{10... | collective-permute-start | bytes 393224 | tf_op jit(solution)/shard_map/ppermute | solution.py:246
  (31 other events, 536.3 us)

commit v2 on v1

--- a/solution.py
+++ b/solution.py
@@ -14,7 +14,7 @@
 NT = (((1,), (1,)), ((), ()))
 TN = (((0,), (0,)), ((), ()))
 HEAD = 16
-VMEM_LIMIT = 60 * 1024 * 1024
+VMEM_LIMIT = 63 * 1024 * 1024
 
 
 def params():
@@ -48,8 +48,8 @@
             out_ref[rows, n * DH : (n + 1) * DH] = kv_ref[n, pl.ds(s, seg, stride=stored), :].astype(BF)
     lane = lax.broadcasted_iota(jnp.int32, (HEAD, 2 * DH), 1)
     row = jnp.zeros((HEAD, 2 * DH), F32)
-    for r in range(2 * ids_ref.shape[0]):
-        row = jnp.where(lane == r, ids_ref[r // 2, r % 2].astype(F32), row)
+    for r in range(2 * ids_ref.shape[1]):
+        row = jnp.where(lane == r, ids_ref[r % 2, r // 2].astype(F32), row)
     out_ref[:HEAD, :] = row.astype(BF)
 
 
@@ -113,7 +113,7 @@
             all_ids_ref[pl.ds(owner, 1), :] = row[:1, :]
 
     def place(r):
-        i = ids_ref[r // 2, r % 2]
+        i = ids_ref[r % 2, r // 2]
         owner, slot = i // stored, lax.rem(i, stored)
         dx = lax.rem(owner // 2 - my_x + n_x, n_x)
         dc = lax.rem(lax.rem(owner, 2) + my_c, 2)
@@ -239,7 +239,7 @@
     seg = encoded.shape[1] // enc_width
     block_len = rows // blocks
     piece = seg // n_y
-    core = lax.axis_index("c")
+    ids = neighbours.T
     place = jnp.stack([lax.axis_index(a) for a in ("x", "c", "y", "z")]).astype(jnp.int32)
 
     def shift(axis, n, k):
@@ -256,7 +256,7 @@
         (jax.ShapeDtypeStruct((HEAD + stored * seg, 2 * DH), BF), jax.ShapeDtypeStruct((enc_width, 2 * DH), BF)),
         "svvv", 470_000_000, 3 << 20,
         scratch=(pltpu.VMEM((2, seg * stored, DH), F32),),
-    )(neighbours, enc_rows, w_key, w_value)
+    )(ids, enc_rows, w_key, w_value)
     after, before, kv_other = x_up(kv), x_down(kv), swap(kv)
 
     w_query_, w_out_, kv_other = tie((w_query, w_out, kv_other))
@@ -265,7 +265,9 @@
         jax.ShapeDtypeStruct((n_z, n_y, DH, DH), BF), "saa", 0, 2 << 20,
         scratch=(pltpu.SemaphoreType.DMA((n_z * n_y,)),),
     )(place, w_out_, w_query_)
-    after, before, mine = tie((after, before, mine))
+    y_up, y_down = shift("y", n_y, -1), shift("y", n_y, 1)
+    pair_up, pair_down = y_up(pair), y_down(pair)
+    after, before, mine, pair_up, pair_down = tie((after, before, mine, pair_up, pair_down))
     mine = lax.all_to_all(mine, "z", 0, 0, tiled=True)
 
     cut = HEAD + stored // 2 * seg
@@ -275,16 +277,13 @@
         "aa", 0, 1 << 20, scratch=(pltpu.SemaphoreType.DMA((2,)),),
     )(after, before)
     far_lo, far_hi = x_up(next_lo), x_down(next_hi)
-    pair_, far_lo, far_hi = tie((pair, far_lo, far_hi))
     kv_all = [kv, after, far_lo, far_hi, before, kv_other] + [swap(a) for a in (after, far_lo, far_hi, before)]
-
-    y_up, y_down = shift("y", n_y, -1), shift("y", n_y, 1)
-    pair_up, pair_down = y_up(pair_), y_down(pair_)
     pairs = [pair, pair_up, y_up(pair_up), pair_down]
 
     queries = jnp.dot(hidden, w_query, preferred_element_type=F32).astype(BF)
     grad_attn = lax.dot_general(cotangent, w_out, NT, preferred_element_type=F32).astype(BF)
 
+    queries, grad_attn, pairs = tie((queries, grad_attn, pairs))
     other = swap(mine)
 
     slab = jax.ShapeDtypeStruct((rows, DH), BF)
@@ -301,7 +300,7 @@
             pltpu.VMEM((owners, kv.shape[0], 2 * DH), BF),
             pltpu.SemaphoreType.DMA((len(kv_all),)),
         ),
-    )(place, neighbours, queries, grad_attn, *kv_all)
+    )(place, ids, queries, grad_attn, *kv_all)
 
     def ring(own):
         pieces = {0: own}

time: 162 us -> 129 us (0.80)
  waiting for transfers between devices: 48.1 us -> 21 us
  local copies, waits for them, and re-layouts: 5.16 us -> 2.38 us
    ppermute x33, waiting for transfers between devices: 47.1 us -> 20.2 us  [shift(): return lambda a: lax.ppermute(a, axis, [(i, (i + k) % n) for i in range(n)])]
    unnamed x55 -> x46, local copies, waits for them, and re-layouts: 5.16 us -> 2.38 us
    dot_general x1, matrix products: 4.39 us -> 1.91 us  [shards(): lax.dot_general(cotangent, w_out, NT, preferred_element_type=F32).astype(BF)]
    ppermute x33, starting transfers between devices: 43.8 us -> 42 us  [shift(): return lambda a: lax.ppermute(a, axis, [(i, (i + k) % n) for i in range(n)])]
  transfers between devices with their start and end apart: 36 -> 36, of which waited for: 13 -> 13; matrix products, arithmetic and copies ran while one was open for 7% -> 8% of each run, Pallas kernels for 17% -> 21%
where the time goes in v2:
time: 129 us; the launch traced here: 128 us
  starting transfers between devices  63.2 us (49%)
  Pallas kernels  29.8 us (23%)
  waiting for transfers between devices  21 us (16%)
  matrix products  6.3 us (5%)
  other arithmetic  4.61 us (4%)
  local copies, waits for them, and re-layouts  2.38 us (2%)
    ppermute x33, starting transfers between devices, shift(): return lambda a: lax.ppermute(a, axis, [(i, (i + k) % n) for i in range(n)])  42 us
    ppermute x33, waiting for transfers between devices, shift(): return lambda a: lax.ppermute(a, axis, [(i, (i + k) % n) for i in range(n)])  20.2 us
    all_to_all x1, starting transfers between devices, shards(): mine = lax.all_to_all(mine, 'z', 0, 0, tiled=True)  8.58 us
    pallas_call x1, Pallas kernels, shards(): call(functools.partial(attention_body, (blocks, block_len, n_x, n_y, cap,...  7.93 us
    pallas_call x2, Pallas kernels, summed(): call(functools.partial(head_sum_body, n_z, n_y, second), (jax.ShapeDtypeS...  7.67 us
    all_to_all x1, starting transfers between devices, shards(): lax.all_to_all(enc_part.reshape(n_z, -1, enc_width), 'z', 0, 0, tiled=True)  6.47 us
    all_to_all x1, starting transfers between devices, shards(): lax.all_to_all(outgoing.reshape(owners * n_y, cap, piece, 2 * DH), dp + (...  6.14 us
    pallas_call x1, Pallas kernels, shards(): call(functools.partial(encoded_body, stored), jax.ShapeDtypeStruct((piece...  5.98 us
  transfers between devices with their start and end apart: 36, of which 13 were waited for; matrix products, arithmetic and copies ran while one was open for 8% of the time, Pallas kernels for 21%

profile of v2, /device:TPU:32, one launch (start us, length us, event | category | flops | bytes accessed | tf_op | source)
XLA Modules:
  0.0 128.2 jit_solution(18018749377960902728)
XLA Ops:
  0.6 3.2 %shard_map.103 = (bf16[1040,256]{1,0:T(8,128)(2,1)}, bf16[896,256]{1,0:T(8,128)(2,1)}) custom-call(s32[2,8]{1,0:T(2,128)} %bitcast.26, bf16[1024,896]{1,0:T(8,128)(2,1)} %bitcast.23, bf16[896,128]{1,0:T(8,128)(2,1)} %wk_ref.1, bf16[896,128]{1,0:T(8,128)(2,1)} %wv_ref.1), custom_call_target="tpu_custom_call" | custom-call | flops 470000000 | bytes 3145728 | tf_op jit(solution)/shard_map/pallas_call | solution.py:254
  3.9 1.5 %collective-permute-start.1 = (bf16[1040,256]{1,0:T(8,128)(2,1)}, bf16[1040,256]{1,0:T(8,128)(2,1)S(1)}, u32[]{:S(2)}, u32[]{:S(2)}) collective-permute-start(bf16[1040,256]{1,0:T(8,128)(2,1)} %get-tuple-element.68.refs_0_), channel_id=1, source_target_pairs={{0,64},{64,128},{128,192},{192,0},{1,65},{65,129},{129,193},{193,1... | collective-permute-start | bytes 1597448 | tf_op jit(solution)/shard_map/ppermute | solution.py:246
  5.4 1.7 %collective-permute-start = (bf16[1040,256]{1,0:T(8,128)(2,1)}, bf16[1040,256]{1,0:T(8,128)(2,1)}, u32[]{:S(2)}, u32[]{:S(2)}) collective-permute-start(bf16[1040,256]{1,0:T(8,128)(2,1)} %get-tuple-element.68.refs_0_), channel_id=1, source_target_pairs={{0,192},{64,0},{128,64},{192,128},{1,193},{65,1},{129,65},{193,129... | collective-permute-start | bytes 1597448 | tf_op jit(solution)/shard_map/ppermute | solution.py:246
  7.1 1.6 %collective-permute-start.4 = (bf16[896,256]{1,0:T(8,128)(2,1)}, bf16[896,256]{1,0:T(8,128)(2,1)}, u32[]{:S(2)}, u32[]{:S(2)}) collective-permute-start(bf16[896,256]{1,0:T(8,128)(2,1)} %get-tuple-element.101.refs_0_), channel_id=1, source_target_pairs={{0,8},{8,16},{16,24},{24,0},{1,9},{9,17},{17,25},{25,1},{2,10},{10... | collective-permute-start | bytes 1376264 | tf_op jit(solution)/shard_map/ppermute | solution.py:246
  8.7 1.7 %collective-permute-start.3 = (bf16[896,256]{1,0:T(8,128)(2,1)}, bf16[896,256]{1,0:T(8,128)(2,1)}, u32[]{:S(2)}, u32[]{:S(2)}) collective-permute-start(bf16[896,256]{1,0:T(8,128)(2,1)} %get-tuple-element.101.refs_0_), channel_id=1, source_target_pairs={{0,24},{8,0},{16,8},{24,16},{1,25},{9,1},{17,9},{25,17},{2,26},{10... | collective-permute-start | bytes 1376264 | tf_op jit(solution)/shard_map/ppermute | solution.py:246
  10.9 3.1 %shard_map.104 = bf16[8,4,128,128]{3,2,1,0:T(8,128)(2,1)} custom-call(s32[4]{0:T(128)} %pad_add_fusion.pos_ref, bf16[128,4096]{1,0:T(8,128)(2,1)} %wo_ref, bf16[4096,128]{1,0:T(8,128)(2,1)} %wq_ref), custom_call_target="tpu_custom_call" | custom-call | bytes 2097152 | tf_op jit(solution)/shard_map/pallas_call | solution.py:263
  14.1 7.0 %collective-permute-done.4.refs_3_ = bf16[896,256]{1,0:T(8,128)(2,1)} collective-permute-done((bf16[896,256]{1,0:T(8,128)(2,1)}, bf16[896,256]{1,0:T(8,128)(2,1)}, u32[]{:S(2)}, u32[]{:S(2)}) %collective-permute-start.4) | collective-permute-done | bytes 458784 | tf_op jit(solution)/shard_map/ppermute | solution.py:246
  21.1 8.6 %all-to-all-start.1 = ((bf16[8,4,128,128]{3,2,1,0:T(8,128)(2,1)}), bf16[8,4,128,128]{3,2,1,0:T(8,128)(2,1)}, u32[]{:S(2)}, u32[]{:S(2)}) async-start(bf16[8,4,128,128]{3,2,1,0:T(8,128)(2,1)} %shard_map.104), calls=%async_computation.1 | async-start | bytes 2097152 | tf_op jit(solution)/shard_map/all_to_all | solution.py:271
  29.7 1.9 %shard_map.105 = (bf16[528,256]{1,0:T(8,128)(2,1)}, bf16[512,256]{1,0:T(8,128)(2,1)}) custom-call(bf16[1040,256]{1,0:T(8,128)(2,1)} %collective-permute-done.after_ref.refs_1_, bf16[1040,256]{1,0:T(8,128)(2,1)} %copy-done), custom_call_target="tpu_custom_call" | custom-call | bytes 1048576 | tf_op jit(solution)/shard_map/pallas_call | solution.py:274
  32.2 2.9 %collective-permute-start.5 = (bf16[896,256]{1,0:T(8,128)(2,1)}, bf16[896,256]{1,0:T(8,128)(2,1)S(1)}, u32[]{:S(2)}, u32[]{:S(2)}) collective-permute-start(bf16[896,256]{1,0:T(8,128)(2,1)} %collective-permute-done.3.refs_1_), channel_id=1, source_target_pairs={{0,24},{8,0},{16,8},{24,16},{1,25},{9,1},{17,9},{25,17},{2,26},{10... | collective-permute-start | bytes 1376264 | tf_op jit(solution)/shard_map/ppermute | solution.py:246
  35.5 2.9 %collective-permute-start.6 = (bf16[528,256]{1,0:T(8,128)(2,1)}, bf16[528,256]{1,0:T(8,128)(2,1)S(1)}, u32[]{:S(2)}, u32[]{:S(2)}) collective-permute-start(bf16[528,256]{1,0:T(8,128)(2,1)} %get-tuple-element.77), channel_id=1, source_target_pairs={{0,192},{64,0},{128,64},{192,128},{1,193},{65,1},{129,65},{193,129... | collective-permute-start | bytes 811016 | tf_op jit(solution)/shard_map/ppermute | solution.py:246
  38.3 4.4 %convolution_convert_fusion.1.q_ref = bf16[512,128]{1,0:T(8,128)(2,1)} fusion(bf16[512,4096]{1,0:T(8,128)(2,1)} %param.8, bf16[4096,128]{1,0:T(8,128)(2,1)} %wq_ref), kind=kOutput, calls=%fused_computation.1 | convolution fusion | flops 536936448 | bytes 5373952 | tf_op jit(solution)/shard_map/dot_general | solution.py:283
  42.7 1.8 %collective-permute-done.7.refs_3_ = bf16[512,256]{1,0:T(8,128)(2,1)S(1)} collective-permute-done((bf16[512,256]{1,0:T(8,128)(2,1)}, bf16[512,256]{1,0:T(8,128)(2,1)S(1)}, u32[]{:S(2)}, u32[]{:S(2)}) %collective-permute-start.7) | collective-permute-done | bytes 262176 | tf_op jit(solution)/shard_map/ppermute | solution.py:246
  45.1 1.9 %convolution_convert_fusion.g_ref = bf16[512,128]{1,0:T(8,128)(2,1)} fusion(bf16[512,4096]{1,0:T(8,128)(2,1)S(1)} %copy-done.22, bf16[128,4096]{1,0:T(8,128)(2,1)S(1)} %copy-done.1), kind=kOutput, calls=%fused_computation | convolution fusion | flops 536936448 | bytes 5373952 | tf_op jit(solution)/shard_map/dot_general | solution.py:284
  48.7 7.9 %shard_map.106 = (bf16[512,128]{1,0:T(8,128)(2,1)}, bf16[512,128]{1,0:T(8,128)(2,1)}, bf16[8,4,4,32,256]{4,3,2,1,0:T(8,128)(2,1)}, s32[8,128]{1,0:T(8,128)}) custom-call(s32[4]{0:T(128)} %pad_add_fusion.pos_ref, s32[2,8]{1,0:T(2,128)} %bitcast.27, bf16[512,128]{1,0:T(8,128)(2,1)} %convolution_convert_fusion.1.q_ref, ...), custom_call_target="tpu_custom_call" | custom-call | flops 500000000 | bytes 7340032 | tf_op jit(solution)/shard_map/pallas_call | solution.py:290
  56.7 6.1 %all-to-all-start = ((bf16[32,4,32,256]{3,2,1,0:T(8,128)(2,1)}), bf16[32,4,32,256]{3,2,1,0:T(8,128)(2,1)}, u32[]{:S(2)}, u32[]{:S(2)}) async-start(bf16[32,4,32,256]{3,2,1,0:T(8,128)(2,1)} %bitcast.22), calls=%async_computation | async-start | bytes 4194304 | tf_op jit(solution)/shard_map/all_to_all | solution.py:315
  67.2 2.3 %collective-permute-done.12.refs_1_ = bf16[512,128]{1,0:T(8,128)(2,1)S(1)} collective-permute-done((bf16[512,128]{1,0:T(8,128)(2,1)S(1)}, bf16[512,128]{1,0:T(8,128)(2,1)S(1)}, u32[]{:S(2)}, u32[]{:S(2)}) %collective-permute-start.12) | collective-permute-done | bytes 131104 | tf_op jit(solution)/shard_map/ppermute | solution.py:246
  77.2 2.5 %collective-permute-start.21 = (bf16[512,128]{1,0:T(8,128)(2,1)S(1)}, bf16[512,128]{1,0:T(8,128)(2,1)S(1)}, u32[]{:S(2)}, u32[]{:S(2)}) collective-permute-start(bf16[512,128]{1,0:T(8,128)(2,1)S(1)} %collective-permute-done.20.refs_2_), channel_id=1, source_target_pairs={{0,7},{1,0},{2,1},{3,2},{4,3},{5,4},{6,5},{7,6},{8,15},{9,8},{10,9... | collective-permute-start | bytes 393224 | tf_op jit(solution)/shard_map/ppermute | solution.py:246
  81.0 1.5 %collective-permute-start.25 = (bf16[512,128]{1,0:T(8,128)(2,1)S(1)}, bf16[512,128]{1,0:T(8,128)(2,1)S(1)}, u32[]{:S(2)}, u32[]{:S(2)}) collective-permute-start(bf16[512,128]{1,0:T(8,128)(2,1)S(1)} %collective-permute-done.24.refs_6_), channel_id=1, source_target_pairs={{0,1},{1,2},{2,3},{3,4},{4,5},{5,6},{6,7},{7,0},{8,9},{9,10},{10,1... | collective-permute-start | bytes 393224 | tf_op jit(solution)/shard_map/ppermute | solution.py:246
  82.5 1.5 %collective-permute-start.15 = (bf16[512,128]{1,0:T(8,128)(2,1)S(1)}, bf16[512,128]{1,0:T(8,128)(2,1)S(1)}, u32[]{:S(2)}, u32[]{:S(2)}) collective-permute-start(bf16[512,128]{1,0:T(8,128)(2,1)S(1)} %collective-permute-done.14.refs_3_), channel_id=1, source_target_pairs={{0,7},{1,0},{2,1},{3,2},{4,3},{5,4},{6,5},{7,6},{8,15},{9,8},{10,9... | collective-permute-start | bytes 393224 | tf_op jit(solution)/shard_map/ppermute | solution.py:246
  84.1 3.1 %collective-permute-start.22 = (bf16[512,128]{1,0:T(8,128)(2,1)S(1)}, bf16[512,128]{1,0:T(8,128)(2,1)}, u32[]{:S(2)}, u32[]{:S(2)}) collective-permute-start(bf16[512,128]{1,0:T(8,128)(2,1)S(1)} %collective-permute-done.21.refs_3_), channel_id=1, source_target_pairs={{0,7},{1,0},{2,1},{3,2},{4,3},{5,4},{6,5},{7,6},{8,15},{9,8},{10,9... | collective-permute-start | bytes 393224 | tf_op jit(solution)/shard_map/ppermute | solution.py:246
  91.1 6.0 %shard_map.107 = bf16[256,896]{1,0:T(8,128)(2,1)} custom-call(s32[4]{0:T(128)} %pad_add_fusion.pos_ref, s32[8,128]{1,0:T(8,128)} %get-tuple-element.99.ids_ref, bf16[8,4,4,32,256]{4,3,2,1,0:T(8,128)(2,1)} %bitcast.9.ret_ref, bf16[896,256]{1,0:T(8,128)(2,1)} %get-tuple-element.101.refs_0_, bf16[896,256]{1,0:T(8,128)(2,1)} %collective-permute-done.3.refs_1_, ...), custom_call_target="tpu_custom_call" | custom-call | flops 500000000 | bytes 5242880 | tf_op jit(solution)/shard_map/pallas_call | solution.py:320
  97.1 6.5 %all-to-all-start.2 = ((bf16[8,32,896]{2,1,0:T(8,128)(2,1)}), bf16[8,32,896]{2,1,0:T(8,128)(2,1)S(1)}, u32[]{:S(2)}, u32[]{:S(2)}) async-start(bf16[8,32,896]{2,1,0:T(8,128)(2,1)} %bitcast.24), calls=%async_computation.2 | async-start | bytes 917504 | tf_op jit(solution)/shard_map/all_to_all | solution.py:332
  103.6 3.8 %shard_map.109 = (f32[512,128]{1,0:T(8,128)}, bf16[512,128]{1,0:T(8,128)(2,1)}, bf16[512,128]{1,0:T(8,128)(2,1)}, bf16[512,128]{1,0:T(8,128)(2,1)}) custom-call(s32[4]{0:T(128)} %pad_add_fusion.pos_ref, bf16[512,128]{1,0:T(8,128)(2,1)} %get-tuple-element.118.refs_0_, bf16[512,128]{1,0:T(8,128)(2,1)} %copy-done.13, bf16[512,128]{1,0:T(8,128)(2,1)} %copy-done.16, ...), custom_call_target="tpu_custom_call" | custom-call | flops 540000000 | bytes 3145728 | tf_op jit(solution)/shard_map/pallas_call | solution.py:337
  107.5 1.6 %collective-permute-start.30 = (bf16[512,128]{1,0:T(8,128)(2,1)}, bf16[512,128]{1,0:T(8,128)(2,1)S(1)}, u32[]{:S(2)}, u32[]{:S(2)}) collective-permute-start(bf16[512,128]{1,0:T(8,128)(2,1)} %get-tuple-element.127), channel_id=1, source_target_pairs={{0,8},{8,16},{16,24},{24,0},{1,9},{9,17},{17,25},{25,1},{2,10},{10... | collective-permute-start | bytes 393224 | tf_op jit(solution)/shard_map/ppermute | solution.py:246
  109.1 2.7 %collective-permute-start.31 = (bf16[512,128]{1,0:T(8,128)(2,1)}, bf16[512,128]{1,0:T(8,128)(2,1)S(1)}, u32[]{:S(2)}, u32[]{:S(2)}) collective-permute-start(bf16[512,128]{1,0:T(8,128)(2,1)} %get-tuple-element.128), channel_id=1, source_target_pairs={{0,16},{8,24},{16,0},{24,8},{1,17},{9,25},{17,1},{25,9},{2,18},{10... | collective-permute-start | bytes 393224 | tf_op jit(solution)/shard_map/ppermute | solution.py:246
  111.8 1.5 %collective-permute-start.32 = (bf16[512,128]{1,0:T(8,128)(2,1)}, bf16[512,128]{1,0:T(8,128)(2,1)S(1)}, u32[]{:S(2)}, u32[]{:S(2)}) collective-permute-start(bf16[512,128]{1,0:T(8,128)(2,1)} %get-tuple-element.129), channel_id=1, source_target_pairs={{0,24},{8,0},{16,8},{24,16},{1,25},{9,1},{17,9},{25,17},{2,26},{10... | collective-permute-start | bytes 393224 | tf_op jit(solution)/shard_map/ppermute | solution.py:246
  113.2 3.8 %shard_map.108 = (f32[512,128]{1,0:T(8,128)}, bf16[512,128]{1,0:T(8,128)(2,1)}, bf16[512,128]{1,0:T(8,128)(2,1)}, bf16[512,128]{1,0:T(8,128)(2,1)}) custom-call(s32[4]{0:T(128)} %pad_add_fusion.pos_ref, bf16[512,128]{1,0:T(8,128)(2,1)} %get-tuple-element.105.refs_0_, bf16[512,128]{1,0:T(8,128)(2,1)} %copy-done.9, bf16[512,128]{1,0:T(8,128)(2,1)} %copy-done.11, ...), custom_call_target="tpu_custom_call" | custom-call | flops 540000000 | bytes 3145728 | tf_op jit(solution)/shard_map/pallas_call | solution.py:337
  118.6 1.9 %collective-permute-start.29 = (bf16[512,128]{1,0:T(8,128)(2,1)}, bf16[512,128]{1,0:T(8,128)(2,1)S(1)}, u32[]{:S(2)}, u32[]{:S(2)}) collective-permute-start(bf16[512,128]{1,0:T(8,128)(2,1)} %get-tuple-element.117), channel_id=1, source_target_pairs={{0,24},{8,0},{16,8},{24,16},{1,25},{9,1},{17,9},{25,17},{2,26},{10... | collective-permute-start | bytes 393224 | tf_op jit(solution)/shard_map/ppermute | solution.py:246
  120.5 1.7 %add_convert_fusion = bf16[512,128]{1,0:T(8,128)(2,1)} fusion(bf16[512,128]{1,0:T(8,128)(2,1)S(1)} %collective-permute-done.32, bf16[512,128]{1,0:T(8,128)(2,1)S(1)} %collective-permute-done.31, f32[512,128]{1,0:T(8,128)} %get-tuple-element.126, bf16[512,128]{1,0:T(8,128)(2,1)S(1)} %collective-permute-done.30), kind=kLoop, calls=%fused_computation.2 | loop fusion | flops 458752 | bytes 786432 | tf_op jit(solution)/shard_map/convert_element_type | solution.py:350
  122.2 2.8 %collective-permute-done.27 = bf16[512,128]{1,0:T(8,128)(2,1)S(1)} collective-permute-done((bf16[512,128]{1,0:T(8,128)(2,1)}, bf16[512,128]{1,0:T(8,128)(2,1)S(1)}, u32[]{:S(2)}, u32[]{:S(2)}) %collective-permute-start.27) | collective-permute-done | bytes 131104 | tf_op jit(solution)/shard_map/ppermute | solution.py:246
  125.9 1.7 %add_convert_fusion.1 = bf16[512,128]{1,0:T(8,128)(2,1)} fusion(bf16[512,128]{1,0:T(8,128)(2,1)S(1)} %collective-permute-done.29, bf16[512,128]{1,0:T(8,128)(2,1)S(1)} %collective-permute-done.28, f32[512,128]{1,0:T(8,128)} %get-tuple-element.114, bf16[512,128]{1,0:T(8,128)(2,1)S(1)} %collective-permute-done.27), kind=kLoop, calls=%fused_computation.3 | loop fusion | flops 458752 | bytes 786432 | tf_op jit(solution)/shard_map/convert_element_type | solution.py:350
  (99 shorter events, 24.2 us)
Async XLA Ops:
  3.9 7.1 %collective-permute-start.2 = (bf16[1040,256]{1,0:T(8,128)(2,1)}, bf16[1040,256]{1,0:T(8,128)(2,1)}, u32[]{:S(2)}, u32[]{:S(2)}) collective-permute-start(bf16[1040,256]{1,0:T(8,128)(2,1)} %get-tuple-element.68.refs_0_), channel_id=1, source_target_pairs={{0,32},{32,0},{1,33},{33,1},{2,34},{34,2},{3,35},{35,3},{4,36},{36... | collective-permute-start | bytes 1597448 | tf_op jit(solution)/shard_map/ppermute | solution.py:246
  3.9 17.2 %collective-permute-start.1 = (bf16[1040,256]{1,0:T(8,128)(2,1)}, bf16[1040,256]{1,0:T(8,128)(2,1)S(1)}, u32[]{:S(2)}, u32[]{:S(2)}) collective-permute-start(bf16[1040,256]{1,0:T(8,128)(2,1)} %get-tuple-element.68.refs_0_), channel_id=1, source_target_pairs={{0,64},{64,128},{128,192},{192,0},{1,65},{65,129},{129,193},{193,1... | collective-permute-start | bytes 1597448 | tf_op jit(solution)/shard_map/ppermute | solution.py:246
  5.4 15.7 %collective-permute-start = (bf16[1040,256]{1,0:T(8,128)(2,1)}, bf16[1040,256]{1,0:T(8,128)(2,1)}, u32[]{:S(2)}, u32[]{:S(2)}) collective-permute-start(bf16[1040,256]{1,0:T(8,128)(2,1)} %get-tuple-element.68.refs_0_), channel_id=1, source_target_pairs={{0,192},{64,0},{128,64},{192,128},{1,193},{65,1},{129,65},{193,129... | collective-permute-start | bytes 1597448 | tf_op jit(solution)/shard_map/ppermute | solution.py:246
  7.1 14.0 %collective-permute-start.4 = (bf16[896,256]{1,0:T(8,128)(2,1)}, bf16[896,256]{1,0:T(8,128)(2,1)}, u32[]{:S(2)}, u32[]{:S(2)}) collective-permute-start(bf16[896,256]{1,0:T(8,128)(2,1)} %get-tuple-element.101.refs_0_), channel_id=1, source_target_pairs={{0,8},{8,16},{16,24},{24,0},{1,9},{9,17},{17,25},{25,1},{2,10},{10... | collective-permute-start | bytes 1376264 | tf_op jit(solution)/shard_map/ppermute | solution.py:246
  8.7 12.4 %collective-permute-start.3 = (bf16[896,256]{1,0:T(8,128)(2,1)}, bf16[896,256]{1,0:T(8,128)(2,1)}, u32[]{:S(2)}, u32[]{:S(2)}) collective-permute-start(bf16[896,256]{1,0:T(8,128)(2,1)} %get-tuple-element.101.refs_0_), channel_id=1, source_target_pairs={{0,24},{8,0},{16,8},{24,16},{1,25},{9,1},{17,9},{25,17},{2,26},{10... | collective-permute-start | bytes 1376264 | tf_op jit(solution)/shard_map/ppermute | solution.py:246
  21.1 35.6 %all-to-all-start.1 = ((bf16[8,4,128,128]{3,2,1,0:T(8,128)(2,1)}), bf16[8,4,128,128]{3,2,1,0:T(8,128)(2,1)}, u32[]{:S(2)}, u32[]{:S(2)}) async-start(bf16[8,4,128,128]{3,2,1,0:T(8,128)(2,1)} %shard_map.104), calls=%async_computation.1 | async-start | bytes 2097152 | tf_op jit(solution)/shard_map/all_to_all | solution.py:271
  29.7 17.3 %collective-permute-start.8 = (bf16[1040,256]{1,0:T(8,128)(2,1)}, bf16[1040,256]{1,0:T(8,128)(2,1)}, u32[]{:S(2)}, u32[]{:S(2)}) collective-permute-start(bf16[1040,256]{1,0:T(8,128)(2,1)} %collective-permute-done.after_ref.refs_1_), channel_id=1, source_target_pairs={{0,32},{32,0},{1,33},{33,1},{2,34},{34,2},{3,35},{35,3},{4,36},{36... | collective-permute-start | bytes 1597448 | tf_op jit(solution)/shard_map/ppermute | solution.py:246
  31.6 15.4 %collective-permute-start.11 = (bf16[1040,256]{1,0:T(8,128)(2,1)}, bf16[1040,256]{1,0:T(8,128)(2,1)S(1)}, u32[]{:S(2)}, u32[]{:S(2)}) collective-permute-start(bf16[1040,256]{1,0:T(8,128)(2,1)} %copy-done), channel_id=1, source_target_pairs={{0,32},{32,0},{1,33},{33,1},{2,34},{34,2},{3,35},{35,3},{4,36},{36... | collective-permute-start | bytes 1597448 | tf_op jit(solution)/shard_map/ppermute | solution.py:246
  32.2 14.8 %collective-permute-start.5 = (bf16[896,256]{1,0:T(8,128)(2,1)}, bf16[896,256]{1,0:T(8,128)(2,1)S(1)}, u32[]{:S(2)}, u32[]{:S(2)}) collective-permute-start(bf16[896,256]{1,0:T(8,128)(2,1)} %collective-permute-done.3.refs_1_), channel_id=1, source_target_pairs={{0,24},{8,0},{16,8},{24,16},{1,25},{9,1},{17,9},{25,17},{2,26},{10... | collective-permute-start | bytes 1376264 | tf_op jit(solution)/shard_map/ppermute | solution.py:246
  35.1 9.4 %collective-permute-start.7 = (bf16[512,256]{1,0:T(8,128)(2,1)}, bf16[512,256]{1,0:T(8,128)(2,1)S(1)}, u32[]{:S(2)}, u32[]{:S(2)}) collective-permute-start(bf16[512,256]{1,0:T(8,128)(2,1)} %get-tuple-element.78), channel_id=1, source_target_pairs={{0,64},{64,128},{128,192},{192,0},{1,65},{65,129},{129,193},{193,1... | collective-permute-start | bytes 786440 | tf_op jit(solution)/shard_map/ppermute | solution.py:246
  35.5 9.1 %collective-permute-start.6 = (bf16[528,256]{1,0:T(8,128)(2,1)}, bf16[528,256]{1,0:T(8,128)(2,1)S(1)}, u32[]{:S(2)}, u32[]{:S(2)}) collective-permute-start(bf16[528,256]{1,0:T(8,128)(2,1)} %get-tuple-element.77), channel_id=1, source_target_pairs={{0,192},{64,0},{128,64},{192,128},{1,193},{65,1},{129,65},{193,129... | collective-permute-start | bytes 811016 | tf_op jit(solution)/shard_map/ppermute | solution.py:246
  56.7 34.5 %all-to-all-start = ((bf16[32,4,32,256]{3,2,1,0:T(8,128)(2,1)}), bf16[32,4,32,256]{3,2,1,0:T(8,128)(2,1)}, u32[]{:S(2)}, u32[]{:S(2)}) async-start(bf16[32,4,32,256]{3,2,1,0:T(8,128)(2,1)} %bitcast.22), calls=%async_computation | async-start | bytes 4194304 | tf_op jit(solution)/shard_map/all_to_all | solution.py:315
  62.8 40.8 %collective-permute-start.26 = (bf16[8,4,128,128]{3,2,1,0:T(8,128)(2,1)}, bf16[8,4,128,128]{3,2,1,0:T(8,128)(2,1)}, u32[]{:S(2)}, u32[]{:S(2)}) collective-permute-start(bf16[8,4,128,128]{3,2,1,0:T(8,128)(2,1)} %all-to-all-done.1.refs_8_), channel_id=1, source_target_pairs={{0,32},{32,0},{1,33},{33,1},{2,34},{34,2},{3,35},{35,3},{4,36},{36... | collective-permute-start | bytes 3145736 | tf_op jit(solution)/shard_map/ppermute | solution.py:246
  63.1 6.3 %collective-permute-start.12 = (bf16[512,128]{1,0:T(8,128)(2,1)S(1)}, bf16[512,128]{1,0:T(8,128)(2,1)S(1)}, u32[]{:S(2)}, u32[]{:S(2)}) collective-permute-start(bf16[512,128]{1,0:T(8,128)(2,1)S(1)} %copy-done.7), channel_id=1, source_target_pairs={{0,7},{1,0},{2,1},{3,2},{4,3},{5,4},{6,5},{7,6},{8,15},{9,8},{10,9... | collective-permute-start | bytes 393224 | tf_op jit(solution)/shard_map/ppermute | solution.py:246
  64.6 7.6 %collective-permute-start.19 = (bf16[512,128]{1,0:T(8,128)(2,1)S(1)}, bf16[512,128]{1,0:T(8,128)(2,1)S(1)}, u32[]{:S(2)}, u32[]{:S(2)}) collective-permute-start(bf16[512,128]{1,0:T(8,128)(2,1)S(1)} %copy-done.8), channel_id=1, source_target_pairs={{0,7},{1,0},{2,1},{3,2},{4,3},{5,4},{6,5},{7,6},{8,15},{9,8},{10,9... | collective-permute-start | bytes 393224 | tf_op jit(solution)/shard_map/ppermute | solution.py:246
  65.5 8.2 %collective-permute-start.16 = (bf16[512,128]{1,0:T(8,128)(2,1)S(1)}, bf16[512,128]{1,0:T(8,128)(2,1)S(1)}, u32[]{:S(2)}, u32[]{:S(2)}) collective-permute-start(bf16[512,128]{1,0:T(8,128)(2,1)S(1)} %copy-done.7), channel_id=1, source_target_pairs={{0,1},{1,2},{2,3},{3,4},{4,5},{5,6},{6,7},{7,0},{8,9},{9,10},{10,1... | collective-permute-start | bytes 393224 | tf_op jit(solution)/shard_map/ppermute | solution.py:246
  66.6 7.6 %collective-permute-start.23 = (bf16[512,128]{1,0:T(8,128)(2,1)S(1)}, bf16[512,128]{1,0:T(8,128)(2,1)S(1)}, u32[]{:S(2)}, u32[]{:S(2)}) collective-permute-start(bf16[512,128]{1,0:T(8,128)(2,1)S(1)} %copy-done.8), channel_id=1, source_target_pairs={{0,1},{1,2},{2,3},{3,4},{4,5},{5,6},{6,7},{7,0},{8,9},{9,10},{10,1... | collective-permute-start | bytes 393224 | tf_op jit(solution)/shard_map/ppermute | solution.py:246
  73.6 6.2 %collective-permute-start.17 = (bf16[512,128]{1,0:T(8,128)(2,1)S(1)}, bf16[512,128]{1,0:T(8,128)(2,1)S(1)}, u32[]{:S(2)}, u32[]{:S(2)}) collective-permute-start(bf16[512,128]{1,0:T(8,128)(2,1)S(1)} %collective-permute-done.16.refs_7_), channel_id=1, source_target_pairs={{0,1},{1,2},{2,3},{3,4},{4,5},{5,6},{6,7},{7,0},{8,9},{9,10},{10,1... | collective-permute-start | bytes 393224 | tf_op jit(solution)/shard_map/ppermute | solution.py:246
  74.2 6.8 %collective-permute-start.24 = (bf16[512,128]{1,0:T(8,128)(2,1)S(1)}, bf16[512,128]{1,0:T(8,128)(2,1)S(1)}, u32[]{:S(2)}, u32[]{:S(2)}) collective-permute-start(bf16[512,128]{1,0:T(8,128)(2,1)S(1)} %collective-permute-done.23.refs_7_), channel_id=1, source_target_pairs={{0,1},{1,2},{2,3},{3,4},{4,5},{5,6},{6,7},{7,0},{8,9},{9,10},{10,1... | collective-permute-start | bytes 393224 | tf_op jit(solution)/shard_map/ppermute | solution.py:246
  75.1 7.5 %collective-permute-start.14 = (bf16[512,128]{1,0:T(8,128)(2,1)S(1)}, bf16[512,128]{1,0:T(8,128)(2,1)S(1)}, u32[]{:S(2)}, u32[]{:S(2)}) collective-permute-start(bf16[512,128]{1,0:T(8,128)(2,1)S(1)} %collective-permute-done.13.refs_2_), channel_id=1, source_target_pairs={{0,7},{1,0},{2,1},{3,2},{4,3},{5,4},{6,5},{7,6},{8,15},{9,8},{10,9... | collective-permute-start | bytes 393224 | tf_op jit(solution)/shard_map/ppermute | solution.py:246
  77.2 6.8 %collective-permute-start.21 = (bf16[512,128]{1,0:T(8,128)(2,1)S(1)}, bf16[512,128]{1,0:T(8,128)(2,1)S(1)}, u32[]{:S(2)}, u32[]{:S(2)}) collective-permute-start(bf16[512,128]{1,0:T(8,128)(2,1)S(1)} %collective-permute-done.20.refs_2_), channel_id=1, source_target_pairs={{0,7},{1,0},{2,1},{3,2},{4,3},{5,4},{6,5},{7,6},{8,15},{9,8},{10,9... | collective-permute-start | bytes 393224 | tf_op jit(solution)/shard_map/ppermute | solution.py:246
  79.8 7.4 %collective-permute-start.18 = (bf16[512,128]{1,0:T(8,128)(2,1)S(1)}, bf16[512,128]{1,0:T(8,128)(2,1)S(1)}, u32[]{:S(2)}, u32[]{:S(2)}) collective-permute-start(bf16[512,128]{1,0:T(8,128)(2,1)S(1)} %collective-permute-done.17.refs_6_), channel_id=1, source_target_pairs={{0,1},{1,2},{2,3},{3,4},{4,5},{5,6},{6,7},{7,0},{8,9},{9,10},{10,1... | collective-permute-start | bytes 393224 | tf_op jit(solution)/shard_map/ppermute | solution.py:246
  81.0 6.8 %collective-permute-start.25 = (bf16[512,128]{1,0:T(8,128)(2,1)S(1)}, bf16[512,128]{1,0:T(8,128)(2,1)S(1)}, u32[]{:S(2)}, u32[]{:S(2)}) collective-permute-start(bf16[512,128]{1,0:T(8,128)(2,1)S(1)} %collective-permute-done.24.refs_6_), channel_id=1, source_target_pairs={{0,1},{1,2},{2,3},{3,4},{4,5},{5,6},{6,7},{7,0},{8,9},{9,10},{10,1... | collective-permute-start | bytes 393224 | tf_op jit(solution)/shard_map/ppermute | solution.py:246
  82.5 6.3 %collective-permute-start.15 = (bf16[512,128]{1,0:T(8,128)(2,1)S(1)}, bf16[512,128]{1,0:T(8,128)(2,1)S(1)}, u32[]{:S(2)}, u32[]{:S(2)}) collective-permute-start(bf16[512,128]{1,0:T(8,128)(2,1)S(1)} %collective-permute-done.14.refs_3_), channel_id=1, source_target_pairs={{0,7},{1,0},{2,1},{3,2},{4,3},{5,4},{6,5},{7,6},{8,15},{9,8},{10,9... | collective-permute-start | bytes 393224 | tf_op jit(solution)/shard_map/ppermute | solution.py:246
  84.1 6.3 %collective-permute-start.22 = (bf16[512,128]{1,0:T(8,128)(2,1)S(1)}, bf16[512,128]{1,0:T(8,128)(2,1)}, u32[]{:S(2)}, u32[]{:S(2)}) collective-permute-start(bf16[512,128]{1,0:T(8,128)(2,1)S(1)} %collective-permute-done.21.refs_3_), channel_id=1, source_target_pairs={{0,7},{1,0},{2,1},{3,2},{4,3},{5,4},{6,5},{7,6},{8,15},{9,8},{10,9... | collective-permute-start | bytes 393224 | tf_op jit(solution)/shard_map/ppermute | solution.py:246
  97.1 30.4 %all-to-all-start.2 = ((bf16[8,32,896]{2,1,0:T(8,128)(2,1)}), bf16[8,32,896]{2,1,0:T(8,128)(2,1)S(1)}, u32[]{:S(2)}, u32[]{:S(2)}) async-start(bf16[8,32,896]{2,1,0:T(8,128)(2,1)} %bitcast.24), calls=%async_computation.2 | async-start | bytes 917504 | tf_op jit(solution)/shard_map/all_to_all | solution.py:332
  107.5 11.2 %collective-permute-start.30 = (bf16[512,128]{1,0:T(8,128)(2,1)}, bf16[512,128]{1,0:T(8,128)(2,1)S(1)}, u32[]{:S(2)}, u32[]{:S(2)}) collective-permute-start(bf16[512,128]{1,0:T(8,128)(2,1)} %get-tuple-element.127), channel_id=1, source_target_pairs={{0,8},{8,16},{16,24},{24,0},{1,9},{9,17},{17,25},{25,1},{2,10},{10... | collective-permute-start | bytes 393224 | tf_op jit(solution)/shard_map/ppermute | solution.py:246
  109.1 11.4 %collective-permute-start.31 = (bf16[512,128]{1,0:T(8,128)(2,1)}, bf16[512,128]{1,0:T(8,128)(2,1)S(1)}, u32[]{:S(2)}, u32[]{:S(2)}) collective-permute-start(bf16[512,128]{1,0:T(8,128)(2,1)} %get-tuple-element.128), channel_id=1, source_target_pairs={{0,16},{8,24},{16,0},{24,8},{1,17},{9,25},{17,1},{25,9},{2,18},{10... | collective-permute-start | bytes 393224 | tf_op jit(solution)/shard_map/ppermute | solution.py:246
  111.8 8.7 %collective-permute-start.32 = (bf16[512,128]{1,0:T(8,128)(2,1)}, bf16[512,128]{1,0:T(8,128)(2,1)S(1)}, u32[]{:S(2)}, u32[]{:S(2)}) collective-permute-start(bf16[512,128]{1,0:T(8,128)(2,1)} %get-tuple-element.129), channel_id=1, source_target_pairs={{0,24},{8,0},{16,8},{24,16},{1,25},{9,1},{17,9},{25,17},{2,26},{10... | collective-permute-start | bytes 393224 | tf_op jit(solution)/shard_map/ppermute | solution.py:246
  117.1 7.9 %collective-permute-start.27 = (bf16[512,128]{1,0:T(8,128)(2,1)}, bf16[512,128]{1,0:T(8,128)(2,1)S(1)}, u32[]{:S(2)}, u32[]{:S(2)}) collective-permute-start(bf16[512,128]{1,0:T(8,128)(2,1)} %get-tuple-element.115), channel_id=1, source_target_pairs={{0,8},{8,16},{16,24},{24,0},{1,9},{9,17},{17,25},{25,1},{2,10},{10... | collective-permute-start | bytes 393224 | tf_op jit(solution)/shard_map/ppermute | solution.py:246
  117.7 7.2 %collective-permute-start.28 = (bf16[512,128]{1,0:T(8,128)(2,1)}, bf16[512,128]{1,0:T(8,128)(2,1)S(1)}, u32[]{:S(2)}, u32[]{:S(2)}) collective-permute-start(bf16[512,128]{1,0:T(8,128)(2,1)} %get-tuple-element.116), channel_id=1, source_target_pairs={{0,16},{8,24},{16,0},{24,8},{1,17},{9,25},{17,1},{25,9},{2,18},{10... | collective-permute-start | bytes 393224 | tf_op jit(solution)/shard_map/ppermute | solution.py:246
  118.6 7.2 %collective-permute-start.29 = (bf16[512,128]{1,0:T(8,128)(2,1)}, bf16[512,128]{1,0:T(8,128)(2,1)S(1)}, u32[]{:S(2)}, u32[]{:S(2)}) collective-permute-start(bf16[512,128]{1,0:T(8,128)(2,1)} %get-tuple-element.117), channel_id=1, source_target_pairs={{0,24},{8,0},{16,8},{24,16},{1,25},{9,1},{17,9},{25,17},{2,26},{10... | collective-permute-start | bytes 393224 | tf_op jit(solution)/shard_map/ppermute | solution.py:246
  (27 other events, 256.1 us)

commit v3 on v2

--- a/solution.py
+++ b/solution.py
@@ -24,19 +24,39 @@
 def call(body, out_shape, in_spaces, flops, moved, scratch=(), out_space="v"):
     spaces = {"s": pltpu.SMEM, "v": pltpu.VMEM, "a": pltpu.HBM}
     single = not isinstance(out_shape, (tuple, list))
-    out = pl.BlockSpec(memory_space=spaces[out_space])
+    outs = [out_shape] if single else out_shape
+    out = tuple(pl.BlockSpec(memory_space=spaces[k]) for k in out_space * (len(outs) if len(out_space) == 1 else 1))
     return pl.pallas_call(
         body,
         out_shape=out_shape,
         in_specs=[pl.BlockSpec(memory_space=spaces[k]) for k in in_spaces],
-        out_specs=out if single else (out,) * len(out_shape),
+        out_specs=out[0] if single else out,
         scratch_shapes=list(scratch),
         compiler_params=params(),
         cost_estimate=pl.CostEstimate(flops=flops, bytes_accessed=moved, transcendentals=0),
     )
 
 
-def keys_values_body(stored, ids_ref, x_ref, wk_ref, wv_ref, out_ref, pair_ref, kv_ref):
+def keys_values_body(stored, n_z, n_y, pos_ref, ids_ref, x_ref, wk_ref, wv_ref, wo_ref, wq_ref, out_ref, pair_ref, w_ref, kv_ref, sem):
+    def moved(block):
+        return [
+            pltpu.make_async_copy(block((y * n_z + z) * DH), w_ref.at[z, y], sem.at[y * n_z + z])
+            for y in range(n_y)
+            for z in range(n_z)
+        ]
+
+    copies = moved(lambda at: wq_ref.at[at : at + DH, :])
+
+    @pl.when(pos_ref[1] == 0)
+    def _():
+        for copy in moved(lambda at: wo_ref.at[:, at : at + DH]):
+            copy.start()
+
+    @pl.when(pos_ref[1] != 0)
+    def _():
+        for copy in copies:
+            copy.start()
+
     pair = jnp.concatenate([wk_ref[...], wv_ref[...]], axis=1)
     pair_ref[...] = pair
     seg = x_ref.shape[0] // stored
@@ -46,6 +66,8 @@
         for s in range(stored):
             rows = slice(HEAD + s * seg, HEAD + (s + 1) * seg)
             out_ref[rows, n * DH : (n + 1) * DH] = kv_ref[n, pl.ds(s, seg, stride=stored), :].astype(BF)
+    for copy in copies:
+        copy.wait()
     lane = lax.broadcasted_iota(jnp.int32, (HEAD, 2 * DH), 1)
     row = jnp.zeros((HEAD, 2 * DH), F32)
     for r in range(2 * ids_ref.shape[1]):
@@ -64,64 +86,44 @@
         copy.wait()
 
 
-def weights_body(n_z, n_y, pos_ref, wo_ref, wq_ref, out_ref, sem):
-    def move(block):
-        copies = [
-            pltpu.make_async_copy(block((y * n_z + z) * DH), out_ref.at[z, y], sem.at[y * n_z + z])
-            for y in range(n_y)
-            for z in range(n_z)
-        ]
-        for copy in copies:
-            copy.start()
-        for copy in copies:
-            copy.wait()
-
-    @pl.when(pos_ref[1] == 0)
-    def _():
-        move(lambda at: wo_ref.at[:, at : at + DH])
-
-    @pl.when(pos_ref[1] != 0)
-    def _():
-        move(lambda at: wq_ref.at[at : at + DH, :])
-
-
 def attention_body(geom, pos_ref, ids_ref, q_ref, g_ref, *refs):
     blocks, block_len, n_x, n_y, cap, stored, seg = geom
-    kv_refs, (attn_ref, gq_ref, out_ref, all_ids_ref, kv_ref, sem) = refs[:-6], refs[-6:]
+    kv_refs, (attn_ref, gq_ref, out_ref, all_ids_ref, kv_ref, stage_ref, head_ref, sem) = refs[:-8], refs[-8:]
     inv_root = 1.0 / math.sqrt(DH)
     piece = seg // n_y
+    cut = HEAD + stored // 2 * seg
     my_x, my_c = pos_ref[0], pos_ref[1]
-    copies = []
-    for i, ref in enumerate(kv_refs):
-        c, k = i // 5, i % 5
-        cut = HEAD + stored // 2 * seg
-        if k < 2:
-            to = kv_ref.at[c * n_x + k]
-        elif k == 4:
-            to = kv_ref.at[c * n_x + 3]
-        else:
-            to = kv_ref.at[c * n_x + 2, :cut] if k == 2 else kv_ref.at[c * n_x + 2, cut:]
-        copies.append(pltpu.make_async_copy(ref, to, sem.at[i]))
-        copies[-1].start()
-    out_ref[...] = jnp.zeros_like(out_ref)
-    for copy in copies:
-        copy.wait()
-    for c in range(2):
-        for d in range(n_x):
-            owner = lax.rem(my_x + d, n_x) * 2 + lax.rem(my_c + c, 2)
-            row = kv_ref[c * n_x + d, :HEAD, :DH].astype(F32).astype(jnp.int32)
-            all_ids_ref[pl.ds(owner, 1), :] = row[:1, :]
-
-    def place(r):
+    requests = 2 * blocks
+    parts = len(kv_refs) // 2
+
+    spots = []
+    for r in range(requests):
         i = ids_ref[r % 2, r // 2]
         owner, slot = i // stored, lax.rem(i, stored)
         dx = lax.rem(owner // 2 - my_x + n_x, n_x)
         dc = lax.rem(lax.rem(owner, 2) + my_c, 2)
-        return owner, dc * n_x + dx, pl.multiple_of(HEAD + slot * seg, HEAD)
-
-    spots = [place(r) for r in range(2 * blocks)]
+        part = dx + jnp.where(dx == 3, 1, jnp.where((dx == 2) & (slot >= stored // 2), 1, 0))
+        row = HEAD + slot * seg - jnp.where(part == 3, cut, 0)
+        row = pl.multiple_of(row, HEAD)
+        spots.append(owner)
+        for k, ref in enumerate(kv_refs):
+
+            @pl.when(dc * parts + part == k)
+            def _(ref=ref, row=row, r=r):
+                pltpu.make_async_copy(ref.at[pl.ds(row, seg), :], kv_ref.at[r], sem.at[r]).start()
+
+    heads = [(c, d) for c in range(2) for d in range(n_x)]
+    head_copies = []
+    for i, (c, d) in enumerate(heads):
+        ref = kv_refs[c * parts + (4 if d == 3 else d)]
+        head_copies.append(pltpu.make_async_copy(ref.at[:HEAD, :DH], head_ref.at[i], sem.at[requests + i]))
+        head_copies[-1].start()
+
+    sent = []
+    for r in range(requests):
+        pltpu.make_async_copy(kv_refs[0].at[:seg, :], kv_ref.at[r], sem.at[r]).wait()
     for c in range(blocks):
-        both = [kv_ref[spots[r][1], pl.ds(spots[r][2], seg), :] for r in (2 * c, 2 * c + 1)]
+        both = [kv_ref[r] for r in (2 * c, 2 * c + 1)]
         k = jnp.concatenate([b[:, :DH] for b in both], axis=0)
         v = jnp.concatenate([b[:, DH:] for b in both], axis=0)
         rows = slice(c * block_len, (c + 1) * block_len)
@@ -139,12 +141,22 @@
         gk = (lax.dot_general(gs, q, TN, preferred_element_type=F32) * inv_root).astype(BF)
         for j in range(2):
             r = 2 * c + j
-            owner = spots[r][0]
-            pos = sum([(spots[i][0] == owner).astype(jnp.int32) for i in range(r)], jnp.int32(0))
+            owner = spots[r]
+            pos = sum([(spots[i] == owner).astype(jnp.int32) for i in range(r)], jnp.int32(0))
             for y in range(n_y):
                 part = slice(j * seg + y * piece, j * seg + (y + 1) * piece)
-                out_ref[owner, y, pos, :, :DH] = gk[part, :]
-                out_ref[owner, y, pos, :, DH:] = gv[part, :]
+                stage_ref[r, y, :, :DH] = gk[part, :]
+                stage_ref[r, y, :, DH:] = gv[part, :]
+            sent.append(
+                pltpu.make_async_copy(stage_ref.at[r], out_ref.at[owner, :, pos], sem.at[requests + len(heads) + r])
+            )
+            sent[-1].start()
+    for i, (c, d) in enumerate(heads):
+        head_copies[i].wait()
+        owner = lax.rem(my_x + d, n_x) * 2 + lax.rem(my_c + c, 2)
+        all_ids_ref[pl.ds(owner, 1), :] = head_ref[i].astype(F32).astype(jnp.int32)[:1, :]
+    for copy in sent:
+        copy.wait()
 
 
 def encoded_body(stored, pos_ref, ids_ref, ret_ref, *refs):
@@ -251,39 +263,37 @@
     tie = lax.optimization_barrier
 
     enc_rows = encoded.reshape(stored, seg, enc_width).transpose(1, 0, 2).reshape(seg * stored, enc_width)
-    kv, pair = call(
-        functools.partial(keys_values_body, stored),
-        (jax.ShapeDtypeStruct((HEAD + stored * seg, 2 * DH), BF), jax.ShapeDtypeStruct((enc_width, 2 * DH), BF)),
-        "svvv", 470_000_000, 3 << 20,
-        scratch=(pltpu.VMEM((2, seg * stored, DH), F32),),
-    )(ids, enc_rows, w_key, w_value)
+    kv, pair, mine = call(
+        functools.partial(keys_values_body, stored, n_z, n_y),
+        (
+            jax.ShapeDtypeStruct((HEAD + stored * seg, 2 * DH), BF),
+            jax.ShapeDtypeStruct((enc_width, 2 * DH), BF),
+            jax.ShapeDtypeStruct((n_z, n_y, DH, DH), BF),
+        ),
+        "ssvvvaa", 470_000_000, 5 << 20,
+        scratch=(pltpu.VMEM((2, seg * stored, DH), F32), pltpu.SemaphoreType.DMA((n_z * n_y,))),
+    )(place, ids, enc_rows, w_key, w_value, w_out, w_query)
     after, before, kv_other = x_up(kv), x_down(kv), swap(kv)
-
-    w_query_, w_out_, kv_other = tie((w_query, w_out, kv_other))
-    mine = call(
-        functools.partial(weights_body, n_z, n_y),
-        jax.ShapeDtypeStruct((n_z, n_y, DH, DH), BF), "saa", 0, 2 << 20,
-        scratch=(pltpu.SemaphoreType.DMA((n_z * n_y,)),),
-    )(place, w_out_, w_query_)
+    mine = lax.all_to_all(mine, "z", 0, 0, tiled=True)
     y_up, y_down = shift("y", n_y, -1), shift("y", n_y, 1)
     pair_up, pair_down = y_up(pair), y_down(pair)
-    after, before, mine, pair_up, pair_down = tie((after, before, mine, pair_up, pair_down))
-    mine = lax.all_to_all(mine, "z", 0, 0, tiled=True)
+    queries = jnp.dot(hidden, w_query, preferred_element_type=F32).astype(BF)
+    grad_attn = lax.dot_general(cotangent, w_out, NT, preferred_element_type=F32).astype(BF)
+    after, before, pair_up, pair_down, queries, grad_attn = tie(
+        (after, before, pair_up, pair_down, queries, grad_attn)
+    )
 
     cut = HEAD + stored // 2 * seg
     next_lo, next_hi = call(
         functools.partial(halves_body, cut),
         (jax.ShapeDtypeStruct((cut, 2 * DH), BF), jax.ShapeDtypeStruct((kv.shape[0] - cut, 2 * DH), BF)),
-        "aa", 0, 1 << 20, scratch=(pltpu.SemaphoreType.DMA((2,)),),
+        "aa", 0, 0, scratch=(pltpu.SemaphoreType.DMA((2,)),),
     )(after, before)
     far_lo, far_hi = x_up(next_lo), x_down(next_hi)
     kv_all = [kv, after, far_lo, far_hi, before, kv_other] + [swap(a) for a in (after, far_lo, far_hi, before)]
     pairs = [pair, pair_up, y_up(pair_up), pair_down]
 
-    queries = jnp.dot(hidden, w_query, preferred_element_type=F32).astype(BF)
-    grad_attn = lax.dot_general(cotangent, w_out, NT, preferred_element_type=F32).astype(BF)
-
-    queries, grad_attn, pairs = tie((queries, grad_attn, pairs))
+    queries, pairs = tie((queries, pairs))
     other = swap(mine)
 
     slab = jax.ShapeDtypeStruct((rows, DH), BF)
@@ -295,11 +305,14 @@
             jax.ShapeDtypeStruct((owners, n_y, cap, piece, 2 * DH), BF),
             jax.ShapeDtypeStruct((owners, DH), jnp.int32),
         ),
-        "ssvv" + "a" * len(kv_all), 500_000_000, 7 << 20,
+        "ssvv" + "a" * len(kv_all), 0, 0,
         scratch=(
-            pltpu.VMEM((owners, kv.shape[0], 2 * DH), BF),
-            pltpu.SemaphoreType.DMA((len(kv_all),)),
+            pltpu.VMEM((blocks * per_block, seg, 2 * DH), BF),
+            pltpu.VMEM((blocks * per_block, n_y, piece, 2 * DH), BF),
+            pltpu.VMEM((owners, HEAD, DH), BF),
+            pltpu.SemaphoreType.DMA((2 * blocks * per_block + owners,)),
         ),
+        out_space="vvav",
     )(place, ids, queries, grad_attn, *kv_all)
 
     def ring(own):
@@ -316,7 +329,9 @@
         outgoing.reshape(owners * n_y, cap, piece, 2 * DH), dp + ("y",), 0, 0, tiled=True
     ).reshape(owners, n_y, cap, piece, 2 * DH)
     attn_all, gq_all = ring(attn), ring(gq)
-    attn_all, gq_all, returned = tie((attn_all, gq_all, returned))
+    last = n_z // 2
+    early = [a for ring_ in (attn_all, gq_all) for k, a in enumerate(ring_) if k != last]
+    _, returned = tie((early, returned))
     enc_part = call(
         functools.partial(encoded_body, stored),
         jax.ShapeDtypeStruct((piece * stored, enc_width), BF), "ssa" + "a" * n_y, 500_000_000, 5 << 20,

time: 129 us -> 128 us (level)
  Pallas kernels: 29.8 us -> 27.6 us
    pallas_call x2 -> x1, Pallas kernels: 6.35 us -> 4.52 us  [shards(): call(functools.partial(keys_values_body, stored, n_z, n_y), (jax.ShapeDty...]
    all_to_all x1, waiting for transfers between devices: 0.79 us -> 2.51 us  [shards(): lax.all_to_all(outgoing.reshape(owners * n_y, cap, piece, 2 * DH), dp + (...]
    ppermute x33, starting transfers between devices: 42 us -> 40.5 us  [shift(): return lambda a: lax.ppermute(a, axis, [(i, (i + k) % n) for i in range(n)])]
  transfers between devices with their start and end apart: 36 -> 36, of which waited for: 13 -> 16; matrix products, arithmetic and copies ran while one was open for 8% -> 8% of each run, Pallas kernels for 21% -> 18%
where the time goes in v3:
time: 128 us; the launch traced here: 127 us
  starting transfers between devices  63.5 us (50%)
  Pallas kernels  27.6 us (22%)
  waiting for transfers between devices  22 us (17%)
  matrix products  6.31 us (5%)
  other arithmetic  4.64 us (4%)
  local copies, waits for them, and re-layouts  2.28 us (2%)
    ppermute x33, starting transfers between devices, shift(): return lambda a: lax.ppermute(a, axis, [(i, (i + k) % n) for i in range(n)])  40.5 us
    ppermute x33, waiting for transfers between devices, shift(): return lambda a: lax.ppermute(a, axis, [(i, (i + k) % n) for i in range(n)])  19.5 us
    all_to_all x1, starting transfers between devices, shards(): mine = lax.all_to_all(mine, 'z', 0, 0, tiled=True)  8.71 us
    pallas_call x2, Pallas kernels, summed(): call(functools.partial(head_sum_body, n_z, n_y, second), (jax.ShapeDtypeS...  7.68 us
    pallas_call x1, Pallas kernels, shards(): call(functools.partial(attention_body, (blocks, block_len, n_x, n_y, cap,...  7.43 us
    all_to_all x1, starting transfers between devices, shards(): lax.all_to_all(enc_part.reshape(n_z, -1, enc_width), 'z', 0, 0, tiled=True)  7.23 us
    all_to_all x1, starting transfers between devices, shards(): lax.all_to_all(outgoing.reshape(owners * n_y, cap, piece, 2 * DH), dp + (...  7.05 us
    pallas_call x1, Pallas kernels, shards(): call(functools.partial(encoded_body, stored), jax.ShapeDtypeStruct((piece...  6.14 us
  transfers between devices with their start and end apart: 36, of which 16 were waited for; matrix products, arithmetic and copies ran while one was open for 8% of the time, Pallas kernels for 18%

profile of v3, /device:TPU:32, one launch (start us, length us, event | category | flops | bytes accessed | tf_op | source)
XLA Modules:
  0.0 127.2 jit_solution(10480101806942265979)
XLA Ops:
  1.2 4.5 %shard_map.103 = (bf16[1040,256]{1,0:T(8,128)(2,1)}, bf16[896,256]{1,0:T(8,128)(2,1)}, bf16[8,4,128,128]{3,2,1,0:T(8,128)(2,1)}) custom-call(s32[4]{0:T(128)} %pad_add_fusion.pos_ref, s32[2,8]{1,0:T(2,128)} %bitcast.26, bf16[1024,896]{1,0:T(8,128)(2,1)} %bitcast.23, bf16[896,128]{1,0:T(8,128)(2,1)} %wk_ref.1, bf16[896,128]{1,0:T(8,128)(2,1)} %wv_ref.1, ...), custom_call_target="tpu_custom_call" | custom-call | flops 470000000 | bytes 5242880 | tf_op jit(solution)/shard_map/pallas_call | solution.py:266
  5.8 8.7 %all-to-all-start.1 = ((bf16[8,4,128,128]{3,2,1,0:T(8,128)(2,1)}), bf16[8,4,128,128]{3,2,1,0:T(8,128)(2,1)}, u32[]{:S(2)}, u32[]{:S(2)}) async-start(bf16[8,4,128,128]{3,2,1,0:T(8,128)(2,1)} %get-tuple-element.77), calls=%async_computation.1 | async-start | bytes 2097152 | tf_op jit(solution)/shard_map/all_to_all | solution.py:277
  14.5 1.6 %collective-permute-start.3 = (bf16[896,256]{1,0:T(8,128)(2,1)}, bf16[896,256]{1,0:T(8,128)(2,1)S(1)}, u32[]{:S(2)}, u32[]{:S(2)}) collective-permute-start(bf16[896,256]{1,0:T(8,128)(2,1)} %get-tuple-element.65.refs_0_), channel_id=1, source_target_pairs={{0,8},{8,16},{16,24},{24,0},{1,9},{9,17},{17,25},{25,1},{2,10},{10... | collective-permute-start | bytes 1376264 | tf_op jit(solution)/shard_map/ppermute | solution.py:258
  16.1 1.7 %collective-permute-start.2 = (bf16[896,256]{1,0:T(8,128)(2,1)}, bf16[896,256]{1,0:T(8,128)(2,1)S(1)}, u32[]{:S(2)}, u32[]{:S(2)}) collective-permute-start(bf16[896,256]{1,0:T(8,128)(2,1)} %get-tuple-element.65.refs_0_), channel_id=1, source_target_pairs={{0,24},{8,0},{16,8},{24,16},{1,25},{9,1},{17,9},{25,17},{2,26},{10... | collective-permute-start | bytes 1376264 | tf_op jit(solution)/shard_map/ppermute | solution.py:258
  19.2 1.7 %collective-permute-start = (bf16[1040,256]{1,0:T(8,128)(2,1)}, bf16[1040,256]{1,0:T(8,128)(2,1)}, u32[]{:S(2)}, u32[]{:S(2)}) collective-permute-start(bf16[1040,256]{1,0:T(8,128)(2,1)} %get-tuple-element.49.refs_0_), channel_id=1, source_target_pairs={{0,192},{64,0},{128,64},{192,128},{1,193},{65,1},{129,65},{193,129... | collective-permute-start | bytes 1597448 | tf_op jit(solution)/shard_map/ppermute | solution.py:258
  21.0 4.4 %convolution_convert_fusion.1.q_ref = bf16[512,128]{1,0:T(8,128)(2,1)} fusion(bf16[512,4096]{1,0:T(8,128)(2,1)} %param.8, bf16[4096,128]{1,0:T(8,128)(2,1)} %wq_ref.1), kind=kOutput, calls=%fused_computation.1 | convolution fusion | flops 536936448 | bytes 5373952 | tf_op jit(solution)/shard_map/dot_general | solution.py:280
  25.4 1.9 %convolution_convert_fusion.g_ref = bf16[512,128]{1,0:T(8,128)(2,1)} fusion(bf16[512,4096]{1,0:T(8,128)(2,1)S(1)} %copy-done.21, bf16[128,4096]{1,0:T(8,128)(2,1)S(1)} %copy-done.1), kind=kOutput, calls=%fused_computation | convolution fusion | flops 536936448 | bytes 5373952 | tf_op jit(solution)/shard_map/dot_general | solution.py:281
  27.7 4.3 %collective-permute-done.1.before_ref.refs_4_ = bf16[1040,256]{1,0:T(8,128)(2,1)S(1)} collective-permute-done((bf16[1040,256]{1,0:T(8,128)(2,1)}, bf16[1040,256]{1,0:T(8,128)(2,1)S(1)}, u32[]{:S(2)}, u32[]{:S(2)}) %collective-permute-start.1) | collective-permute-done | bytes 532512 | tf_op jit(solution)/shard_map/ppermute | solution.py:258
  32.8 1.9 %shard_map.104 = (bf16[528,256]{1,0:T(8,128)(2,1)}, bf16[512,256]{1,0:T(8,128)(2,1)}) custom-call(bf16[1040,256]{1,0:T(8,128)(2,1)} %collective-permute-done.after_ref.refs_1_, bf16[1040,256]{1,0:T(8,128)(2,1)} %copy-done), custom_call_target="tpu_custom_call" | custom-call | tf_op jit(solution)/shard_map/pallas_call | solution.py:287
  35.6 1.7 %collective-permute-start.4 = (bf16[896,256]{1,0:T(8,128)(2,1)}, bf16[896,256]{1,0:T(8,128)(2,1)S(1)}, u32[]{:S(2)}, u32[]{:S(2)}) collective-permute-start(bf16[896,256]{1,0:T(8,128)(2,1)} %copy-done.4), channel_id=1, source_target_pairs={{0,24},{8,0},{16,8},{24,16},{1,25},{9,1},{17,9},{25,17},{2,26},{10... | collective-permute-start | bytes 1376264 | tf_op jit(solution)/shard_map/ppermute | solution.py:258
  37.2 2.5 %collective-permute-start.5 = (bf16[528,256]{1,0:T(8,128)(2,1)}, bf16[528,256]{1,0:T(8,128)(2,1)S(1)}, u32[]{:S(2)}, u32[]{:S(2)}) collective-permute-start(bf16[528,256]{1,0:T(8,128)(2,1)} %get-tuple-element.58), channel_id=1, source_target_pairs={{0,192},{64,0},{128,64},{192,128},{1,193},{65,1},{129,65},{193,129... | collective-permute-start | bytes 811016 | tf_op jit(solution)/shard_map/ppermute | solution.py:258
  40.2 2.4 %collective-permute-done.6.refs_3_ = bf16[512,256]{1,0:T(8,128)(2,1)S(1)} collective-permute-done((bf16[512,256]{1,0:T(8,128)(2,1)}, bf16[512,256]{1,0:T(8,128)(2,1)S(1)}, u32[]{:S(2)}, u32[]{:S(2)}) %collective-permute-start.6) | collective-permute-done | bytes 262176 | tf_op jit(solution)/shard_map/ppermute | solution.py:258
  44.0 1.6 %collective-permute-done.4.refs_2_ = bf16[896,256]{1,0:T(8,128)(2,1)S(1)} collective-permute-done((bf16[896,256]{1,0:T(8,128)(2,1)}, bf16[896,256]{1,0:T(8,128)(2,1)S(1)}, u32[]{:S(2)}, u32[]{:S(2)}) %collective-permute-start.4) | collective-permute-done | bytes 458784 | tf_op jit(solution)/shard_map/ppermute | solution.py:258
  47.8 7.4 %shard_map.105 = (bf16[512,128]{1,0:T(8,128)(2,1)}, bf16[512,128]{1,0:T(8,128)(2,1)}, bf16[8,4,4,32,256]{4,3,2,1,0:T(8,128)(2,1)}, s32[8,128]{1,0:T(8,128)}) custom-call(s32[4]{0:T(128)} %pad_add_fusion.pos_ref, s32[2,8]{1,0:T(2,128)} %bitcast.27, bf16[512,128]{1,0:T(8,128)(2,1)} %convolution_convert_fusion.1.q_ref, ...), custom_call_target="tpu_custom_call" | custom-call | tf_op jit(solution)/shard_map/pallas_call | solution.py:300
  55.3 7.0 %all-to-all-start = ((bf16[32,4,32,256]{3,2,1,0:T(8,128)(2,1)}), bf16[32,4,32,256]{3,2,1,0:T(8,128)(2,1)}, u32[]{:S(2)}, u32[]{:S(2)}) async-start(bf16[32,4,32,256]{3,2,1,0:T(8,128)(2,1)} %bitcast.22), calls=%async_computation | async-start | bytes 4194304 | tf_op jit(solution)/shard_map/all_to_all | solution.py:328
  63.3 2.6 %collective-permute-start.19 = (bf16[512,128]{1,0:T(8,128)(2,1)S(1)}, bf16[512,128]{1,0:T(8,128)(2,1)S(1)}, u32[]{:S(2)}, u32[]{:S(2)}) collective-permute-start(bf16[512,128]{1,0:T(8,128)(2,1)S(1)} %copy-done.10), channel_id=1, source_target_pairs={{0,7},{1,0},{2,1},{3,2},{4,3},{5,4},{6,5},{7,6},{8,15},{9,8},{10,9... | collective-permute-start | bytes 393224 | tf_op jit(solution)/shard_map/ppermute | solution.py:258
  66.7 2.3 %collective-permute-done.12.refs_1_ = bf16[512,128]{1,0:T(8,128)(2,1)S(1)} collective-permute-done((bf16[512,128]{1,0:T(8,128)(2,1)S(1)}, bf16[512,128]{1,0:T(8,128)(2,1)S(1)}, u32[]{:S(2)}, u32[]{:S(2)}) %collective-permute-start.12) | collective-permute-done | bytes 131104 | tf_op jit(solution)/shard_map/ppermute | solution.py:258
  69.7 2.0 %collective-permute-done.19.refs_1_ = bf16[512,128]{1,0:T(8,128)(2,1)S(1)} collective-permute-done((bf16[512,128]{1,0:T(8,128)(2,1)S(1)}, bf16[512,128]{1,0:T(8,128)(2,1)S(1)}, u32[]{:S(2)}, u32[]{:S(2)}) %collective-permute-start.19) | collective-permute-done | bytes 131104 | tf_op jit(solution)/shard_map/ppermute | solution.py:258
  71.7 1.7 %collective-permute-start.20 = (bf16[512,128]{1,0:T(8,128)(2,1)S(1)}, bf16[512,128]{1,0:T(8,128)(2,1)S(1)}, u32[]{:S(2)}, u32[]{:S(2)}) collective-permute-start(bf16[512,128]{1,0:T(8,128)(2,1)S(1)} %collective-permute-done.19.refs_1_), channel_id=1, source_target_pairs={{0,7},{1,0},{2,1},{3,2},{4,3},{5,4},{6,5},{7,6},{8,15},{9,8},{10,9... | collective-permute-start | bytes 393224 | tf_op jit(solution)/shard_map/ppermute | solution.py:258
  76.8 3.4 %collective-permute-start.21 = (bf16[512,128]{1,0:T(8,128)(2,1)S(1)}, bf16[512,128]{1,0:T(8,128)(2,1)}, u32[]{:S(2)}, u32[]{:S(2)}) collective-permute-start(bf16[512,128]{1,0:T(8,128)(2,1)S(1)} %collective-permute-done.20.refs_2_), channel_id=1, source_target_pairs={{0,7},{1,0},{2,1},{3,2},{4,3},{5,4},{6,5},{7,6},{8,15},{9,8},{10,9... | collective-permute-start | bytes 393224 | tf_op jit(solution)/shard_map/ppermute | solution.py:258
  82.7 1.7 %collective-permute-start.15 = (bf16[512,128]{1,0:T(8,128)(2,1)S(1)}, bf16[512,128]{1,0:T(8,128)(2,1)}, u32[]{:S(2)}, u32[]{:S(2)}) collective-permute-start(bf16[512,128]{1,0:T(8,128)(2,1)S(1)} %collective-permute-done.14.refs_3_), channel_id=1, source_target_pairs={{0,7},{1,0},{2,1},{3,2},{4,3},{5,4},{6,5},{7,6},{8,15},{9,8},{10,9... | collective-permute-start | bytes 393224 | tf_op jit(solution)/shard_map/ppermute | solution.py:258
  84.5 3.1 %collective-permute-start.22 = (bf16[512,128]{1,0:T(8,128)(2,1)}, bf16[512,128]{1,0:T(8,128)(2,1)}, u32[]{:S(2)}, u32[]{:S(2)}) collective-permute-start(bf16[512,128]{1,0:T(8,128)(2,1)} %collective-permute-done.21.refs_3_), channel_id=1, source_target_pairs={{0,7},{1,0},{2,1},{3,2},{4,3},{5,4},{6,5},{7,6},{8,15},{9,8},{10,9... | collective-permute-start | bytes 393224 | tf_op jit(solution)/shard_map/ppermute | solution.py:258
  88.1 2.5 %all-to-all-done = bf16[32,4,32,256]{3,2,1,0:T(8,128)(2,1)} async-done(((bf16[32,4,32,256]{3,2,1,0:T(8,128)(2,1)}), bf16[32,4,32,256]{3,2,1,0:T(8,128)(2,1)}, u32[]{:S(2)}, u32[]{:S(2)}) %all-to-all-start) | async-done | bytes 2097184 | tf_op jit(solution)/shard_map/all_to_all | solution.py:328
  90.6 6.1 %shard_map.106 = bf16[256,896]{1,0:T(8,128)(2,1)} custom-call(s32[4]{0:T(128)} %pad_add_fusion.pos_ref, s32[8,128]{1,0:T(8,128)} %get-tuple-element.62.ids_ref, bf16[8,4,4,32,256]{4,3,2,1,0:T(8,128)(2,1)} %bitcast.9.ret_ref, bf16[896,256]{1,0:T(8,128)(2,1)} %get-tuple-element.65.refs_0_, bf16[896,256]{1,0:T(8,128)(2,1)} %copy-done.4, ...), custom_call_target="tpu_custom_call" | custom-call | flops 500000000 | bytes 5242880 | tf_op jit(solution)/shard_map/pallas_call | solution.py:335
  96.8 7.2 %all-to-all-start.2 = ((bf16[8,32,896]{2,1,0:T(8,128)(2,1)}), bf16[8,32,896]{2,1,0:T(8,128)(2,1)S(1)}, u32[]{:S(2)}, u32[]{:S(2)}) async-start(bf16[8,32,896]{2,1,0:T(8,128)(2,1)} %bitcast.24), calls=%async_computation.2 | async-start | bytes 917504 | tf_op jit(solution)/shard_map/all_to_all | solution.py:347
  104.1 3.9 %shard_map.108 = (f32[512,128]{1,0:T(8,128)}, bf16[512,128]{1,0:T(8,128)(2,1)}, bf16[512,128]{1,0:T(8,128)(2,1)}, bf16[512,128]{1,0:T(8,128)(2,1)}) custom-call(s32[4]{0:T(128)} %pad_add_fusion.pos_ref, bf16[512,128]{1,0:T(8,128)(2,1)} %get-tuple-element.82.refs_0_, bf16[512,128]{1,0:T(8,128)(2,1)} %copy-done.15, bf16[512,128]{1,0:T(8,128)(2,1)} %copy-done.18, ...), custom_call_target="tpu_custom_call" | custom-call | flops 540000000 | bytes 3145728 | tf_op jit(solution)/shard_map/pallas_call | solution.py:352
  108.3 3.1 %collective-permute-start.31 = (bf16[512,128]{1,0:T(8,128)(2,1)}, bf16[512,128]{1,0:T(8,128)(2,1)S(1)}, u32[]{:S(2)}, u32[]{:S(2)}) collective-permute-start(bf16[512,128]{1,0:T(8,128)(2,1)} %get-tuple-element.92), channel_id=1, source_target_pairs={{0,16},{8,24},{16,0},{24,8},{1,17},{9,25},{17,1},{25,9},{2,18},{10... | collective-permute-start | bytes 393224 | tf_op jit(solution)/shard_map/ppermute | solution.py:258
  112.3 3.8 %shard_map.107 = (f32[512,128]{1,0:T(8,128)}, bf16[512,128]{1,0:T(8,128)(2,1)}, bf16[512,128]{1,0:T(8,128)(2,1)}, bf16[512,128]{1,0:T(8,128)(2,1)}) custom-call(s32[4]{0:T(128)} %pad_add_fusion.pos_ref, bf16[512,128]{1,0:T(8,128)(2,1)} %get-tuple-element.69.refs_0_, bf16[512,128]{1,0:T(8,128)(2,1)} %copy-done.11, bf16[512,128]{1,0:T(8,128)(2,1)} %copy-done.13, ...), custom_call_target="tpu_custom_call" | custom-call | flops 540000000 | bytes 3145728 | tf_op jit(solution)/shard_map/pallas_call | solution.py:352
  118.2 2.5 %collective-permute-start.29 = (bf16[512,128]{1,0:T(8,128)(2,1)}, bf16[512,128]{1,0:T(8,128)(2,1)S(1)}, u32[]{:S(2)}, u32[]{:S(2)}) collective-permute-start(bf16[512,128]{1,0:T(8,128)(2,1)} %get-tuple-element.81), channel_id=1, source_target_pairs={{0,24},{8,0},{16,8},{24,16},{1,25},{9,1},{17,9},{25,17},{2,26},{10... | collective-permute-start | bytes 393224 | tf_op jit(solution)/shard_map/ppermute | solution.py:258
  120.8 1.7 %add_convert_fusion = bf16[512,128]{1,0:T(8,128)(2,1)} fusion(bf16[512,128]{1,0:T(8,128)(2,1)S(1)} %collective-permute-done.32, bf16[512,128]{1,0:T(8,128)(2,1)S(1)} %collective-permute-done.31, f32[512,128]{1,0:T(8,128)} %get-tuple-element.90, bf16[512,128]{1,0:T(8,128)(2,1)S(1)} %collective-permute-done.30), kind=kLoop, calls=%fused_computation.2 | loop fusion | flops 458752 | bytes 786432 | tf_op jit(solution)/shard_map/convert_element_type | solution.py:365
  122.4 2.0 %collective-permute-done.27 = bf16[512,128]{1,0:T(8,128)(2,1)S(1)} collective-permute-done((bf16[512,128]{1,0:T(8,128)(2,1)}, bf16[512,128]{1,0:T(8,128)(2,1)S(1)}, u32[]{:S(2)}, u32[]{:S(2)}) %collective-permute-start.27) | collective-permute-done | bytes 131104 | tf_op jit(solution)/shard_map/ppermute | solution.py:258
  124.8 1.7 %add_convert_fusion.1 = bf16[512,128]{1,0:T(8,128)(2,1)} fusion(bf16[512,128]{1,0:T(8,128)(2,1)S(1)} %collective-permute-done.29, bf16[512,128]{1,0:T(8,128)(2,1)S(1)} %collective-permute-done.28, f32[512,128]{1,0:T(8,128)} %get-tuple-element.78, bf16[512,128]{1,0:T(8,128)(2,1)S(1)} %collective-permute-done.27), kind=kLoop, calls=%fused_computation.3 | loop fusion | flops 458752 | bytes 786432 | tf_op jit(solution)/shard_map/convert_element_type | solution.py:365
  (96 shorter events, 21.8 us)
Async XLA Ops:
  5.8 49.5 %all-to-all-start.1 = ((bf16[8,4,128,128]{3,2,1,0:T(8,128)(2,1)}), bf16[8,4,128,128]{3,2,1,0:T(8,128)(2,1)}, u32[]{:S(2)}, u32[]{:S(2)}) async-start(bf16[8,4,128,128]{3,2,1,0:T(8,128)(2,1)} %get-tuple-element.77), calls=%async_computation.1 | async-start | bytes 2097152 | tf_op jit(solution)/shard_map/all_to_all | solution.py:277
  14.5 13.2 %collective-permute-start.3 = (bf16[896,256]{1,0:T(8,128)(2,1)}, bf16[896,256]{1,0:T(8,128)(2,1)S(1)}, u32[]{:S(2)}, u32[]{:S(2)}) collective-permute-start(bf16[896,256]{1,0:T(8,128)(2,1)} %get-tuple-element.65.refs_0_), channel_id=1, source_target_pairs={{0,8},{8,16},{16,24},{24,0},{1,9},{9,17},{17,25},{25,1},{2,10},{10... | collective-permute-start | bytes 1376264 | tf_op jit(solution)/shard_map/ppermute | solution.py:258
  16.1 11.6 %collective-permute-start.2 = (bf16[896,256]{1,0:T(8,128)(2,1)}, bf16[896,256]{1,0:T(8,128)(2,1)S(1)}, u32[]{:S(2)}, u32[]{:S(2)}) collective-permute-start(bf16[896,256]{1,0:T(8,128)(2,1)} %get-tuple-element.65.refs_0_), channel_id=1, source_target_pairs={{0,24},{8,0},{16,8},{24,16},{1,25},{9,1},{17,9},{25,17},{2,26},{10... | collective-permute-start | bytes 1376264 | tf_op jit(solution)/shard_map/ppermute | solution.py:258
  17.7 14.3 %collective-permute-start.1 = (bf16[1040,256]{1,0:T(8,128)(2,1)}, bf16[1040,256]{1,0:T(8,128)(2,1)S(1)}, u32[]{:S(2)}, u32[]{:S(2)}) collective-permute-start(bf16[1040,256]{1,0:T(8,128)(2,1)} %get-tuple-element.49.refs_0_), channel_id=1, source_target_pairs={{0,64},{64,128},{128,192},{192,0},{1,65},{65,129},{129,193},{193,1... | collective-permute-start | bytes 1597448 | tf_op jit(solution)/shard_map/ppermute | solution.py:258
  19.2 12.9 %collective-permute-start = (bf16[1040,256]{1,0:T(8,128)(2,1)}, bf16[1040,256]{1,0:T(8,128)(2,1)}, u32[]{:S(2)}, u32[]{:S(2)}) collective-permute-start(bf16[1040,256]{1,0:T(8,128)(2,1)} %get-tuple-element.49.refs_0_), channel_id=1, source_target_pairs={{0,192},{64,0},{128,64},{192,128},{1,193},{65,1},{129,65},{193,129... | collective-permute-start | bytes 1597448 | tf_op jit(solution)/shard_map/ppermute | solution.py:258
  34.7 7.9 %collective-permute-start.6 = (bf16[512,256]{1,0:T(8,128)(2,1)}, bf16[512,256]{1,0:T(8,128)(2,1)S(1)}, u32[]{:S(2)}, u32[]{:S(2)}) collective-permute-start(bf16[512,256]{1,0:T(8,128)(2,1)} %get-tuple-element.59), channel_id=1, source_target_pairs={{0,64},{64,128},{128,192},{192,0},{1,65},{65,129},{129,193},{193,1... | collective-permute-start | bytes 786440 | tf_op jit(solution)/shard_map/ppermute | solution.py:258
  35.6 10.0 %collective-permute-start.4 = (bf16[896,256]{1,0:T(8,128)(2,1)}, bf16[896,256]{1,0:T(8,128)(2,1)S(1)}, u32[]{:S(2)}, u32[]{:S(2)}) collective-permute-start(bf16[896,256]{1,0:T(8,128)(2,1)} %copy-done.4), channel_id=1, source_target_pairs={{0,24},{8,0},{16,8},{24,16},{1,25},{9,1},{17,9},{25,17},{2,26},{10... | collective-permute-start | bytes 1376264 | tf_op jit(solution)/shard_map/ppermute | solution.py:258
  37.2 6.8 %collective-permute-start.5 = (bf16[528,256]{1,0:T(8,128)(2,1)}, bf16[528,256]{1,0:T(8,128)(2,1)S(1)}, u32[]{:S(2)}, u32[]{:S(2)}) collective-permute-start(bf16[528,256]{1,0:T(8,128)(2,1)} %get-tuple-element.58), channel_id=1, source_target_pairs={{0,192},{64,0},{128,64},{192,128},{1,193},{65,1},{129,65},{193,129... | collective-permute-start | bytes 811016 | tf_op jit(solution)/shard_map/ppermute | solution.py:258
  39.7 5.9 %collective-permute-start.7 = (bf16[1040,256]{1,0:T(8,128)(2,1)}, bf16[1040,256]{1,0:T(8,128)(2,1)S(1)}, u32[]{:S(2)}, u32[]{:S(2)}) collective-permute-start(bf16[1040,256]{1,0:T(8,128)(2,1)} %get-tuple-element.49.refs_0_), channel_id=1, source_target_pairs={{0,32},{32,0},{1,33},{33,1},{2,34},{34,2},{3,35},{35,3},{4,36},{36... | collective-permute-start | bytes 1597448 | tf_op jit(solution)/shard_map/ppermute | solution.py:258
  39.7 7.4 %collective-permute-start.8 = (bf16[1040,256]{1,0:T(8,128)(2,1)}, bf16[1040,256]{1,0:T(8,128)(2,1)}, u32[]{:S(2)}, u32[]{:S(2)}) collective-permute-start(bf16[1040,256]{1,0:T(8,128)(2,1)} %collective-permute-done.after_ref.refs_1_), channel_id=1, source_target_pairs={{0,32},{32,0},{1,33},{33,1},{2,34},{34,2},{3,35},{35,3},{4,36},{36... | collective-permute-start | bytes 1597448 | tf_op jit(solution)/shard_map/ppermute | solution.py:258
  55.3 35.4 %all-to-all-start = ((bf16[32,4,32,256]{3,2,1,0:T(8,128)(2,1)}), bf16[32,4,32,256]{3,2,1,0:T(8,128)(2,1)}, u32[]{:S(2)}, u32[]{:S(2)}) async-start(bf16[32,4,32,256]{3,2,1,0:T(8,128)(2,1)} %bitcast.22), calls=%async_computation | async-start | bytes 4194304 | tf_op jit(solution)/shard_map/all_to_all | solution.py:328
  62.3 41.7 %collective-permute-start.26 = (bf16[8,4,128,128]{3,2,1,0:T(8,128)(2,1)}, bf16[8,4,128,128]{3,2,1,0:T(8,128)(2,1)}, u32[]{:S(2)}, u32[]{:S(2)}) collective-permute-start(bf16[8,4,128,128]{3,2,1,0:T(8,128)(2,1)} %all-to-all-done.1.refs_8_), channel_id=1, source_target_pairs={{0,32},{32,0},{1,33},{33,1},{2,34},{34,2},{3,35},{35,3},{4,36},{36... | collective-permute-start | bytes 3145736 | tf_op jit(solution)/shard_map/ppermute | solution.py:258
  62.6 6.3 %collective-permute-start.12 = (bf16[512,128]{1,0:T(8,128)(2,1)S(1)}, bf16[512,128]{1,0:T(8,128)(2,1)S(1)}, u32[]{:S(2)}, u32[]{:S(2)}) collective-permute-start(bf16[512,128]{1,0:T(8,128)(2,1)S(1)} %copy-done.9), channel_id=1, source_target_pairs={{0,7},{1,0},{2,1},{3,2},{4,3},{5,4},{6,5},{7,6},{8,15},{9,8},{10,9... | collective-permute-start | bytes 393224 | tf_op jit(solution)/shard_map/ppermute | solution.py:258
  63.3 8.4 %collective-permute-start.19 = (bf16[512,128]{1,0:T(8,128)(2,1)S(1)}, bf16[512,128]{1,0:T(8,128)(2,1)S(1)}, u32[]{:S(2)}, u32[]{:S(2)}) collective-permute-start(bf16[512,128]{1,0:T(8,128)(2,1)S(1)} %copy-done.10), channel_id=1, source_target_pairs={{0,7},{1,0},{2,1},{3,2},{4,3},{5,4},{6,5},{7,6},{8,15},{9,8},{10,9... | collective-permute-start | bytes 393224 | tf_op jit(solution)/shard_map/ppermute | solution.py:258
  65.9 7.5 %collective-permute-start.16 = (bf16[512,128]{1,0:T(8,128)(2,1)S(1)}, bf16[512,128]{1,0:T(8,128)(2,1)S(1)}, u32[]{:S(2)}, u32[]{:S(2)}) collective-permute-start(bf16[512,128]{1,0:T(8,128)(2,1)S(1)} %copy-done.9), channel_id=1, source_target_pairs={{0,1},{1,2},{2,3},{3,4},{4,5},{5,6},{6,7},{7,0},{8,9},{9,10},{10,1... | collective-permute-start | bytes 393224 | tf_op jit(solution)/shard_map/ppermute | solution.py:258
  65.9 8.0 %collective-permute-start.23 = (bf16[512,128]{1,0:T(8,128)(2,1)S(1)}, bf16[512,128]{1,0:T(8,128)(2,1)S(1)}, u32[]{:S(2)}, u32[]{:S(2)}) collective-permute-start(bf16[512,128]{1,0:T(8,128)(2,1)S(1)} %copy-done.10), channel_id=1, source_target_pairs={{0,1},{1,2},{2,3},{3,4},{4,5},{5,6},{6,7},{7,0},{8,9},{9,10},{10,1... | collective-permute-start | bytes 393224 | tf_op jit(solution)/shard_map/ppermute | solution.py:258
  68.9 6.4 %collective-permute-start.13 = (bf16[512,128]{1,0:T(8,128)(2,1)S(1)}, bf16[512,128]{1,0:T(8,128)(2,1)S(1)}, u32[]{:S(2)}, u32[]{:S(2)}) collective-permute-start(bf16[512,128]{1,0:T(8,128)(2,1)S(1)} %collective-permute-done.12.refs_1_), channel_id=1, source_target_pairs={{0,7},{1,0},{2,1},{3,2},{4,3},{5,4},{6,5},{7,6},{8,15},{9,8},{10,9... | collective-permute-start | bytes 393224 | tf_op jit(solution)/shard_map/ppermute | solution.py:258
  73.4 6.8 %collective-permute-start.17 = (bf16[512,128]{1,0:T(8,128)(2,1)S(1)}, bf16[512,128]{1,0:T(8,128)(2,1)S(1)}, u32[]{:S(2)}, u32[]{:S(2)}) collective-permute-start(bf16[512,128]{1,0:T(8,128)(2,1)S(1)} %collective-permute-done.16.refs_7_), channel_id=1, source_target_pairs={{0,1},{1,2},{2,3},{3,4},{4,5},{5,6},{6,7},{7,0},{8,9},{9,10},{10,1... | collective-permute-start | bytes 393224 | tf_op jit(solution)/shard_map/ppermute | solution.py:258
  73.8 7.6 %collective-permute-start.24 = (bf16[512,128]{1,0:T(8,128)(2,1)S(1)}, bf16[512,128]{1,0:T(8,128)(2,1)S(1)}, u32[]{:S(2)}, u32[]{:S(2)}) collective-permute-start(bf16[512,128]{1,0:T(8,128)(2,1)S(1)} %collective-permute-done.23.refs_7_), channel_id=1, source_target_pairs={{0,1},{1,2},{2,3},{3,4},{4,5},{5,6},{6,7},{7,0},{8,9},{9,10},{10,1... | collective-permute-start | bytes 393224 | tf_op jit(solution)/shard_map/ppermute | solution.py:258
  75.4 7.3 %collective-permute-start.14 = (bf16[512,128]{1,0:T(8,128)(2,1)S(1)}, bf16[512,128]{1,0:T(8,128)(2,1)S(1)}, u32[]{:S(2)}, u32[]{:S(2)}) collective-permute-start(bf16[512,128]{1,0:T(8,128)(2,1)S(1)} %collective-permute-done.13.refs_2_), channel_id=1, source_target_pairs={{0,7},{1,0},{2,1},{3,2},{4,3},{5,4},{6,5},{7,6},{8,15},{9,8},{10,9... | collective-permute-start | bytes 393224 | tf_op jit(solution)/shard_map/ppermute | solution.py:258
  76.8 7.7 %collective-permute-start.21 = (bf16[512,128]{1,0:T(8,128)(2,1)S(1)}, bf16[512,128]{1,0:T(8,128)(2,1)}, u32[]{:S(2)}, u32[]{:S(2)}) collective-permute-start(bf16[512,128]{1,0:T(8,128)(2,1)S(1)} %collective-permute-done.20.refs_2_), channel_id=1, source_target_pairs={{0,7},{1,0},{2,1},{3,2},{4,3},{5,4},{6,5},{7,6},{8,15},{9,8},{10,9... | collective-permute-start | bytes 393224 | tf_op jit(solution)/shard_map/ppermute | solution.py:258
  80.2 7.4 %collective-permute-start.18 = (bf16[512,128]{1,0:T(8,128)(2,1)S(1)}, bf16[512,128]{1,0:T(8,128)(2,1)S(1)}, u32[]{:S(2)}, u32[]{:S(2)}) collective-permute-start(bf16[512,128]{1,0:T(8,128)(2,1)S(1)} %collective-permute-done.17.refs_6_), channel_id=1, source_target_pairs={{0,1},{1,2},{2,3},{3,4},{4,5},{5,6},{6,7},{7,0},{8,9},{9,10},{10,1... | collective-permute-start | bytes 393224 | tf_op jit(solution)/shard_map/ppermute | solution.py:258
  81.4 6.7 %collective-permute-start.25 = (bf16[512,128]{1,0:T(8,128)(2,1)S(1)}, bf16[512,128]{1,0:T(8,128)(2,1)}, u32[]{:S(2)}, u32[]{:S(2)}) collective-permute-start(bf16[512,128]{1,0:T(8,128)(2,1)S(1)} %collective-permute-done.24.refs_6_), channel_id=1, source_target_pairs={{0,1},{1,2},{2,3},{3,4},{4,5},{5,6},{6,7},{7,0},{8,9},{9,10},{10,1... | collective-permute-start | bytes 393224 | tf_op jit(solution)/shard_map/ppermute | solution.py:258
  82.7 14.1 %collective-permute-start.15 = (bf16[512,128]{1,0:T(8,128)(2,1)S(1)}, bf16[512,128]{1,0:T(8,128)(2,1)}, u32[]{:S(2)}, u32[]{:S(2)}) collective-permute-start(bf16[512,128]{1,0:T(8,128)(2,1)S(1)} %collective-permute-done.14.refs_3_), channel_id=1, source_target_pairs={{0,7},{1,0},{2,1},{3,2},{4,3},{5,4},{6,5},{7,6},{8,15},{9,8},{10,9... | collective-permute-start | bytes 393224 | tf_op jit(solution)/shard_map/ppermute | solution.py:258
  84.5 12.3 %collective-permute-start.22 = (bf16[512,128]{1,0:T(8,128)(2,1)}, bf16[512,128]{1,0:T(8,128)(2,1)}, u32[]{:S(2)}, u32[]{:S(2)}) collective-permute-start(bf16[512,128]{1,0:T(8,128)(2,1)} %collective-permute-done.21.refs_3_), channel_id=1, source_target_pairs={{0,7},{1,0},{2,1},{3,2},{4,3},{5,4},{6,5},{7,6},{8,15},{9,8},{10,9... | collective-permute-start | bytes 393224 | tf_op jit(solution)/shard_map/ppermute | solution.py:258
  96.8 29.7 %all-to-all-start.2 = ((bf16[8,32,896]{2,1,0:T(8,128)(2,1)}), bf16[8,32,896]{2,1,0:T(8,128)(2,1)S(1)}, u32[]{:S(2)}, u32[]{:S(2)}) async-start(bf16[8,32,896]{2,1,0:T(8,128)(2,1)} %bitcast.24), calls=%async_computation.2 | async-start | bytes 917504 | tf_op jit(solution)/shard_map/all_to_all | solution.py:347
  108.0 10.3 %collective-permute-start.30 = (bf16[512,128]{1,0:T(8,128)(2,1)}, bf16[512,128]{1,0:T(8,128)(2,1)S(1)}, u32[]{:S(2)}, u32[]{:S(2)}) collective-permute-start(bf16[512,128]{1,0:T(8,128)(2,1)} %get-tuple-element.91), channel_id=1, source_target_pairs={{0,8},{8,16},{16,24},{24,0},{1,9},{9,17},{17,25},{25,1},{2,10},{10... | collective-permute-start | bytes 393224 | tf_op jit(solution)/shard_map/ppermute | solution.py:258
  108.3 12.4 %collective-permute-start.31 = (bf16[512,128]{1,0:T(8,128)(2,1)}, bf16[512,128]{1,0:T(8,128)(2,1)S(1)}, u32[]{:S(2)}, u32[]{:S(2)}) collective-permute-start(bf16[512,128]{1,0:T(8,128)(2,1)} %get-tuple-element.92), channel_id=1, source_target_pairs={{0,16},{8,24},{16,0},{24,8},{1,17},{9,25},{17,1},{25,9},{2,18},{10... | collective-permute-start | bytes 393224 | tf_op jit(solution)/shard_map/ppermute | solution.py:258
  111.4 9.4 %collective-permute-start.32 = (bf16[512,128]{1,0:T(8,128)(2,1)}, bf16[512,128]{1,0:T(8,128)(2,1)S(1)}, u32[]{:S(2)}, u32[]{:S(2)}) collective-permute-start(bf16[512,128]{1,0:T(8,128)(2,1)} %get-tuple-element.93), channel_id=1, source_target_pairs={{0,24},{8,0},{16,8},{24,16},{1,25},{9,1},{17,9},{25,17},{2,26},{10... | collective-permute-start | bytes 393224 | tf_op jit(solution)/shard_map/ppermute | solution.py:258
  116.1 8.3 %collective-permute-start.27 = (bf16[512,128]{1,0:T(8,128)(2,1)}, bf16[512,128]{1,0:T(8,128)(2,1)S(1)}, u32[]{:S(2)}, u32[]{:S(2)}) collective-permute-start(bf16[512,128]{1,0:T(8,128)(2,1)} %get-tuple-element.79), channel_id=1, source_target_pairs={{0,8},{8,16},{16,24},{24,0},{1,9},{9,17},{17,25},{25,1},{2,10},{10... | collective-permute-start | bytes 393224 | tf_op jit(solution)/shard_map/ppermute | solution.py:258
  117.3 7.1 %collective-permute-start.28 = (bf16[512,128]{1,0:T(8,128)(2,1)}, bf16[512,128]{1,0:T(8,128)(2,1)S(1)}, u32[]{:S(2)}, u32[]{:S(2)}) collective-permute-start(bf16[512,128]{1,0:T(8,128)(2,1)} %get-tuple-element.80), channel_id=1, source_target_pairs={{0,16},{8,24},{16,0},{24,8},{1,17},{9,25},{17,1},{25,9},{2,18},{10... | collective-permute-start | bytes 393224 | tf_op jit(solution)/shard_map/ppermute | solution.py:258
  118.2 6.6 %collective-permute-start.29 = (bf16[512,128]{1,0:T(8,128)(2,1)}, bf16[512,128]{1,0:T(8,128)(2,1)S(1)}, u32[]{:S(2)}, u32[]{:S(2)}) collective-permute-start(bf16[512,128]{1,0:T(8,128)(2,1)} %get-tuple-element.81), channel_id=1, source_target_pairs={{0,24},{8,0},{16,8},{24,16},{1,25},{9,1},{17,9},{25,17},{2,26},{10... | collective-permute-start | bytes 393224 | tf_op jit(solution)/shard_map/ppermute | solution.py:258
  (26 other events, 284.1 us)

commit v4 on v3

--- a/solution.py
+++ b/solution.py
@@ -159,16 +159,34 @@
         copy.wait()
 
 
-def encoded_body(stored, pos_ref, ids_ref, ret_ref, *refs):
+def tail_body(stored, n_z, pos_ref, ids_ref, ret_ref, *refs):
     owners, n_y, cap, piece, _ = ret_ref.shape
-    w_refs, (out_ref, got_ref, w_ref, acc_ref, prod_ref, sem) = refs[:n_y], refs[n_y:]
-    me = pos_ref[0] * 2 + pos_ref[1]
-    my_y = pos_ref[2]
+    pair_refs, refs = refs[:n_y], refs[n_y:]
+    piece_refs, (mine, other), refs = refs[: 2 * n_z], refs[2 * n_z : 2 * n_z + 2], refs[2 * n_z + 2 :]
+    out_ref, sums, refs = refs[0], refs[1 : 1 + 2 * n_y], refs[1 + 2 * n_y :]
+    got_ref, pair_ref, acc_ref, prod_ref, a_ref, w_ref, sem = refs
+    my_c, my_y, my_z = (pos_ref[i] for i in range(1, 4))
+    me = pos_ref[0] * 2 + my_c
+
     for d in range(owners):
         pltpu.make_async_copy(ret_ref.at[d], got_ref.at[d], sem.at[d]).start()
-    weights = [pltpu.make_async_copy(w_refs[y], w_ref.at[y], sem.at[owners + y]) for y in range(n_y)]
-    for copy in weights:
+    first = owners
+    pair_copies = [pltpu.make_async_copy(pair_refs[y], pair_ref.at[y], sem.at[first + y]) for y in range(n_y)]
+    first += n_y
+    piece_copies = [
+        pltpu.make_async_copy(
+            piece_refs[k], a_ref.at[k // n_z, :, (k % n_z) * DH : (k % n_z + 1) * DH], sem.at[first + k]
+        )
+        for k in range(2 * n_z)
+    ]
+    first += 2 * n_z
+    weight_copies = [
+        pltpu.make_async_copy(mine, w_ref.at[my_c], sem.at[first]),
+        pltpu.make_async_copy(other, w_ref.at[1 - my_c], sem.at[first + 1]),
+    ]
+    for copy in pair_copies + piece_copies + weight_copies:
         copy.start()
+
     acc_ref[...] = jnp.zeros_like(acc_ref)
 
     def from_device(d, carry):
@@ -188,14 +206,14 @@
         return carry
 
     lax.fori_loop(0, owners, from_device, 0)
+    for copy in pair_copies + piece_copies + weight_copies:
+        copy.wait()
     lanes = prod_ref.shape[0]
-    for copy in weights:
-        copy.wait()
     both = [acc_ref[lax.rem(my_y + y, n_y)].astype(BF).reshape(stored * piece, 2 * DH) for y in range(n_y)]
     both = jnp.concatenate(both, axis=1)
     for n in range(0, lanes, 2):
         wide = min(2, lanes - n)
-        w = jnp.concatenate([w_ref[y, n * DH : (n + wide) * DH, :] for y in range(n_y)], axis=1)
+        w = jnp.concatenate([pair_ref[y, n * DH : (n + wide) * DH, :] for y in range(n_y)], axis=1)
         term = lax.dot_general(both, w, NT, preferred_element_type=F32)
         for i in range(wide):
             prod_ref[n + i] = term[:, i * DH : (i + 1) * DH]
@@ -204,39 +222,19 @@
             two = [prod_ref[n, pl.ds(t + k, stored, stride=piece), :] for k in range(2)]
             out_ref[pl.ds(t * stored, 2 * stored), n * DH : (n + 1) * DH] = jnp.concatenate(two, axis=0).astype(BF)
 
-
-def head_sum_body(n_z, n_y, second, pos_ref, *refs):
-    pieces, mine, other = refs[:n_z], refs[n_z], refs[n_z + 1]
-    *outs, a_ref, w_ref, sem = refs[n_z + 2 :]
-    my_c, my_y, my_z = (pos_ref[i] for i in range(1, 4))
-
-    @pl.when(my_c == second)
-    def _():
-        pltpu.make_async_copy(mine, w_ref, sem.at[n_z]).start()
-
-    @pl.when(my_c != second)
-    def _():
-        pltpu.make_async_copy(other, w_ref, sem.at[n_z]).start()
-
-    copies = [
-        pltpu.make_async_copy(pieces[j], a_ref.at[:, j * DH : (j + 1) * DH], sem.at[j]) for j in range(n_z)
-    ]
-    for copy in copies:
-        copy.start()
-    pltpu.make_async_copy(mine, w_ref, sem.at[n_z]).wait()
-    for copy in copies:
-        copy.wait()
     heads = [lax.rem(my_z + j, n_z) for j in range(n_z)]
-    for k in range(0, n_y, 2):
-        at = [lax.rem(my_y + k + i, n_y) for i in range(2)]
-        if second:
-            w = [jnp.concatenate([w_ref[h, at[i]] for h in heads], axis=1) for i in range(2)]
-            total = lax.dot_general(a_ref[...], jnp.concatenate(w, axis=0), NT, preferred_element_type=F32)
-        else:
-            w = [jnp.concatenate([w_ref[h, at[i]] for h in heads], axis=0) for i in range(2)]
-            total = jnp.dot(a_ref[...], jnp.concatenate(w, axis=1), preferred_element_type=F32)
-        for i in range(2):
-            outs[k + i][...] = total[:, i * DH : (i + 1) * DH].astype(outs[k + i].dtype)
+    for second in range(2):
+        for k in range(0, n_y, 2):
+            at = [lax.rem(my_y + k + i, n_y) for i in range(2)]
+            if second:
+                w = [jnp.concatenate([w_ref[1, h, at[i]] for h in heads], axis=1) for i in range(2)]
+                total = lax.dot_general(a_ref[1], jnp.concatenate(w, axis=0), NT, preferred_element_type=F32)
+            else:
+                w = [jnp.concatenate([w_ref[0, h, at[i]] for h in heads], axis=0) for i in range(2)]
+                total = jnp.dot(a_ref[0], jnp.concatenate(w, axis=1), preferred_element_type=F32)
+            for i in range(2):
+                ref = sums[second * n_y + k + i]
+                ref[...] = total[:, i * DH : (i + 1) * DH].astype(ref.dtype)
 
 
 def shards(hidden, encoded, neighbours, w_query, w_key, w_value, w_out, cotangent):
@@ -276,12 +274,11 @@
     after, before, kv_other = x_up(kv), x_down(kv), swap(kv)
     mine = lax.all_to_all(mine, "z", 0, 0, tiled=True)
     y_up, y_down = shift("y", n_y, -1), shift("y", n_y, 1)
-    pair_up, pair_down = y_up(pair), y_down(pair)
     queries = jnp.dot(hidden, w_query, preferred_element_type=F32).astype(BF)
     grad_attn = lax.dot_general(cotangent, w_out, NT, preferred_element_type=F32).astype(BF)
-    after, before, pair_up, pair_down, queries, grad_attn = tie(
-        (after, before, pair_up, pair_down, queries, grad_attn)
-    )
+    pair_, queries = tie((pair, queries))
+    pair_up, pair_down = y_up(pair_), y_down(pair_)
+    after, before, queries, grad_attn = tie((after, before, queries, grad_attn))
 
     cut = HEAD + stored // 2 * seg
     next_lo, next_hi = call(
@@ -289,6 +286,7 @@
         (jax.ShapeDtypeStruct((cut, 2 * DH), BF), jax.ShapeDtypeStruct((kv.shape[0] - cut, 2 * DH), BF)),
         "aa", 0, 0, scratch=(pltpu.SemaphoreType.DMA((2,)),),
     )(after, before)
+    next_lo, next_hi, pair_up, pair_down = tie((next_lo, next_hi, pair_up, pair_down))
     far_lo, far_hi = x_up(next_lo), x_down(next_hi)
     kv_all = [kv, after, far_lo, far_hi, before, kv_other] + [swap(a) for a in (after, far_lo, far_hi, before)]
     pairs = [pair, pair_up, y_up(pair_up), pair_down]
@@ -329,42 +327,32 @@
         outgoing.reshape(owners * n_y, cap, piece, 2 * DH), dp + ("y",), 0, 0, tiled=True
     ).reshape(owners, n_y, cap, piece, 2 * DH)
     attn_all, gq_all = ring(attn), ring(gq)
-    last = n_z // 2
-    early = [a for ring_ in (attn_all, gq_all) for k, a in enumerate(ring_) if k != last]
-    _, returned = tie((early, returned))
-    enc_part = call(
-        functools.partial(encoded_body, stored),
-        jax.ShapeDtypeStruct((piece * stored, enc_width), BF), "ssa" + "a" * n_y, 500_000_000, 5 << 20,
+    sums = (jax.ShapeDtypeStruct((rows, DH), F32),) + (slab,) * (n_y - 1)
+    enc_part, *sums = call(
+        functools.partial(tail_body, stored, n_z),
+        (jax.ShapeDtypeStruct((piece * stored, enc_width), BF),) + sums + sums,
+        "ssa" + "a" * (n_y + 2 * n_z + 2), 1_580_000_000, 10 << 20,
         scratch=(
             pltpu.VMEM((owners, n_y, cap, piece, 2 * DH), BF),
             pltpu.VMEM((n_y, enc_width, 2 * DH), BF),
             pltpu.VMEM((n_y, stored, piece, 2 * DH), F32),
             pltpu.VMEM((enc_width // DH, stored * piece, DH), F32),
-            pltpu.SemaphoreType.DMA((owners + n_y,)),
+            pltpu.VMEM((2, rows, n_z * DH), BF),
+            pltpu.VMEM((2, n_z, n_y, DH, DH), BF),
+            pltpu.SemaphoreType.DMA((owners + n_y + 2 * n_z + 2,)),
         ),
-    )(place, ids_all, returned, *pairs)
-    attn_all, gq_all, enc_part = tie((attn_all, gq_all, enc_part))
+    )(place, ids_all, returned, *pairs, *attn_all, *gq_all, mine, other)
     enc_parts = lax.all_to_all(enc_part.reshape(n_z, -1, enc_width), "z", 0, 0, tiled=True)
     enc_rows_sum = jnp.sum(enc_parts.astype(F32), axis=0).astype(BF)
     grad_encoded = enc_rows_sum.reshape(seg // (n_y * n_z), stored, enc_width).transpose(1, 0, 2).reshape(stored, -1)
 
-    def summed(pieces, second):
-        parts = call(
-            functools.partial(head_sum_body, n_z, n_y, second),
-            (jax.ShapeDtypeStruct((rows, DH), F32),) + (slab,) * (n_y - 1),
-            "s" + "a" * (n_z + 2), 540_000_000, 3 << 20,
-            scratch=(
-                pltpu.VMEM((rows, n_z * DH), BF),
-                pltpu.VMEM((n_z, n_y, DH, DH), BF),
-                pltpu.SemaphoreType.DMA((n_z + 1,)),
-            ),
-        )(place, *pieces, mine, other)
+    def summed(parts):
         total = parts[0]
         for k in range(1, n_y):
             total = total + shift("y", n_y, k)(parts[k]).astype(F32)
         return total.astype(BF)
 
-    return summed(attn_all, 0), summed(gq_all, 1), grad_encoded
+    return summed(sums[:n_y]), summed(sums[n_y:]), grad_encoded
 
 
 def solution(mesh):

time: 128 us -> 125 us (0.977)
  Pallas kernels: 27.6 us -> 21.5 us
  starting transfers between devices: 63.5 us -> 66.4 us
    pallas_call x3 -> x1, Pallas kernels: 13.8 us -> 7.81 us  [shards(): call(functools.partial(tail_body, stored, n_z), (jax.ShapeDtypeStruct((pi...]
    all_to_all x1, waiting for transfers between devices: 2.51 us -> 0.01 us  [shards(): lax.all_to_all(outgoing.reshape(owners * n_y, cap, piece, 2 * DH), dp + (...]
    ppermute x33, waiting for transfers between devices: 19.5 us -> 21.6 us  [shift(): return lambda a: lax.ppermute(a, axis, [(i, (i + k) % n) for i in range(n)])]
    ppermute x33, starting transfers between devices: 40.5 us -> 42.4 us  [shift(): return lambda a: lax.ppermute(a, axis, [(i, (i + k) % n) for i in range(n)])]
    unnamed x44 -> x48, local copies, waits for them, and re-layouts: 2.28 us -> 2.65 us
  transfers between devices with their start and end apart: 36 -> 36, of which waited for: 16 -> 18; matrix products, arithmetic and copies ran while one was open for 8% -> 8% of each run, Pallas kernels for 18% -> 7%
where the time goes in v4:
time: 125 us; the launch traced here: 124 us
  starting transfers between devices  66.4 us (53%)
  waiting for transfers between devices  21.6 us (17%)
  Pallas kernels  21.5 us (17%)
  matrix products  6.31 us (5%)
  other arithmetic  4.63 us (4%)
  local copies, waits for them, and re-layouts  2.65 us (2%)
    ppermute x33, starting transfers between devices, shift(): return lambda a: lax.ppermute(a, axis, [(i, (i + k) % n) for i in range(n)])  42.4 us
    ppermute x33, waiting for transfers between devices, shift(): return lambda a: lax.ppermute(a, axis, [(i, (i + k) % n) for i in range(n)])  21.6 us
    all_to_all x1, starting transfers between devices, shards(): mine = lax.all_to_all(mine, 'z', 0, 0, tiled=True)  8.71 us
    all_to_all x1, starting transfers between devices, shards(): lax.all_to_all(outgoing.reshape(owners * n_y, cap, piece, 2 * DH), dp + (...  7.83 us
    pallas_call x1, Pallas kernels, shards(): call(functools.partial(tail_body, stored, n_z), (jax.ShapeDtypeStruct((pi...  7.81 us
    all_to_all x1, starting transfers between devices, shards(): lax.all_to_all(enc_part.reshape(n_z, -1, enc_width), 'z', 0, 0, tiled=True)  7.47 us
    pallas_call x1, Pallas kernels, shards(): call(functools.partial(attention_body, (blocks, block_len, n_x, n_y, cap,...  7.41 us
    pallas_call x1, Pallas kernels, shards(): call(functools.partial(keys_values_body, stored, n_z, n_y), (jax.ShapeDty...  4.46 us
  transfers between devices with their start and end apart: 36, of which 18 were waited for; matrix products, arithmetic and copies ran while one was open for 8% of the time, Pallas kernels for 7%

profile of v4, /device:TPU:32, one launch (start us, length us, event | category | flops | bytes accessed | tf_op | source)
XLA Modules:
  0.0 124.0 jit_solution(867024629607873884)
XLA Ops:
  1.2 4.5 %shard_map.103 = (bf16[1040,256]{1,0:T(8,128)(2,1)}, bf16[896,256]{1,0:T(8,128)(2,1)}, bf16[8,4,128,128]{3,2,1,0:T(8,128)(2,1)}) custom-call(s32[4]{0:T(128)} %pad_add_fusion.pos_ref, s32[2,8]{1,0:T(2,128)} %bitcast.26, bf16[1024,896]{1,0:T(8,128)(2,1)} %bitcast.23, bf16[896,128]{1,0:T(8,128)(2,1)} %wk_ref.1, bf16[896,128]{1,0:T(8,128)(2,1)} %wv_ref.1, ...), custom_call_target="tpu_custom_call" | custom-call | flops 470000000 | bytes 5242880 | tf_op jit(solution)/shard_map/pallas_call | solution.py:264
  5.7 8.7 %all-to-all-start.1 = ((bf16[8,4,128,128]{3,2,1,0:T(8,128)(2,1)}), bf16[8,4,128,128]{3,2,1,0:T(8,128)(2,1)}, u32[]{:S(2)}, u32[]{:S(2)}) async-start(bf16[8,4,128,128]{3,2,1,0:T(8,128)(2,1)} %get-tuple-element.59), calls=%async_computation.1 | async-start | bytes 2097152 | tf_op jit(solution)/shard_map/all_to_all | solution.py:275
  14.4 1.5 %collective-permute-start.1 = (bf16[1040,256]{1,0:T(8,128)(2,1)}, bf16[1040,256]{1,0:T(8,128)(2,1)S(1)}, u32[]{:S(2)}, u32[]{:S(2)}) collective-permute-start(bf16[1040,256]{1,0:T(8,128)(2,1)} %get-tuple-element.36.refs_0_), channel_id=1, source_target_pairs={{0,64},{64,128},{128,192},{192,0},{1,65},{65,129},{129,193},{193,1... | collective-permute-start | bytes 1597448 | tf_op jit(solution)/shard_map/ppermute | solution.py:256
  15.9 1.7 %collective-permute-start = (bf16[1040,256]{1,0:T(8,128)(2,1)}, bf16[1040,256]{1,0:T(8,128)(2,1)}, u32[]{:S(2)}, u32[]{:S(2)}) collective-permute-start(bf16[1040,256]{1,0:T(8,128)(2,1)} %get-tuple-element.36.refs_0_), channel_id=1, source_target_pairs={{0,192},{64,0},{128,64},{192,128},{1,193},{65,1},{129,65},{193,129... | collective-permute-start | bytes 1597448 | tf_op jit(solution)/shard_map/ppermute | solution.py:256
  17.7 4.4 %convolution_convert_fusion.1.q_ref = bf16[512,128]{1,0:T(8,128)(2,1)} fusion(bf16[512,4096]{1,0:T(8,128)(2,1)} %param.8, bf16[4096,128]{1,0:T(8,128)(2,1)} %wq_ref.1), kind=kOutput, calls=%fused_computation.1 | convolution fusion | flops 536936448 | bytes 5373952 | tf_op jit(solution)/shard_map/dot_general | solution.py:277
  22.0 1.6 %collective-permute-start.3 = (bf16[896,256]{1,0:T(8,128)(2,1)}, bf16[896,256]{1,0:T(8,128)(2,1)}, u32[]{:S(2)}, u32[]{:S(2)}) collective-permute-start(bf16[896,256]{1,0:T(8,128)(2,1)} %get-tuple-element.53.refs_0_), channel_id=1, source_target_pairs={{0,8},{8,16},{16,24},{24,0},{1,9},{9,17},{17,25},{25,1},{2,10},{10... | collective-permute-start | bytes 1376264 | tf_op jit(solution)/shard_map/ppermute | solution.py:256
  23.6 1.7 %collective-permute-start.2 = (bf16[896,256]{1,0:T(8,128)(2,1)}, bf16[896,256]{1,0:T(8,128)(2,1)}, u32[]{:S(2)}, u32[]{:S(2)}) collective-permute-start(bf16[896,256]{1,0:T(8,128)(2,1)} %get-tuple-element.53.refs_0_), channel_id=1, source_target_pairs={{0,24},{8,0},{16,8},{24,16},{1,25},{9,1},{17,9},{25,17},{2,26},{10... | collective-permute-start | bytes 1376264 | tf_op jit(solution)/shard_map/ppermute | solution.py:256
  25.3 1.9 %convolution_convert_fusion.g_ref = bf16[512,128]{1,0:T(8,128)(2,1)} fusion(bf16[512,4096]{1,0:T(8,128)(2,1)S(1)} %copy-done.23, bf16[128,4096]{1,0:T(8,128)(2,1)S(1)} %copy-done.1), kind=kOutput, calls=%fused_computation | convolution fusion | flops 536936448 | bytes 5373952 | tf_op jit(solution)/shard_map/dot_general | solution.py:278
  27.2 1.9 %collective-permute-done.1.before_ref.refs_4_ = bf16[1040,256]{1,0:T(8,128)(2,1)S(1)} collective-permute-done((bf16[1040,256]{1,0:T(8,128)(2,1)}, bf16[1040,256]{1,0:T(8,128)(2,1)S(1)}, u32[]{:S(2)}, u32[]{:S(2)}) %collective-permute-start.1) | collective-permute-done | bytes 532512 | tf_op jit(solution)/shard_map/ppermute | solution.py:256
  29.9 1.9 %shard_map.104 = (bf16[528,256]{1,0:T(8,128)(2,1)}, bf16[512,256]{1,0:T(8,128)(2,1)}) custom-call(bf16[1040,256]{1,0:T(8,128)(2,1)} %collective-permute-done.after_ref.refs_1_, bf16[1040,256]{1,0:T(8,128)(2,1)} %copy-done), custom_call_target="tpu_custom_call" | custom-call | tf_op jit(solution)/shard_map/pallas_call | solution.py:284
  31.8 3.0 %collective-permute-done.3.refs_3_ = bf16[896,256]{1,0:T(8,128)(2,1)} collective-permute-done((bf16[896,256]{1,0:T(8,128)(2,1)}, bf16[896,256]{1,0:T(8,128)(2,1)}, u32[]{:S(2)}, u32[]{:S(2)}) %collective-permute-start.3) | collective-permute-done | bytes 458784 | tf_op jit(solution)/shard_map/ppermute | solution.py:256
  35.1 2.9 %collective-permute-start.4 = (bf16[896,256]{1,0:T(8,128)(2,1)}, bf16[896,256]{1,0:T(8,128)(2,1)S(1)}, u32[]{:S(2)}, u32[]{:S(2)}) collective-permute-start(bf16[896,256]{1,0:T(8,128)(2,1)} %collective-permute-done.2.refs_1_), channel_id=1, source_target_pairs={{0,24},{8,0},{16,8},{24,16},{1,25},{9,1},{17,9},{25,17},{2,26},{10... | collective-permute-start | bytes 1376264 | tf_op jit(solution)/shard_map/ppermute | solution.py:256
  38.0 3.0 %collective-permute-start.5 = (bf16[528,256]{1,0:T(8,128)(2,1)}, bf16[528,256]{1,0:T(8,128)(2,1)S(1)}, u32[]{:S(2)}, u32[]{:S(2)}) collective-permute-start(bf16[528,256]{1,0:T(8,128)(2,1)} %get-tuple-element.49), channel_id=1, source_target_pairs={{0,192},{64,0},{128,64},{192,128},{1,193},{65,1},{129,65},{193,129... | collective-permute-start | bytes 811016 | tf_op jit(solution)/shard_map/ppermute | solution.py:256
  42.6 2.7 %collective-permute-done.5.refs_2_ = bf16[528,256]{1,0:T(8,128)(2,1)S(1)} collective-permute-done((bf16[528,256]{1,0:T(8,128)(2,1)}, bf16[528,256]{1,0:T(8,128)(2,1)S(1)}, u32[]{:S(2)}, u32[]{:S(2)}) %collective-permute-start.5) | collective-permute-done | bytes 270368 | tf_op jit(solution)/shard_map/ppermute | solution.py:256
  47.9 7.4 %shard_map.105 = (bf16[512,128]{1,0:T(8,128)(2,1)}, bf16[512,128]{1,0:T(8,128)(2,1)}, bf16[8,4,4,32,256]{4,3,2,1,0:T(8,128)(2,1)}, s32[8,128]{1,0:T(8,128)}) custom-call(s32[4]{0:T(128)} %pad_add_fusion.pos_ref, s32[2,8]{1,0:T(2,128)} %bitcast.27, bf16[512,128]{1,0:T(8,128)(2,1)} %convolution_convert_fusion.1.q_ref, ...), custom_call_target="tpu_custom_call" | custom-call | tf_op jit(solution)/shard_map/pallas_call | solution.py:298
  55.3 7.8 %all-to-all-start = ((bf16[32,4,32,256]{3,2,1,0:T(8,128)(2,1)}), bf16[32,4,32,256]{3,2,1,0:T(8,128)(2,1)}, u32[]{:S(2)}, u32[]{:S(2)}) async-start(bf16[32,4,32,256]{3,2,1,0:T(8,128)(2,1)} %bitcast.22), calls=%async_computation | async-start | bytes 4194304 | tf_op jit(solution)/shard_map/all_to_all | solution.py:326
  64.1 2.6 %collective-permute-start.19 = (bf16[512,128]{1,0:T(8,128)(2,1)S(1)}, bf16[512,128]{1,0:T(8,128)(2,1)S(1)}, u32[]{:S(2)}, u32[]{:S(2)}) collective-permute-start(bf16[512,128]{1,0:T(8,128)(2,1)S(1)} %copy-done.8), channel_id=1, source_target_pairs={{0,7},{1,0},{2,1},{3,2},{4,3},{5,4},{6,5},{7,6},{8,15},{9,8},{10,9... | collective-permute-start | bytes 393224 | tf_op jit(solution)/shard_map/ppermute | solution.py:256
  67.5 2.3 %collective-permute-done.12.refs_5_ = bf16[512,128]{1,0:T(8,128)(2,1)S(1)} collective-permute-done((bf16[512,128]{1,0:T(8,128)(2,1)S(1)}, bf16[512,128]{1,0:T(8,128)(2,1)S(1)}, u32[]{:S(2)}, u32[]{:S(2)}) %collective-permute-start.12) | collective-permute-done | bytes 131104 | tf_op jit(solution)/shard_map/ppermute | solution.py:256
  70.5 2.0 %collective-permute-done.19.refs_13_ = bf16[512,128]{1,0:T(8,128)(2,1)S(1)} collective-permute-done((bf16[512,128]{1,0:T(8,128)(2,1)S(1)}, bf16[512,128]{1,0:T(8,128)(2,1)S(1)}, u32[]{:S(2)}, u32[]{:S(2)}) %collective-permute-start.19) | collective-permute-done | bytes 131104 | tf_op jit(solution)/shard_map/ppermute | solution.py:256
  72.5 1.7 %collective-permute-start.20 = (bf16[512,128]{1,0:T(8,128)(2,1)S(1)}, bf16[512,128]{1,0:T(8,128)(2,1)S(1)}, u32[]{:S(2)}, u32[]{:S(2)}) collective-permute-start(bf16[512,128]{1,0:T(8,128)(2,1)S(1)} %collective-permute-done.19.refs_13_), channel_id=1, source_target_pairs={{0,7},{1,0},{2,1},{3,2},{4,3},{5,4},{6,5},{7,6},{8,15},{9,8},{10,9... | collective-permute-start | bytes 393224 | tf_op jit(solution)/shard_map/ppermute | solution.py:256
  74.7 1.6 %collective-permute-start.24 = (bf16[512,128]{1,0:T(8,128)(2,1)S(1)}, bf16[512,128]{1,0:T(8,128)(2,1)S(1)}, u32[]{:S(2)}, u32[]{:S(2)}) collective-permute-start(bf16[512,128]{1,0:T(8,128)(2,1)S(1)} %collective-permute-done.23.refs_19_), channel_id=1, source_target_pairs={{0,1},{1,2},{2,3},{3,4},{4,5},{5,6},{6,7},{7,0},{8,9},{9,10},{10,1... | collective-permute-start | bytes 393224 | tf_op jit(solution)/shard_map/ppermute | solution.py:256
  77.6 3.4 %collective-permute-start.21 = (bf16[512,128]{1,0:T(8,128)(2,1)S(1)}, bf16[512,128]{1,0:T(8,128)(2,1)S(1)}, u32[]{:S(2)}, u32[]{:S(2)}) collective-permute-start(bf16[512,128]{1,0:T(8,128)(2,1)S(1)} %collective-permute-done.20.refs_14_), channel_id=1, source_target_pairs={{0,7},{1,0},{2,1},{3,2},{4,3},{5,4},{6,5},{7,6},{8,15},{9,8},{10,9... | collective-permute-start | bytes 393224 | tf_op jit(solution)/shard_map/ppermute | solution.py:256
  83.5 1.8 %collective-permute-start.15 = (bf16[512,128]{1,0:T(8,128)(2,1)S(1)}, bf16[512,128]{1,0:T(8,128)(2,1)S(1)}, u32[]{:S(2)}, u32[]{:S(2)}) collective-permute-start(bf16[512,128]{1,0:T(8,128)(2,1)S(1)} %collective-permute-done.14.refs_7_), channel_id=1, source_target_pairs={{0,7},{1,0},{2,1},{3,2},{4,3},{5,4},{6,5},{7,6},{8,15},{9,8},{10,9... | collective-permute-start | bytes 393224 | tf_op jit(solution)/shard_map/ppermute | solution.py:256
  85.3 3.2 %collective-permute-start.22 = (bf16[512,128]{1,0:T(8,128)(2,1)S(1)}, bf16[512,128]{1,0:T(8,128)(2,1)S(1)}, u32[]{:S(2)}, u32[]{:S(2)}) collective-permute-start(bf16[512,128]{1,0:T(8,128)(2,1)S(1)} %collective-permute-done.21.refs_15_), channel_id=1, source_target_pairs={{0,7},{1,0},{2,1},{3,2},{4,3},{5,4},{6,5},{7,6},{8,15},{9,8},{10,9... | collective-permute-start | bytes 393224 | tf_op jit(solution)/shard_map/ppermute | solution.py:256
  92.0 7.8 %shard_map.106 = (bf16[256,896]{1,0:T(8,128)(2,1)}, f32[512,128]{1,0:T(8,128)}, bf16[512,128]{1,0:T(8,128)(2,1)}, bf16[512,128]{1,0:T(8,128)(2,1)}, bf16[512,128...) custom-call(s32[4]{0:T(128)} %pad_add_fusion.pos_ref, ...), custom_call_target="tpu_custom_call" | custom-call | flops 1580000000 | bytes 10485760 | tf_op jit(solution)/shard_map/pallas_call | solution.py:331
  99.8 7.5 %all-to-all-start.2 = ((bf16[8,32,896]{2,1,0:T(8,128)(2,1)}), bf16[8,32,896]{2,1,0:T(8,128)(2,1)S(1)}, u32[]{:S(2)}, u32[]{:S(2)}) async-start(bf16[8,32,896]{2,1,0:T(8,128)(2,1)} %bitcast.24), calls=%async_computation.2 | async-start | bytes 917504 | tf_op jit(solution)/shard_map/all_to_all | solution.py:345
  107.3 1.6 %collective-permute-start.27 = (bf16[512,128]{1,0:T(8,128)(2,1)}, bf16[512,128]{1,0:T(8,128)(2,1)S(1)}, u32[]{:S(2)}, u32[]{:S(2)}) collective-permute-start(bf16[512,128]{1,0:T(8,128)(2,1)} %get-tuple-element.61), channel_id=1, source_target_pairs={{0,8},{8,16},{16,24},{24,0},{1,9},{9,17},{17,25},{25,1},{2,10},{10... | collective-permute-start | bytes 393224 | tf_op jit(solution)/shard_map/ppermute | solution.py:256
  108.8 2.7 %collective-permute-start.28 = (bf16[512,128]{1,0:T(8,128)(2,1)}, bf16[512,128]{1,0:T(8,128)(2,1)S(1)}, u32[]{:S(2)}, u32[]{:S(2)}) collective-permute-start(bf16[512,128]{1,0:T(8,128)(2,1)} %get-tuple-element.62), channel_id=1, source_target_pairs={{0,16},{8,24},{16,0},{24,8},{1,17},{9,25},{17,1},{25,9},{2,18},{10... | collective-permute-start | bytes 393224 | tf_op jit(solution)/shard_map/ppermute | solution.py:256
  114.4 2.3 %collective-permute-start.32 = (bf16[512,128]{1,0:T(8,128)(2,1)}, bf16[512,128]{1,0:T(8,128)(2,1)S(1)}, u32[]{:S(2)}, u32[]{:S(2)}) collective-permute-start(bf16[512,128]{1,0:T(8,128)(2,1)} %get-tuple-element.67), channel_id=1, source_target_pairs={{0,24},{8,0},{16,8},{24,16},{1,25},{9,1},{17,9},{25,17},{2,26},{10... | collective-permute-start | bytes 393224 | tf_op jit(solution)/shard_map/ppermute | solution.py:256
  116.7 1.7 %collective-permute-done.28 = bf16[512,128]{1,0:T(8,128)(2,1)S(1)} collective-permute-done((bf16[512,128]{1,0:T(8,128)(2,1)}, bf16[512,128]{1,0:T(8,128)(2,1)S(1)}, u32[]{:S(2)}, u32[]{:S(2)}) %collective-permute-start.28) | collective-permute-done | bytes 131104 | tf_op jit(solution)/shard_map/ppermute | solution.py:256
  118.4 1.7 %add_convert_fusion.1 = bf16[512,128]{1,0:T(8,128)(2,1)} fusion(bf16[512,128]{1,0:T(8,128)(2,1)S(1)} %collective-permute-done.29, bf16[512,128]{1,0:T(8,128)(2,1)S(1)} %collective-permute-done.28, f32[512,128]{1,0:T(8,128)} %get-tuple-element.60, bf16[512,128]{1,0:T(8,128)(2,1)S(1)} %collective-permute-done.27), kind=kLoop, calls=%fused_computation.3 | loop fusion | flops 458752 | bytes 786432 | tf_op jit(solution)/shard_map/convert_element_type | solution.py:353
  121.6 1.7 %add_convert_fusion = bf16[512,128]{1,0:T(8,128)(2,1)} fusion(bf16[512,128]{1,0:T(8,128)(2,1)S(1)} %collective-permute-done.32, bf16[512,128]{1,0:T(8,128)(2,1)S(1)} %collective-permute-done.31, f32[512,128]{1,0:T(8,128)} %get-tuple-element.64, bf16[512,128]{1,0:T(8,128)(2,1)S(1)} %collective-permute-done.30), kind=kLoop, calls=%fused_computation.2 | loop fusion | flops 458752 | bytes 786432 | tf_op jit(solution)/shard_map/convert_element_type | solution.py:353
  (98 shorter events, 21.4 us)
Async XLA Ops:
  5.7 49.6 %all-to-all-start.1 = ((bf16[8,4,128,128]{3,2,1,0:T(8,128)(2,1)}), bf16[8,4,128,128]{3,2,1,0:T(8,128)(2,1)}, u32[]{:S(2)}, u32[]{:S(2)}) async-start(bf16[8,4,128,128]{3,2,1,0:T(8,128)(2,1)} %get-tuple-element.59), calls=%async_computation.1 | async-start | bytes 2097152 | tf_op jit(solution)/shard_map/all_to_all | solution.py:275
  14.4 14.7 %collective-permute-start.1 = (bf16[1040,256]{1,0:T(8,128)(2,1)}, bf16[1040,256]{1,0:T(8,128)(2,1)S(1)}, u32[]{:S(2)}, u32[]{:S(2)}) collective-permute-start(bf16[1040,256]{1,0:T(8,128)(2,1)} %get-tuple-element.36.refs_0_), channel_id=1, source_target_pairs={{0,64},{64,128},{128,192},{192,0},{1,65},{65,129},{129,193},{193,1... | collective-permute-start | bytes 1597448 | tf_op jit(solution)/shard_map/ppermute | solution.py:256
  15.9 13.3 %collective-permute-start = (bf16[1040,256]{1,0:T(8,128)(2,1)}, bf16[1040,256]{1,0:T(8,128)(2,1)}, u32[]{:S(2)}, u32[]{:S(2)}) collective-permute-start(bf16[1040,256]{1,0:T(8,128)(2,1)} %get-tuple-element.36.refs_0_), channel_id=1, source_target_pairs={{0,192},{64,0},{128,64},{192,128},{1,193},{65,1},{129,65},{193,129... | collective-permute-start | bytes 1597448 | tf_op jit(solution)/shard_map/ppermute | solution.py:256
  22.0 12.7 %collective-permute-start.3 = (bf16[896,256]{1,0:T(8,128)(2,1)}, bf16[896,256]{1,0:T(8,128)(2,1)}, u32[]{:S(2)}, u32[]{:S(2)}) collective-permute-start(bf16[896,256]{1,0:T(8,128)(2,1)} %get-tuple-element.53.refs_0_), channel_id=1, source_target_pairs={{0,8},{8,16},{16,24},{24,0},{1,9},{9,17},{17,25},{25,1},{2,10},{10... | collective-permute-start | bytes 1376264 | tf_op jit(solution)/shard_map/ppermute | solution.py:256
  23.6 11.2 %collective-permute-start.2 = (bf16[896,256]{1,0:T(8,128)(2,1)}, bf16[896,256]{1,0:T(8,128)(2,1)}, u32[]{:S(2)}, u32[]{:S(2)}) collective-permute-start(bf16[896,256]{1,0:T(8,128)(2,1)} %get-tuple-element.53.refs_0_), channel_id=1, source_target_pairs={{0,24},{8,0},{16,8},{24,16},{1,25},{9,1},{17,9},{25,17},{2,26},{10... | collective-permute-start | bytes 1376264 | tf_op jit(solution)/shard_map/ppermute | solution.py:256
  34.8 7.8 %collective-permute-start.6 = (bf16[512,256]{1,0:T(8,128)(2,1)}, bf16[512,256]{1,0:T(8,128)(2,1)S(1)}, u32[]{:S(2)}, u32[]{:S(2)}) collective-permute-start(bf16[512,256]{1,0:T(8,128)(2,1)} %get-tuple-element.50), channel_id=1, source_target_pairs={{0,64},{64,128},{128,192},{192,0},{1,65},{65,129},{129,193},{193,1... | collective-permute-start | bytes 786440 | tf_op jit(solution)/shard_map/ppermute | solution.py:256
  35.1 10.5 %collective-permute-start.4 = (bf16[896,256]{1,0:T(8,128)(2,1)}, bf16[896,256]{1,0:T(8,128)(2,1)S(1)}, u32[]{:S(2)}, u32[]{:S(2)}) collective-permute-start(bf16[896,256]{1,0:T(8,128)(2,1)} %collective-permute-done.2.refs_1_), channel_id=1, source_target_pairs={{0,24},{8,0},{16,8},{24,16},{1,25},{9,1},{17,9},{25,17},{2,26},{10... | collective-permute-start | bytes 1376264 | tf_op jit(solution)/shard_map/ppermute | solution.py:256
  38.0 7.2 %collective-permute-start.5 = (bf16[528,256]{1,0:T(8,128)(2,1)}, bf16[528,256]{1,0:T(8,128)(2,1)S(1)}, u32[]{:S(2)}, u32[]{:S(2)}) collective-permute-start(bf16[528,256]{1,0:T(8,128)(2,1)} %get-tuple-element.49), channel_id=1, source_target_pairs={{0,192},{64,0},{128,64},{192,128},{1,193},{65,1},{129,65},{193,129... | collective-permute-start | bytes 811016 | tf_op jit(solution)/shard_map/ppermute | solution.py:256
  41.0 6.2 %collective-permute-start.8 = (bf16[1040,256]{1,0:T(8,128)(2,1)}, bf16[1040,256]{1,0:T(8,128)(2,1)}, u32[]{:S(2)}, u32[]{:S(2)}) collective-permute-start(bf16[1040,256]{1,0:T(8,128)(2,1)} %collective-permute-done.after_ref.refs_1_), channel_id=1, source_target_pairs={{0,32},{32,0},{1,33},{33,1},{2,34},{34,2},{3,35},{35,3},{4,36},{36... | collective-permute-start | bytes 1597448 | tf_op jit(solution)/shard_map/ppermute | solution.py:256
  42.6 5.3 %collective-permute-start.11 = (bf16[1040,256]{1,0:T(8,128)(2,1)}, bf16[1040,256]{1,0:T(8,128)(2,1)}, u32[]{:S(2)}, u32[]{:S(2)}) collective-permute-start(bf16[1040,256]{1,0:T(8,128)(2,1)} %copy-done), channel_id=1, source_target_pairs={{0,32},{32,0},{1,33},{33,1},{2,34},{34,2},{3,35},{35,3},{4,36},{36... | collective-permute-start | bytes 1597448 | tf_op jit(solution)/shard_map/ppermute | solution.py:256
  55.3 36.6 %all-to-all-start = ((bf16[32,4,32,256]{3,2,1,0:T(8,128)(2,1)}), bf16[32,4,32,256]{3,2,1,0:T(8,128)(2,1)}, u32[]{:S(2)}, u32[]{:S(2)}) async-start(bf16[32,4,32,256]{3,2,1,0:T(8,128)(2,1)} %bitcast.22), calls=%async_computation | async-start | bytes 4194304 | tf_op jit(solution)/shard_map/all_to_all | solution.py:326
  63.2 28.7 %collective-permute-start.26 = (bf16[8,4,128,128]{3,2,1,0:T(8,128)(2,1)}, bf16[8,4,128,128]{3,2,1,0:T(8,128)(2,1)}, u32[]{:S(2)}, u32[]{:S(2)}) collective-permute-start(bf16[8,4,128,128]{3,2,1,0:T(8,128)(2,1)} %all-to-all-done.1.refs_20_), channel_id=1, source_target_pairs={{0,32},{32,0},{1,33},{33,1},{2,34},{34,2},{3,35},{35,3},{4,36},{36... | collective-permute-start | bytes 3145736 | tf_op jit(solution)/shard_map/ppermute | solution.py:256
  63.5 6.3 %collective-permute-start.12 = (bf16[512,128]{1,0:T(8,128)(2,1)S(1)}, bf16[512,128]{1,0:T(8,128)(2,1)S(1)}, u32[]{:S(2)}, u32[]{:S(2)}) collective-permute-start(bf16[512,128]{1,0:T(8,128)(2,1)S(1)} %copy-done.7), channel_id=1, source_target_pairs={{0,7},{1,0},{2,1},{3,2},{4,3},{5,4},{6,5},{7,6},{8,15},{9,8},{10,9... | collective-permute-start | bytes 393224 | tf_op jit(solution)/shard_map/ppermute | solution.py:256
  64.1 8.4 %collective-permute-start.19 = (bf16[512,128]{1,0:T(8,128)(2,1)S(1)}, bf16[512,128]{1,0:T(8,128)(2,1)S(1)}, u32[]{:S(2)}, u32[]{:S(2)}) collective-permute-start(bf16[512,128]{1,0:T(8,128)(2,1)S(1)} %copy-done.8), channel_id=1, source_target_pairs={{0,7},{1,0},{2,1},{3,2},{4,3},{5,4},{6,5},{7,6},{8,15},{9,8},{10,9... | collective-permute-start | bytes 393224 | tf_op jit(solution)/shard_map/ppermute | solution.py:256
  66.7 7.5 %collective-permute-start.16 = (bf16[512,128]{1,0:T(8,128)(2,1)S(1)}, bf16[512,128]{1,0:T(8,128)(2,1)S(1)}, u32[]{:S(2)}, u32[]{:S(2)}) collective-permute-start(bf16[512,128]{1,0:T(8,128)(2,1)S(1)} %copy-done.7), channel_id=1, source_target_pairs={{0,1},{1,2},{2,3},{3,4},{4,5},{5,6},{6,7},{7,0},{8,9},{9,10},{10,1... | collective-permute-start | bytes 393224 | tf_op jit(solution)/shard_map/ppermute | solution.py:256
  66.7 8.0 %collective-permute-start.23 = (bf16[512,128]{1,0:T(8,128)(2,1)S(1)}, bf16[512,128]{1,0:T(8,128)(2,1)S(1)}, u32[]{:S(2)}, u32[]{:S(2)}) collective-permute-start(bf16[512,128]{1,0:T(8,128)(2,1)S(1)} %copy-done.8), channel_id=1, source_target_pairs={{0,1},{1,2},{2,3},{3,4},{4,5},{5,6},{6,7},{7,0},{8,9},{9,10},{10,1... | collective-permute-start | bytes 393224 | tf_op jit(solution)/shard_map/ppermute | solution.py:256
  69.8 6.4 %collective-permute-start.13 = (bf16[512,128]{1,0:T(8,128)(2,1)S(1)}, bf16[512,128]{1,0:T(8,128)(2,1)S(1)}, u32[]{:S(2)}, u32[]{:S(2)}) collective-permute-start(bf16[512,128]{1,0:T(8,128)(2,1)S(1)} %collective-permute-done.12.refs_5_), channel_id=1, source_target_pairs={{0,7},{1,0},{2,1},{3,2},{4,3},{5,4},{6,5},{7,6},{8,15},{9,8},{10,9... | collective-permute-start | bytes 393224 | tf_op jit(solution)/shard_map/ppermute | solution.py:256
  74.2 6.8 %collective-permute-start.17 = (bf16[512,128]{1,0:T(8,128)(2,1)S(1)}, bf16[512,128]{1,0:T(8,128)(2,1)S(1)}, u32[]{:S(2)}, u32[]{:S(2)}) collective-permute-start(bf16[512,128]{1,0:T(8,128)(2,1)S(1)} %collective-permute-done.16.refs_11_), channel_id=1, source_target_pairs={{0,1},{1,2},{2,3},{3,4},{4,5},{5,6},{6,7},{7,0},{8,9},{9,10},{10,1... | collective-permute-start | bytes 393224 | tf_op jit(solution)/shard_map/ppermute | solution.py:256
  74.7 7.6 %collective-permute-start.24 = (bf16[512,128]{1,0:T(8,128)(2,1)S(1)}, bf16[512,128]{1,0:T(8,128)(2,1)S(1)}, u32[]{:S(2)}, u32[]{:S(2)}) collective-permute-start(bf16[512,128]{1,0:T(8,128)(2,1)S(1)} %collective-permute-done.23.refs_19_), channel_id=1, source_target_pairs={{0,1},{1,2},{2,3},{3,4},{4,5},{5,6},{6,7},{7,0},{8,9},{9,10},{10,1... | collective-permute-start | bytes 393224 | tf_op jit(solution)/shard_map/ppermute | solution.py:256
  76.2 7.3 %collective-permute-start.14 = (bf16[512,128]{1,0:T(8,128)(2,1)S(1)}, bf16[512,128]{1,0:T(8,128)(2,1)S(1)}, u32[]{:S(2)}, u32[]{:S(2)}) collective-permute-start(bf16[512,128]{1,0:T(8,128)(2,1)S(1)} %collective-permute-done.13.refs_6_), channel_id=1, source_target_pairs={{0,7},{1,0},{2,1},{3,2},{4,3},{5,4},{6,5},{7,6},{8,15},{9,8},{10,9... | collective-permute-start | bytes 393224 | tf_op jit(solution)/shard_map/ppermute | solution.py:256
  77.6 7.7 %collective-permute-start.21 = (bf16[512,128]{1,0:T(8,128)(2,1)S(1)}, bf16[512,128]{1,0:T(8,128)(2,1)S(1)}, u32[]{:S(2)}, u32[]{:S(2)}) collective-permute-start(bf16[512,128]{1,0:T(8,128)(2,1)S(1)} %collective-permute-done.20.refs_14_), channel_id=1, source_target_pairs={{0,7},{1,0},{2,1},{3,2},{4,3},{5,4},{6,5},{7,6},{8,15},{9,8},{10,9... | collective-permute-start | bytes 393224 | tf_op jit(solution)/shard_map/ppermute | solution.py:256
  81.0 7.5 %collective-permute-start.18 = (bf16[512,128]{1,0:T(8,128)(2,1)S(1)}, bf16[512,128]{1,0:T(8,128)(2,1)S(1)}, u32[]{:S(2)}, u32[]{:S(2)}) collective-permute-start(bf16[512,128]{1,0:T(8,128)(2,1)S(1)} %collective-permute-done.17.refs_10_), channel_id=1, source_target_pairs={{0,1},{1,2},{2,3},{3,4},{4,5},{5,6},{6,7},{7,0},{8,9},{9,10},{10,1... | collective-permute-start | bytes 393224 | tf_op jit(solution)/shard_map/ppermute | solution.py:256
  82.2 6.6 %collective-permute-start.25 = (bf16[512,128]{1,0:T(8,128)(2,1)S(1)}, bf16[512,128]{1,0:T(8,128)(2,1)S(1)}, u32[]{:S(2)}, u32[]{:S(2)}) collective-permute-start(bf16[512,128]{1,0:T(8,128)(2,1)S(1)} %collective-permute-done.24.refs_18_), channel_id=1, source_target_pairs={{0,1},{1,2},{2,3},{3,4},{4,5},{5,6},{6,7},{7,0},{8,9},{9,10},{10,1... | collective-permute-start | bytes 393224 | tf_op jit(solution)/shard_map/ppermute | solution.py:256
  83.5 6.3 %collective-permute-start.15 = (bf16[512,128]{1,0:T(8,128)(2,1)S(1)}, bf16[512,128]{1,0:T(8,128)(2,1)S(1)}, u32[]{:S(2)}, u32[]{:S(2)}) collective-permute-start(bf16[512,128]{1,0:T(8,128)(2,1)S(1)} %collective-permute-done.14.refs_7_), channel_id=1, source_target_pairs={{0,7},{1,0},{2,1},{3,2},{4,3},{5,4},{6,5},{7,6},{8,15},{9,8},{10,9... | collective-permute-start | bytes 393224 | tf_op jit(solution)/shard_map/ppermute | solution.py:256
  85.3 5.9 %collective-permute-start.22 = (bf16[512,128]{1,0:T(8,128)(2,1)S(1)}, bf16[512,128]{1,0:T(8,128)(2,1)S(1)}, u32[]{:S(2)}, u32[]{:S(2)}) collective-permute-start(bf16[512,128]{1,0:T(8,128)(2,1)S(1)} %collective-permute-done.21.refs_15_), channel_id=1, source_target_pairs={{0,7},{1,0},{2,1},{3,2},{4,3},{5,4},{6,5},{7,6},{8,15},{9,8},{10,9... | collective-permute-start | bytes 393224 | tf_op jit(solution)/shard_map/ppermute | solution.py:256
  99.8 23.5 %all-to-all-start.2 = ((bf16[8,32,896]{2,1,0:T(8,128)(2,1)}), bf16[8,32,896]{2,1,0:T(8,128)(2,1)S(1)}, u32[]{:S(2)}, u32[]{:S(2)}) async-start(bf16[8,32,896]{2,1,0:T(8,128)(2,1)} %bitcast.24), calls=%async_computation.2 | async-start | bytes 917504 | tf_op jit(solution)/shard_map/all_to_all | solution.py:345
  107.3 7.2 %collective-permute-start.27 = (bf16[512,128]{1,0:T(8,128)(2,1)}, bf16[512,128]{1,0:T(8,128)(2,1)S(1)}, u32[]{:S(2)}, u32[]{:S(2)}) collective-permute-start(bf16[512,128]{1,0:T(8,128)(2,1)} %get-tuple-element.61), channel_id=1, source_target_pairs={{0,8},{8,16},{16,24},{24,0},{1,9},{9,17},{17,25},{25,1},{2,10},{10... | collective-permute-start | bytes 393224 | tf_op jit(solution)/shard_map/ppermute | solution.py:256
  108.8 9.5 %collective-permute-start.28 = (bf16[512,128]{1,0:T(8,128)(2,1)}, bf16[512,128]{1,0:T(8,128)(2,1)S(1)}, u32[]{:S(2)}, u32[]{:S(2)}) collective-permute-start(bf16[512,128]{1,0:T(8,128)(2,1)} %get-tuple-element.62), channel_id=1, source_target_pairs={{0,16},{8,24},{16,0},{24,8},{1,17},{9,25},{17,1},{25,9},{2,18},{10... | collective-permute-start | bytes 393224 | tf_op jit(solution)/shard_map/ppermute | solution.py:256
  111.5 6.9 %collective-permute-start.29 = (bf16[512,128]{1,0:T(8,128)(2,1)}, bf16[512,128]{1,0:T(8,128)(2,1)S(1)}, u32[]{:S(2)}, u32[]{:S(2)}) collective-permute-start(bf16[512,128]{1,0:T(8,128)(2,1)} %get-tuple-element.63), channel_id=1, source_target_pairs={{0,24},{8,0},{16,8},{24,16},{1,25},{9,1},{17,9},{25,17},{2,26},{10... | collective-permute-start | bytes 393224 | tf_op jit(solution)/shard_map/ppermute | solution.py:256
  113.0 7.1 %collective-permute-start.30 = (bf16[512,128]{1,0:T(8,128)(2,1)}, bf16[512,128]{1,0:T(8,128)(2,1)S(1)}, u32[]{:S(2)}, u32[]{:S(2)}) collective-permute-start(bf16[512,128]{1,0:T(8,128)(2,1)} %get-tuple-element.65), channel_id=1, source_target_pairs={{0,8},{8,16},{16,24},{24,0},{1,9},{9,17},{17,25},{25,1},{2,10},{10... | collective-permute-start | bytes 393224 | tf_op jit(solution)/shard_map/ppermute | solution.py:256
  113.5 7.6 %collective-permute-start.31 = (bf16[512,128]{1,0:T(8,128)(2,1)}, bf16[512,128]{1,0:T(8,128)(2,1)S(1)}, u32[]{:S(2)}, u32[]{:S(2)}) collective-permute-start(bf16[512,128]{1,0:T(8,128)(2,1)} %get-tuple-element.66), channel_id=1, source_target_pairs={{0,16},{8,24},{16,0},{24,8},{1,17},{9,25},{17,1},{25,9},{2,18},{10... | collective-permute-start | bytes 393224 | tf_op jit(solution)/shard_map/ppermute | solution.py:256
  114.4 7.2 %collective-permute-start.32 = (bf16[512,128]{1,0:T(8,128)(2,1)}, bf16[512,128]{1,0:T(8,128)(2,1)S(1)}, u32[]{:S(2)}, u32[]{:S(2)}) collective-permute-start(bf16[512,128]{1,0:T(8,128)(2,1)} %get-tuple-element.67), channel_id=1, source_target_pairs={{0,24},{8,0},{16,8},{24,16},{1,25},{9,1},{17,9},{25,17},{2,26},{10... | collective-permute-start | bytes 393224 | tf_op jit(solution)/shard_map/ppermute | solution.py:256
  (28 other events, 208.5 us)

commit v5 on v4

--- a/solution.py
+++ b/solution.py
@@ -171,7 +171,8 @@
     for d in range(owners):
         pltpu.make_async_copy(ret_ref.at[d], got_ref.at[d], sem.at[d]).start()
     first = owners
-    pair_copies = [pltpu.make_async_copy(pair_refs[y], pair_ref.at[y], sem.at[first + y]) for y in range(n_y)]
+    to = (0, 1 + 2 * my_c, 2, 3 - 2 * my_c)
+    pair_copies = [pltpu.make_async_copy(pair_refs[y], pair_ref.at[to[y]], sem.at[first + y]) for y in range(n_y)]
     first += n_y
     piece_copies = [
         pltpu.make_async_copy(
@@ -273,11 +274,16 @@
     )(place, ids, enc_rows, w_key, w_value, w_out, w_query)
     after, before, kv_other = x_up(kv), x_down(kv), swap(kv)
     mine = lax.all_to_all(mine, "z", 0, 0, tiled=True)
-    y_up, y_down = shift("y", n_y, -1), shift("y", n_y, 1)
+
+    ways = [(c * n_y + y, c * n_y + (y + 2 * c - 1) % n_y) for c in range(n_c) for y in range(n_y)]
+
+    def along_y(a):
+        return lax.ppermute(a, ("c", "y"), ways)
+
     queries = jnp.dot(hidden, w_query, preferred_element_type=F32).astype(BF)
     grad_attn = lax.dot_general(cotangent, w_out, NT, preferred_element_type=F32).astype(BF)
     pair_, queries = tie((pair, queries))
-    pair_up, pair_down = y_up(pair_), y_down(pair_)
+    pair_next = along_y(pair_)
     after, before, queries, grad_attn = tie((after, before, queries, grad_attn))
 
     cut = HEAD + stored // 2 * seg
@@ -286,10 +292,9 @@
         (jax.ShapeDtypeStruct((cut, 2 * DH), BF), jax.ShapeDtypeStruct((kv.shape[0] - cut, 2 * DH), BF)),
         "aa", 0, 0, scratch=(pltpu.SemaphoreType.DMA((2,)),),
     )(after, before)
-    next_lo, next_hi, pair_up, pair_down = tie((next_lo, next_hi, pair_up, pair_down))
     far_lo, far_hi = x_up(next_lo), x_down(next_hi)
     kv_all = [kv, after, far_lo, far_hi, before, kv_other] + [swap(a) for a in (after, far_lo, far_hi, before)]
-    pairs = [pair, pair_up, y_up(pair_up), pair_down]
+    pairs = [pair, pair_next, along_y(pair_next), swap(pair_next)]
 
     queries, pairs = tie((queries, pairs))
     other = swap(mine)

time: 125 us -> 123 us (0.984)
    ppermute x33 -> x31, starting transfers between devices: 42.4 us -> 35.2 us  [shift(): return lambda a: lax.ppermute(a, axis, [(i, (i + k) % n) for i in range(n)])]
    ppermute x0 -> x2, starting transfers between devices: none -> 6.11 us  [along_y(): return lax.ppermute(a, ('c', 'y'), ways)]
    ppermute x33 -> x31, waiting for transfers between devices: 21.6 us -> 20.4 us  [shift(): return lambda a: lax.ppermute(a, axis, [(i, (i + k) % n) for i in range(n)])]
    unnamed x48 -> x50, local copies, waits for them, and re-layouts: 2.65 us -> 2.12 us
  transfers between devices with their start and end apart: 36 -> 36, of which waited for: 18 -> 16; matrix products, arithmetic and copies ran while one was open for 8% -> 8% of each run, Pallas kernels for 7% -> 8%
where the time goes in v5:
time: 123 us; the launch traced here: 122 us
  starting transfers between devices  65.3 us (53%)
  Pallas kernels  21.6 us (18%)
  waiting for transfers between devices  21.4 us (17%)
  matrix products  6.3 us (5%)
  other arithmetic  4.66 us (4%)
  local copies, waits for them, and re-layouts  2.12 us (2%)
    ppermute x31, starting transfers between devices, shift(): return lambda a: lax.ppermute(a, axis, [(i, (i + k) % n) for i in range(n)])  35.2 us
    ppermute x31, waiting for transfers between devices, shift(): return lambda a: lax.ppermute(a, axis, [(i, (i + k) % n) for i in range(n)])  20.4 us
    all_to_all x1, starting transfers between devices, shards(): mine = lax.all_to_all(mine, 'z', 0, 0, tiled=True)  8.71 us
    all_to_all x1, starting transfers between devices, shards(): lax.all_to_all(outgoing.reshape(owners * n_y, cap, piece, 2 * DH), dp + (...  7.82 us
    pallas_call x1, Pallas kernels, shards(): call(functools.partial(tail_body, stored, n_z), (jax.ShapeDtypeStruct((pi...  7.81 us
    all_to_all x1, starting transfers between devices, shards(): lax.all_to_all(enc_part.reshape(n_z, -1, enc_width), 'z', 0, 0, tiled=True)  7.47 us
    pallas_call x1, Pallas kernels, shards(): call(functools.partial(attention_body, (blocks, block_len, n_x, n_y, cap,...  7.46 us
    ppermute x2, starting transfers between devices, along_y(): return lax.ppermute(a, ('c', 'y'), ways)  6.11 us
  transfers between devices with their start and end apart: 36, of which 16 were waited for; matrix products, arithmetic and copies ran while one was open for 8% of the time, Pallas kernels for 8%

profile of v5, /device:TPU:32, one launch (start us, length us, event | category | flops | bytes accessed | tf_op | source)
XLA Modules:
  0.0 122.2 jit_solution(721812933435938401)
XLA Ops:
  1.3 4.5 %shard_map.103 = (bf16[1040,256]{1,0:T(8,128)(2,1)}, bf16[896,256]{1,0:T(8,128)(2,1)}, bf16[8,4,128,128]{3,2,1,0:T(8,128)(2,1)}) custom-call(s32[4]{0:T(128)} %pad_add_fusion.pos_ref, s32[2,8]{1,0:T(2,128)} %bitcast.26, bf16[1024,896]{1,0:T(8,128)(2,1)} %bitcast.23, bf16[896,128]{1,0:T(8,128)(2,1)} %wk_ref.1, bf16[896,128]{1,0:T(8,128)(2,1)} %wv_ref.1, ...), custom_call_target="tpu_custom_call" | custom-call | flops 470000000 | bytes 5242880 | tf_op jit(solution)/shard_map/pallas_call | solution.py:265
  5.8 8.7 %all-to-all-start.1 = ((bf16[8,4,128,128]{3,2,1,0:T(8,128)(2,1)}), bf16[8,4,128,128]{3,2,1,0:T(8,128)(2,1)}, u32[]{:S(2)}, u32[]{:S(2)}) async-start(bf16[8,4,128,128]{3,2,1,0:T(8,128)(2,1)} %get-tuple-element.51), calls=%async_computation.1 | async-start | bytes 2097152 | tf_op jit(solution)/shard_map/all_to_all | solution.py:276
  14.5 1.5 %collective-permute-start.1 = (bf16[1040,256]{1,0:T(8,128)(2,1)}, bf16[1040,256]{1,0:T(8,128)(2,1)S(1)}, u32[]{:S(2)}, u32[]{:S(2)}) collective-permute-start(bf16[1040,256]{1,0:T(8,128)(2,1)} %get-tuple-element.32.refs_0_), channel_id=1, source_target_pairs={{0,64},{64,128},{128,192},{192,0},{1,65},{65,129},{129,193},{193,1... | collective-permute-start | bytes 1597448 | tf_op jit(solution)/shard_map/ppermute | solution.py:257
  16.0 1.7 %collective-permute-start = (bf16[1040,256]{1,0:T(8,128)(2,1)}, bf16[1040,256]{1,0:T(8,128)(2,1)}, u32[]{:S(2)}, u32[]{:S(2)}) collective-permute-start(bf16[1040,256]{1,0:T(8,128)(2,1)} %get-tuple-element.32.refs_0_), channel_id=1, source_target_pairs={{0,192},{64,0},{128,64},{192,128},{1,193},{65,1},{129,65},{193,129... | collective-permute-start | bytes 1597448 | tf_op jit(solution)/shard_map/ppermute | solution.py:257
  17.7 4.4 %convolution_convert_fusion.1.q_ref = bf16[512,128]{1,0:T(8,128)(2,1)} fusion(bf16[512,4096]{1,0:T(8,128)(2,1)} %param.8, bf16[4096,128]{1,0:T(8,128)(2,1)} %wq_ref.1), kind=kOutput, calls=%fused_computation.1 | convolution fusion | flops 536936448 | bytes 5373952 | tf_op jit(solution)/shard_map/dot_general | solution.py:283
  22.1 3.0 %collective-permute-start.2 = (bf16[896,256]{1,0:T(8,128)(2,1)}, bf16[896,256]{1,0:T(8,128)(2,1)}, u32[]{:S(2)}, u32[]{:S(2)}) collective-permute-start(bf16[896,256]{1,0:T(8,128)(2,1)} %get-tuple-element.45.refs_0_), channel_id=1, source_target_pairs={{0,24},{8,0},{16,8},{24,16},{32,40},{40,48},{48,56},{56,32},{1,25}... | collective-permute-start | bytes 1376264 | tf_op jit(solution)/shard_map/ppermute | solution.py:281
  25.1 1.9 %convolution_convert_fusion.g_ref = bf16[512,128]{1,0:T(8,128)(2,1)} fusion(bf16[512,4096]{1,0:T(8,128)(2,1)S(1)} %copy-done.24, bf16[128,4096]{1,0:T(8,128)(2,1)S(1)} %copy-done.1), kind=kOutput, calls=%fused_computation | convolution fusion | flops 536936448 | bytes 5373952 | tf_op jit(solution)/shard_map/dot_general | solution.py:284
  27.0 2.1 %collective-permute-done.1.before_ref.refs_4_ = bf16[1040,256]{1,0:T(8,128)(2,1)S(1)} collective-permute-done((bf16[1040,256]{1,0:T(8,128)(2,1)}, bf16[1040,256]{1,0:T(8,128)(2,1)S(1)}, u32[]{:S(2)}, u32[]{:S(2)}) %collective-permute-start.1) | collective-permute-done | bytes 532512 | tf_op jit(solution)/shard_map/ppermute | solution.py:257
  30.0 1.8 %shard_map.104 = (bf16[528,256]{1,0:T(8,128)(2,1)}, bf16[512,256]{1,0:T(8,128)(2,1)}) custom-call(bf16[1040,256]{1,0:T(8,128)(2,1)} %collective-permute-done.after_ref.refs_1_, bf16[1040,256]{1,0:T(8,128)(2,1)} %copy-done), custom_call_target="tpu_custom_call" | custom-call | tf_op jit(solution)/shard_map/pallas_call | solution.py:290
  31.8 2.3 %collective-permute-start.5 = (bf16[528,256]{1,0:T(8,128)(2,1)}, bf16[528,256]{1,0:T(8,128)(2,1)S(1)}, u32[]{:S(2)}, u32[]{:S(2)}) collective-permute-start(bf16[528,256]{1,0:T(8,128)(2,1)} %get-tuple-element.41), channel_id=1, source_target_pairs={{0,192},{64,0},{128,64},{192,128},{1,193},{65,1},{129,65},{193,129... | collective-permute-start | bytes 811016 | tf_op jit(solution)/shard_map/ppermute | solution.py:257
  34.2 3.1 %collective-permute-start.3 = (bf16[896,256]{1,0:T(8,128)(2,1)}, bf16[896,256]{1,0:T(8,128)(2,1)S(1)}, u32[]{:S(2)}, u32[]{:S(2)}) collective-permute-start(bf16[896,256]{1,0:T(8,128)(2,1)} %collective-permute-done.2.refs_1_), channel_id=1, source_target_pairs={{0,24},{8,0},{16,8},{24,16},{32,40},{40,48},{48,56},{56,32},{1,25}... | collective-permute-start | bytes 1376264 | tf_op jit(solution)/shard_map/ppermute | solution.py:281
  37.3 4.7 %collective-permute-done.6.refs_3_ = bf16[512,256]{1,0:T(8,128)(2,1)S(1)} collective-permute-done((bf16[512,256]{1,0:T(8,128)(2,1)}, bf16[512,256]{1,0:T(8,128)(2,1)S(1)}, u32[]{:S(2)}, u32[]{:S(2)}) %collective-permute-start.6) | collective-permute-done | bytes 262176 | tf_op jit(solution)/shard_map/ppermute | solution.py:257
  43.6 1.8 %collective-permute-done.10.refs_8_ = bf16[512,256]{1,0:T(8,128)(2,1)S(1)} collective-permute-done((bf16[512,256]{1,0:T(8,128)(2,1)S(1)}, bf16[512,256]{1,0:T(8,128)(2,1)S(1)}, u32[]{:S(2)}, u32[]{:S(2)}) %collective-permute-start.10) | collective-permute-done | bytes 262176 | tf_op jit(solution)/shard_map/ppermute | solution.py:257
  46.1 7.5 %shard_map.105 = (bf16[512,128]{1,0:T(8,128)(2,1)}, bf16[512,128]{1,0:T(8,128)(2,1)}, bf16[8,4,4,32,256]{4,3,2,1,0:T(8,128)(2,1)}, s32[8,128]{1,0:T(8,128)}) custom-call(s32[4]{0:T(128)} %pad_add_fusion.pos_ref, s32[2,8]{1,0:T(2,128)} %bitcast.27, bf16[512,128]{1,0:T(8,128)(2,1)} %convolution_convert_fusion.1.q_ref, ...), custom_call_target="tpu_custom_call" | custom-call | tf_op jit(solution)/shard_map/pallas_call | solution.py:303
  53.6 7.8 %all-to-all-start = ((bf16[32,4,32,256]{3,2,1,0:T(8,128)(2,1)}), bf16[32,4,32,256]{3,2,1,0:T(8,128)(2,1)}, u32[]{:S(2)}, u32[]{:S(2)}) async-start(bf16[32,4,32,256]{3,2,1,0:T(8,128)(2,1)} %bitcast.22), calls=%async_computation | async-start | bytes 4194304 | tf_op jit(solution)/shard_map/all_to_all | solution.py:331
  62.1 2.9 %collective-permute-start.19 = (bf16[512,128]{1,0:T(8,128)(2,1)S(1)}, bf16[512,128]{1,0:T(8,128)(2,1)S(1)}, u32[]{:S(2)}, u32[]{:S(2)}) collective-permute-start(bf16[512,128]{1,0:T(8,128)(2,1)S(1)} %copy-done.9), channel_id=1, source_target_pairs={{0,7},{1,0},{2,1},{3,2},{4,3},{5,4},{6,5},{7,6},{8,15},{9,8},{10,9... | collective-permute-start | bytes 393224 | tf_op jit(solution)/shard_map/ppermute | solution.py:257
  65.8 2.3 %collective-permute-done.12.refs_5_ = bf16[512,128]{1,0:T(8,128)(2,1)S(1)} collective-permute-done((bf16[512,128]{1,0:T(8,128)(2,1)S(1)}, bf16[512,128]{1,0:T(8,128)(2,1)S(1)}, u32[]{:S(2)}, u32[]{:S(2)}) %collective-permute-start.12) | collective-permute-done | bytes 131104 | tf_op jit(solution)/shard_map/ppermute | solution.py:257
  68.8 2.0 %collective-permute-done.19.refs_13_ = bf16[512,128]{1,0:T(8,128)(2,1)S(1)} collective-permute-done((bf16[512,128]{1,0:T(8,128)(2,1)S(1)}, bf16[512,128]{1,0:T(8,128)(2,1)S(1)}, u32[]{:S(2)}, u32[]{:S(2)}) %collective-permute-start.19) | collective-permute-done | bytes 131104 | tf_op jit(solution)/shard_map/ppermute | solution.py:257
  70.8 1.7 %collective-permute-start.20 = (bf16[512,128]{1,0:T(8,128)(2,1)S(1)}, bf16[512,128]{1,0:T(8,128)(2,1)S(1)}, u32[]{:S(2)}, u32[]{:S(2)}) collective-permute-start(bf16[512,128]{1,0:T(8,128)(2,1)S(1)} %collective-permute-done.19.refs_13_), channel_id=1, source_target_pairs={{0,7},{1,0},{2,1},{3,2},{4,3},{5,4},{6,5},{7,6},{8,15},{9,8},{10,9... | collective-permute-start | bytes 393224 | tf_op jit(solution)/shard_map/ppermute | solution.py:257
  72.9 1.6 %collective-permute-start.24 = (bf16[512,128]{1,0:T(8,128)(2,1)S(1)}, bf16[512,128]{1,0:T(8,128)(2,1)S(1)}, u32[]{:S(2)}, u32[]{:S(2)}) collective-permute-start(bf16[512,128]{1,0:T(8,128)(2,1)S(1)} %collective-permute-done.23.refs_19_), channel_id=1, source_target_pairs={{0,1},{1,2},{2,3},{3,4},{4,5},{5,6},{6,7},{7,0},{8,9},{9,10},{10,1... | collective-permute-start | bytes 393224 | tf_op jit(solution)/shard_map/ppermute | solution.py:257
  75.9 3.4 %collective-permute-start.21 = (bf16[512,128]{1,0:T(8,128)(2,1)S(1)}, bf16[512,128]{1,0:T(8,128)(2,1)S(1)}, u32[]{:S(2)}, u32[]{:S(2)}) collective-permute-start(bf16[512,128]{1,0:T(8,128)(2,1)S(1)} %collective-permute-done.20.refs_14_), channel_id=1, source_target_pairs={{0,7},{1,0},{2,1},{3,2},{4,3},{5,4},{6,5},{7,6},{8,15},{9,8},{10,9... | collective-permute-start | bytes 393224 | tf_op jit(solution)/shard_map/ppermute | solution.py:257
  81.8 1.8 %collective-permute-start.15 = (bf16[512,128]{1,0:T(8,128)(2,1)S(1)}, bf16[512,128]{1,0:T(8,128)(2,1)S(1)}, u32[]{:S(2)}, u32[]{:S(2)}) collective-permute-start(bf16[512,128]{1,0:T(8,128)(2,1)S(1)} %collective-permute-done.14.refs_7_), channel_id=1, source_target_pairs={{0,7},{1,0},{2,1},{3,2},{4,3},{5,4},{6,5},{7,6},{8,15},{9,8},{10,9... | collective-permute-start | bytes 393224 | tf_op jit(solution)/shard_map/ppermute | solution.py:257
  83.6 3.2 %collective-permute-start.22 = (bf16[512,128]{1,0:T(8,128)(2,1)S(1)}, bf16[512,128]{1,0:T(8,128)(2,1)S(1)}, u32[]{:S(2)}, u32[]{:S(2)}) collective-permute-start(bf16[512,128]{1,0:T(8,128)(2,1)S(1)} %collective-permute-done.21.refs_15_), channel_id=1, source_target_pairs={{0,7},{1,0},{2,1},{3,2},{4,3},{5,4},{6,5},{7,6},{8,15},{9,8},{10,9... | collective-permute-start | bytes 393224 | tf_op jit(solution)/shard_map/ppermute | solution.py:257
  90.2 7.8 %shard_map.106 = (bf16[256,896]{1,0:T(8,128)(2,1)}, f32[512,128]{1,0:T(8,128)}, bf16[512,128]{1,0:T(8,128)(2,1)}, bf16[512,128]{1,0:T(8,128)(2,1)}, bf16[512,128...) custom-call(s32[4]{0:T(128)} %pad_add_fusion.pos_ref, ...), custom_call_target="tpu_custom_call" | custom-call | flops 1580000000 | bytes 10485760 | tf_op jit(solution)/shard_map/pallas_call | solution.py:336
  98.1 7.5 %all-to-all-start.2 = ((bf16[8,32,896]{2,1,0:T(8,128)(2,1)}), bf16[8,32,896]{2,1,0:T(8,128)(2,1)S(1)}, u32[]{:S(2)}, u32[]{:S(2)}) async-start(bf16[8,32,896]{2,1,0:T(8,128)(2,1)} %bitcast.24), calls=%async_computation.2 | async-start | bytes 917504 | tf_op jit(solution)/shard_map/all_to_all | solution.py:350
  105.5 1.6 %collective-permute-start.27 = (bf16[512,128]{1,0:T(8,128)(2,1)}, bf16[512,128]{1,0:T(8,128)(2,1)S(1)}, u32[]{:S(2)}, u32[]{:S(2)}) collective-permute-start(bf16[512,128]{1,0:T(8,128)(2,1)} %get-tuple-element.53), channel_id=1, source_target_pairs={{0,8},{8,16},{16,24},{24,0},{1,9},{9,17},{17,25},{25,1},{2,10},{10... | collective-permute-start | bytes 393224 | tf_op jit(solution)/shard_map/ppermute | solution.py:257
  107.1 2.7 %collective-permute-start.28 = (bf16[512,128]{1,0:T(8,128)(2,1)}, bf16[512,128]{1,0:T(8,128)(2,1)S(1)}, u32[]{:S(2)}, u32[]{:S(2)}) collective-permute-start(bf16[512,128]{1,0:T(8,128)(2,1)} %get-tuple-element.54), channel_id=1, source_target_pairs={{0,16},{8,24},{16,0},{24,8},{1,17},{9,25},{17,1},{25,9},{2,18},{10... | collective-permute-start | bytes 393224 | tf_op jit(solution)/shard_map/ppermute | solution.py:257
  109.8 1.5 %collective-permute-start.29 = (bf16[512,128]{1,0:T(8,128)(2,1)}, bf16[512,128]{1,0:T(8,128)(2,1)S(1)}, u32[]{:S(2)}, u32[]{:S(2)}) collective-permute-start(bf16[512,128]{1,0:T(8,128)(2,1)} %get-tuple-element.55), channel_id=1, source_target_pairs={{0,24},{8,0},{16,8},{24,16},{1,25},{9,1},{17,9},{25,17},{2,26},{10... | collective-permute-start | bytes 393224 | tf_op jit(solution)/shard_map/ppermute | solution.py:257
  112.7 2.3 %collective-permute-start.32 = (bf16[512,128]{1,0:T(8,128)(2,1)}, bf16[512,128]{1,0:T(8,128)(2,1)S(1)}, u32[]{:S(2)}, u32[]{:S(2)}) collective-permute-start(bf16[512,128]{1,0:T(8,128)(2,1)} %get-tuple-element.59), channel_id=1, source_target_pairs={{0,24},{8,0},{16,8},{24,16},{1,25},{9,1},{17,9},{25,17},{2,26},{10... | collective-permute-start | bytes 393224 | tf_op jit(solution)/shard_map/ppermute | solution.py:257
  114.9 1.7 %collective-permute-done.28 = bf16[512,128]{1,0:T(8,128)(2,1)S(1)} collective-permute-done((bf16[512,128]{1,0:T(8,128)(2,1)}, bf16[512,128]{1,0:T(8,128)(2,1)S(1)}, u32[]{:S(2)}, u32[]{:S(2)}) %collective-permute-start.28) | collective-permute-done | bytes 131104 | tf_op jit(solution)/shard_map/ppermute | solution.py:257
  116.6 1.7 %add_convert_fusion.1 = bf16[512,128]{1,0:T(8,128)(2,1)} fusion(bf16[512,128]{1,0:T(8,128)(2,1)S(1)} %collective-permute-done.29, bf16[512,128]{1,0:T(8,128)(2,1)S(1)} %collective-permute-done.28, f32[512,128]{1,0:T(8,128)} %get-tuple-element.52, bf16[512,128]{1,0:T(8,128)(2,1)S(1)} %collective-permute-done.27), kind=kLoop, calls=%fused_computation.3 | loop fusion | flops 458752 | bytes 786432 | tf_op jit(solution)/shard_map/convert_element_type | solution.py:358
  119.9 1.7 %add_convert_fusion = bf16[512,128]{1,0:T(8,128)(2,1)} fusion(bf16[512,128]{1,0:T(8,128)(2,1)S(1)} %collective-permute-done.32, bf16[512,128]{1,0:T(8,128)(2,1)S(1)} %collective-permute-done.31, f32[512,128]{1,0:T(8,128)} %get-tuple-element.56, bf16[512,128]{1,0:T(8,128)(2,1)S(1)} %collective-permute-done.30), kind=kLoop, calls=%fused_computation.2 | loop fusion | flops 458752 | bytes 786432 | tf_op jit(solution)/shard_map/convert_element_type | solution.py:358
  (100 shorter events, 17.4 us)
Async XLA Ops:
  5.8 47.8 %all-to-all-start.1 = ((bf16[8,4,128,128]{3,2,1,0:T(8,128)(2,1)}), bf16[8,4,128,128]{3,2,1,0:T(8,128)(2,1)}, u32[]{:S(2)}, u32[]{:S(2)}) async-start(bf16[8,4,128,128]{3,2,1,0:T(8,128)(2,1)} %get-tuple-element.51), calls=%async_computation.1 | async-start | bytes 2097152 | tf_op jit(solution)/shard_map/all_to_all | solution.py:276
  14.5 14.7 %collective-permute-start.1 = (bf16[1040,256]{1,0:T(8,128)(2,1)}, bf16[1040,256]{1,0:T(8,128)(2,1)S(1)}, u32[]{:S(2)}, u32[]{:S(2)}) collective-permute-start(bf16[1040,256]{1,0:T(8,128)(2,1)} %get-tuple-element.32.refs_0_), channel_id=1, source_target_pairs={{0,64},{64,128},{128,192},{192,0},{1,65},{65,129},{129,193},{193,1... | collective-permute-start | bytes 1597448 | tf_op jit(solution)/shard_map/ppermute | solution.py:257
  16.0 13.3 %collective-permute-start = (bf16[1040,256]{1,0:T(8,128)(2,1)}, bf16[1040,256]{1,0:T(8,128)(2,1)}, u32[]{:S(2)}, u32[]{:S(2)}) collective-permute-start(bf16[1040,256]{1,0:T(8,128)(2,1)} %get-tuple-element.32.refs_0_), channel_id=1, source_target_pairs={{0,192},{64,0},{128,64},{192,128},{1,193},{65,1},{129,65},{193,129... | collective-permute-start | bytes 1597448 | tf_op jit(solution)/shard_map/ppermute | solution.py:257
  22.1 12.1 %collective-permute-start.2 = (bf16[896,256]{1,0:T(8,128)(2,1)}, bf16[896,256]{1,0:T(8,128)(2,1)}, u32[]{:S(2)}, u32[]{:S(2)}) collective-permute-start(bf16[896,256]{1,0:T(8,128)(2,1)} %get-tuple-element.45.refs_0_), channel_id=1, source_target_pairs={{0,24},{8,0},{16,8},{24,16},{32,40},{40,48},{48,56},{56,32},{1,25}... | collective-permute-start | bytes 1376264 | tf_op jit(solution)/shard_map/ppermute | solution.py:281
  31.8 10.1 %collective-permute-start.5 = (bf16[528,256]{1,0:T(8,128)(2,1)}, bf16[528,256]{1,0:T(8,128)(2,1)S(1)}, u32[]{:S(2)}, u32[]{:S(2)}) collective-permute-start(bf16[528,256]{1,0:T(8,128)(2,1)} %get-tuple-element.41), channel_id=1, source_target_pairs={{0,192},{64,0},{128,64},{192,128},{1,193},{65,1},{129,65},{193,129... | collective-permute-start | bytes 811016 | tf_op jit(solution)/shard_map/ppermute | solution.py:257
  34.2 7.8 %collective-permute-start.6 = (bf16[512,256]{1,0:T(8,128)(2,1)}, bf16[512,256]{1,0:T(8,128)(2,1)S(1)}, u32[]{:S(2)}, u32[]{:S(2)}) collective-permute-start(bf16[512,256]{1,0:T(8,128)(2,1)} %get-tuple-element.42), channel_id=1, source_target_pairs={{0,64},{64,128},{128,192},{192,0},{1,65},{65,129},{129,193},{193,1... | collective-permute-start | bytes 786440 | tf_op jit(solution)/shard_map/ppermute | solution.py:257
  34.2 8.3 %collective-permute-start.4 = (bf16[896,256]{1,0:T(8,128)(2,1)}, bf16[896,256]{1,0:T(8,128)(2,1)S(1)}, u32[]{:S(2)}, u32[]{:S(2)}) collective-permute-start(bf16[896,256]{1,0:T(8,128)(2,1)} %collective-permute-done.2.refs_1_), channel_id=1, source_target_pairs={{0,32},{32,0},{1,33},{33,1},{2,34},{34,2},{3,35},{35,3},{4,36},{36... | collective-permute-start | bytes 1376264 | tf_op jit(solution)/shard_map/ppermute | solution.py:257
  34.2 9.4 %collective-permute-start.3 = (bf16[896,256]{1,0:T(8,128)(2,1)}, bf16[896,256]{1,0:T(8,128)(2,1)S(1)}, u32[]{:S(2)}, u32[]{:S(2)}) collective-permute-start(bf16[896,256]{1,0:T(8,128)(2,1)} %collective-permute-done.2.refs_1_), channel_id=1, source_target_pairs={{0,24},{8,0},{16,8},{24,16},{32,40},{40,48},{48,56},{56,32},{1,25}... | collective-permute-start | bytes 1376264 | tf_op jit(solution)/shard_map/ppermute | solution.py:281
  37.3 6.3 %collective-permute-start.7 = (bf16[1040,256]{1,0:T(8,128)(2,1)}, bf16[1040,256]{1,0:T(8,128)(2,1)S(1)}, u32[]{:S(2)}, u32[]{:S(2)}) collective-permute-start(bf16[1040,256]{1,0:T(8,128)(2,1)} %get-tuple-element.32.refs_0_), channel_id=1, source_target_pairs={{0,32},{32,0},{1,33},{33,1},{2,34},{34,2},{3,35},{35,3},{4,36},{36... | collective-permute-start | bytes 1597448 | tf_op jit(solution)/shard_map/ppermute | solution.py:257
  53.6 36.6 %all-to-all-start = ((bf16[32,4,32,256]{3,2,1,0:T(8,128)(2,1)}), bf16[32,4,32,256]{3,2,1,0:T(8,128)(2,1)}, u32[]{:S(2)}, u32[]{:S(2)}) async-start(bf16[32,4,32,256]{3,2,1,0:T(8,128)(2,1)} %bitcast.22), calls=%async_computation | async-start | bytes 4194304 | tf_op jit(solution)/shard_map/all_to_all | solution.py:331
  61.4 28.8 %collective-permute-start.26 = (bf16[8,4,128,128]{3,2,1,0:T(8,128)(2,1)}, bf16[8,4,128,128]{3,2,1,0:T(8,128)(2,1)}, u32[]{:S(2)}, u32[]{:S(2)}) collective-permute-start(bf16[8,4,128,128]{3,2,1,0:T(8,128)(2,1)} %all-to-all-done.1.refs_20_), channel_id=1, source_target_pairs={{0,32},{32,0},{1,33},{33,1},{2,34},{34,2},{3,35},{35,3},{4,36},{36... | collective-permute-start | bytes 3145736 | tf_op jit(solution)/shard_map/ppermute | solution.py:257
  61.7 6.3 %collective-permute-start.12 = (bf16[512,128]{1,0:T(8,128)(2,1)S(1)}, bf16[512,128]{1,0:T(8,128)(2,1)S(1)}, u32[]{:S(2)}, u32[]{:S(2)}) collective-permute-start(bf16[512,128]{1,0:T(8,128)(2,1)S(1)} %copy-done.8), channel_id=1, source_target_pairs={{0,7},{1,0},{2,1},{3,2},{4,3},{5,4},{6,5},{7,6},{8,15},{9,8},{10,9... | collective-permute-start | bytes 393224 | tf_op jit(solution)/shard_map/ppermute | solution.py:257
  62.1 8.7 %collective-permute-start.19 = (bf16[512,128]{1,0:T(8,128)(2,1)S(1)}, bf16[512,128]{1,0:T(8,128)(2,1)S(1)}, u32[]{:S(2)}, u32[]{:S(2)}) collective-permute-start(bf16[512,128]{1,0:T(8,128)(2,1)S(1)} %copy-done.9), channel_id=1, source_target_pairs={{0,7},{1,0},{2,1},{3,2},{4,3},{5,4},{6,5},{7,6},{8,15},{9,8},{10,9... | collective-permute-start | bytes 393224 | tf_op jit(solution)/shard_map/ppermute | solution.py:257
  65.0 7.5 %collective-permute-start.16 = (bf16[512,128]{1,0:T(8,128)(2,1)S(1)}, bf16[512,128]{1,0:T(8,128)(2,1)S(1)}, u32[]{:S(2)}, u32[]{:S(2)}) collective-permute-start(bf16[512,128]{1,0:T(8,128)(2,1)S(1)} %copy-done.8), channel_id=1, source_target_pairs={{0,1},{1,2},{2,3},{3,4},{4,5},{5,6},{6,7},{7,0},{8,9},{9,10},{10,1... | collective-permute-start | bytes 393224 | tf_op jit(solution)/shard_map/ppermute | solution.py:257
  65.0 8.0 %collective-permute-start.23 = (bf16[512,128]{1,0:T(8,128)(2,1)S(1)}, bf16[512,128]{1,0:T(8,128)(2,1)S(1)}, u32[]{:S(2)}, u32[]{:S(2)}) collective-permute-start(bf16[512,128]{1,0:T(8,128)(2,1)S(1)} %copy-done.9), channel_id=1, source_target_pairs={{0,1},{1,2},{2,3},{3,4},{4,5},{5,6},{6,7},{7,0},{8,9},{9,10},{10,1... | collective-permute-start | bytes 393224 | tf_op jit(solution)/shard_map/ppermute | solution.py:257
  68.0 6.4 %collective-permute-start.13 = (bf16[512,128]{1,0:T(8,128)(2,1)S(1)}, bf16[512,128]{1,0:T(8,128)(2,1)S(1)}, u32[]{:S(2)}, u32[]{:S(2)}) collective-permute-start(bf16[512,128]{1,0:T(8,128)(2,1)S(1)} %collective-permute-done.12.refs_5_), channel_id=1, source_target_pairs={{0,7},{1,0},{2,1},{3,2},{4,3},{5,4},{6,5},{7,6},{8,15},{9,8},{10,9... | collective-permute-start | bytes 393224 | tf_op jit(solution)/shard_map/ppermute | solution.py:257
  70.8 5.1 %collective-permute-start.20 = (bf16[512,128]{1,0:T(8,128)(2,1)S(1)}, bf16[512,128]{1,0:T(8,128)(2,1)S(1)}, u32[]{:S(2)}, u32[]{:S(2)}) collective-permute-start(bf16[512,128]{1,0:T(8,128)(2,1)S(1)} %collective-permute-done.19.refs_13_), channel_id=1, source_target_pairs={{0,7},{1,0},{2,1},{3,2},{4,3},{5,4},{6,5},{7,6},{8,15},{9,8},{10,9... | collective-permute-start | bytes 393224 | tf_op jit(solution)/shard_map/ppermute | solution.py:257
  72.5 6.8 %collective-permute-start.17 = (bf16[512,128]{1,0:T(8,128)(2,1)S(1)}, bf16[512,128]{1,0:T(8,128)(2,1)S(1)}, u32[]{:S(2)}, u32[]{:S(2)}) collective-permute-start(bf16[512,128]{1,0:T(8,128)(2,1)S(1)} %collective-permute-done.16.refs_11_), channel_id=1, source_target_pairs={{0,1},{1,2},{2,3},{3,4},{4,5},{5,6},{6,7},{7,0},{8,9},{9,10},{10,1... | collective-permute-start | bytes 393224 | tf_op jit(solution)/shard_map/ppermute | solution.py:257
  72.9 7.6 %collective-permute-start.24 = (bf16[512,128]{1,0:T(8,128)(2,1)S(1)}, bf16[512,128]{1,0:T(8,128)(2,1)S(1)}, u32[]{:S(2)}, u32[]{:S(2)}) collective-permute-start(bf16[512,128]{1,0:T(8,128)(2,1)S(1)} %collective-permute-done.23.refs_19_), channel_id=1, source_target_pairs={{0,1},{1,2},{2,3},{3,4},{4,5},{5,6},{6,7},{7,0},{8,9},{9,10},{10,1... | collective-permute-start | bytes 393224 | tf_op jit(solution)/shard_map/ppermute | solution.py:257
  74.5 7.3 %collective-permute-start.14 = (bf16[512,128]{1,0:T(8,128)(2,1)S(1)}, bf16[512,128]{1,0:T(8,128)(2,1)S(1)}, u32[]{:S(2)}, u32[]{:S(2)}) collective-permute-start(bf16[512,128]{1,0:T(8,128)(2,1)S(1)} %collective-permute-done.13.refs_6_), channel_id=1, source_target_pairs={{0,7},{1,0},{2,1},{3,2},{4,3},{5,4},{6,5},{7,6},{8,15},{9,8},{10,9... | collective-permute-start | bytes 393224 | tf_op jit(solution)/shard_map/ppermute | solution.py:257
  75.9 7.7 %collective-permute-start.21 = (bf16[512,128]{1,0:T(8,128)(2,1)S(1)}, bf16[512,128]{1,0:T(8,128)(2,1)S(1)}, u32[]{:S(2)}, u32[]{:S(2)}) collective-permute-start(bf16[512,128]{1,0:T(8,128)(2,1)S(1)} %collective-permute-done.20.refs_14_), channel_id=1, source_target_pairs={{0,7},{1,0},{2,1},{3,2},{4,3},{5,4},{6,5},{7,6},{8,15},{9,8},{10,9... | collective-permute-start | bytes 393224 | tf_op jit(solution)/shard_map/ppermute | solution.py:257
  79.3 7.5 %collective-permute-start.18 = (bf16[512,128]{1,0:T(8,128)(2,1)S(1)}, bf16[512,128]{1,0:T(8,128)(2,1)S(1)}, u32[]{:S(2)}, u32[]{:S(2)}) collective-permute-start(bf16[512,128]{1,0:T(8,128)(2,1)S(1)} %collective-permute-done.17.refs_10_), channel_id=1, source_target_pairs={{0,1},{1,2},{2,3},{3,4},{4,5},{5,6},{6,7},{7,0},{8,9},{9,10},{10,1... | collective-permute-start | bytes 393224 | tf_op jit(solution)/shard_map/ppermute | solution.py:257
  80.5 6.6 %collective-permute-start.25 = (bf16[512,128]{1,0:T(8,128)(2,1)S(1)}, bf16[512,128]{1,0:T(8,128)(2,1)S(1)}, u32[]{:S(2)}, u32[]{:S(2)}) collective-permute-start(bf16[512,128]{1,0:T(8,128)(2,1)S(1)} %collective-permute-done.24.refs_18_), channel_id=1, source_target_pairs={{0,1},{1,2},{2,3},{3,4},{4,5},{5,6},{6,7},{7,0},{8,9},{9,10},{10,1... | collective-permute-start | bytes 393224 | tf_op jit(solution)/shard_map/ppermute | solution.py:257
  81.8 6.3 %collective-permute-start.15 = (bf16[512,128]{1,0:T(8,128)(2,1)S(1)}, bf16[512,128]{1,0:T(8,128)(2,1)S(1)}, u32[]{:S(2)}, u32[]{:S(2)}) collective-permute-start(bf16[512,128]{1,0:T(8,128)(2,1)S(1)} %collective-permute-done.14.refs_7_), channel_id=1, source_target_pairs={{0,7},{1,0},{2,1},{3,2},{4,3},{5,4},{6,5},{7,6},{8,15},{9,8},{10,9... | collective-permute-start | bytes 393224 | tf_op jit(solution)/shard_map/ppermute | solution.py:257
  83.6 5.9 %collective-permute-start.22 = (bf16[512,128]{1,0:T(8,128)(2,1)S(1)}, bf16[512,128]{1,0:T(8,128)(2,1)S(1)}, u32[]{:S(2)}, u32[]{:S(2)}) collective-permute-start(bf16[512,128]{1,0:T(8,128)(2,1)S(1)} %collective-permute-done.21.refs_15_), channel_id=1, source_target_pairs={{0,7},{1,0},{2,1},{3,2},{4,3},{5,4},{6,5},{7,6},{8,15},{9,8},{10,9... | collective-permute-start | bytes 393224 | tf_op jit(solution)/shard_map/ppermute | solution.py:257
  98.1 23.5 %all-to-all-start.2 = ((bf16[8,32,896]{2,1,0:T(8,128)(2,1)}), bf16[8,32,896]{2,1,0:T(8,128)(2,1)S(1)}, u32[]{:S(2)}, u32[]{:S(2)}) async-start(bf16[8,32,896]{2,1,0:T(8,128)(2,1)} %bitcast.24), calls=%async_computation.2 | async-start | bytes 917504 | tf_op jit(solution)/shard_map/all_to_all | solution.py:350
  105.5 7.2 %collective-permute-start.27 = (bf16[512,128]{1,0:T(8,128)(2,1)}, bf16[512,128]{1,0:T(8,128)(2,1)S(1)}, u32[]{:S(2)}, u32[]{:S(2)}) collective-permute-start(bf16[512,128]{1,0:T(8,128)(2,1)} %get-tuple-element.53), channel_id=1, source_target_pairs={{0,8},{8,16},{16,24},{24,0},{1,9},{9,17},{17,25},{25,1},{2,10},{10... | collective-permute-start | bytes 393224 | tf_op jit(solution)/shard_map/ppermute | solution.py:257
  107.1 9.6 %collective-permute-start.28 = (bf16[512,128]{1,0:T(8,128)(2,1)}, bf16[512,128]{1,0:T(8,128)(2,1)S(1)}, u32[]{:S(2)}, u32[]{:S(2)}) collective-permute-start(bf16[512,128]{1,0:T(8,128)(2,1)} %get-tuple-element.54), channel_id=1, source_target_pairs={{0,16},{8,24},{16,0},{24,8},{1,17},{9,25},{17,1},{25,9},{2,18},{10... | collective-permute-start | bytes 393224 | tf_op jit(solution)/shard_map/ppermute | solution.py:257
  109.8 6.9 %collective-permute-start.29 = (bf16[512,128]{1,0:T(8,128)(2,1)}, bf16[512,128]{1,0:T(8,128)(2,1)S(1)}, u32[]{:S(2)}, u32[]{:S(2)}) collective-permute-start(bf16[512,128]{1,0:T(8,128)(2,1)} %get-tuple-element.55), channel_id=1, source_target_pairs={{0,24},{8,0},{16,8},{24,16},{1,25},{9,1},{17,9},{25,17},{2,26},{10... | collective-permute-start | bytes 393224 | tf_op jit(solution)/shard_map/ppermute | solution.py:257
  111.2 7.1 %collective-permute-start.30 = (bf16[512,128]{1,0:T(8,128)(2,1)}, bf16[512,128]{1,0:T(8,128)(2,1)S(1)}, u32[]{:S(2)}, u32[]{:S(2)}) collective-permute-start(bf16[512,128]{1,0:T(8,128)(2,1)} %get-tuple-element.57), channel_id=1, source_target_pairs={{0,8},{8,16},{16,24},{24,0},{1,9},{9,17},{17,25},{25,1},{2,10},{10... | collective-permute-start | bytes 393224 | tf_op jit(solution)/shard_map/ppermute | solution.py:257
  111.8 7.6 %collective-permute-start.31 = (bf16[512,128]{1,0:T(8,128)(2,1)}, bf16[512,128]{1,0:T(8,128)(2,1)S(1)}, u32[]{:S(2)}, u32[]{:S(2)}) collective-permute-start(bf16[512,128]{1,0:T(8,128)(2,1)} %get-tuple-element.58), channel_id=1, source_target_pairs={{0,16},{8,24},{16,0},{24,8},{1,17},{9,25},{17,1},{25,9},{2,18},{10... | collective-permute-start | bytes 393224 | tf_op jit(solution)/shard_map/ppermute | solution.py:257
  112.7 7.2 %collective-permute-start.32 = (bf16[512,128]{1,0:T(8,128)(2,1)}, bf16[512,128]{1,0:T(8,128)(2,1)S(1)}, u32[]{:S(2)}, u32[]{:S(2)}) collective-permute-start(bf16[512,128]{1,0:T(8,128)(2,1)} %get-tuple-element.59), channel_id=1, source_target_pairs={{0,24},{8,0},{16,8},{24,16},{1,25},{9,1},{17,9},{25,17},{2,26},{10... | collective-permute-start | bytes 393224 | tf_op jit(solution)/shard_map/ppermute | solution.py:257
  (29 other events, 209.5 us)

commit v6 on v5

--- a/solution.py
+++ b/solution.py
@@ -14,7 +14,8 @@
 NT = (((1,), (1,)), ((), ()))
 TN = (((0,), (0,)), ((), ()))
 HEAD = 16
-VMEM_LIMIT = 63 * 1024 * 1024
+GROUP = 8
+VMEM_LIMIT = 64 * 1024 * 1024 - 64 * 1024
 
 
 def params():
@@ -119,38 +120,51 @@
         head_copies.append(pltpu.make_async_copy(ref.at[:HEAD, :DH], head_ref.at[i], sem.at[requests + i]))
         head_copies[-1].start()
 
-    sent = []
     for r in range(requests):
         pltpu.make_async_copy(kv_refs[0].at[:seg, :], kv_ref.at[r], sem.at[r]).wait()
-    for c in range(blocks):
+
+    def context(c):
         both = [kv_ref[r] for r in (2 * c, 2 * c + 1)]
-        k = jnp.concatenate([b[:, :DH] for b in both], axis=0)
-        v = jnp.concatenate([b[:, DH:] for b in both], axis=0)
-        rows = slice(c * block_len, (c + 1) * block_len)
-        q = q_ref[rows, :]
-        g = g_ref[rows, :]
-        s = lax.dot_general(q, k, NT, preferred_element_type=F32) * inv_root
-        e = jnp.exp(s - jnp.max(s, axis=-1, keepdims=True))
-        p = e / jnp.sum(e, axis=-1, keepdims=True)
-        ph = p.astype(BF)
-        gp = lax.dot_general(g, v, NT, preferred_element_type=F32)
-        attn_ref[rows, :] = jnp.dot(ph, v, preferred_element_type=F32).astype(BF)
-        gs = (p * (gp - jnp.sum(p * gp, axis=-1, keepdims=True))).astype(BF)
-        gq_ref[rows, :] = (jnp.dot(gs, k, preferred_element_type=F32) * inv_root).astype(BF)
-        gv = lax.dot_general(ph, g, TN, preferred_element_type=F32).astype(BF)
-        gk = (lax.dot_general(gs, q, TN, preferred_element_type=F32) * inv_root).astype(BF)
-        for j in range(2):
-            r = 2 * c + j
-            owner = spots[r]
-            pos = sum([(spots[i] == owner).astype(jnp.int32) for i in range(r)], jnp.int32(0))
-            for y in range(n_y):
-                part = slice(j * seg + y * piece, j * seg + (y + 1) * piece)
-                stage_ref[r, y, :, :DH] = gk[part, :]
-                stage_ref[r, y, :, DH:] = gv[part, :]
-            sent.append(
-                pltpu.make_async_copy(stage_ref.at[r], out_ref.at[owner, :, pos], sem.at[requests + len(heads) + r])
-            )
-            sent[-1].start()
+        return [jnp.concatenate([b[:, at : at + DH] for b in both], axis=0) for at in (0, DH)]
+
+    def rows(c):
+        return slice(c * block_len, (c + 1) * block_len)
+
+    sent = []
+    for first in range(0, blocks, GROUP):
+        group = range(first, first + GROUP)
+        scores, grad_probs, probs, grad_scores = {}, {}, {}, {}
+        for c in group:
+            k, v = context(c)
+            scores[c] = lax.dot_general(q_ref[rows(c), :], k, NT, preferred_element_type=F32) * inv_root
+            grad_probs[c] = lax.dot_general(g_ref[rows(c), :], v, NT, preferred_element_type=F32)
+        for c in group:
+            e = jnp.exp(scores[c] - jnp.max(scores[c], axis=-1, keepdims=True))
+            p = e / jnp.sum(e, axis=-1, keepdims=True)
+            probs[c] = p.astype(BF)
+            gp = grad_probs[c]
+            grad_scores[c] = (p * (gp - jnp.sum(p * gp, axis=-1, keepdims=True))).astype(BF)
+        for c in group:
+            k, v = context(c)
+            attn_ref[rows(c), :] = jnp.dot(probs[c], v, preferred_element_type=F32).astype(BF)
+            gq_ref[rows(c), :] = (jnp.dot(grad_scores[c], k, preferred_element_type=F32) * inv_root).astype(BF)
+        for c in group:
+            gv = lax.dot_general(probs[c], g_ref[rows(c), :], TN, preferred_element_type=F32).astype(BF)
+            gk = lax.dot_general(grad_scores[c], q_ref[rows(c), :], TN, preferred_element_type=F32)
+            gk = (gk * inv_root).astype(BF)
+            for j in range(2):
+                r = 2 * c + j
+                owner = spots[r]
+                pos = sum([(spots[i] == owner).astype(jnp.int32) for i in range(r)], jnp.int32(0))
+                for y in range(n_y):
+                    part = slice(j * seg + y * piece, j * seg + (y + 1) * piece)
+                    stage_ref[r, y, :, :DH] = gk[part, :]
+                    stage_ref[r, y, :, DH:] = gv[part, :]
+                copy = pltpu.make_async_copy(
+                    stage_ref.at[r], out_ref.at[owner, :, pos], sem.at[requests + len(heads) + r]
+                )
+                copy.start()
+                sent.append(copy)
     for i, (c, d) in enumerate(heads):
         head_copies[i].wait()
         owner = lax.rem(my_x + d, n_x) * 2 + lax.rem(my_c + c, 2)
@@ -318,20 +332,22 @@
         out_space="vvav",
     )(place, ids, queries, grad_attn, *kv_all)
 
-    def ring(own):
+    def ring(own, long_way, short_way, sign):
         pieces = {0: own}
+        last = own
         for k in range(1, n_z // 2 + 1):
-            pieces[k] = z_up(pieces[k - 1])
+            last = long_way(last)
+            pieces[(sign * k) % n_z] = last
         last = own
         for k in range(1, n_z - n_z // 2):
-            last = z_down(last)
-            pieces[n_z - k] = last
+            last = short_way(last)
+            pieces[(-sign * k) % n_z] = last
         return [pieces[k] for k in range(n_z)]
 
     returned = lax.all_to_all(
         outgoing.reshape(owners * n_y, cap, piece, 2 * DH), dp + ("y",), 0, 0, tiled=True
     ).reshape(owners, n_y, cap, piece, 2 * DH)
-    attn_all, gq_all = ring(attn), ring(gq)
+    attn_all, gq_all = ring(attn, z_up, z_down, 1), ring(gq, z_down, z_up, -1)
     sums = (jax.ShapeDtypeStruct((rows, DH), F32),) + (slab,) * (n_y - 1)
     enc_part, *sums = call(
         functools.partial(tail_body, stored, n_z),

time: 123 us -> 123 us (level)
  waiting for transfers between devices: 21.4 us -> 24.9 us
  Pallas kernels: 21.6 us -> 19.4 us
    ppermute x31, waiting for transfers between devices: 20.4 us -> 24.5 us  [shift(): return lambda a: lax.ppermute(a, axis, [(i, (i + k) % n) for i in range(n)])]
    pallas_call x1, Pallas kernels: 7.46 us -> 5.36 us  [shards(): call(functools.partial(attention_body, (blocks, block_len, n_x, n_y, cap,...]
  transfers between devices with their start and end apart: 36 -> 36, of which waited for: 16 -> 15; matrix products, arithmetic and copies ran while one was open for 8% -> 8% of each run, Pallas kernels for 8% -> 6%
where the time goes in v6:
time: 123 us; the launch traced here: 122 us
  starting transfers between devices  64.4 us (52%)
  waiting for transfers between devices  24.9 us (20%)
  Pallas kernels  19.4 us (16%)
  matrix products  6.31 us (5%)
  other arithmetic  4.63 us (4%)
  local copies, waits for them, and re-layouts  1.67 us (1%)
    ppermute x31, starting transfers between devices, shift(): return lambda a: lax.ppermute(a, axis, [(i, (i + k) % n) for i in range(n)])  34.9 us
    ppermute x31, waiting for transfers between devices, shift(): return lambda a: lax.ppermute(a, axis, [(i, (i + k) % n) for i in range(n)])  24.5 us
    all_to_all x1, starting transfers between devices, shards(): mine = lax.all_to_all(mine, 'z', 0, 0, tiled=True)  8.71 us
    all_to_all x1, starting transfers between devices, shards(): lax.all_to_all(outgoing.reshape(owners * n_y, cap, piece, 2 * DH), dp + (...  7.95 us
    pallas_call x1, Pallas kernels, shards(): call(functools.partial(tail_body, stored, n_z), (jax.ShapeDtypeStruct((pi...  7.76 us
    all_to_all x1, starting transfers between devices, shards(): lax.all_to_all(enc_part.reshape(n_z, -1, enc_width), 'z', 0, 0, tiled=True)  6.7 us
    ppermute x2, starting transfers between devices, along_y(): return lax.ppermute(a, ('c', 'y'), ways)  6.1 us
    pallas_call x1, Pallas kernels, shards(): call(functools.partial(attention_body, (blocks, block_len, n_x, n_y, cap,...  5.36 us
  transfers between devices with their start and end apart: 36, of which 15 were waited for; matrix products, arithmetic and copies ran while one was open for 8% of the time, Pallas kernels for 6%

profile of v6, /device:TPU:32, one launch (start us, length us, event | category | flops | bytes accessed | tf_op | source)
XLA Modules:
  0.0 122.2 jit_solution(246120124207450292)
XLA Ops:
  1.2 4.5 %shard_map.103 = (bf16[1040,256]{1,0:T(8,128)(2,1)}, bf16[896,256]{1,0:T(8,128)(2,1)}, bf16[8,4,128,128]{3,2,1,0:T(8,128)(2,1)}) custom-call(s32[4]{0:T(128)} %pad_add_fusion.pos_ref, s32[2,8]{1,0:T(2,128)} %bitcast.26, bf16[1024,896]{1,0:T(8,128)(2,1)} %bitcast.23, bf16[896,128]{1,0:T(8,128)(2,1)} %wk_ref.1, bf16[896,128]{1,0:T(8,128)(2,1)} %wv_ref.1, ...), custom_call_target="tpu_custom_call" | custom-call | flops 470000000 | bytes 5242880 | tf_op jit(solution)/shard_map/pallas_call | solution.py:279
  5.7 8.7 %all-to-all-start.1 = ((bf16[8,4,128,128]{3,2,1,0:T(8,128)(2,1)}), bf16[8,4,128,128]{3,2,1,0:T(8,128)(2,1)}, u32[]{:S(2)}, u32[]{:S(2)}) async-start(bf16[8,4,128,128]{3,2,1,0:T(8,128)(2,1)} %get-tuple-element.51), calls=%async_computation.1 | async-start | bytes 2097152 | tf_op jit(solution)/shard_map/all_to_all | solution.py:290
  14.4 1.5 %collective-permute-start.1 = (bf16[1040,256]{1,0:T(8,128)(2,1)}, bf16[1040,256]{1,0:T(8,128)(2,1)}, u32[]{:S(2)}, u32[]{:S(2)}) collective-permute-start(bf16[1040,256]{1,0:T(8,128)(2,1)} %get-tuple-element.32.refs_0_), channel_id=1, source_target_pairs={{0,64},{64,128},{128,192},{192,0},{1,65},{65,129},{129,193},{193,1... | collective-permute-start | bytes 1597448 | tf_op jit(solution)/shard_map/ppermute | solution.py:271
  15.9 1.7 %collective-permute-start = (bf16[1040,256]{1,0:T(8,128)(2,1)}, bf16[1040,256]{1,0:T(8,128)(2,1)}, u32[]{:S(2)}, u32[]{:S(2)}) collective-permute-start(bf16[1040,256]{1,0:T(8,128)(2,1)} %get-tuple-element.32.refs_0_), channel_id=1, source_target_pairs={{0,192},{64,0},{128,64},{192,128},{1,193},{65,1},{129,65},{193,129... | collective-permute-start | bytes 1597448 | tf_op jit(solution)/shard_map/ppermute | solution.py:271
  17.7 4.4 %convolution_convert_fusion.1.q_ref = bf16[512,128]{1,0:T(8,128)(2,1)} fusion(bf16[512,4096]{1,0:T(8,128)(2,1)} %param.8, bf16[4096,128]{1,0:T(8,128)(2,1)} %wq_ref.1), kind=kOutput, calls=%fused_computation.1 | convolution fusion | flops 536936448 | bytes 5373952 | tf_op jit(solution)/shard_map/dot_general | solution.py:297
  22.0 3.0 %collective-permute-start.2 = (bf16[896,256]{1,0:T(8,128)(2,1)}, bf16[896,256]{1,0:T(8,128)(2,1)}, u32[]{:S(2)}, u32[]{:S(2)}) collective-permute-start(bf16[896,256]{1,0:T(8,128)(2,1)} %get-tuple-element.45.refs_0_), channel_id=1, source_target_pairs={{0,24},{8,0},{16,8},{24,16},{32,40},{40,48},{48,56},{56,32},{1,25}... | collective-permute-start | bytes 1376264 | tf_op jit(solution)/shard_map/ppermute | solution.py:295
  25.1 1.9 %convolution_convert_fusion.g_ref = bf16[512,128]{1,0:T(8,128)(2,1)} fusion(bf16[512,4096]{1,0:T(8,128)(2,1)S(1)} %copy-done.20, bf16[128,4096]{1,0:T(8,128)(2,1)S(1)} %copy-done), kind=kOutput, calls=%fused_computation | convolution fusion | flops 536936448 | bytes 5373952 | tf_op jit(solution)/shard_map/dot_general | solution.py:298
  27.0 2.2 %collective-permute-done.1.before_ref.refs_4_ = bf16[1040,256]{1,0:T(8,128)(2,1)} collective-permute-done((bf16[1040,256]{1,0:T(8,128)(2,1)}, bf16[1040,256]{1,0:T(8,128)(2,1)}, u32[]{:S(2)}, u32[]{:S(2)}) %collective-permute-start.1) | collective-permute-done | bytes 532512 | tf_op jit(solution)/shard_map/ppermute | solution.py:271
  29.2 1.9 %shard_map.104 = (bf16[528,256]{1,0:T(8,128)(2,1)}, bf16[512,256]{1,0:T(8,128)(2,1)}) custom-call(bf16[1040,256]{1,0:T(8,128)(2,1)} %collective-permute-done.after_ref.refs_1_, bf16[1040,256]{1,0:T(8,128)(2,1)} %collective-permute-done.1.before_ref.refs_4_), custom_call_target="tpu_custom_call" | custom-call | tf_op jit(solution)/shard_map/pallas_call | solution.py:304
  31.1 3.0 %collective-permute-start.5 = (bf16[528,256]{1,0:T(8,128)(2,1)}, bf16[528,256]{1,0:T(8,128)(2,1)S(1)}, u32[]{:S(2)}, u32[]{:S(2)}) collective-permute-start(bf16[528,256]{1,0:T(8,128)(2,1)} %get-tuple-element.41), channel_id=1, source_target_pairs={{0,192},{64,0},{128,64},{192,128},{1,193},{65,1},{129,65},{193,129... | collective-permute-start | bytes 811016 | tf_op jit(solution)/shard_map/ppermute | solution.py:271
  34.1 3.1 %collective-permute-start.3 = (bf16[896,256]{1,0:T(8,128)(2,1)}, bf16[896,256]{1,0:T(8,128)(2,1)}, u32[]{:S(2)}, u32[]{:S(2)}) collective-permute-start(bf16[896,256]{1,0:T(8,128)(2,1)} %collective-permute-done.2.refs_1_), channel_id=1, source_target_pairs={{0,24},{8,0},{16,8},{24,16},{32,40},{40,48},{48,56},{56,32},{1,25}... | collective-permute-start | bytes 1376264 | tf_op jit(solution)/shard_map/ppermute | solution.py:295
  37.2 4.7 %collective-permute-done.6.refs_3_ = bf16[512,256]{1,0:T(8,128)(2,1)S(1)} collective-permute-done((bf16[512,256]{1,0:T(8,128)(2,1)}, bf16[512,256]{1,0:T(8,128)(2,1)S(1)}, u32[]{:S(2)}, u32[]{:S(2)}) %collective-permute-start.6) | collective-permute-done | bytes 262176 | tf_op jit(solution)/shard_map/ppermute | solution.py:271
  43.5 1.8 %collective-permute-done.10.refs_8_ = bf16[512,256]{1,0:T(8,128)(2,1)S(1)} collective-permute-done((bf16[512,256]{1,0:T(8,128)(2,1)S(1)}, bf16[512,256]{1,0:T(8,128)(2,1)S(1)}, u32[]{:S(2)}, u32[]{:S(2)}) %collective-permute-start.10) | collective-permute-done | bytes 262176 | tf_op jit(solution)/shard_map/ppermute | solution.py:271
  46.1 5.4 %shard_map.105 = (bf16[512,128]{1,0:T(8,128)(2,1)}, bf16[512,128]{1,0:T(8,128)(2,1)}, bf16[8,4,4,32,256]{4,3,2,1,0:T(8,128)(2,1)}, s32[8,128]{1,0:T(8,128)}) custom-call(s32[4]{0:T(128)} %pad_add_fusion.pos_ref, s32[2,8]{1,0:T(2,128)} %bitcast.27, bf16[512,128]{1,0:T(8,128)(2,1)} %convolution_convert_fusion.1.q_ref, ...), custom_call_target="tpu_custom_call" | custom-call | tf_op jit(solution)/shard_map/pallas_call | solution.py:317
  51.5 7.9 %all-to-all-start = ((bf16[32,4,32,256]{3,2,1,0:T(8,128)(2,1)}), bf16[32,4,32,256]{3,2,1,0:T(8,128)(2,1)}, u32[]{:S(2)}, u32[]{:S(2)}) async-start(bf16[32,4,32,256]{3,2,1,0:T(8,128)(2,1)} %bitcast.22), calls=%async_computation | async-start | bytes 4194304 | tf_op jit(solution)/shard_map/all_to_all | solution.py:347
  60.1 1.7 %collective-permute-start.22 = (bf16[512,128]{1,0:T(8,128)(2,1)S(1)}, bf16[512,128]{1,0:T(8,128)(2,1)S(1)}, u32[]{:S(2)}, u32[]{:S(2)}) collective-permute-start(bf16[512,128]{1,0:T(8,128)(2,1)S(1)} %copy-done.5), channel_id=1, source_target_pairs={{0,1},{1,2},{2,3},{3,4},{4,5},{5,6},{6,7},{7,0},{8,9},{9,10},{10,1... | collective-permute-start | bytes 393224 | tf_op jit(solution)/shard_map/ppermute | solution.py:271
  63.8 1.7 %collective-permute-done.12.refs_5_ = bf16[512,128]{1,0:T(8,128)(2,1)S(1)} collective-permute-done((bf16[512,128]{1,0:T(8,128)(2,1)S(1)}, bf16[512,128]{1,0:T(8,128)(2,1)S(1)}, u32[]{:S(2)}, u32[]{:S(2)}) %collective-permute-start.12) | collective-permute-done | bytes 131104 | tf_op jit(solution)/shard_map/ppermute | solution.py:271
  70.5 2.0 %collective-permute-start.20 = (bf16[512,128]{1,0:T(8,128)(2,1)S(1)}, bf16[512,128]{1,0:T(8,128)(2,1)S(1)}, u32[]{:S(2)}, u32[]{:S(2)}) collective-permute-start(bf16[512,128]{1,0:T(8,128)(2,1)S(1)} %collective-permute-done.19.refs_13_), channel_id=1, source_target_pairs={{0,7},{1,0},{2,1},{3,2},{4,3},{5,4},{6,5},{7,6},{8,15},{9,8},{10,9... | collective-permute-start | bytes 393224 | tf_op jit(solution)/shard_map/ppermute | solution.py:271
  72.5 3.3 %collective-permute-start.14 = (bf16[512,128]{1,0:T(8,128)(2,1)S(1)}, bf16[512,128]{1,0:T(8,128)(2,1)S(1)}, u32[]{:S(2)}, u32[]{:S(2)}) collective-permute-start(bf16[512,128]{1,0:T(8,128)(2,1)S(1)} %collective-permute-done.13.refs_6_), channel_id=1, source_target_pairs={{0,7},{1,0},{2,1},{3,2},{4,3},{5,4},{6,5},{7,6},{8,15},{9,8},{10,9... | collective-permute-start | bytes 393224 | tf_op jit(solution)/shard_map/ppermute | solution.py:271
  77.2 3.4 %collective-permute-start.21 = (bf16[512,128]{1,0:T(8,128)(2,1)S(1)}, bf16[512,128]{1,0:T(8,128)(2,1)S(1)}, u32[]{:S(2)}, u32[]{:S(2)}) collective-permute-start(bf16[512,128]{1,0:T(8,128)(2,1)S(1)} %collective-permute-done.20.refs_14_), channel_id=1, source_target_pairs={{0,7},{1,0},{2,1},{3,2},{4,3},{5,4},{6,5},{7,6},{8,15},{9,8},{10,9... | collective-permute-start | bytes 393224 | tf_op jit(solution)/shard_map/ppermute | solution.py:271
  80.6 3.5 %collective-permute-start.15 = (bf16[512,128]{1,0:T(8,128)(2,1)S(1)}, bf16[512,128]{1,0:T(8,128)(2,1)S(1)}, u32[]{:S(2)}, u32[]{:S(2)}) collective-permute-start(bf16[512,128]{1,0:T(8,128)(2,1)S(1)} %collective-permute-done.14.refs_7_), channel_id=1, source_target_pairs={{0,7},{1,0},{2,1},{3,2},{4,3},{5,4},{6,5},{7,6},{8,15},{9,8},{10,9... | collective-permute-start | bytes 393224 | tf_op jit(solution)/shard_map/ppermute | solution.py:271
  84.5 2.1 %collective-permute-done.15.refs_8_ = bf16[512,128]{1,0:T(8,128)(2,1)S(1)} collective-permute-done((bf16[512,128]{1,0:T(8,128)(2,1)S(1)}, bf16[512,128]{1,0:T(8,128)(2,1)S(1)}, u32[]{:S(2)}, u32[]{:S(2)}) %collective-permute-start.15) | collective-permute-done | bytes 131104 | tf_op jit(solution)/shard_map/ppermute | solution.py:271
  86.6 2.5 %collective-permute-done.25.refs_16_ = bf16[512,128]{1,0:T(8,128)(2,1)S(1)} collective-permute-done((bf16[512,128]{1,0:T(8,128)(2,1)S(1)}, bf16[512,128]{1,0:T(8,128)(2,1)S(1)}, u32[]{:S(2)}, u32[]{:S(2)}) %collective-permute-start.25) | collective-permute-done | bytes 131104 | tf_op jit(solution)/shard_map/ppermute | solution.py:271
  89.8 7.8 %shard_map.106 = (bf16[256,896]{1,0:T(8,128)(2,1)}, f32[512,128]{1,0:T(8,128)}, bf16[512,128]{1,0:T(8,128)(2,1)}, bf16[512,128]{1,0:T(8,128)(2,1)}, bf16[512,128...) custom-call(s32[4]{0:T(128)} %pad_add_fusion.pos_ref, ...), custom_call_target="tpu_custom_call" | custom-call | flops 1580000000 | bytes 10485760 | tf_op jit(solution)/shard_map/pallas_call | solution.py:352
  97.6 6.7 %all-to-all-start.2 = ((bf16[8,32,896]{2,1,0:T(8,128)(2,1)}), bf16[8,32,896]{2,1,0:T(8,128)(2,1)S(1)}, u32[]{:S(2)}, u32[]{:S(2)}) async-start(bf16[8,32,896]{2,1,0:T(8,128)(2,1)} %bitcast.24), calls=%async_computation.2 | async-start | bytes 917504 | tf_op jit(solution)/shard_map/all_to_all | solution.py:366
  104.3 1.8 %collective-permute-start.27 = (bf16[512,128]{1,0:T(8,128)(2,1)}, bf16[512,128]{1,0:T(8,128)(2,1)S(1)}, u32[]{:S(2)}, u32[]{:S(2)}) collective-permute-start(bf16[512,128]{1,0:T(8,128)(2,1)} %get-tuple-element.53), channel_id=1, source_target_pairs={{0,8},{8,16},{16,24},{24,0},{1,9},{9,17},{17,25},{25,1},{2,10},{10... | collective-permute-start | bytes 393224 | tf_op jit(solution)/shard_map/ppermute | solution.py:271
  106.1 2.7 %collective-permute-start.28 = (bf16[512,128]{1,0:T(8,128)(2,1)}, bf16[512,128]{1,0:T(8,128)(2,1)S(1)}, u32[]{:S(2)}, u32[]{:S(2)}) collective-permute-start(bf16[512,128]{1,0:T(8,128)(2,1)} %get-tuple-element.54), channel_id=1, source_target_pairs={{0,16},{8,24},{16,0},{24,8},{1,17},{9,25},{17,1},{25,9},{2,18},{10... | collective-permute-start | bytes 393224 | tf_op jit(solution)/shard_map/ppermute | solution.py:271
  108.7 1.5 %collective-permute-start.29 = (bf16[512,128]{1,0:T(8,128)(2,1)}, bf16[512,128]{1,0:T(8,128)(2,1)S(1)}, u32[]{:S(2)}, u32[]{:S(2)}) collective-permute-start(bf16[512,128]{1,0:T(8,128)(2,1)} %get-tuple-element.55), channel_id=1, source_target_pairs={{0,24},{8,0},{16,8},{24,16},{1,25},{9,1},{17,9},{25,17},{2,26},{10... | collective-permute-start | bytes 393224 | tf_op jit(solution)/shard_map/ppermute | solution.py:271
  111.7 2.9 %collective-permute-done.27 = bf16[512,128]{1,0:T(8,128)(2,1)S(1)} collective-permute-done((bf16[512,128]{1,0:T(8,128)(2,1)}, bf16[512,128]{1,0:T(8,128)(2,1)S(1)}, u32[]{:S(2)}, u32[]{:S(2)}) %collective-permute-start.27) | collective-permute-done | bytes 131104 | tf_op jit(solution)/shard_map/ppermute | solution.py:271
  115.7 1.7 %add_convert_fusion.1 = bf16[512,128]{1,0:T(8,128)(2,1)} fusion(bf16[512,128]{1,0:T(8,128)(2,1)S(1)} %collective-permute-done.29, bf16[512,128]{1,0:T(8,128)(2,1)S(1)} %collective-permute-done.28, f32[512,128]{1,0:T(8,128)} %get-tuple-element.52, bf16[512,128]{1,0:T(8,128)(2,1)S(1)} %collective-permute-done.27), kind=kLoop, calls=%fused_computation.3 | loop fusion | flops 458752 | bytes 786432 | tf_op jit(solution)/shard_map/convert_element_type | solution.py:374
  118.0 1.8 %collective-permute-done.32 = bf16[512,128]{1,0:T(8,128)(2,1)S(1)} collective-permute-done((bf16[512,128]{1,0:T(8,128)(2,1)}, bf16[512,128]{1,0:T(8,128)(2,1)S(1)}, u32[]{:S(2)}, u32[]{:S(2)}) %collective-permute-start.32) | collective-permute-done | bytes 131104 | tf_op jit(solution)/shard_map/ppermute | solution.py:271
  119.8 1.7 %add_convert_fusion = bf16[512,128]{1,0:T(8,128)(2,1)} fusion(bf16[512,128]{1,0:T(8,128)(2,1)S(1)} %collective-permute-done.32, bf16[512,128]{1,0:T(8,128)(2,1)S(1)} %collective-permute-done.31, f32[512,128]{1,0:T(8,128)} %get-tuple-element.56, bf16[512,128]{1,0:T(8,128)(2,1)S(1)} %collective-permute-done.30), kind=kLoop, calls=%fused_computation.2 | loop fusion | flops 458752 | bytes 786432 | tf_op jit(solution)/shard_map/convert_element_type | solution.py:374
  (92 shorter events, 17.1 us)
Async XLA Ops:
  5.7 45.7 %all-to-all-start.1 = ((bf16[8,4,128,128]{3,2,1,0:T(8,128)(2,1)}), bf16[8,4,128,128]{3,2,1,0:T(8,128)(2,1)}, u32[]{:S(2)}, u32[]{:S(2)}) async-start(bf16[8,4,128,128]{3,2,1,0:T(8,128)(2,1)} %get-tuple-element.51), calls=%async_computation.1 | async-start | bytes 2097152 | tf_op jit(solution)/shard_map/all_to_all | solution.py:290
  14.4 14.8 %collective-permute-start.1 = (bf16[1040,256]{1,0:T(8,128)(2,1)}, bf16[1040,256]{1,0:T(8,128)(2,1)}, u32[]{:S(2)}, u32[]{:S(2)}) collective-permute-start(bf16[1040,256]{1,0:T(8,128)(2,1)} %get-tuple-element.32.refs_0_), channel_id=1, source_target_pairs={{0,64},{64,128},{128,192},{192,0},{1,65},{65,129},{129,193},{193,1... | collective-permute-start | bytes 1597448 | tf_op jit(solution)/shard_map/ppermute | solution.py:271
  15.9 13.3 %collective-permute-start = (bf16[1040,256]{1,0:T(8,128)(2,1)}, bf16[1040,256]{1,0:T(8,128)(2,1)}, u32[]{:S(2)}, u32[]{:S(2)}) collective-permute-start(bf16[1040,256]{1,0:T(8,128)(2,1)} %get-tuple-element.32.refs_0_), channel_id=1, source_target_pairs={{0,192},{64,0},{128,64},{192,128},{1,193},{65,1},{129,65},{193,129... | collective-permute-start | bytes 1597448 | tf_op jit(solution)/shard_map/ppermute | solution.py:271
  22.0 12.1 %collective-permute-start.2 = (bf16[896,256]{1,0:T(8,128)(2,1)}, bf16[896,256]{1,0:T(8,128)(2,1)}, u32[]{:S(2)}, u32[]{:S(2)}) collective-permute-start(bf16[896,256]{1,0:T(8,128)(2,1)} %get-tuple-element.45.refs_0_), channel_id=1, source_target_pairs={{0,24},{8,0},{16,8},{24,16},{32,40},{40,48},{48,56},{56,32},{1,25}... | collective-permute-start | bytes 1376264 | tf_op jit(solution)/shard_map/ppermute | solution.py:295
  31.1 10.8 %collective-permute-start.5 = (bf16[528,256]{1,0:T(8,128)(2,1)}, bf16[528,256]{1,0:T(8,128)(2,1)S(1)}, u32[]{:S(2)}, u32[]{:S(2)}) collective-permute-start(bf16[528,256]{1,0:T(8,128)(2,1)} %get-tuple-element.41), channel_id=1, source_target_pairs={{0,192},{64,0},{128,64},{192,128},{1,193},{65,1},{129,65},{193,129... | collective-permute-start | bytes 811016 | tf_op jit(solution)/shard_map/ppermute | solution.py:271
  34.1 7.8 %collective-permute-start.6 = (bf16[512,256]{1,0:T(8,128)(2,1)}, bf16[512,256]{1,0:T(8,128)(2,1)S(1)}, u32[]{:S(2)}, u32[]{:S(2)}) collective-permute-start(bf16[512,256]{1,0:T(8,128)(2,1)} %get-tuple-element.42), channel_id=1, source_target_pairs={{0,64},{64,128},{128,192},{192,0},{1,65},{65,129},{129,193},{193,1... | collective-permute-start | bytes 786440 | tf_op jit(solution)/shard_map/ppermute | solution.py:271
  34.1 8.3 %collective-permute-start.4 = (bf16[896,256]{1,0:T(8,128)(2,1)}, bf16[896,256]{1,0:T(8,128)(2,1)}, u32[]{:S(2)}, u32[]{:S(2)}) collective-permute-start(bf16[896,256]{1,0:T(8,128)(2,1)} %collective-permute-done.2.refs_1_), channel_id=1, source_target_pairs={{0,32},{32,0},{1,33},{33,1},{2,34},{34,2},{3,35},{35,3},{4,36},{36... | collective-permute-start | bytes 1376264 | tf_op jit(solution)/shard_map/ppermute | solution.py:271
  34.1 9.4 %collective-permute-start.3 = (bf16[896,256]{1,0:T(8,128)(2,1)}, bf16[896,256]{1,0:T(8,128)(2,1)}, u32[]{:S(2)}, u32[]{:S(2)}) collective-permute-start(bf16[896,256]{1,0:T(8,128)(2,1)} %collective-permute-done.2.refs_1_), channel_id=1, source_target_pairs={{0,24},{8,0},{16,8},{24,16},{32,40},{40,48},{48,56},{56,32},{1,25}... | collective-permute-start | bytes 1376264 | tf_op jit(solution)/shard_map/ppermute | solution.py:295
  37.2 6.3 %collective-permute-start.7 = (bf16[1040,256]{1,0:T(8,128)(2,1)}, bf16[1040,256]{1,0:T(8,128)(2,1)}, u32[]{:S(2)}, u32[]{:S(2)}) collective-permute-start(bf16[1040,256]{1,0:T(8,128)(2,1)} %get-tuple-element.32.refs_0_), channel_id=1, source_target_pairs={{0,32},{32,0},{1,33},{33,1},{2,34},{34,2},{3,35},{35,3},{4,36},{36... | collective-permute-start | bytes 1597448 | tf_op jit(solution)/shard_map/ppermute | solution.py:271
  51.5 38.4 %all-to-all-start = ((bf16[32,4,32,256]{3,2,1,0:T(8,128)(2,1)}), bf16[32,4,32,256]{3,2,1,0:T(8,128)(2,1)}, u32[]{:S(2)}, u32[]{:S(2)}) async-start(bf16[32,4,32,256]{3,2,1,0:T(8,128)(2,1)} %bitcast.22), calls=%async_computation | async-start | bytes 4194304 | tf_op jit(solution)/shard_map/all_to_all | solution.py:347
  59.4 30.4 %collective-permute-start.26 = (bf16[8,4,128,128]{3,2,1,0:T(8,128)(2,1)}, bf16[8,4,128,128]{3,2,1,0:T(8,128)(2,1)}, u32[]{:S(2)}, u32[]{:S(2)}) collective-permute-start(bf16[8,4,128,128]{3,2,1,0:T(8,128)(2,1)} %all-to-all-done.1.refs_20_), channel_id=1, source_target_pairs={{0,32},{32,0},{1,33},{33,1},{2,34},{34,2},{3,35},{35,3},{4,36},{36... | collective-permute-start | bytes 3145736 | tf_op jit(solution)/shard_map/ppermute | solution.py:271
  59.7 5.7 %collective-permute-start.12 = (bf16[512,128]{1,0:T(8,128)(2,1)S(1)}, bf16[512,128]{1,0:T(8,128)(2,1)S(1)}, u32[]{:S(2)}, u32[]{:S(2)}) collective-permute-start(bf16[512,128]{1,0:T(8,128)(2,1)S(1)} %copy-done.4), channel_id=1, source_target_pairs={{0,7},{1,0},{2,1},{3,2},{4,3},{5,4},{6,5},{7,6},{8,15},{9,8},{10,9... | collective-permute-start | bytes 393224 | tf_op jit(solution)/shard_map/ppermute | solution.py:271
  60.1 7.2 %collective-permute-start.22 = (bf16[512,128]{1,0:T(8,128)(2,1)S(1)}, bf16[512,128]{1,0:T(8,128)(2,1)S(1)}, u32[]{:S(2)}, u32[]{:S(2)}) collective-permute-start(bf16[512,128]{1,0:T(8,128)(2,1)S(1)} %copy-done.5), channel_id=1, source_target_pairs={{0,1},{1,2},{2,3},{3,4},{4,5},{5,6},{6,7},{7,0},{8,9},{9,10},{10,1... | collective-permute-start | bytes 393224 | tf_op jit(solution)/shard_map/ppermute | solution.py:271
  61.7 7.7 %collective-permute-start.16 = (bf16[512,128]{1,0:T(8,128)(2,1)S(1)}, bf16[512,128]{1,0:T(8,128)(2,1)S(1)}, u32[]{:S(2)}, u32[]{:S(2)}) collective-permute-start(bf16[512,128]{1,0:T(8,128)(2,1)S(1)} %copy-done.4), channel_id=1, source_target_pairs={{0,1},{1,2},{2,3},{3,4},{4,5},{5,6},{6,7},{7,0},{8,9},{9,10},{10,1... | collective-permute-start | bytes 393224 | tf_op jit(solution)/shard_map/ppermute | solution.py:271
  63.2 7.3 %collective-permute-start.19 = (bf16[512,128]{1,0:T(8,128)(2,1)S(1)}, bf16[512,128]{1,0:T(8,128)(2,1)S(1)}, u32[]{:S(2)}, u32[]{:S(2)}) collective-permute-start(bf16[512,128]{1,0:T(8,128)(2,1)S(1)} %copy-done.5), channel_id=1, source_target_pairs={{0,7},{1,0},{2,1},{3,2},{4,3},{5,4},{6,5},{7,6},{8,15},{9,8},{10,9... | collective-permute-start | bytes 393224 | tf_op jit(solution)/shard_map/ppermute | solution.py:271
  65.4 7.1 %collective-permute-start.13 = (bf16[512,128]{1,0:T(8,128)(2,1)S(1)}, bf16[512,128]{1,0:T(8,128)(2,1)S(1)}, u32[]{:S(2)}, u32[]{:S(2)}) collective-permute-start(bf16[512,128]{1,0:T(8,128)(2,1)S(1)} %collective-permute-done.12.refs_5_), channel_id=1, source_target_pairs={{0,7},{1,0},{2,1},{3,2},{4,3},{5,4},{6,5},{7,6},{8,15},{9,8},{10,9... | collective-permute-start | bytes 393224 | tf_op jit(solution)/shard_map/ppermute | solution.py:271
  67.2 8.6 %collective-permute-start.23 = (bf16[512,128]{1,0:T(8,128)(2,1)S(1)}, bf16[512,128]{1,0:T(8,128)(2,1)S(1)}, u32[]{:S(2)}, u32[]{:S(2)}) collective-permute-start(bf16[512,128]{1,0:T(8,128)(2,1)S(1)} %collective-permute-done.22.refs_19_), channel_id=1, source_target_pairs={{0,1},{1,2},{2,3},{3,4},{4,5},{5,6},{6,7},{7,0},{8,9},{9,10},{10,1... | collective-permute-start | bytes 393224 | tf_op jit(solution)/shard_map/ppermute | solution.py:271
  69.4 6.8 %collective-permute-start.17 = (bf16[512,128]{1,0:T(8,128)(2,1)S(1)}, bf16[512,128]{1,0:T(8,128)(2,1)S(1)}, u32[]{:S(2)}, u32[]{:S(2)}) collective-permute-start(bf16[512,128]{1,0:T(8,128)(2,1)S(1)} %collective-permute-done.16.refs_11_), channel_id=1, source_target_pairs={{0,1},{1,2},{2,3},{3,4},{4,5},{5,6},{6,7},{7,0},{8,9},{9,10},{10,1... | collective-permute-start | bytes 393224 | tf_op jit(solution)/shard_map/ppermute | solution.py:271
  70.5 6.7 %collective-permute-start.20 = (bf16[512,128]{1,0:T(8,128)(2,1)S(1)}, bf16[512,128]{1,0:T(8,128)(2,1)S(1)}, u32[]{:S(2)}, u32[]{:S(2)}) collective-permute-start(bf16[512,128]{1,0:T(8,128)(2,1)S(1)} %collective-permute-done.19.refs_13_), channel_id=1, source_target_pairs={{0,7},{1,0},{2,1},{3,2},{4,3},{5,4},{6,5},{7,6},{8,15},{9,8},{10,9... | collective-permute-start | bytes 393224 | tf_op jit(solution)/shard_map/ppermute | solution.py:271
  72.5 8.1 %collective-permute-start.14 = (bf16[512,128]{1,0:T(8,128)(2,1)S(1)}, bf16[512,128]{1,0:T(8,128)(2,1)S(1)}, u32[]{:S(2)}, u32[]{:S(2)}) collective-permute-start(bf16[512,128]{1,0:T(8,128)(2,1)S(1)} %collective-permute-done.13.refs_6_), channel_id=1, source_target_pairs={{0,7},{1,0},{2,1},{3,2},{4,3},{5,4},{6,5},{7,6},{8,15},{9,8},{10,9... | collective-permute-start | bytes 393224 | tf_op jit(solution)/shard_map/ppermute | solution.py:271
  75.8 8.3 %collective-permute-start.24 = (bf16[512,128]{1,0:T(8,128)(2,1)S(1)}, bf16[512,128]{1,0:T(8,128)(2,1)S(1)}, u32[]{:S(2)}, u32[]{:S(2)}) collective-permute-start(bf16[512,128]{1,0:T(8,128)(2,1)S(1)} %collective-permute-done.23.refs_18_), channel_id=1, source_target_pairs={{0,1},{1,2},{2,3},{3,4},{4,5},{5,6},{6,7},{7,0},{8,9},{9,10},{10,1... | collective-permute-start | bytes 393224 | tf_op jit(solution)/shard_map/ppermute | solution.py:271
  76.3 7.9 %collective-permute-start.18 = (bf16[512,128]{1,0:T(8,128)(2,1)S(1)}, bf16[512,128]{1,0:T(8,128)(2,1)S(1)}, u32[]{:S(2)}, u32[]{:S(2)}) collective-permute-start(bf16[512,128]{1,0:T(8,128)(2,1)S(1)} %collective-permute-done.17.refs_10_), channel_id=1, source_target_pairs={{0,1},{1,2},{2,3},{3,4},{4,5},{5,6},{6,7},{7,0},{8,9},{9,10},{10,1... | collective-permute-start | bytes 393224 | tf_op jit(solution)/shard_map/ppermute | solution.py:271
  77.2 7.3 %collective-permute-start.21 = (bf16[512,128]{1,0:T(8,128)(2,1)S(1)}, bf16[512,128]{1,0:T(8,128)(2,1)S(1)}, u32[]{:S(2)}, u32[]{:S(2)}) collective-permute-start(bf16[512,128]{1,0:T(8,128)(2,1)S(1)} %collective-permute-done.20.refs_14_), channel_id=1, source_target_pairs={{0,7},{1,0},{2,1},{3,2},{4,3},{5,4},{6,5},{7,6},{8,15},{9,8},{10,9... | collective-permute-start | bytes 393224 | tf_op jit(solution)/shard_map/ppermute | solution.py:271
  80.6 6.0 %collective-permute-start.15 = (bf16[512,128]{1,0:T(8,128)(2,1)S(1)}, bf16[512,128]{1,0:T(8,128)(2,1)S(1)}, u32[]{:S(2)}, u32[]{:S(2)}) collective-permute-start(bf16[512,128]{1,0:T(8,128)(2,1)S(1)} %collective-permute-done.14.refs_7_), channel_id=1, source_target_pairs={{0,7},{1,0},{2,1},{3,2},{4,3},{5,4},{6,5},{7,6},{8,15},{9,8},{10,9... | collective-permute-start | bytes 393224 | tf_op jit(solution)/shard_map/ppermute | solution.py:271
  84.1 5.0 %collective-permute-start.25 = (bf16[512,128]{1,0:T(8,128)(2,1)S(1)}, bf16[512,128]{1,0:T(8,128)(2,1)S(1)}, u32[]{:S(2)}, u32[]{:S(2)}) collective-permute-start(bf16[512,128]{1,0:T(8,128)(2,1)S(1)} %collective-permute-done.24.refs_17_), channel_id=1, source_target_pairs={{0,1},{1,2},{2,3},{3,4},{4,5},{5,6},{6,7},{7,0},{8,9},{9,10},{10,1... | collective-permute-start | bytes 393224 | tf_op jit(solution)/shard_map/ppermute | solution.py:271
  97.6 23.9 %all-to-all-start.2 = ((bf16[8,32,896]{2,1,0:T(8,128)(2,1)}), bf16[8,32,896]{2,1,0:T(8,128)(2,1)S(1)}, u32[]{:S(2)}, u32[]{:S(2)}) async-start(bf16[8,32,896]{2,1,0:T(8,128)(2,1)} %bitcast.24), calls=%async_computation.2 | async-start | bytes 917504 | tf_op jit(solution)/shard_map/all_to_all | solution.py:366
  104.3 10.3 %collective-permute-start.27 = (bf16[512,128]{1,0:T(8,128)(2,1)}, bf16[512,128]{1,0:T(8,128)(2,1)S(1)}, u32[]{:S(2)}, u32[]{:S(2)}) collective-permute-start(bf16[512,128]{1,0:T(8,128)(2,1)} %get-tuple-element.53), channel_id=1, source_target_pairs={{0,8},{8,16},{16,24},{24,0},{1,9},{9,17},{17,25},{25,1},{2,10},{10... | collective-permute-start | bytes 393224 | tf_op jit(solution)/shard_map/ppermute | solution.py:271
  106.1 8.6 %collective-permute-start.28 = (bf16[512,128]{1,0:T(8,128)(2,1)}, bf16[512,128]{1,0:T(8,128)(2,1)S(1)}, u32[]{:S(2)}, u32[]{:S(2)}) collective-permute-start(bf16[512,128]{1,0:T(8,128)(2,1)} %get-tuple-element.54), channel_id=1, source_target_pairs={{0,16},{8,24},{16,0},{24,8},{1,17},{9,25},{17,1},{25,9},{2,18},{10... | collective-permute-start | bytes 393224 | tf_op jit(solution)/shard_map/ppermute | solution.py:271
  108.7 7.0 %collective-permute-start.29 = (bf16[512,128]{1,0:T(8,128)(2,1)}, bf16[512,128]{1,0:T(8,128)(2,1)S(1)}, u32[]{:S(2)}, u32[]{:S(2)}) collective-permute-start(bf16[512,128]{1,0:T(8,128)(2,1)} %get-tuple-element.55), channel_id=1, source_target_pairs={{0,24},{8,0},{16,8},{24,16},{1,25},{9,1},{17,9},{25,17},{2,26},{10... | collective-permute-start | bytes 393224 | tf_op jit(solution)/shard_map/ppermute | solution.py:271
  110.2 7.8 %collective-permute-start.30 = (bf16[512,128]{1,0:T(8,128)(2,1)}, bf16[512,128]{1,0:T(8,128)(2,1)S(1)}, u32[]{:S(2)}, u32[]{:S(2)}) collective-permute-start(bf16[512,128]{1,0:T(8,128)(2,1)} %get-tuple-element.57), channel_id=1, source_target_pairs={{0,8},{8,16},{16,24},{24,0},{1,9},{9,17},{17,25},{25,1},{2,10},{10... | collective-permute-start | bytes 393224 | tf_op jit(solution)/shard_map/ppermute | solution.py:271
  110.8 7.2 %collective-permute-start.31 = (bf16[512,128]{1,0:T(8,128)(2,1)}, bf16[512,128]{1,0:T(8,128)(2,1)S(1)}, u32[]{:S(2)}, u32[]{:S(2)}) collective-permute-start(bf16[512,128]{1,0:T(8,128)(2,1)} %get-tuple-element.58), channel_id=1, source_target_pairs={{0,16},{8,24},{16,0},{24,8},{1,17},{9,25},{17,1},{25,9},{2,18},{10... | collective-permute-start | bytes 393224 | tf_op jit(solution)/shard_map/ppermute | solution.py:271
  114.6 5.2 %collective-permute-start.32 = (bf16[512,128]{1,0:T(8,128)(2,1)}, bf16[512,128]{1,0:T(8,128)(2,1)S(1)}, u32[]{:S(2)}, u32[]{:S(2)}) collective-permute-start(bf16[512,128]{1,0:T(8,128)(2,1)} %get-tuple-element.59), channel_id=1, source_target_pairs={{0,24},{8,0},{16,8},{24,16},{1,25},{9,1},{17,9},{25,17},{2,26},{10... | collective-permute-start | bytes 393224 | tf_op jit(solution)/shard_map/ppermute | solution.py:271
  (25 other events, 129.6 us)

commit v7 on v6

--- a/solution.py
+++ b/solution.py
@@ -38,7 +38,7 @@
     )
 
 
-def keys_values_body(stored, n_z, n_y, pos_ref, ids_ref, x_ref, wk_ref, wv_ref, wo_ref, wq_ref, out_ref, pair_ref, w_ref, kv_ref, sem):
+def keys_values_body(stored, n_z, n_y, ids_ref, x_ref, wk_ref, wv_ref, wo_ref, wq_ref, out_ref, pair_ref, w_ref, kv_ref, sem):
     def moved(block):
         return [
             pltpu.make_async_copy(block((y * n_z + z) * DH), w_ref.at[z, y], sem.at[y * n_z + z])
@@ -48,12 +48,14 @@
 
     copies = moved(lambda at: wq_ref.at[at : at + DH, :])
 
-    @pl.when(pos_ref[1] == 0)
+    core = lax.axis_index("c")
+
+    @pl.when(core == 0)
     def _():
         for copy in moved(lambda at: wo_ref.at[:, at : at + DH]):
             copy.start()
 
-    @pl.when(pos_ref[1] != 0)
+    @pl.when(core != 0)
     def _():
         for copy in copies:
             copy.start()
@@ -283,9 +285,9 @@
             jax.ShapeDtypeStruct((enc_width, 2 * DH), BF),
             jax.ShapeDtypeStruct((n_z, n_y, DH, DH), BF),
         ),
-        "ssvvvaa", 470_000_000, 5 << 20,
+        "svvvaa", 470_000_000, 5 << 20,
         scratch=(pltpu.VMEM((2, seg * stored, DH), F32), pltpu.SemaphoreType.DMA((n_z * n_y,))),
-    )(place, ids, enc_rows, w_key, w_value, w_out, w_query)
+    )(ids, enc_rows, w_key, w_value, w_out, w_query)
     after, before, kv_other = x_up(kv), x_down(kv), swap(kv)
     mine = lax.all_to_all(mine, "z", 0, 0, tiled=True)
 
@@ -332,22 +334,20 @@
         out_space="vvav",
     )(place, ids, queries, grad_attn, *kv_all)
 
-    def ring(own, long_way, short_way, sign):
+    def ring(own):
         pieces = {0: own}
-        last = own
         for k in range(1, n_z // 2 + 1):
-            last = long_way(last)
-            pieces[(sign * k) % n_z] = last
+            pieces[k] = z_up(pieces[k - 1])
         last = own
         for k in range(1, n_z - n_z // 2):
-            last = short_way(last)
-            pieces[(-sign * k) % n_z] = last
+            last = z_down(last)
+            pieces[n_z - k] = last
         return [pieces[k] for k in range(n_z)]
 
     returned = lax.all_to_all(
         outgoing.reshape(owners * n_y, cap, piece, 2 * DH), dp + ("y",), 0, 0, tiled=True
     ).reshape(owners, n_y, cap, piece, 2 * DH)
-    attn_all, gq_all = ring(attn, z_up, z_down, 1), ring(gq, z_down, z_up, -1)
+    attn_all, gq_all = ring(attn), ring(gq)
     sums = (jax.ShapeDtypeStruct((rows, DH), F32),) + (slab,) * (n_y - 1)
     enc_part, *sums = call(
         functools.partial(tail_body, stored, n_z),
@@ -365,7 +365,6 @@
     )(place, ids_all, returned, *pairs, *attn_all, *gq_all, mine, other)
     enc_parts = lax.all_to_all(enc_part.reshape(n_z, -1, enc_width), "z", 0, 0, tiled=True)
     enc_rows_sum = jnp.sum(enc_parts.astype(F32), axis=0).astype(BF)
-    grad_encoded = enc_rows_sum.reshape(seg // (n_y * n_z), stored, enc_width).transpose(1, 0, 2).reshape(stored, -1)
 
     def summed(parts):
         total = parts[0]
@@ -373,7 +372,10 @@
             total = total + shift("y", n_y, k)(parts[k]).astype(F32)
         return total.astype(BF)
 
-    return summed(sums[:n_y]), summed(sums[n_y:]), grad_encoded
+    attended = summed(sums[:n_y])
+    own, enc_rows_sum = tie((sums[n_y], enc_rows_sum))
+    grad_encoded = enc_rows_sum.reshape(seg // (n_y * n_z), stored, enc_width).transpose(1, 0, 2).reshape(stored, -1)
+    return attended, summed([own, *sums[n_y + 1 :]]), grad_encoded
 
 
 def solution(mesh):

time: 123 us -> 120 us (0.976)
  waiting for transfers between devices: 24.9 us -> 19.4 us
  starting transfers between devices: 64.4 us -> 66.6 us
    ppermute x31, waiting for transfers between devices: 24.5 us -> 18.4 us  [shift(): return lambda a: lax.ppermute(a, axis, [(i, (i + k) % n) for i in range(n)])]
    ppermute x31, starting transfers between devices: 34.9 us -> 36.7 us  [shift(): return lambda a: lax.ppermute(a, axis, [(i, (i + k) % n) for i in range(n)])]
  transfers between devices with their start and end apart: 36 -> 36, of which waited for: 15 -> 14; matrix products, arithmetic and copies ran while one was open for 8% -> 8% of each run, Pallas kernels for 6% -> 6%
where the time goes in v7:
time: 120 us; the launch traced here: 119 us
  starting transfers between devices  66.6 us (55%)
  Pallas kernels  19.5 us (16%)
  waiting for transfers between devices  19.4 us (16%)
  matrix products  6.31 us (5%)
  other arithmetic  4.68 us (4%)
  local copies, waits for them, and re-layouts  1.67 us (1%)
    ppermute x31, starting transfers between devices, shift(): return lambda a: lax.ppermute(a, axis, [(i, (i + k) % n) for i in range(n)])  36.7 us
    ppermute x31, waiting for transfers between devices, shift(): return lambda a: lax.ppermute(a, axis, [(i, (i + k) % n) for i in range(n)])  18.4 us
    all_to_all x1, starting transfers between devices, shards(): mine = lax.all_to_all(mine, 'z', 0, 0, tiled=True)  8.71 us
    all_to_all x1, starting transfers between devices, shards(): lax.all_to_all(outgoing.reshape(owners * n_y, cap, piece, 2 * DH), dp + (...  7.92 us
    pallas_call x1, Pallas kernels, shards(): call(functools.partial(tail_body, stored, n_z), (jax.ShapeDtypeStruct((pi...  7.76 us
    all_to_all x1, starting transfers between devices, shards(): lax.all_to_all(enc_part.reshape(n_z, -1, enc_width), 'z', 0, 0, tiled=True)  7.19 us
    ppermute x2, starting transfers between devices, along_y(): return lax.ppermute(a, ('c', 'y'), ways)  6.11 us
    pallas_call x1, Pallas kernels, shards(): call(functools.partial(attention_body, (blocks, block_len, n_x, n_y, cap,...  5.41 us
  transfers between devices with their start and end apart: 36, of which 14 were waited for; matrix products, arithmetic and copies ran while one was open for 8% of the time, Pallas kernels for 6%

profile of v7, /device:TPU:32, one launch (start us, length us, event | category | flops | bytes accessed | tf_op | source)
XLA Modules:
  0.0 118.9 jit_solution(18373726915817181445)
XLA Ops:
  0.6 4.5 %shard_map.103 = (bf16[1040,256]{1,0:T(8,128)(2,1)}, bf16[896,256]{1,0:T(8,128)(2,1)}, bf16[8,4,128,128]{3,2,1,0:T(8,128)(2,1)}) custom-call(s32[2,8]{1,0:T(2,128)} %bitcast.26, bf16[1024,896]{1,0:T(8,128)(2,1)} %bitcast.23, bf16[896,128]{1,0:T(8,128)(2,1)} %wk_ref.1, bf16[896,128]{1,0:T(8,128)(2,1)} %wv_ref.1, bf16[128,4096]{1,0:T(8,128)(2,1)} %wo_ref.1, ...), custom_call_target="tpu_custom_call" | custom-call | flops 470000000 | bytes 5242880 | tf_op jit(solution)/shard_map/pallas_call | solution.py:281
  5.1 8.7 %all-to-all-start.1 = ((bf16[8,4,128,128]{3,2,1,0:T(8,128)(2,1)}), bf16[8,4,128,128]{3,2,1,0:T(8,128)(2,1)}, u32[]{:S(2)}, u32[]{:S(2)}) async-start(bf16[8,4,128,128]{3,2,1,0:T(8,128)(2,1)} %get-tuple-element.53), calls=%async_computation.1 | async-start | bytes 2097152 | tf_op jit(solution)/shard_map/all_to_all | solution.py:292
  13.8 1.5 %collective-permute-start.1 = (bf16[1040,256]{1,0:T(8,128)(2,1)}, bf16[1040,256]{1,0:T(8,128)(2,1)}, u32[]{:S(2)}, u32[]{:S(2)}) collective-permute-start(bf16[1040,256]{1,0:T(8,128)(2,1)} %get-tuple-element.34.refs_0_), channel_id=1, source_target_pairs={{0,64},{64,128},{128,192},{192,0},{1,65},{65,129},{129,193},{193,1... | collective-permute-start | bytes 1597448 | tf_op jit(solution)/shard_map/ppermute | solution.py:273
  15.3 1.7 %collective-permute-start = (bf16[1040,256]{1,0:T(8,128)(2,1)}, bf16[1040,256]{1,0:T(8,128)(2,1)}, u32[]{:S(2)}, u32[]{:S(2)}) collective-permute-start(bf16[1040,256]{1,0:T(8,128)(2,1)} %get-tuple-element.34.refs_0_), channel_id=1, source_target_pairs={{0,192},{64,0},{128,64},{192,128},{1,193},{65,1},{129,65},{193,129... | collective-permute-start | bytes 1597448 | tf_op jit(solution)/shard_map/ppermute | solution.py:273
  17.1 4.4 %convolution_convert_fusion.1.q_ref = bf16[512,128]{1,0:T(8,128)(2,1)} fusion(bf16[512,4096]{1,0:T(8,128)(2,1)} %param.8, bf16[4096,128]{1,0:T(8,128)(2,1)} %wq_ref.1), kind=kOutput, calls=%fused_computation.1 | convolution fusion | flops 536936448 | bytes 5373952 | tf_op jit(solution)/shard_map/dot_general | solution.py:299
  21.5 3.0 %collective-permute-start.2 = (bf16[896,256]{1,0:T(8,128)(2,1)}, bf16[896,256]{1,0:T(8,128)(2,1)}, u32[]{:S(2)}, u32[]{:S(2)}) collective-permute-start(bf16[896,256]{1,0:T(8,128)(2,1)} %get-tuple-element.47.refs_0_), channel_id=1, source_target_pairs={{0,24},{8,0},{16,8},{24,16},{32,40},{40,48},{48,56},{56,32},{1,25}... | collective-permute-start | bytes 1376264 | tf_op jit(solution)/shard_map/ppermute | solution.py:297
  24.5 1.9 %convolution_convert_fusion.g_ref = bf16[512,128]{1,0:T(8,128)(2,1)} fusion(bf16[512,4096]{1,0:T(8,128)(2,1)S(1)} %copy-done.20, bf16[128,4096]{1,0:T(8,128)(2,1)S(1)} %copy-done), kind=kOutput, calls=%fused_computation | convolution fusion | flops 536936448 | bytes 5373952 | tf_op jit(solution)/shard_map/dot_general | solution.py:300
  26.4 2.2 %collective-permute-done.1.before_ref.refs_4_ = bf16[1040,256]{1,0:T(8,128)(2,1)} collective-permute-done((bf16[1040,256]{1,0:T(8,128)(2,1)}, bf16[1040,256]{1,0:T(8,128)(2,1)}, u32[]{:S(2)}, u32[]{:S(2)}) %collective-permute-start.1) | collective-permute-done | bytes 532512 | tf_op jit(solution)/shard_map/ppermute | solution.py:273
  28.6 1.9 %shard_map.104 = (bf16[528,256]{1,0:T(8,128)(2,1)}, bf16[512,256]{1,0:T(8,128)(2,1)}) custom-call(bf16[1040,256]{1,0:T(8,128)(2,1)} %collective-permute-done.after_ref.refs_1_, bf16[1040,256]{1,0:T(8,128)(2,1)} %collective-permute-done.1.before_ref.refs_4_), custom_call_target="tpu_custom_call" | custom-call | tf_op jit(solution)/shard_map/pallas_call | solution.py:306
  30.5 3.0 %collective-permute-start.5 = (bf16[528,256]{1,0:T(8,128)(2,1)}, bf16[528,256]{1,0:T(8,128)(2,1)S(1)}, u32[]{:S(2)}, u32[]{:S(2)}) collective-permute-start(bf16[528,256]{1,0:T(8,128)(2,1)} %get-tuple-element.43), channel_id=1, source_target_pairs={{0,192},{64,0},{128,64},{192,128},{1,193},{65,1},{129,65},{193,129... | collective-permute-start | bytes 811016 | tf_op jit(solution)/shard_map/ppermute | solution.py:273
  33.5 3.1 %collective-permute-start.3 = (bf16[896,256]{1,0:T(8,128)(2,1)}, bf16[896,256]{1,0:T(8,128)(2,1)}, u32[]{:S(2)}, u32[]{:S(2)}) collective-permute-start(bf16[896,256]{1,0:T(8,128)(2,1)} %collective-permute-done.2.refs_1_), channel_id=1, source_target_pairs={{0,24},{8,0},{16,8},{24,16},{32,40},{40,48},{48,56},{56,32},{1,25}... | collective-permute-start | bytes 1376264 | tf_op jit(solution)/shard_map/ppermute | solution.py:297
  36.6 4.7 %collective-permute-done.6.refs_3_ = bf16[512,256]{1,0:T(8,128)(2,1)S(1)} collective-permute-done((bf16[512,256]{1,0:T(8,128)(2,1)}, bf16[512,256]{1,0:T(8,128)(2,1)S(1)}, u32[]{:S(2)}, u32[]{:S(2)}) %collective-permute-start.6) | collective-permute-done | bytes 262176 | tf_op jit(solution)/shard_map/ppermute | solution.py:273
  45.5 5.4 %shard_map.105 = (bf16[512,128]{1,0:T(8,128)(2,1)}, bf16[512,128]{1,0:T(8,128)(2,1)}, bf16[8,4,4,32,256]{4,3,2,1,0:T(8,128)(2,1)}, s32[8,128]{1,0:T(8,128)}) custom-call(s32[4]{0:T(128)} %pad_add_fusion.pos_ref, s32[2,8]{1,0:T(2,128)} %bitcast.27, bf16[512,128]{1,0:T(8,128)(2,1)} %convolution_convert_fusion.1.q_ref, ...), custom_call_target="tpu_custom_call" | custom-call | tf_op jit(solution)/shard_map/pallas_call | solution.py:319
  50.9 7.9 %all-to-all-start = ((bf16[32,4,32,256]{3,2,1,0:T(8,128)(2,1)}), bf16[32,4,32,256]{3,2,1,0:T(8,128)(2,1)}, u32[]{:S(2)}, u32[]{:S(2)}) async-start(bf16[32,4,32,256]{3,2,1,0:T(8,128)(2,1)} %bitcast.22), calls=%async_computation | async-start | bytes 4194304 | tf_op jit(solution)/shard_map/all_to_all | solution.py:347
  59.5 2.9 %collective-permute-start.19 = (bf16[512,128]{1,0:T(8,128)(2,1)S(1)}, bf16[512,128]{1,0:T(8,128)(2,1)S(1)}, u32[]{:S(2)}, u32[]{:S(2)}) collective-permute-start(bf16[512,128]{1,0:T(8,128)(2,1)S(1)} %copy-done.5), channel_id=1, source_target_pairs={{0,7},{1,0},{2,1},{3,2},{4,3},{5,4},{6,5},{7,6},{8,15},{9,8},{10,9... | collective-permute-start | bytes 393224 | tf_op jit(solution)/shard_map/ppermute | solution.py:273
  63.2 2.3 %collective-permute-done.12.refs_5_ = bf16[512,128]{1,0:T(8,128)(2,1)S(1)} collective-permute-done((bf16[512,128]{1,0:T(8,128)(2,1)S(1)}, bf16[512,128]{1,0:T(8,128)(2,1)S(1)}, u32[]{:S(2)}, u32[]{:S(2)}) %collective-permute-start.12) | collective-permute-done | bytes 131104 | tf_op jit(solution)/shard_map/ppermute | solution.py:273
  66.2 2.0 %collective-permute-done.19.refs_13_ = bf16[512,128]{1,0:T(8,128)(2,1)S(1)} collective-permute-done((bf16[512,128]{1,0:T(8,128)(2,1)S(1)}, bf16[512,128]{1,0:T(8,128)(2,1)S(1)}, u32[]{:S(2)}, u32[]{:S(2)}) %collective-permute-start.19) | collective-permute-done | bytes 131104 | tf_op jit(solution)/shard_map/ppermute | solution.py:273
  68.2 1.7 %collective-permute-start.20 = (bf16[512,128]{1,0:T(8,128)(2,1)S(1)}, bf16[512,128]{1,0:T(8,128)(2,1)S(1)}, u32[]{:S(2)}, u32[]{:S(2)}) collective-permute-start(bf16[512,128]{1,0:T(8,128)(2,1)S(1)} %collective-permute-done.19.refs_13_), channel_id=1, source_target_pairs={{0,7},{1,0},{2,1},{3,2},{4,3},{5,4},{6,5},{7,6},{8,15},{9,8},{10,9... | collective-permute-start | bytes 393224 | tf_op jit(solution)/shard_map/ppermute | solution.py:273
  70.3 1.6 %collective-permute-start.24 = (bf16[512,128]{1,0:T(8,128)(2,1)S(1)}, bf16[512,128]{1,0:T(8,128)(2,1)S(1)}, u32[]{:S(2)}, u32[]{:S(2)}) collective-permute-start(bf16[512,128]{1,0:T(8,128)(2,1)S(1)} %collective-permute-done.23.refs_19_), channel_id=1, source_target_pairs={{0,1},{1,2},{2,3},{3,4},{4,5},{5,6},{6,7},{7,0},{8,9},{9,10},{10,1... | collective-permute-start | bytes 393224 | tf_op jit(solution)/shard_map/ppermute | solution.py:273
  73.3 3.5 %collective-permute-start.21 = (bf16[512,128]{1,0:T(8,128)(2,1)S(1)}, bf16[512,128]{1,0:T(8,128)(2,1)S(1)}, u32[]{:S(2)}, u32[]{:S(2)}) collective-permute-start(bf16[512,128]{1,0:T(8,128)(2,1)S(1)} %collective-permute-done.20.refs_14_), channel_id=1, source_target_pairs={{0,7},{1,0},{2,1},{3,2},{4,3},{5,4},{6,5},{7,6},{8,15},{9,8},{10,9... | collective-permute-start | bytes 393224 | tf_op jit(solution)/shard_map/ppermute | solution.py:273
  79.2 2.0 %collective-permute-start.15 = (bf16[512,128]{1,0:T(8,128)(2,1)S(1)}, bf16[512,128]{1,0:T(8,128)(2,1)S(1)}, u32[]{:S(2)}, u32[]{:S(2)}) collective-permute-start(bf16[512,128]{1,0:T(8,128)(2,1)S(1)} %collective-permute-done.14.refs_7_), channel_id=1, source_target_pairs={{0,7},{1,0},{2,1},{3,2},{4,3},{5,4},{6,5},{7,6},{8,15},{9,8},{10,9... | collective-permute-start | bytes 393224 | tf_op jit(solution)/shard_map/ppermute | solution.py:273
  81.2 3.3 %collective-permute-start.22 = (bf16[512,128]{1,0:T(8,128)(2,1)S(1)}, bf16[512,128]{1,0:T(8,128)(2,1)S(1)}, u32[]{:S(2)}, u32[]{:S(2)}) collective-permute-start(bf16[512,128]{1,0:T(8,128)(2,1)S(1)} %collective-permute-done.21.refs_15_), channel_id=1, source_target_pairs={{0,7},{1,0},{2,1},{3,2},{4,3},{5,4},{6,5},{7,6},{8,15},{9,8},{10,9... | collective-permute-start | bytes 393224 | tf_op jit(solution)/shard_map/ppermute | solution.py:273
  85.9 1.4 %collective-permute-done.22.refs_16_ = bf16[512,128]{1,0:T(8,128)(2,1)S(1)} collective-permute-done((bf16[512,128]{1,0:T(8,128)(2,1)S(1)}, bf16[512,128]{1,0:T(8,128)(2,1)S(1)}, u32[]{:S(2)}, u32[]{:S(2)}) %collective-permute-start.22) | collective-permute-done | bytes 131104 | tf_op jit(solution)/shard_map/ppermute | solution.py:273
  88.0 7.8 %shard_map.106 = (bf16[256,896]{1,0:T(8,128)(2,1)}, f32[512,128]{1,0:T(8,128)}, bf16[512,128]{1,0:T(8,128)(2,1)}, bf16[512,128]{1,0:T(8,128)(2,1)}, bf16[512,128...) custom-call(s32[4]{0:T(128)} %pad_add_fusion.pos_ref, ...), custom_call_target="tpu_custom_call" | custom-call | flops 1580000000 | bytes 10485760 | tf_op jit(solution)/shard_map/pallas_call | solution.py:352
  95.7 7.2 %all-to-all-start.2 = ((bf16[8,32,896]{2,1,0:T(8,128)(2,1)}), bf16[8,32,896]{2,1,0:T(8,128)(2,1)S(1)}, u32[]{:S(2)}, u32[]{:S(2)}) async-start(bf16[8,32,896]{2,1,0:T(8,128)(2,1)} %bitcast.24), calls=%async_computation.2 | async-start | bytes 917504 | tf_op jit(solution)/shard_map/all_to_all | solution.py:366
  102.9 1.6 %collective-permute-start.27 = (bf16[512,128]{1,0:T(8,128)(2,1)}, bf16[512,128]{1,0:T(8,128)(2,1)S(1)}, u32[]{:S(2)}, u32[]{:S(2)}) collective-permute-start(bf16[512,128]{1,0:T(8,128)(2,1)} %get-tuple-element.55), channel_id=1, source_target_pairs={{0,8},{8,16},{16,24},{24,0},{1,9},{9,17},{17,25},{25,1},{2,10},{10... | collective-permute-start | bytes 393224 | tf_op jit(solution)/shard_map/ppermute | solution.py:273
  104.5 2.7 %collective-permute-start.28 = (bf16[512,128]{1,0:T(8,128)(2,1)}, bf16[512,128]{1,0:T(8,128)(2,1)S(1)}, u32[]{:S(2)}, u32[]{:S(2)}) collective-permute-start(bf16[512,128]{1,0:T(8,128)(2,1)} %get-tuple-element.56), channel_id=1, source_target_pairs={{0,16},{8,24},{16,0},{24,8},{1,17},{9,25},{17,1},{25,9},{2,18},{10... | collective-permute-start | bytes 393224 | tf_op jit(solution)/shard_map/ppermute | solution.py:273
  107.2 1.5 %collective-permute-start.29 = (bf16[512,128]{1,0:T(8,128)(2,1)}, bf16[512,128]{1,0:T(8,128)(2,1)S(1)}, u32[]{:S(2)}, u32[]{:S(2)}) collective-permute-start(bf16[512,128]{1,0:T(8,128)(2,1)} %get-tuple-element.57), channel_id=1, source_target_pairs={{0,24},{8,0},{16,8},{24,16},{1,25},{9,1},{17,9},{25,17},{2,26},{10... | collective-permute-start | bytes 393224 | tf_op jit(solution)/shard_map/ppermute | solution.py:273
  110.1 2.3 %collective-permute-start.32 = (bf16[512,128]{1,0:T(8,128)(2,1)}, bf16[512,128]{1,0:T(8,128)(2,1)S(1)}, u32[]{:S(2)}, u32[]{:S(2)}) collective-permute-start(bf16[512,128]{1,0:T(8,128)(2,1)} %get-tuple-element.63), channel_id=1, source_target_pairs={{0,24},{8,0},{16,8},{24,16},{1,25},{9,1},{17,9},{25,17},{2,26},{10... | collective-permute-start | bytes 393224 | tf_op jit(solution)/shard_map/ppermute | solution.py:273
  112.3 1.4 %collective-permute-done.28 = bf16[512,128]{1,0:T(8,128)(2,1)S(1)} collective-permute-done((bf16[512,128]{1,0:T(8,128)(2,1)}, bf16[512,128]{1,0:T(8,128)(2,1)S(1)}, u32[]{:S(2)}, u32[]{:S(2)}) %collective-permute-start.28) | collective-permute-done | bytes 131104 | tf_op jit(solution)/shard_map/ppermute | solution.py:273
  113.8 1.7 %add_convert_fusion.1 = bf16[512,128]{1,0:T(8,128)(2,1)} fusion(bf16[512,128]{1,0:T(8,128)(2,1)S(1)} %collective-permute-done.29, bf16[512,128]{1,0:T(8,128)(2,1)S(1)} %collective-permute-done.28, f32[512,128]{1,0:T(8,128)} %get-tuple-element.54, bf16[512,128]{1,0:T(8,128)(2,1)S(1)} %collective-permute-done.27), kind=kLoop, calls=%fused_computation.3 | loop fusion | flops 458752 | bytes 786432 | tf_op jit(solution)/shard_map/convert_element_type | solution.py:373
  117.3 1.7 %add_convert_fusion = bf16[512,128]{1,0:T(8,128)(2,1)} fusion(bf16[512,128]{1,0:T(8,128)(2,1)S(1)} %collective-permute-done.32, bf16[512,128]{1,0:T(8,128)(2,1)S(1)} %collective-permute-done.31, f32[512,128]{1,0:T(8,128)} %get-tuple-element.60, bf16[512,128]{1,0:T(8,128)(2,1)S(1)} %collective-permute-done.30), kind=kLoop, calls=%fused_computation.2 | loop fusion | flops 458752 | bytes 786432 | tf_op jit(solution)/shard_map/convert_element_type | solution.py:373
  (92 shorter events, 15.9 us)
Async XLA Ops:
  5.1 45.8 %all-to-all-start.1 = ((bf16[8,4,128,128]{3,2,1,0:T(8,128)(2,1)}), bf16[8,4,128,128]{3,2,1,0:T(8,128)(2,1)}, u32[]{:S(2)}, u32[]{:S(2)}) async-start(bf16[8,4,128,128]{3,2,1,0:T(8,128)(2,1)} %get-tuple-element.53), calls=%async_computation.1 | async-start | bytes 2097152 | tf_op jit(solution)/shard_map/all_to_all | solution.py:292
  13.8 14.8 %collective-permute-start.1 = (bf16[1040,256]{1,0:T(8,128)(2,1)}, bf16[1040,256]{1,0:T(8,128)(2,1)}, u32[]{:S(2)}, u32[]{:S(2)}) collective-permute-start(bf16[1040,256]{1,0:T(8,128)(2,1)} %get-tuple-element.34.refs_0_), channel_id=1, source_target_pairs={{0,64},{64,128},{128,192},{192,0},{1,65},{65,129},{129,193},{193,1... | collective-permute-start | bytes 1597448 | tf_op jit(solution)/shard_map/ppermute | solution.py:273
  15.3 13.3 %collective-permute-start = (bf16[1040,256]{1,0:T(8,128)(2,1)}, bf16[1040,256]{1,0:T(8,128)(2,1)}, u32[]{:S(2)}, u32[]{:S(2)}) collective-permute-start(bf16[1040,256]{1,0:T(8,128)(2,1)} %get-tuple-element.34.refs_0_), channel_id=1, source_target_pairs={{0,192},{64,0},{128,64},{192,128},{1,193},{65,1},{129,65},{193,129... | collective-permute-start | bytes 1597448 | tf_op jit(solution)/shard_map/ppermute | solution.py:273
  21.5 12.1 %collective-permute-start.2 = (bf16[896,256]{1,0:T(8,128)(2,1)}, bf16[896,256]{1,0:T(8,128)(2,1)}, u32[]{:S(2)}, u32[]{:S(2)}) collective-permute-start(bf16[896,256]{1,0:T(8,128)(2,1)} %get-tuple-element.47.refs_0_), channel_id=1, source_target_pairs={{0,24},{8,0},{16,8},{24,16},{32,40},{40,48},{48,56},{56,32},{1,25}... | collective-permute-start | bytes 1376264 | tf_op jit(solution)/shard_map/ppermute | solution.py:297
  30.5 10.8 %collective-permute-start.5 = (bf16[528,256]{1,0:T(8,128)(2,1)}, bf16[528,256]{1,0:T(8,128)(2,1)S(1)}, u32[]{:S(2)}, u32[]{:S(2)}) collective-permute-start(bf16[528,256]{1,0:T(8,128)(2,1)} %get-tuple-element.43), channel_id=1, source_target_pairs={{0,192},{64,0},{128,64},{192,128},{1,193},{65,1},{129,65},{193,129... | collective-permute-start | bytes 811016 | tf_op jit(solution)/shard_map/ppermute | solution.py:273
  33.5 7.8 %collective-permute-start.6 = (bf16[512,256]{1,0:T(8,128)(2,1)}, bf16[512,256]{1,0:T(8,128)(2,1)S(1)}, u32[]{:S(2)}, u32[]{:S(2)}) collective-permute-start(bf16[512,256]{1,0:T(8,128)(2,1)} %get-tuple-element.44), channel_id=1, source_target_pairs={{0,64},{64,128},{128,192},{192,0},{1,65},{65,129},{129,193},{193,1... | collective-permute-start | bytes 786440 | tf_op jit(solution)/shard_map/ppermute | solution.py:273
  33.5 8.3 %collective-permute-start.4 = (bf16[896,256]{1,0:T(8,128)(2,1)}, bf16[896,256]{1,0:T(8,128)(2,1)}, u32[]{:S(2)}, u32[]{:S(2)}) collective-permute-start(bf16[896,256]{1,0:T(8,128)(2,1)} %collective-permute-done.2.refs_1_), channel_id=1, source_target_pairs={{0,32},{32,0},{1,33},{33,1},{2,34},{34,2},{3,35},{35,3},{4,36},{36... | collective-permute-start | bytes 1376264 | tf_op jit(solution)/shard_map/ppermute | solution.py:273
  33.5 9.4 %collective-permute-start.3 = (bf16[896,256]{1,0:T(8,128)(2,1)}, bf16[896,256]{1,0:T(8,128)(2,1)}, u32[]{:S(2)}, u32[]{:S(2)}) collective-permute-start(bf16[896,256]{1,0:T(8,128)(2,1)} %collective-permute-done.2.refs_1_), channel_id=1, source_target_pairs={{0,24},{8,0},{16,8},{24,16},{32,40},{40,48},{48,56},{56,32},{1,25}... | collective-permute-start | bytes 1376264 | tf_op jit(solution)/shard_map/ppermute | solution.py:297
  36.6 7.0 %collective-permute-start.7 = (bf16[1040,256]{1,0:T(8,128)(2,1)}, bf16[1040,256]{1,0:T(8,128)(2,1)}, u32[]{:S(2)}, u32[]{:S(2)}) collective-permute-start(bf16[1040,256]{1,0:T(8,128)(2,1)} %get-tuple-element.34.refs_0_), channel_id=1, source_target_pairs={{0,32},{32,0},{1,33},{33,1},{2,34},{34,2},{3,35},{35,3},{4,36},{36... | collective-permute-start | bytes 1597448 | tf_op jit(solution)/shard_map/ppermute | solution.py:273
  50.9 37.1 %all-to-all-start = ((bf16[32,4,32,256]{3,2,1,0:T(8,128)(2,1)}), bf16[32,4,32,256]{3,2,1,0:T(8,128)(2,1)}, u32[]{:S(2)}, u32[]{:S(2)}) async-start(bf16[32,4,32,256]{3,2,1,0:T(8,128)(2,1)} %bitcast.22), calls=%async_computation | async-start | bytes 4194304 | tf_op jit(solution)/shard_map/all_to_all | solution.py:347
  58.8 29.1 %collective-permute-start.26 = (bf16[8,4,128,128]{3,2,1,0:T(8,128)(2,1)}, bf16[8,4,128,128]{3,2,1,0:T(8,128)(2,1)}, u32[]{:S(2)}, u32[]{:S(2)}) collective-permute-start(bf16[8,4,128,128]{3,2,1,0:T(8,128)(2,1)} %all-to-all-done.1.refs_20_), channel_id=1, source_target_pairs={{0,32},{32,0},{1,33},{33,1},{2,34},{34,2},{3,35},{35,3},{4,36},{36... | collective-permute-start | bytes 3145736 | tf_op jit(solution)/shard_map/ppermute | solution.py:273
  59.1 6.3 %collective-permute-start.12 = (bf16[512,128]{1,0:T(8,128)(2,1)S(1)}, bf16[512,128]{1,0:T(8,128)(2,1)S(1)}, u32[]{:S(2)}, u32[]{:S(2)}) collective-permute-start(bf16[512,128]{1,0:T(8,128)(2,1)S(1)} %copy-done.4), channel_id=1, source_target_pairs={{0,7},{1,0},{2,1},{3,2},{4,3},{5,4},{6,5},{7,6},{8,15},{9,8},{10,9... | collective-permute-start | bytes 393224 | tf_op jit(solution)/shard_map/ppermute | solution.py:273
  59.5 8.7 %collective-permute-start.19 = (bf16[512,128]{1,0:T(8,128)(2,1)S(1)}, bf16[512,128]{1,0:T(8,128)(2,1)S(1)}, u32[]{:S(2)}, u32[]{:S(2)}) collective-permute-start(bf16[512,128]{1,0:T(8,128)(2,1)S(1)} %copy-done.5), channel_id=1, source_target_pairs={{0,7},{1,0},{2,1},{3,2},{4,3},{5,4},{6,5},{7,6},{8,15},{9,8},{10,9... | collective-permute-start | bytes 393224 | tf_op jit(solution)/shard_map/ppermute | solution.py:273
  62.4 7.5 %collective-permute-start.16 = (bf16[512,128]{1,0:T(8,128)(2,1)S(1)}, bf16[512,128]{1,0:T(8,128)(2,1)S(1)}, u32[]{:S(2)}, u32[]{:S(2)}) collective-permute-start(bf16[512,128]{1,0:T(8,128)(2,1)S(1)} %copy-done.4), channel_id=1, source_target_pairs={{0,1},{1,2},{2,3},{3,4},{4,5},{5,6},{6,7},{7,0},{8,9},{9,10},{10,1... | collective-permute-start | bytes 393224 | tf_op jit(solution)/shard_map/ppermute | solution.py:273
  62.4 8.0 %collective-permute-start.23 = (bf16[512,128]{1,0:T(8,128)(2,1)S(1)}, bf16[512,128]{1,0:T(8,128)(2,1)S(1)}, u32[]{:S(2)}, u32[]{:S(2)}) collective-permute-start(bf16[512,128]{1,0:T(8,128)(2,1)S(1)} %copy-done.5), channel_id=1, source_target_pairs={{0,1},{1,2},{2,3},{3,4},{4,5},{5,6},{6,7},{7,0},{8,9},{9,10},{10,1... | collective-permute-start | bytes 393224 | tf_op jit(solution)/shard_map/ppermute | solution.py:273
  65.5 6.5 %collective-permute-start.13 = (bf16[512,128]{1,0:T(8,128)(2,1)S(1)}, bf16[512,128]{1,0:T(8,128)(2,1)S(1)}, u32[]{:S(2)}, u32[]{:S(2)}) collective-permute-start(bf16[512,128]{1,0:T(8,128)(2,1)S(1)} %collective-permute-done.12.refs_5_), channel_id=1, source_target_pairs={{0,7},{1,0},{2,1},{3,2},{4,3},{5,4},{6,5},{7,6},{8,15},{9,8},{10,9... | collective-permute-start | bytes 393224 | tf_op jit(solution)/shard_map/ppermute | solution.py:273
  68.2 5.1 %collective-permute-start.20 = (bf16[512,128]{1,0:T(8,128)(2,1)S(1)}, bf16[512,128]{1,0:T(8,128)(2,1)S(1)}, u32[]{:S(2)}, u32[]{:S(2)}) collective-permute-start(bf16[512,128]{1,0:T(8,128)(2,1)S(1)} %collective-permute-done.19.refs_13_), channel_id=1, source_target_pairs={{0,7},{1,0},{2,1},{3,2},{4,3},{5,4},{6,5},{7,6},{8,15},{9,8},{10,9... | collective-permute-start | bytes 393224 | tf_op jit(solution)/shard_map/ppermute | solution.py:273
  69.9 6.8 %collective-permute-start.17 = (bf16[512,128]{1,0:T(8,128)(2,1)S(1)}, bf16[512,128]{1,0:T(8,128)(2,1)S(1)}, u32[]{:S(2)}, u32[]{:S(2)}) collective-permute-start(bf16[512,128]{1,0:T(8,128)(2,1)S(1)} %collective-permute-done.16.refs_11_), channel_id=1, source_target_pairs={{0,1},{1,2},{2,3},{3,4},{4,5},{5,6},{6,7},{7,0},{8,9},{9,10},{10,1... | collective-permute-start | bytes 393224 | tf_op jit(solution)/shard_map/ppermute | solution.py:273
  70.3 7.6 %collective-permute-start.24 = (bf16[512,128]{1,0:T(8,128)(2,1)S(1)}, bf16[512,128]{1,0:T(8,128)(2,1)S(1)}, u32[]{:S(2)}, u32[]{:S(2)}) collective-permute-start(bf16[512,128]{1,0:T(8,128)(2,1)S(1)} %collective-permute-done.23.refs_19_), channel_id=1, source_target_pairs={{0,1},{1,2},{2,3},{3,4},{4,5},{5,6},{6,7},{7,0},{8,9},{9,10},{10,1... | collective-permute-start | bytes 393224 | tf_op jit(solution)/shard_map/ppermute | solution.py:273
  72.0 7.2 %collective-permute-start.14 = (bf16[512,128]{1,0:T(8,128)(2,1)S(1)}, bf16[512,128]{1,0:T(8,128)(2,1)S(1)}, u32[]{:S(2)}, u32[]{:S(2)}) collective-permute-start(bf16[512,128]{1,0:T(8,128)(2,1)S(1)} %collective-permute-done.13.refs_6_), channel_id=1, source_target_pairs={{0,7},{1,0},{2,1},{3,2},{4,3},{5,4},{6,5},{7,6},{8,15},{9,8},{10,9... | collective-permute-start | bytes 393224 | tf_op jit(solution)/shard_map/ppermute | solution.py:273
  73.3 7.9 %collective-permute-start.21 = (bf16[512,128]{1,0:T(8,128)(2,1)S(1)}, bf16[512,128]{1,0:T(8,128)(2,1)S(1)}, u32[]{:S(2)}, u32[]{:S(2)}) collective-permute-start(bf16[512,128]{1,0:T(8,128)(2,1)S(1)} %collective-permute-done.20.refs_14_), channel_id=1, source_target_pairs={{0,7},{1,0},{2,1},{3,2},{4,3},{5,4},{6,5},{7,6},{8,15},{9,8},{10,9... | collective-permute-start | bytes 393224 | tf_op jit(solution)/shard_map/ppermute | solution.py:273
  76.8 7.7 %collective-permute-start.18 = (bf16[512,128]{1,0:T(8,128)(2,1)S(1)}, bf16[512,128]{1,0:T(8,128)(2,1)S(1)}, u32[]{:S(2)}, u32[]{:S(2)}) collective-permute-start(bf16[512,128]{1,0:T(8,128)(2,1)S(1)} %collective-permute-done.17.refs_10_), channel_id=1, source_target_pairs={{0,1},{1,2},{2,3},{3,4},{4,5},{5,6},{6,7},{7,0},{8,9},{9,10},{10,1... | collective-permute-start | bytes 393224 | tf_op jit(solution)/shard_map/ppermute | solution.py:273
  77.9 6.6 %collective-permute-start.25 = (bf16[512,128]{1,0:T(8,128)(2,1)S(1)}, bf16[512,128]{1,0:T(8,128)(2,1)S(1)}, u32[]{:S(2)}, u32[]{:S(2)}) collective-permute-start(bf16[512,128]{1,0:T(8,128)(2,1)S(1)} %collective-permute-done.24.refs_18_), channel_id=1, source_target_pairs={{0,1},{1,2},{2,3},{3,4},{4,5},{5,6},{6,7},{7,0},{8,9},{9,10},{10,1... | collective-permute-start | bytes 393224 | tf_op jit(solution)/shard_map/ppermute | solution.py:273
  79.2 6.7 %collective-permute-start.15 = (bf16[512,128]{1,0:T(8,128)(2,1)S(1)}, bf16[512,128]{1,0:T(8,128)(2,1)S(1)}, u32[]{:S(2)}, u32[]{:S(2)}) collective-permute-start(bf16[512,128]{1,0:T(8,128)(2,1)S(1)} %collective-permute-done.14.refs_7_), channel_id=1, source_target_pairs={{0,7},{1,0},{2,1},{3,2},{4,3},{5,4},{6,5},{7,6},{8,15},{9,8},{10,9... | collective-permute-start | bytes 393224 | tf_op jit(solution)/shard_map/ppermute | solution.py:273
  81.2 6.1 %collective-permute-start.22 = (bf16[512,128]{1,0:T(8,128)(2,1)S(1)}, bf16[512,128]{1,0:T(8,128)(2,1)S(1)}, u32[]{:S(2)}, u32[]{:S(2)}) collective-permute-start(bf16[512,128]{1,0:T(8,128)(2,1)S(1)} %collective-permute-done.21.refs_15_), channel_id=1, source_target_pairs={{0,7},{1,0},{2,1},{3,2},{4,3},{5,4},{6,5},{7,6},{8,15},{9,8},{10,9... | collective-permute-start | bytes 393224 | tf_op jit(solution)/shard_map/ppermute | solution.py:273
  95.7 20.3 %all-to-all-start.2 = ((bf16[8,32,896]{2,1,0:T(8,128)(2,1)}), bf16[8,32,896]{2,1,0:T(8,128)(2,1)S(1)}, u32[]{:S(2)}, u32[]{:S(2)}) async-start(bf16[8,32,896]{2,1,0:T(8,128)(2,1)} %bitcast.24), calls=%async_computation.2 | async-start | bytes 917504 | tf_op jit(solution)/shard_map/all_to_all | solution.py:366
  102.9 7.2 %collective-permute-start.27 = (bf16[512,128]{1,0:T(8,128)(2,1)}, bf16[512,128]{1,0:T(8,128)(2,1)S(1)}, u32[]{:S(2)}, u32[]{:S(2)}) collective-permute-start(bf16[512,128]{1,0:T(8,128)(2,1)} %get-tuple-element.55), channel_id=1, source_target_pairs={{0,8},{8,16},{16,24},{24,0},{1,9},{9,17},{17,25},{25,1},{2,10},{10... | collective-permute-start | bytes 393224 | tf_op jit(solution)/shard_map/ppermute | solution.py:273
  104.5 9.3 %collective-permute-start.28 = (bf16[512,128]{1,0:T(8,128)(2,1)}, bf16[512,128]{1,0:T(8,128)(2,1)S(1)}, u32[]{:S(2)}, u32[]{:S(2)}) collective-permute-start(bf16[512,128]{1,0:T(8,128)(2,1)} %get-tuple-element.56), channel_id=1, source_target_pairs={{0,16},{8,24},{16,0},{24,8},{1,17},{9,25},{17,1},{25,9},{2,18},{10... | collective-permute-start | bytes 393224 | tf_op jit(solution)/shard_map/ppermute | solution.py:273
  107.2 6.6 %collective-permute-start.29 = (bf16[512,128]{1,0:T(8,128)(2,1)}, bf16[512,128]{1,0:T(8,128)(2,1)S(1)}, u32[]{:S(2)}, u32[]{:S(2)}) collective-permute-start(bf16[512,128]{1,0:T(8,128)(2,1)} %get-tuple-element.57), channel_id=1, source_target_pairs={{0,24},{8,0},{16,8},{24,16},{1,25},{9,1},{17,9},{25,17},{2,26},{10... | collective-permute-start | bytes 393224 | tf_op jit(solution)/shard_map/ppermute | solution.py:273
  108.6 8.1 %collective-permute-start.30 = (bf16[512,128]{1,0:T(8,128)(2,1)}, bf16[512,128]{1,0:T(8,128)(2,1)S(1)}, u32[]{:S(2)}, u32[]{:S(2)}) collective-permute-start(bf16[512,128]{1,0:T(8,128)(2,1)} %get-tuple-element.61), channel_id=1, source_target_pairs={{0,8},{8,16},{16,24},{24,0},{1,9},{9,17},{17,25},{25,1},{2,10},{10... | collective-permute-start | bytes 393224 | tf_op jit(solution)/shard_map/ppermute | solution.py:273
  109.2 7.5 %collective-permute-start.31 = (bf16[512,128]{1,0:T(8,128)(2,1)}, bf16[512,128]{1,0:T(8,128)(2,1)S(1)}, u32[]{:S(2)}, u32[]{:S(2)}) collective-permute-start(bf16[512,128]{1,0:T(8,128)(2,1)} %get-tuple-element.62), channel_id=1, source_target_pairs={{0,16},{8,24},{16,0},{24,8},{1,17},{9,25},{17,1},{25,9},{2,18},{10... | collective-permute-start | bytes 393224 | tf_op jit(solution)/shard_map/ppermute | solution.py:273
  110.1 7.2 %collective-permute-start.32 = (bf16[512,128]{1,0:T(8,128)(2,1)}, bf16[512,128]{1,0:T(8,128)(2,1)S(1)}, u32[]{:S(2)}, u32[]{:S(2)}) collective-permute-start(bf16[512,128]{1,0:T(8,128)(2,1)} %get-tuple-element.63), channel_id=1, source_target_pairs={{0,24},{8,0},{16,8},{24,16},{1,25},{9,1},{17,9},{25,17},{2,26},{10... | collective-permute-start | bytes 393224 | tf_op jit(solution)/shard_map/ppermute | solution.py:273
  (25 other events, 122.4 us)

commit v8 on v7

--- a/solution.py
+++ b/solution.py
@@ -89,13 +89,13 @@
         copy.wait()
 
 
-def attention_body(geom, pos_ref, ids_ref, q_ref, g_ref, *refs):
+def attention_body(geom, ids_ref, q_ref, g_ref, *refs):
     blocks, block_len, n_x, n_y, cap, stored, seg = geom
     kv_refs, (attn_ref, gq_ref, out_ref, all_ids_ref, kv_ref, stage_ref, head_ref, sem) = refs[:-8], refs[-8:]
     inv_root = 1.0 / math.sqrt(DH)
     piece = seg // n_y
     cut = HEAD + stored // 2 * seg
-    my_x, my_c = pos_ref[0], pos_ref[1]
+    my_x, my_c = lax.axis_index("x"), lax.axis_index("c")
     requests = 2 * blocks
     parts = len(kv_refs) // 2
 
@@ -175,14 +175,14 @@
         copy.wait()
 
 
-def tail_body(stored, n_z, pos_ref, ids_ref, ret_ref, *refs):
+def tail_body(stored, n_z, ids_ref, ret_ref, *refs):
     owners, n_y, cap, piece, _ = ret_ref.shape
     pair_refs, refs = refs[:n_y], refs[n_y:]
     piece_refs, (mine, other), refs = refs[: 2 * n_z], refs[2 * n_z : 2 * n_z + 2], refs[2 * n_z + 2 :]
-    out_ref, sums, refs = refs[0], refs[1 : 1 + 2 * n_y], refs[1 + 2 * n_y :]
-    got_ref, pair_ref, acc_ref, prod_ref, a_ref, w_ref, sem = refs
-    my_c, my_y, my_z = (pos_ref[i] for i in range(1, 4))
-    me = pos_ref[0] * 2 + my_c
+    out_hbm, sums_hbm, refs = refs[0], refs[1 : 1 + 2 * n_y], refs[1 + 2 * n_y :]
+    got_ref, pair_ref, acc_ref, prod_ref, a_ref, w_ref, out_ref, own_ref, sent_ref, sem = refs
+    my_x, my_c, my_y, my_z = (lax.axis_index(a) for a in ("x", "c", "y", "z"))
+    me = my_x * 2 + my_c
 
     for d in range(owners):
         pltpu.make_async_copy(ret_ref.at[d], got_ref.at[d], sem.at[d]).start()
@@ -223,7 +223,7 @@
         return carry
 
     lax.fori_loop(0, owners, from_device, 0)
-    for copy in pair_copies + piece_copies + weight_copies:
+    for copy in pair_copies:
         copy.wait()
     lanes = prod_ref.shape[0]
     both = [acc_ref[lax.rem(my_y + y, n_y)].astype(BF).reshape(stored * piece, 2 * DH) for y in range(n_y)]
@@ -239,6 +239,12 @@
             two = [prod_ref[n, pl.ds(t + k, stored, stride=piece), :] for k in range(2)]
             out_ref[pl.ds(t * stored, 2 * stored), n * DH : (n + 1) * DH] = jnp.concatenate(two, axis=0).astype(BF)
 
+    first += 2
+    leaving = [pltpu.make_async_copy(out_ref, out_hbm, sem.at[first])]
+    leaving[0].start()
+
+    for copy in piece_copies + weight_copies:
+        copy.wait()
     heads = [lax.rem(my_z + j, n_z) for j in range(n_z)]
     for second in range(2):
         for k in range(0, n_y, 2):
@@ -250,8 +256,15 @@
                 w = [jnp.concatenate([w_ref[0, h, at[i]] for h in heads], axis=0) for i in range(2)]
                 total = jnp.dot(a_ref[0], jnp.concatenate(w, axis=1), preferred_element_type=F32)
             for i in range(2):
-                ref = sums[second * n_y + k + i]
+                ref = sent_ref.at[second, k + i - 1] if k + i else own_ref.at[second]
                 ref[...] = total[:, i * DH : (i + 1) * DH].astype(ref.dtype)
+        for k in range(n_y):
+            ref = sent_ref.at[second, k - 1] if k else own_ref.at[second]
+            n = second * n_y + k
+            leaving.append(pltpu.make_async_copy(ref, sums_hbm[n], sem.at[first + 1 + n]))
+            leaving[-1].start()
+    for copy in leaving:
+        copy.wait()
 
 
 def shards(hidden, encoded, neighbours, w_query, w_key, w_value, w_out, cotangent):
@@ -267,7 +280,6 @@
     block_len = rows // blocks
     piece = seg // n_y
     ids = neighbours.T
-    place = jnp.stack([lax.axis_index(a) for a in ("x", "c", "y", "z")]).astype(jnp.int32)
 
     def shift(axis, n, k):
         return lambda a: lax.ppermute(a, axis, [(i, (i + k) % n) for i in range(n)])
@@ -324,7 +336,7 @@
             jax.ShapeDtypeStruct((owners, n_y, cap, piece, 2 * DH), BF),
             jax.ShapeDtypeStruct((owners, DH), jnp.int32),
         ),
-        "ssvv" + "a" * len(kv_all), 0, 0,
+        "svv" + "a" * len(kv_all), 0, 0,
         scratch=(
             pltpu.VMEM((blocks * per_block, seg, 2 * DH), BF),
             pltpu.VMEM((blocks * per_block, n_y, piece, 2 * DH), BF),
@@ -332,7 +344,7 @@
             pltpu.SemaphoreType.DMA((2 * blocks * per_block + owners,)),
         ),
         out_space="vvav",
-    )(place, ids, queries, grad_attn, *kv_all)
+    )(ids, queries, grad_attn, *kv_all)
 
     def ring(own):
         pieces = {0: own}
@@ -352,7 +364,7 @@
     enc_part, *sums = call(
         functools.partial(tail_body, stored, n_z),
         (jax.ShapeDtypeStruct((piece * stored, enc_width), BF),) + sums + sums,
-        "ssa" + "a" * (n_y + 2 * n_z + 2), 1_580_000_000, 10 << 20,
+        "sa" + "a" * (n_y + 2 * n_z + 2), 1_580_000_000, 10 << 20,
         scratch=(
             pltpu.VMEM((owners, n_y, cap, piece, 2 * DH), BF),
             pltpu.VMEM((n_y, enc_width, 2 * DH), BF),
@@ -360,9 +372,13 @@
             pltpu.VMEM((enc_width // DH, stored * piece, DH), F32),
             pltpu.VMEM((2, rows, n_z * DH), BF),
             pltpu.VMEM((2, n_z, n_y, DH, DH), BF),
-            pltpu.SemaphoreType.DMA((owners + n_y + 2 * n_z + 2,)),
+            pltpu.VMEM((piece * stored, enc_width), BF),
+            pltpu.VMEM((2, rows, DH), F32),
+            pltpu.VMEM((2, n_y - 1, rows, DH), BF),
+            pltpu.SemaphoreType.DMA((owners + n_y + 2 * n_z + 2 + 1 + 2 * n_y,)),
         ),
-    )(place, ids_all, returned, *pairs, *attn_all, *gq_all, mine, other)
+        out_space="a",
+    )(ids_all, returned, *pairs, *attn_all, *gq_all, mine, other)
     enc_parts = lax.all_to_all(enc_part.reshape(n_z, -1, enc_width), "z", 0, 0, tiled=True)
     enc_rows_sum = jnp.sum(enc_parts.astype(F32), axis=0).astype(BF)
 

time: 120 us -> 120 us (level)
  transfers between devices with their start and end apart: 36 -> 36, of which waited for: 14 -> 14; matrix products, arithmetic and copies ran while one was open for 8% -> 7% of each run, Pallas kernels for 6% -> 6%
where the time goes in v8:
time: 120 us; the launch traced here: 119 us
  starting transfers between devices  66.6 us (55%)
  waiting for transfers between devices  20 us (17%)
  Pallas kernels  19.3 us (16%)
  matrix products  6.31 us (5%)
  other arithmetic  4.03 us (3%)
  local copies, waits for them, and re-layouts  1.69 us (1%)
    ppermute x31, starting transfers between devices, shift(): return lambda a: lax.ppermute(a, axis, [(i, (i + k) % n) for i in range(n)])  36.7 us
    ppermute x31, waiting for transfers between devices, shift(): return lambda a: lax.ppermute(a, axis, [(i, (i + k) % n) for i in range(n)])  19.1 us
    all_to_all x1, starting transfers between devices, shards(): mine = lax.all_to_all(mine, 'z', 0, 0, tiled=True)  8.71 us
    all_to_all x1, starting transfers between devices, shards(): lax.all_to_all(outgoing.reshape(owners * n_y, cap, piece, 2 * DH), dp + (...  7.9 us
    pallas_call x1, Pallas kernels, shards(): call(functools.partial(tail_body, stored, n_z), (jax.ShapeDtypeStruct((pi...  7.59 us
    all_to_all x1, starting transfers between devices, shards(): lax.all_to_all(enc_part.reshape(n_z, -1, enc_width), 'z', 0, 0, tiled=True)  7.2 us
    ppermute x2, starting transfers between devices, along_y(): return lax.ppermute(a, ('c', 'y'), ways)  6.11 us
    pallas_call x1, Pallas kernels, shards(): call(functools.partial(attention_body, (blocks, block_len, n_x, n_y, cap,...  5.4 us
  transfers between devices with their start and end apart: 36, of which 14 were waited for; matrix products, arithmetic and copies ran while one was open for 7% of the time, Pallas kernels for 6%

profile of v8, /device:TPU:32, one launch (start us, length us, event | category | flops | bytes accessed | tf_op | source)
XLA Modules:
  0.0 118.7 jit_solution(5336516938329267001)
XLA Ops:
  0.6 4.5 %shard_map.103 = (bf16[1040,256]{1,0:T(8,128)(2,1)}, bf16[896,256]{1,0:T(8,128)(2,1)}, bf16[8,4,128,128]{3,2,1,0:T(8,128)(2,1)}) custom-call(s32[2,8]{1,0:T(2,128)} %bitcast.22, bf16[1024,896]{1,0:T(8,128)(2,1)} %bitcast.19, bf16[896,128]{1,0:T(8,128)(2,1)} %wk_ref.1, bf16[896,128]{1,0:T(8,128)(2,1)} %wv_ref.1, bf16[128,4096]{1,0:T(8,128)(2,1)} %wo_ref.1, ...), custom_call_target="tpu_custom_call" | custom-call | flops 470000000 | bytes 5242880 | tf_op jit(solution)/shard_map/pallas_call | solution.py:293
  5.1 8.7 %all-to-all-start.1 = ((bf16[8,4,128,128]{3,2,1,0:T(8,128)(2,1)}), bf16[8,4,128,128]{3,2,1,0:T(8,128)(2,1)}, u32[]{:S(2)}, u32[]{:S(2)}) async-start(bf16[8,4,128,128]{3,2,1,0:T(8,128)(2,1)} %get-tuple-element.53), calls=%async_computation.1 | async-start | bytes 2097152 | tf_op jit(solution)/shard_map/all_to_all | solution.py:304
  13.8 1.5 %collective-permute-start.1 = (bf16[1040,256]{1,0:T(8,128)(2,1)}, bf16[1040,256]{1,0:T(8,128)(2,1)}, u32[]{:S(2)}, u32[]{:S(2)}) collective-permute-start(bf16[1040,256]{1,0:T(8,128)(2,1)} %get-tuple-element.34.refs_0_), channel_id=1, source_target_pairs={{0,64},{64,128},{128,192},{192,0},{1,65},{65,129},{129,193},{193,1... | collective-permute-start | bytes 1597448 | tf_op jit(solution)/shard_map/ppermute | solution.py:285
  15.3 1.7 %collective-permute-start = (bf16[1040,256]{1,0:T(8,128)(2,1)}, bf16[1040,256]{1,0:T(8,128)(2,1)}, u32[]{:S(2)}, u32[]{:S(2)}) collective-permute-start(bf16[1040,256]{1,0:T(8,128)(2,1)} %get-tuple-element.34.refs_0_), channel_id=1, source_target_pairs={{0,192},{64,0},{128,64},{192,128},{1,193},{65,1},{129,65},{193,129... | collective-permute-start | bytes 1597448 | tf_op jit(solution)/shard_map/ppermute | solution.py:285
  17.1 4.4 %convolution_convert_fusion.1.q_ref = bf16[512,128]{1,0:T(8,128)(2,1)} fusion(bf16[512,4096]{1,0:T(8,128)(2,1)} %param.8, bf16[4096,128]{1,0:T(8,128)(2,1)} %wq_ref.1), kind=kOutput, calls=%fused_computation.1 | convolution fusion | flops 536936448 | bytes 5373952 | tf_op jit(solution)/shard_map/dot_general | solution.py:311
  21.5 3.0 %collective-permute-start.2 = (bf16[896,256]{1,0:T(8,128)(2,1)}, bf16[896,256]{1,0:T(8,128)(2,1)}, u32[]{:S(2)}, u32[]{:S(2)}) collective-permute-start(bf16[896,256]{1,0:T(8,128)(2,1)} %get-tuple-element.47.refs_0_), channel_id=1, source_target_pairs={{0,24},{8,0},{16,8},{24,16},{32,40},{40,48},{48,56},{56,32},{1,25}... | collective-permute-start | bytes 1376264 | tf_op jit(solution)/shard_map/ppermute | solution.py:309
  24.5 1.9 %convolution_convert_fusion.g_ref = bf16[512,128]{1,0:T(8,128)(2,1)} fusion(bf16[512,4096]{1,0:T(8,128)(2,1)S(1)} %copy-done.20, bf16[128,4096]{1,0:T(8,128)(2,1)S(1)} %copy-done), kind=kOutput, calls=%fused_computation | convolution fusion | flops 536936448 | bytes 5373952 | tf_op jit(solution)/shard_map/dot_general | solution.py:312
  26.4 2.2 %collective-permute-done.1.before_ref.refs_4_ = bf16[1040,256]{1,0:T(8,128)(2,1)} collective-permute-done((bf16[1040,256]{1,0:T(8,128)(2,1)}, bf16[1040,256]{1,0:T(8,128)(2,1)}, u32[]{:S(2)}, u32[]{:S(2)}) %collective-permute-start.1) | collective-permute-done | bytes 532512 | tf_op jit(solution)/shard_map/ppermute | solution.py:285
  28.6 1.8 %shard_map.104 = (bf16[528,256]{1,0:T(8,128)(2,1)}, bf16[512,256]{1,0:T(8,128)(2,1)}) custom-call(bf16[1040,256]{1,0:T(8,128)(2,1)} %collective-permute-done.after_ref.refs_1_, bf16[1040,256]{1,0:T(8,128)(2,1)} %collective-permute-done.1.before_ref.refs_4_), custom_call_target="tpu_custom_call" | custom-call | tf_op jit(solution)/shard_map/pallas_call | solution.py:318
  30.5 3.0 %collective-permute-start.5 = (bf16[528,256]{1,0:T(8,128)(2,1)}, bf16[528,256]{1,0:T(8,128)(2,1)S(1)}, u32[]{:S(2)}, u32[]{:S(2)}) collective-permute-start(bf16[528,256]{1,0:T(8,128)(2,1)} %get-tuple-element.43), channel_id=1, source_target_pairs={{0,192},{64,0},{128,64},{192,128},{1,193},{65,1},{129,65},{193,129... | collective-permute-start | bytes 811016 | tf_op jit(solution)/shard_map/ppermute | solution.py:285
  33.5 3.1 %collective-permute-start.3 = (bf16[896,256]{1,0:T(8,128)(2,1)}, bf16[896,256]{1,0:T(8,128)(2,1)}, u32[]{:S(2)}, u32[]{:S(2)}) collective-permute-start(bf16[896,256]{1,0:T(8,128)(2,1)} %collective-permute-done.2.refs_1_), channel_id=1, source_target_pairs={{0,24},{8,0},{16,8},{24,16},{32,40},{40,48},{48,56},{56,32},{1,25}... | collective-permute-start | bytes 1376264 | tf_op jit(solution)/shard_map/ppermute | solution.py:309
  36.6 4.7 %collective-permute-done.6.refs_3_ = bf16[512,256]{1,0:T(8,128)(2,1)S(1)} collective-permute-done((bf16[512,256]{1,0:T(8,128)(2,1)}, bf16[512,256]{1,0:T(8,128)(2,1)S(1)}, u32[]{:S(2)}, u32[]{:S(2)}) %collective-permute-start.6) | collective-permute-done | bytes 262176 | tf_op jit(solution)/shard_map/ppermute | solution.py:285
  42.9 1.8 %collective-permute-done.10.refs_8_ = bf16[512,256]{1,0:T(8,128)(2,1)S(1)} collective-permute-done((bf16[512,256]{1,0:T(8,128)(2,1)S(1)}, bf16[512,256]{1,0:T(8,128)(2,1)S(1)}, u32[]{:S(2)}, u32[]{:S(2)}) %collective-permute-start.10) | collective-permute-done | bytes 262176 | tf_op jit(solution)/shard_map/ppermute | solution.py:285
  45.5 5.4 %shard_map.105 = (bf16[512,128]{1,0:T(8,128)(2,1)}, bf16[512,128]{1,0:T(8,128)(2,1)}, bf16[8,4,4,32,256]{4,3,2,1,0:T(8,128)(2,1)}, s32[8,128]{1,0:T(8,128)}) custom-call(s32[2,8]{1,0:T(2,128)} %bitcast.23, bf16[512,128]{1,0:T(8,128)(2,1)} %convolution_convert_fusion.1.q_ref, bf16[512,128]{1,0:T(8,128)(2,1)} %convolution_convert_fusion.g_ref, ...), custom_call_target="tpu_custom_call" | custom-call | tf_op jit(solution)/shard_map/pallas_call | solution.py:331
  50.9 7.9 %all-to-all-start = ((bf16[32,4,32,256]{3,2,1,0:T(8,128)(2,1)}), bf16[32,4,32,256]{3,2,1,0:T(8,128)(2,1)}, u32[]{:S(2)}, u32[]{:S(2)}) async-start(bf16[32,4,32,256]{3,2,1,0:T(8,128)(2,1)} %bitcast.18), calls=%async_computation | async-start | bytes 4194304 | tf_op jit(solution)/shard_map/all_to_all | solution.py:359
  59.5 2.9 %collective-permute-start.19 = (bf16[512,128]{1,0:T(8,128)(2,1)S(1)}, bf16[512,128]{1,0:T(8,128)(2,1)S(1)}, u32[]{:S(2)}, u32[]{:S(2)}) collective-permute-start(bf16[512,128]{1,0:T(8,128)(2,1)S(1)} %copy-done.5), channel_id=1, source_target_pairs={{0,7},{1,0},{2,1},{3,2},{4,3},{5,4},{6,5},{7,6},{8,15},{9,8},{10,9... | collective-permute-start | bytes 393224 | tf_op jit(solution)/shard_map/ppermute | solution.py:285
  63.1 2.3 %collective-permute-done.12.refs_5_ = bf16[512,128]{1,0:T(8,128)(2,1)S(1)} collective-permute-done((bf16[512,128]{1,0:T(8,128)(2,1)S(1)}, bf16[512,128]{1,0:T(8,128)(2,1)S(1)}, u32[]{:S(2)}, u32[]{:S(2)}) %collective-permute-start.12) | collective-permute-done | bytes 131104 | tf_op jit(solution)/shard_map/ppermute | solution.py:285
  66.2 2.0 %collective-permute-done.19.refs_13_ = bf16[512,128]{1,0:T(8,128)(2,1)S(1)} collective-permute-done((bf16[512,128]{1,0:T(8,128)(2,1)S(1)}, bf16[512,128]{1,0:T(8,128)(2,1)S(1)}, u32[]{:S(2)}, u32[]{:S(2)}) %collective-permute-start.19) | collective-permute-done | bytes 131104 | tf_op jit(solution)/shard_map/ppermute | solution.py:285
  68.2 1.7 %collective-permute-start.20 = (bf16[512,128]{1,0:T(8,128)(2,1)S(1)}, bf16[512,128]{1,0:T(8,128)(2,1)S(1)}, u32[]{:S(2)}, u32[]{:S(2)}) collective-permute-start(bf16[512,128]{1,0:T(8,128)(2,1)S(1)} %collective-permute-done.19.refs_13_), channel_id=1, source_target_pairs={{0,7},{1,0},{2,1},{3,2},{4,3},{5,4},{6,5},{7,6},{8,15},{9,8},{10,9... | collective-permute-start | bytes 393224 | tf_op jit(solution)/shard_map/ppermute | solution.py:285
  70.3 1.6 %collective-permute-start.24 = (bf16[512,128]{1,0:T(8,128)(2,1)S(1)}, bf16[512,128]{1,0:T(8,128)(2,1)S(1)}, u32[]{:S(2)}, u32[]{:S(2)}) collective-permute-start(bf16[512,128]{1,0:T(8,128)(2,1)S(1)} %collective-permute-done.23.refs_19_), channel_id=1, source_target_pairs={{0,1},{1,2},{2,3},{3,4},{4,5},{5,6},{6,7},{7,0},{8,9},{9,10},{10,1... | collective-permute-start | bytes 393224 | tf_op jit(solution)/shard_map/ppermute | solution.py:285
  73.2 3.5 %collective-permute-start.21 = (bf16[512,128]{1,0:T(8,128)(2,1)S(1)}, bf16[512,128]{1,0:T(8,128)(2,1)S(1)}, u32[]{:S(2)}, u32[]{:S(2)}) collective-permute-start(bf16[512,128]{1,0:T(8,128)(2,1)S(1)} %collective-permute-done.20.refs_14_), channel_id=1, source_target_pairs={{0,7},{1,0},{2,1},{3,2},{4,3},{5,4},{6,5},{7,6},{8,15},{9,8},{10,9... | collective-permute-start | bytes 393224 | tf_op jit(solution)/shard_map/ppermute | solution.py:285
  79.2 2.0 %collective-permute-start.15 = (bf16[512,128]{1,0:T(8,128)(2,1)S(1)}, bf16[512,128]{1,0:T(8,128)(2,1)S(1)}, u32[]{:S(2)}, u32[]{:S(2)}) collective-permute-start(bf16[512,128]{1,0:T(8,128)(2,1)S(1)} %collective-permute-done.14.refs_7_), channel_id=1, source_target_pairs={{0,7},{1,0},{2,1},{3,2},{4,3},{5,4},{6,5},{7,6},{8,15},{9,8},{10,9... | collective-permute-start | bytes 393224 | tf_op jit(solution)/shard_map/ppermute | solution.py:285
  81.2 3.3 %collective-permute-start.22 = (bf16[512,128]{1,0:T(8,128)(2,1)S(1)}, bf16[512,128]{1,0:T(8,128)(2,1)S(1)}, u32[]{:S(2)}, u32[]{:S(2)}) collective-permute-start(bf16[512,128]{1,0:T(8,128)(2,1)S(1)} %collective-permute-done.21.refs_15_), channel_id=1, source_target_pairs={{0,7},{1,0},{2,1},{3,2},{4,3},{5,4},{6,5},{7,6},{8,15},{9,8},{10,9... | collective-permute-start | bytes 393224 | tf_op jit(solution)/shard_map/ppermute | solution.py:285
  87.9 7.6 %shard_map.106 = (bf16[256,896]{1,0:T(8,128)(2,1)}, f32[512,128]{1,0:T(8,128)}, bf16[512,128]{1,0:T(8,128)(2,1)}, bf16[512,128]{1,0:T(8,128)(2,1)}, bf16[512,128...) custom-call(s32[8,128]{1,0:T(8,128)} %get-tuple-element.45.ids_ref, ...), custom_call_target="tpu_custom_call" | custom-call | flops 1580000000 | bytes 10485760 | tf_op jit(solution)/shard_map/pallas_call | solution.py:364
  95.5 7.2 %all-to-all-start.2 = ((bf16[8,32,896]{2,1,0:T(8,128)(2,1)}), bf16[8,32,896]{2,1,0:T(8,128)(2,1)S(1)}, u32[]{:S(2)}, u32[]{:S(2)}) async-start(bf16[8,32,896]{2,1,0:T(8,128)(2,1)} %bitcast.20), calls=%async_computation.2 | async-start | bytes 917504 | tf_op jit(solution)/shard_map/all_to_all | solution.py:382
  102.7 1.5 %collective-permute-start.27 = (bf16[512,128]{1,0:T(8,128)(2,1)}, bf16[512,128]{1,0:T(8,128)(2,1)S(1)}, u32[]{:S(2)}, u32[]{:S(2)}) collective-permute-start(bf16[512,128]{1,0:T(8,128)(2,1)} %get-tuple-element.55), channel_id=1, source_target_pairs={{0,8},{8,16},{16,24},{24,0},{1,9},{9,17},{17,25},{25,1},{2,10},{10... | collective-permute-start | bytes 393224 | tf_op jit(solution)/shard_map/ppermute | solution.py:285
  104.3 2.7 %collective-permute-start.28 = (bf16[512,128]{1,0:T(8,128)(2,1)}, bf16[512,128]{1,0:T(8,128)(2,1)S(1)}, u32[]{:S(2)}, u32[]{:S(2)}) collective-permute-start(bf16[512,128]{1,0:T(8,128)(2,1)} %get-tuple-element.56), channel_id=1, source_target_pairs={{0,16},{8,24},{16,0},{24,8},{1,17},{9,25},{17,1},{25,9},{2,18},{10... | collective-permute-start | bytes 393224 | tf_op jit(solution)/shard_map/ppermute | solution.py:285
  107.0 1.5 %collective-permute-start.29 = (bf16[512,128]{1,0:T(8,128)(2,1)}, bf16[512,128]{1,0:T(8,128)(2,1)S(1)}, u32[]{:S(2)}, u32[]{:S(2)}) collective-permute-start(bf16[512,128]{1,0:T(8,128)(2,1)} %get-tuple-element.57), channel_id=1, source_target_pairs={{0,24},{8,0},{16,8},{24,16},{1,25},{9,1},{17,9},{25,17},{2,26},{10... | collective-permute-start | bytes 393224 | tf_op jit(solution)/shard_map/ppermute | solution.py:285
  109.9 2.2 %collective-permute-start.32 = (bf16[512,128]{1,0:T(8,128)(2,1)}, bf16[512,128]{1,0:T(8,128)(2,1)S(1)}, u32[]{:S(2)}, u32[]{:S(2)}) collective-permute-start(bf16[512,128]{1,0:T(8,128)(2,1)} %get-tuple-element.63), channel_id=1, source_target_pairs={{0,24},{8,0},{16,8},{24,16},{1,25},{9,1},{17,9},{25,17},{2,26},{10... | collective-permute-start | bytes 393224 | tf_op jit(solution)/shard_map/ppermute | solution.py:285
  112.1 1.5 %collective-permute-done.28 = bf16[512,128]{1,0:T(8,128)(2,1)S(1)} collective-permute-done((bf16[512,128]{1,0:T(8,128)(2,1)}, bf16[512,128]{1,0:T(8,128)(2,1)S(1)}, u32[]{:S(2)}, u32[]{:S(2)}) %collective-permute-start.28) | collective-permute-done | bytes 131104 | tf_op jit(solution)/shard_map/ppermute | solution.py:285
  113.6 1.7 %add_convert_fusion.1 = bf16[512,128]{1,0:T(8,128)(2,1)} fusion(bf16[512,128]{1,0:T(8,128)(2,1)S(1)} %collective-permute-done.29, bf16[512,128]{1,0:T(8,128)(2,1)S(1)} %collective-permute-done.28, f32[512,128]{1,0:T(8,128)} %get-tuple-element.54, bf16[512,128]{1,0:T(8,128)(2,1)S(1)} %collective-permute-done.27), kind=kLoop, calls=%fused_computation.3 | loop fusion | flops 458752 | bytes 786432 | tf_op jit(solution)/shard_map/convert_element_type | solution.py:389
  117.1 1.7 %add_convert_fusion = bf16[512,128]{1,0:T(8,128)(2,1)} fusion(bf16[512,128]{1,0:T(8,128)(2,1)S(1)} %collective-permute-done.32, bf16[512,128]{1,0:T(8,128)(2,1)S(1)} %collective-permute-done.31, f32[512,128]{1,0:T(8,128)} %get-tuple-element.60, bf16[512,128]{1,0:T(8,128)(2,1)S(1)} %collective-permute-done.30), kind=kLoop, calls=%fused_computation.2 | loop fusion | flops 458752 | bytes 786432 | tf_op jit(solution)/shard_map/convert_element_type | solution.py:389
  (91 shorter events, 15.5 us)
Async XLA Ops:
  5.1 45.8 %all-to-all-start.1 = ((bf16[8,4,128,128]{3,2,1,0:T(8,128)(2,1)}), bf16[8,4,128,128]{3,2,1,0:T(8,128)(2,1)}, u32[]{:S(2)}, u32[]{:S(2)}) async-start(bf16[8,4,128,128]{3,2,1,0:T(8,128)(2,1)} %get-tuple-element.53), calls=%async_computation.1 | async-start | bytes 2097152 | tf_op jit(solution)/shard_map/all_to_all | solution.py:304
  13.8 14.8 %collective-permute-start.1 = (bf16[1040,256]{1,0:T(8,128)(2,1)}, bf16[1040,256]{1,0:T(8,128)(2,1)}, u32[]{:S(2)}, u32[]{:S(2)}) collective-permute-start(bf16[1040,256]{1,0:T(8,128)(2,1)} %get-tuple-element.34.refs_0_), channel_id=1, source_target_pairs={{0,64},{64,128},{128,192},{192,0},{1,65},{65,129},{129,193},{193,1... | collective-permute-start | bytes 1597448 | tf_op jit(solution)/shard_map/ppermute | solution.py:285
  15.3 13.3 %collective-permute-start = (bf16[1040,256]{1,0:T(8,128)(2,1)}, bf16[1040,256]{1,0:T(8,128)(2,1)}, u32[]{:S(2)}, u32[]{:S(2)}) collective-permute-start(bf16[1040,256]{1,0:T(8,128)(2,1)} %get-tuple-element.34.refs_0_), channel_id=1, source_target_pairs={{0,192},{64,0},{128,64},{192,128},{1,193},{65,1},{129,65},{193,129... | collective-permute-start | bytes 1597448 | tf_op jit(solution)/shard_map/ppermute | solution.py:285
  21.5 12.1 %collective-permute-start.2 = (bf16[896,256]{1,0:T(8,128)(2,1)}, bf16[896,256]{1,0:T(8,128)(2,1)}, u32[]{:S(2)}, u32[]{:S(2)}) collective-permute-start(bf16[896,256]{1,0:T(8,128)(2,1)} %get-tuple-element.47.refs_0_), channel_id=1, source_target_pairs={{0,24},{8,0},{16,8},{24,16},{32,40},{40,48},{48,56},{56,32},{1,25}... | collective-permute-start | bytes 1376264 | tf_op jit(solution)/shard_map/ppermute | solution.py:309
  30.5 10.8 %collective-permute-start.5 = (bf16[528,256]{1,0:T(8,128)(2,1)}, bf16[528,256]{1,0:T(8,128)(2,1)S(1)}, u32[]{:S(2)}, u32[]{:S(2)}) collective-permute-start(bf16[528,256]{1,0:T(8,128)(2,1)} %get-tuple-element.43), channel_id=1, source_target_pairs={{0,192},{64,0},{128,64},{192,128},{1,193},{65,1},{129,65},{193,129... | collective-permute-start | bytes 811016 | tf_op jit(solution)/shard_map/ppermute | solution.py:285
  33.5 7.8 %collective-permute-start.6 = (bf16[512,256]{1,0:T(8,128)(2,1)}, bf16[512,256]{1,0:T(8,128)(2,1)S(1)}, u32[]{:S(2)}, u32[]{:S(2)}) collective-permute-start(bf16[512,256]{1,0:T(8,128)(2,1)} %get-tuple-element.44), channel_id=1, source_target_pairs={{0,64},{64,128},{128,192},{192,0},{1,65},{65,129},{129,193},{193,1... | collective-permute-start | bytes 786440 | tf_op jit(solution)/shard_map/ppermute | solution.py:285
  33.5 8.3 %collective-permute-start.4 = (bf16[896,256]{1,0:T(8,128)(2,1)}, bf16[896,256]{1,0:T(8,128)(2,1)}, u32[]{:S(2)}, u32[]{:S(2)}) collective-permute-start(bf16[896,256]{1,0:T(8,128)(2,1)} %collective-permute-done.2.refs_1_), channel_id=1, source_target_pairs={{0,32},{32,0},{1,33},{33,1},{2,34},{34,2},{3,35},{35,3},{4,36},{36... | collective-permute-start | bytes 1376264 | tf_op jit(solution)/shard_map/ppermute | solution.py:285
  33.5 9.4 %collective-permute-start.3 = (bf16[896,256]{1,0:T(8,128)(2,1)}, bf16[896,256]{1,0:T(8,128)(2,1)}, u32[]{:S(2)}, u32[]{:S(2)}) collective-permute-start(bf16[896,256]{1,0:T(8,128)(2,1)} %collective-permute-done.2.refs_1_), channel_id=1, source_target_pairs={{0,24},{8,0},{16,8},{24,16},{32,40},{40,48},{48,56},{56,32},{1,25}... | collective-permute-start | bytes 1376264 | tf_op jit(solution)/shard_map/ppermute | solution.py:309
  36.6 6.3 %collective-permute-start.7 = (bf16[1040,256]{1,0:T(8,128)(2,1)}, bf16[1040,256]{1,0:T(8,128)(2,1)}, u32[]{:S(2)}, u32[]{:S(2)}) collective-permute-start(bf16[1040,256]{1,0:T(8,128)(2,1)} %get-tuple-element.34.refs_0_), channel_id=1, source_target_pairs={{0,32},{32,0},{1,33},{33,1},{2,34},{34,2},{3,35},{35,3},{4,36},{36... | collective-permute-start | bytes 1597448 | tf_op jit(solution)/shard_map/ppermute | solution.py:285
  50.9 37.0 %all-to-all-start = ((bf16[32,4,32,256]{3,2,1,0:T(8,128)(2,1)}), bf16[32,4,32,256]{3,2,1,0:T(8,128)(2,1)}, u32[]{:S(2)}, u32[]{:S(2)}) async-start(bf16[32,4,32,256]{3,2,1,0:T(8,128)(2,1)} %bitcast.18), calls=%async_computation | async-start | bytes 4194304 | tf_op jit(solution)/shard_map/all_to_all | solution.py:359
  58.8 29.1 %collective-permute-start.26 = (bf16[8,4,128,128]{3,2,1,0:T(8,128)(2,1)}, bf16[8,4,128,128]{3,2,1,0:T(8,128)(2,1)}, u32[]{:S(2)}, u32[]{:S(2)}) collective-permute-start(bf16[8,4,128,128]{3,2,1,0:T(8,128)(2,1)} %all-to-all-done.1.refs_20_), channel_id=1, source_target_pairs={{0,32},{32,0},{1,33},{33,1},{2,34},{34,2},{3,35},{35,3},{4,36},{36... | collective-permute-start | bytes 3145736 | tf_op jit(solution)/shard_map/ppermute | solution.py:285
  59.1 6.3 %collective-permute-start.12 = (bf16[512,128]{1,0:T(8,128)(2,1)S(1)}, bf16[512,128]{1,0:T(8,128)(2,1)S(1)}, u32[]{:S(2)}, u32[]{:S(2)}) collective-permute-start(bf16[512,128]{1,0:T(8,128)(2,1)S(1)} %copy-done.4), channel_id=1, source_target_pairs={{0,7},{1,0},{2,1},{3,2},{4,3},{5,4},{6,5},{7,6},{8,15},{9,8},{10,9... | collective-permute-start | bytes 393224 | tf_op jit(solution)/shard_map/ppermute | solution.py:285
  59.5 8.7 %collective-permute-start.19 = (bf16[512,128]{1,0:T(8,128)(2,1)S(1)}, bf16[512,128]{1,0:T(8,128)(2,1)S(1)}, u32[]{:S(2)}, u32[]{:S(2)}) collective-permute-start(bf16[512,128]{1,0:T(8,128)(2,1)S(1)} %copy-done.5), channel_id=1, source_target_pairs={{0,7},{1,0},{2,1},{3,2},{4,3},{5,4},{6,5},{7,6},{8,15},{9,8},{10,9... | collective-permute-start | bytes 393224 | tf_op jit(solution)/shard_map/ppermute | solution.py:285
  62.3 7.5 %collective-permute-start.16 = (bf16[512,128]{1,0:T(8,128)(2,1)S(1)}, bf16[512,128]{1,0:T(8,128)(2,1)S(1)}, u32[]{:S(2)}, u32[]{:S(2)}) collective-permute-start(bf16[512,128]{1,0:T(8,128)(2,1)S(1)} %copy-done.4), channel_id=1, source_target_pairs={{0,1},{1,2},{2,3},{3,4},{4,5},{5,6},{6,7},{7,0},{8,9},{9,10},{10,1... | collective-permute-start | bytes 393224 | tf_op jit(solution)/shard_map/ppermute | solution.py:285
  62.3 8.0 %collective-permute-start.23 = (bf16[512,128]{1,0:T(8,128)(2,1)S(1)}, bf16[512,128]{1,0:T(8,128)(2,1)S(1)}, u32[]{:S(2)}, u32[]{:S(2)}) collective-permute-start(bf16[512,128]{1,0:T(8,128)(2,1)S(1)} %copy-done.5), channel_id=1, source_target_pairs={{0,1},{1,2},{2,3},{3,4},{4,5},{5,6},{6,7},{7,0},{8,9},{9,10},{10,1... | collective-permute-start | bytes 393224 | tf_op jit(solution)/shard_map/ppermute | solution.py:285
  65.4 6.5 %collective-permute-start.13 = (bf16[512,128]{1,0:T(8,128)(2,1)S(1)}, bf16[512,128]{1,0:T(8,128)(2,1)S(1)}, u32[]{:S(2)}, u32[]{:S(2)}) collective-permute-start(bf16[512,128]{1,0:T(8,128)(2,1)S(1)} %collective-permute-done.12.refs_5_), channel_id=1, source_target_pairs={{0,7},{1,0},{2,1},{3,2},{4,3},{5,4},{6,5},{7,6},{8,15},{9,8},{10,9... | collective-permute-start | bytes 393224 | tf_op jit(solution)/shard_map/ppermute | solution.py:285
  68.2 5.1 %collective-permute-start.20 = (bf16[512,128]{1,0:T(8,128)(2,1)S(1)}, bf16[512,128]{1,0:T(8,128)(2,1)S(1)}, u32[]{:S(2)}, u32[]{:S(2)}) collective-permute-start(bf16[512,128]{1,0:T(8,128)(2,1)S(1)} %collective-permute-done.19.refs_13_), channel_id=1, source_target_pairs={{0,7},{1,0},{2,1},{3,2},{4,3},{5,4},{6,5},{7,6},{8,15},{9,8},{10,9... | collective-permute-start | bytes 393224 | tf_op jit(solution)/shard_map/ppermute | solution.py:285
  69.9 6.8 %collective-permute-start.17 = (bf16[512,128]{1,0:T(8,128)(2,1)S(1)}, bf16[512,128]{1,0:T(8,128)(2,1)S(1)}, u32[]{:S(2)}, u32[]{:S(2)}) collective-permute-start(bf16[512,128]{1,0:T(8,128)(2,1)S(1)} %collective-permute-done.16.refs_11_), channel_id=1, source_target_pairs={{0,1},{1,2},{2,3},{3,4},{4,5},{5,6},{6,7},{7,0},{8,9},{9,10},{10,1... | collective-permute-start | bytes 393224 | tf_op jit(solution)/shard_map/ppermute | solution.py:285
  70.3 7.6 %collective-permute-start.24 = (bf16[512,128]{1,0:T(8,128)(2,1)S(1)}, bf16[512,128]{1,0:T(8,128)(2,1)S(1)}, u32[]{:S(2)}, u32[]{:S(2)}) collective-permute-start(bf16[512,128]{1,0:T(8,128)(2,1)S(1)} %collective-permute-done.23.refs_19_), channel_id=1, source_target_pairs={{0,1},{1,2},{2,3},{3,4},{4,5},{5,6},{6,7},{7,0},{8,9},{9,10},{10,1... | collective-permute-start | bytes 393224 | tf_op jit(solution)/shard_map/ppermute | solution.py:285
  71.9 7.2 %collective-permute-start.14 = (bf16[512,128]{1,0:T(8,128)(2,1)S(1)}, bf16[512,128]{1,0:T(8,128)(2,1)S(1)}, u32[]{:S(2)}, u32[]{:S(2)}) collective-permute-start(bf16[512,128]{1,0:T(8,128)(2,1)S(1)} %collective-permute-done.13.refs_6_), channel_id=1, source_target_pairs={{0,7},{1,0},{2,1},{3,2},{4,3},{5,4},{6,5},{7,6},{8,15},{9,8},{10,9... | collective-permute-start | bytes 393224 | tf_op jit(solution)/shard_map/ppermute | solution.py:285
  73.2 7.9 %collective-permute-start.21 = (bf16[512,128]{1,0:T(8,128)(2,1)S(1)}, bf16[512,128]{1,0:T(8,128)(2,1)S(1)}, u32[]{:S(2)}, u32[]{:S(2)}) collective-permute-start(bf16[512,128]{1,0:T(8,128)(2,1)S(1)} %collective-permute-done.20.refs_14_), channel_id=1, source_target_pairs={{0,7},{1,0},{2,1},{3,2},{4,3},{5,4},{6,5},{7,6},{8,15},{9,8},{10,9... | collective-permute-start | bytes 393224 | tf_op jit(solution)/shard_map/ppermute | solution.py:285
  76.7 7.7 %collective-permute-start.18 = (bf16[512,128]{1,0:T(8,128)(2,1)S(1)}, bf16[512,128]{1,0:T(8,128)(2,1)S(1)}, u32[]{:S(2)}, u32[]{:S(2)}) collective-permute-start(bf16[512,128]{1,0:T(8,128)(2,1)S(1)} %collective-permute-done.17.refs_10_), channel_id=1, source_target_pairs={{0,1},{1,2},{2,3},{3,4},{4,5},{5,6},{6,7},{7,0},{8,9},{9,10},{10,1... | collective-permute-start | bytes 393224 | tf_op jit(solution)/shard_map/ppermute | solution.py:285
  77.9 6.6 %collective-permute-start.25 = (bf16[512,128]{1,0:T(8,128)(2,1)S(1)}, bf16[512,128]{1,0:T(8,128)(2,1)S(1)}, u32[]{:S(2)}, u32[]{:S(2)}) collective-permute-start(bf16[512,128]{1,0:T(8,128)(2,1)S(1)} %collective-permute-done.24.refs_18_), channel_id=1, source_target_pairs={{0,1},{1,2},{2,3},{3,4},{4,5},{5,6},{6,7},{7,0},{8,9},{9,10},{10,1... | collective-permute-start | bytes 393224 | tf_op jit(solution)/shard_map/ppermute | solution.py:285
  79.2 6.7 %collective-permute-start.15 = (bf16[512,128]{1,0:T(8,128)(2,1)S(1)}, bf16[512,128]{1,0:T(8,128)(2,1)S(1)}, u32[]{:S(2)}, u32[]{:S(2)}) collective-permute-start(bf16[512,128]{1,0:T(8,128)(2,1)S(1)} %collective-permute-done.14.refs_7_), channel_id=1, source_target_pairs={{0,7},{1,0},{2,1},{3,2},{4,3},{5,4},{6,5},{7,6},{8,15},{9,8},{10,9... | collective-permute-start | bytes 393224 | tf_op jit(solution)/shard_map/ppermute | solution.py:285
  81.2 6.1 %collective-permute-start.22 = (bf16[512,128]{1,0:T(8,128)(2,1)S(1)}, bf16[512,128]{1,0:T(8,128)(2,1)S(1)}, u32[]{:S(2)}, u32[]{:S(2)}) collective-permute-start(bf16[512,128]{1,0:T(8,128)(2,1)S(1)} %collective-permute-done.21.refs_15_), channel_id=1, source_target_pairs={{0,7},{1,0},{2,1},{3,2},{4,3},{5,4},{6,5},{7,6},{8,15},{9,8},{10,9... | collective-permute-start | bytes 393224 | tf_op jit(solution)/shard_map/ppermute | solution.py:285
  95.5 20.3 %all-to-all-start.2 = ((bf16[8,32,896]{2,1,0:T(8,128)(2,1)}), bf16[8,32,896]{2,1,0:T(8,128)(2,1)S(1)}, u32[]{:S(2)}, u32[]{:S(2)}) async-start(bf16[8,32,896]{2,1,0:T(8,128)(2,1)} %bitcast.20), calls=%async_computation.2 | async-start | bytes 917504 | tf_op jit(solution)/shard_map/all_to_all | solution.py:382
  102.7 7.2 %collective-permute-start.27 = (bf16[512,128]{1,0:T(8,128)(2,1)}, bf16[512,128]{1,0:T(8,128)(2,1)S(1)}, u32[]{:S(2)}, u32[]{:S(2)}) collective-permute-start(bf16[512,128]{1,0:T(8,128)(2,1)} %get-tuple-element.55), channel_id=1, source_target_pairs={{0,8},{8,16},{16,24},{24,0},{1,9},{9,17},{17,25},{25,1},{2,10},{10... | collective-permute-start | bytes 393224 | tf_op jit(solution)/shard_map/ppermute | solution.py:285
  104.3 9.3 %collective-permute-start.28 = (bf16[512,128]{1,0:T(8,128)(2,1)}, bf16[512,128]{1,0:T(8,128)(2,1)S(1)}, u32[]{:S(2)}, u32[]{:S(2)}) collective-permute-start(bf16[512,128]{1,0:T(8,128)(2,1)} %get-tuple-element.56), channel_id=1, source_target_pairs={{0,16},{8,24},{16,0},{24,8},{1,17},{9,25},{17,1},{25,9},{2,18},{10... | collective-permute-start | bytes 393224 | tf_op jit(solution)/shard_map/ppermute | solution.py:285
  107.0 6.7 %collective-permute-start.29 = (bf16[512,128]{1,0:T(8,128)(2,1)}, bf16[512,128]{1,0:T(8,128)(2,1)S(1)}, u32[]{:S(2)}, u32[]{:S(2)}) collective-permute-start(bf16[512,128]{1,0:T(8,128)(2,1)} %get-tuple-element.57), channel_id=1, source_target_pairs={{0,24},{8,0},{16,8},{24,16},{1,25},{9,1},{17,9},{25,17},{2,26},{10... | collective-permute-start | bytes 393224 | tf_op jit(solution)/shard_map/ppermute | solution.py:285
  108.4 8.1 %collective-permute-start.30 = (bf16[512,128]{1,0:T(8,128)(2,1)}, bf16[512,128]{1,0:T(8,128)(2,1)S(1)}, u32[]{:S(2)}, u32[]{:S(2)}) collective-permute-start(bf16[512,128]{1,0:T(8,128)(2,1)} %get-tuple-element.61), channel_id=1, source_target_pairs={{0,8},{8,16},{16,24},{24,0},{1,9},{9,17},{17,25},{25,1},{2,10},{10... | collective-permute-start | bytes 393224 | tf_op jit(solution)/shard_map/ppermute | solution.py:285
  109.0 7.5 %collective-permute-start.31 = (bf16[512,128]{1,0:T(8,128)(2,1)}, bf16[512,128]{1,0:T(8,128)(2,1)S(1)}, u32[]{:S(2)}, u32[]{:S(2)}) collective-permute-start(bf16[512,128]{1,0:T(8,128)(2,1)} %get-tuple-element.62), channel_id=1, source_target_pairs={{0,16},{8,24},{16,0},{24,8},{1,17},{9,25},{17,1},{25,9},{2,18},{10... | collective-permute-start | bytes 393224 | tf_op jit(solution)/shard_map/ppermute | solution.py:285
  109.9 7.2 %collective-permute-start.32 = (bf16[512,128]{1,0:T(8,128)(2,1)}, bf16[512,128]{1,0:T(8,128)(2,1)S(1)}, u32[]{:S(2)}, u32[]{:S(2)}) collective-permute-start(bf16[512,128]{1,0:T(8,128)(2,1)} %get-tuple-element.63), channel_id=1, source_target_pairs={{0,24},{8,0},{16,8},{24,16},{1,25},{9,1},{17,9},{25,17},{2,26},{10... | collective-permute-start | bytes 393224 | tf_op jit(solution)/shard_map/ppermute | solution.py:285
  (25 other events, 122.4 us)

commit v9 on v8

--- a/solution.py
+++ b/solution.py
@@ -389,9 +389,8 @@
         return total.astype(BF)
 
     attended = summed(sums[:n_y])
-    own, enc_rows_sum = tie((sums[n_y], enc_rows_sum))
     grad_encoded = enc_rows_sum.reshape(seg // (n_y * n_z), stored, enc_width).transpose(1, 0, 2).reshape(stored, -1)
-    return attended, summed([own, *sums[n_y + 1 :]]), grad_encoded
+    return attended, summed(sums[n_y:]), grad_encoded
 
 
 def solution(mesh):

time: 120 us -> 121 us (level)
    ppermute x31, waiting for transfers between devices: 19.1 us -> 20.3 us  [shift(): return lambda a: lax.ppermute(a, axis, [(i, (i + k) % n) for i in range(n)])]
  transfers between devices with their start and end apart: 36 -> 36, of which waited for: 14 -> 15; matrix products, arithmetic and copies ran while one was open for 7% -> 8% of each run, Pallas kernels for 6% -> 6%
where the time goes in v9:
time: 121 us; the launch traced here: 120 us
  starting transfers between devices  66.6 us (55%)
  waiting for transfers between devices  20.7 us (17%)
  Pallas kernels  19.4 us (16%)
  matrix products  6.31 us (5%)
  other arithmetic  4.04 us (3%)
  local copies, waits for them, and re-layouts  1.69 us (1%)
    ppermute x31, starting transfers between devices, shift(): return lambda a: lax.ppermute(a, axis, [(i, (i + k) % n) for i in range(n)])  36.7 us
    ppermute x31, waiting for transfers between devices, shift(): return lambda a: lax.ppermute(a, axis, [(i, (i + k) % n) for i in range(n)])  20.3 us
    all_to_all x1, starting transfers between devices, shards(): mine = lax.all_to_all(mine, 'z', 0, 0, tiled=True)  8.71 us
    all_to_all x1, starting transfers between devices, shards(): lax.all_to_all(outgoing.reshape(owners * n_y, cap, piece, 2 * DH), dp + (...  7.93 us
    pallas_call x1, Pallas kernels, shards(): call(functools.partial(tail_body, stored, n_z), (jax.ShapeDtypeStruct((pi...  7.7 us
    all_to_all x1, starting transfers between devices, shards(): lax.all_to_all(enc_part.reshape(n_z, -1, enc_width), 'z', 0, 0, tiled=True)  7.2 us
    ppermute x2, starting transfers between devices, along_y(): return lax.ppermute(a, ('c', 'y'), ways)  6.11 us
    pallas_call x1, Pallas kernels, shards(): call(functools.partial(attention_body, (blocks, block_len, n_x, n_y, cap,...  5.38 us
  transfers between devices with their start and end apart: 36, of which 15 were waited for; matrix products, arithmetic and copies ran while one was open for 8% of the time, Pallas kernels for 6%

profile of v9, /device:TPU:32, one launch (start us, length us, event | category | flops | bytes accessed | tf_op | source)
XLA Modules:
  0.0 119.6 jit_solution(15371553089660862760)
XLA Ops:
  0.6 4.5 %shard_map.103 = (bf16[1040,256]{1,0:T(8,128)(2,1)}, bf16[896,256]{1,0:T(8,128)(2,1)}, bf16[8,4,128,128]{3,2,1,0:T(8,128)(2,1)}) custom-call(s32[2,8]{1,0:T(2,128)} %bitcast.22, bf16[1024,896]{1,0:T(8,128)(2,1)} %bitcast.19, bf16[896,128]{1,0:T(8,128)(2,1)} %wk_ref.1, bf16[896,128]{1,0:T(8,128)(2,1)} %wv_ref.1, bf16[128,4096]{1,0:T(8,128)(2,1)} %wo_ref.1, ...), custom_call_target="tpu_custom_call" | custom-call | flops 470000000 | bytes 5242880 | tf_op jit(solution)/shard_map/pallas_call | solution.py:293
  5.1 8.7 %all-to-all-start.1 = ((bf16[8,4,128,128]{3,2,1,0:T(8,128)(2,1)}), bf16[8,4,128,128]{3,2,1,0:T(8,128)(2,1)}, u32[]{:S(2)}, u32[]{:S(2)}) async-start(bf16[8,4,128,128]{3,2,1,0:T(8,128)(2,1)} %get-tuple-element.51), calls=%async_computation.1 | async-start | bytes 2097152 | tf_op jit(solution)/shard_map/all_to_all | solution.py:304
  13.8 1.5 %collective-permute-start.1 = (bf16[1040,256]{1,0:T(8,128)(2,1)}, bf16[1040,256]{1,0:T(8,128)(2,1)}, u32[]{:S(2)}, u32[]{:S(2)}) collective-permute-start(bf16[1040,256]{1,0:T(8,128)(2,1)} %get-tuple-element.32.refs_0_), channel_id=1, source_target_pairs={{0,64},{64,128},{128,192},{192,0},{1,65},{65,129},{129,193},{193,1... | collective-permute-start | bytes 1597448 | tf_op jit(solution)/shard_map/ppermute | solution.py:285
  15.3 1.7 %collective-permute-start = (bf16[1040,256]{1,0:T(8,128)(2,1)}, bf16[1040,256]{1,0:T(8,128)(2,1)}, u32[]{:S(2)}, u32[]{:S(2)}) collective-permute-start(bf16[1040,256]{1,0:T(8,128)(2,1)} %get-tuple-element.32.refs_0_), channel_id=1, source_target_pairs={{0,192},{64,0},{128,64},{192,128},{1,193},{65,1},{129,65},{193,129... | collective-permute-start | bytes 1597448 | tf_op jit(solution)/shard_map/ppermute | solution.py:285
  17.1 4.4 %convolution_convert_fusion.1.q_ref = bf16[512,128]{1,0:T(8,128)(2,1)} fusion(bf16[512,4096]{1,0:T(8,128)(2,1)} %param.8, bf16[4096,128]{1,0:T(8,128)(2,1)} %wq_ref.1), kind=kOutput, calls=%fused_computation.1 | convolution fusion | flops 536936448 | bytes 5373952 | tf_op jit(solution)/shard_map/dot_general | solution.py:311
  21.5 3.0 %collective-permute-start.2 = (bf16[896,256]{1,0:T(8,128)(2,1)}, bf16[896,256]{1,0:T(8,128)(2,1)}, u32[]{:S(2)}, u32[]{:S(2)}) collective-permute-start(bf16[896,256]{1,0:T(8,128)(2,1)} %get-tuple-element.45.refs_0_), channel_id=1, source_target_pairs={{0,24},{8,0},{16,8},{24,16},{32,40},{40,48},{48,56},{56,32},{1,25}... | collective-permute-start | bytes 1376264 | tf_op jit(solution)/shard_map/ppermute | solution.py:309
  24.5 1.9 %convolution_convert_fusion.g_ref = bf16[512,128]{1,0:T(8,128)(2,1)} fusion(bf16[512,4096]{1,0:T(8,128)(2,1)S(1)} %copy-done.20, bf16[128,4096]{1,0:T(8,128)(2,1)S(1)} %copy-done), kind=kOutput, calls=%fused_computation | convolution fusion | flops 536936448 | bytes 5373952 | tf_op jit(solution)/shard_map/dot_general | solution.py:312
  26.4 2.2 %collective-permute-done.1.before_ref.refs_4_ = bf16[1040,256]{1,0:T(8,128)(2,1)} collective-permute-done((bf16[1040,256]{1,0:T(8,128)(2,1)}, bf16[1040,256]{1,0:T(8,128)(2,1)}, u32[]{:S(2)}, u32[]{:S(2)}) %collective-permute-start.1) | collective-permute-done | bytes 532512 | tf_op jit(solution)/shard_map/ppermute | solution.py:285
  28.6 1.8 %shard_map.104 = (bf16[528,256]{1,0:T(8,128)(2,1)}, bf16[512,256]{1,0:T(8,128)(2,1)}) custom-call(bf16[1040,256]{1,0:T(8,128)(2,1)} %collective-permute-done.after_ref.refs_1_, bf16[1040,256]{1,0:T(8,128)(2,1)} %collective-permute-done.1.before_ref.refs_4_), custom_call_target="tpu_custom_call" | custom-call | tf_op jit(solution)/shard_map/pallas_call | solution.py:318
  30.5 3.0 %collective-permute-start.5 = (bf16[528,256]{1,0:T(8,128)(2,1)}, bf16[528,256]{1,0:T(8,128)(2,1)S(1)}, u32[]{:S(2)}, u32[]{:S(2)}) collective-permute-start(bf16[528,256]{1,0:T(8,128)(2,1)} %get-tuple-element.41), channel_id=1, source_target_pairs={{0,192},{64,0},{128,64},{192,128},{1,193},{65,1},{129,65},{193,129... | collective-permute-start | bytes 811016 | tf_op jit(solution)/shard_map/ppermute | solution.py:285
  33.5 3.1 %collective-permute-start.3 = (bf16[896,256]{1,0:T(8,128)(2,1)}, bf16[896,256]{1,0:T(8,128)(2,1)}, u32[]{:S(2)}, u32[]{:S(2)}) collective-permute-start(bf16[896,256]{1,0:T(8,128)(2,1)} %collective-permute-done.2.refs_1_), channel_id=1, source_target_pairs={{0,24},{8,0},{16,8},{24,16},{32,40},{40,48},{48,56},{56,32},{1,25}... | collective-permute-start | bytes 1376264 | tf_op jit(solution)/shard_map/ppermute | solution.py:309
  36.6 4.7 %collective-permute-done.6.refs_3_ = bf16[512,256]{1,0:T(8,128)(2,1)S(1)} collective-permute-done((bf16[512,256]{1,0:T(8,128)(2,1)}, bf16[512,256]{1,0:T(8,128)(2,1)S(1)}, u32[]{:S(2)}, u32[]{:S(2)}) %collective-permute-start.6) | collective-permute-done | bytes 262176 | tf_op jit(solution)/shard_map/ppermute | solution.py:285
  42.9 1.8 %collective-permute-done.10.refs_8_ = bf16[512,256]{1,0:T(8,128)(2,1)S(1)} collective-permute-done((bf16[512,256]{1,0:T(8,128)(2,1)S(1)}, bf16[512,256]{1,0:T(8,128)(2,1)S(1)}, u32[]{:S(2)}, u32[]{:S(2)}) %collective-permute-start.10) | collective-permute-done | bytes 262176 | tf_op jit(solution)/shard_map/ppermute | solution.py:285
  45.5 5.4 %shard_map.105 = (bf16[512,128]{1,0:T(8,128)(2,1)}, bf16[512,128]{1,0:T(8,128)(2,1)}, bf16[8,4,4,32,256]{4,3,2,1,0:T(8,128)(2,1)}, s32[8,128]{1,0:T(8,128)}) custom-call(s32[2,8]{1,0:T(2,128)} %bitcast.23, bf16[512,128]{1,0:T(8,128)(2,1)} %convolution_convert_fusion.1.q_ref, bf16[512,128]{1,0:T(8,128)(2,1)} %convolution_convert_fusion.g_ref, ...), custom_call_target="tpu_custom_call" | custom-call | tf_op jit(solution)/shard_map/pallas_call | solution.py:331
  50.9 7.9 %all-to-all-start = ((bf16[32,4,32,256]{3,2,1,0:T(8,128)(2,1)}), bf16[32,4,32,256]{3,2,1,0:T(8,128)(2,1)}, u32[]{:S(2)}, u32[]{:S(2)}) async-start(bf16[32,4,32,256]{3,2,1,0:T(8,128)(2,1)} %bitcast.18), calls=%async_computation | async-start | bytes 4194304 | tf_op jit(solution)/shard_map/all_to_all | solution.py:359
  59.5 2.9 %collective-permute-start.19 = (bf16[512,128]{1,0:T(8,128)(2,1)S(1)}, bf16[512,128]{1,0:T(8,128)(2,1)S(1)}, u32[]{:S(2)}, u32[]{:S(2)}) collective-permute-start(bf16[512,128]{1,0:T(8,128)(2,1)S(1)} %copy-done.5), channel_id=1, source_target_pairs={{0,7},{1,0},{2,1},{3,2},{4,3},{5,4},{6,5},{7,6},{8,15},{9,8},{10,9... | collective-permute-start | bytes 393224 | tf_op jit(solution)/shard_map/ppermute | solution.py:285
  63.2 2.3 %collective-permute-done.12.refs_5_ = bf16[512,128]{1,0:T(8,128)(2,1)S(1)} collective-permute-done((bf16[512,128]{1,0:T(8,128)(2,1)S(1)}, bf16[512,128]{1,0:T(8,128)(2,1)S(1)}, u32[]{:S(2)}, u32[]{:S(2)}) %collective-permute-start.12) | collective-permute-done | bytes 131104 | tf_op jit(solution)/shard_map/ppermute | solution.py:285
  66.2 2.0 %collective-permute-done.19.refs_13_ = bf16[512,128]{1,0:T(8,128)(2,1)S(1)} collective-permute-done((bf16[512,128]{1,0:T(8,128)(2,1)S(1)}, bf16[512,128]{1,0:T(8,128)(2,1)S(1)}, u32[]{:S(2)}, u32[]{:S(2)}) %collective-permute-start.19) | collective-permute-done | bytes 131104 | tf_op jit(solution)/shard_map/ppermute | solution.py:285
  68.2 1.7 %collective-permute-start.20 = (bf16[512,128]{1,0:T(8,128)(2,1)S(1)}, bf16[512,128]{1,0:T(8,128)(2,1)S(1)}, u32[]{:S(2)}, u32[]{:S(2)}) collective-permute-start(bf16[512,128]{1,0:T(8,128)(2,1)S(1)} %collective-permute-done.19.refs_13_), channel_id=1, source_target_pairs={{0,7},{1,0},{2,1},{3,2},{4,3},{5,4},{6,5},{7,6},{8,15},{9,8},{10,9... | collective-permute-start | bytes 393224 | tf_op jit(solution)/shard_map/ppermute | solution.py:285
  70.3 1.6 %collective-permute-start.24 = (bf16[512,128]{1,0:T(8,128)(2,1)S(1)}, bf16[512,128]{1,0:T(8,128)(2,1)S(1)}, u32[]{:S(2)}, u32[]{:S(2)}) collective-permute-start(bf16[512,128]{1,0:T(8,128)(2,1)S(1)} %collective-permute-done.23.refs_19_), channel_id=1, source_target_pairs={{0,1},{1,2},{2,3},{3,4},{4,5},{5,6},{6,7},{7,0},{8,9},{9,10},{10,1... | collective-permute-start | bytes 393224 | tf_op jit(solution)/shard_map/ppermute | solution.py:285
  73.2 3.5 %collective-permute-start.21 = (bf16[512,128]{1,0:T(8,128)(2,1)S(1)}, bf16[512,128]{1,0:T(8,128)(2,1)S(1)}, u32[]{:S(2)}, u32[]{:S(2)}) collective-permute-start(bf16[512,128]{1,0:T(8,128)(2,1)S(1)} %collective-permute-done.20.refs_14_), channel_id=1, source_target_pairs={{0,7},{1,0},{2,1},{3,2},{4,3},{5,4},{6,5},{7,6},{8,15},{9,8},{10,9... | collective-permute-start | bytes 393224 | tf_op jit(solution)/shard_map/ppermute | solution.py:285
  79.2 2.0 %collective-permute-start.15 = (bf16[512,128]{1,0:T(8,128)(2,1)S(1)}, bf16[512,128]{1,0:T(8,128)(2,1)S(1)}, u32[]{:S(2)}, u32[]{:S(2)}) collective-permute-start(bf16[512,128]{1,0:T(8,128)(2,1)S(1)} %collective-permute-done.14.refs_7_), channel_id=1, source_target_pairs={{0,7},{1,0},{2,1},{3,2},{4,3},{5,4},{6,5},{7,6},{8,15},{9,8},{10,9... | collective-permute-start | bytes 393224 | tf_op jit(solution)/shard_map/ppermute | solution.py:285
  81.2 3.3 %collective-permute-start.22 = (bf16[512,128]{1,0:T(8,128)(2,1)S(1)}, bf16[512,128]{1,0:T(8,128)(2,1)S(1)}, u32[]{:S(2)}, u32[]{:S(2)}) collective-permute-start(bf16[512,128]{1,0:T(8,128)(2,1)S(1)} %collective-permute-done.21.refs_15_), channel_id=1, source_target_pairs={{0,7},{1,0},{2,1},{3,2},{4,3},{5,4},{6,5},{7,6},{8,15},{9,8},{10,9... | collective-permute-start | bytes 393224 | tf_op jit(solution)/shard_map/ppermute | solution.py:285
  85.9 1.4 %collective-permute-done.22.refs_16_ = bf16[512,128]{1,0:T(8,128)(2,1)S(1)} collective-permute-done((bf16[512,128]{1,0:T(8,128)(2,1)S(1)}, bf16[512,128]{1,0:T(8,128)(2,1)S(1)}, u32[]{:S(2)}, u32[]{:S(2)}) %collective-permute-start.22) | collective-permute-done | bytes 131104 | tf_op jit(solution)/shard_map/ppermute | solution.py:285
  87.9 7.7 %shard_map.106 = (bf16[256,896]{1,0:T(8,128)(2,1)}, f32[512,128]{1,0:T(8,128)}, bf16[512,128]{1,0:T(8,128)(2,1)}, bf16[512,128]{1,0:T(8,128)(2,1)}, bf16[512,128...) custom-call(s32[8,128]{1,0:T(8,128)} %get-tuple-element.43.ids_ref, ...), custom_call_target="tpu_custom_call" | custom-call | flops 1580000000 | bytes 10485760 | tf_op jit(solution)/shard_map/pallas_call | solution.py:364
  95.7 7.2 %all-to-all-start.2 = ((bf16[8,32,896]{2,1,0:T(8,128)(2,1)}), bf16[8,32,896]{2,1,0:T(8,128)(2,1)S(1)}, u32[]{:S(2)}, u32[]{:S(2)}) async-start(bf16[8,32,896]{2,1,0:T(8,128)(2,1)} %bitcast.20), calls=%async_computation.2 | async-start | bytes 917504 | tf_op jit(solution)/shard_map/all_to_all | solution.py:382
  102.9 1.5 %collective-permute-start.27 = (bf16[512,128]{1,0:T(8,128)(2,1)}, bf16[512,128]{1,0:T(8,128)(2,1)S(1)}, u32[]{:S(2)}, u32[]{:S(2)}) collective-permute-start(bf16[512,128]{1,0:T(8,128)(2,1)} %get-tuple-element.53), channel_id=1, source_target_pairs={{0,8},{8,16},{16,24},{24,0},{1,9},{9,17},{17,25},{25,1},{2,10},{10... | collective-permute-start | bytes 393224 | tf_op jit(solution)/shard_map/ppermute | solution.py:285
  104.4 2.7 %collective-permute-start.28 = (bf16[512,128]{1,0:T(8,128)(2,1)}, bf16[512,128]{1,0:T(8,128)(2,1)S(1)}, u32[]{:S(2)}, u32[]{:S(2)}) collective-permute-start(bf16[512,128]{1,0:T(8,128)(2,1)} %get-tuple-element.54), channel_id=1, source_target_pairs={{0,16},{8,24},{16,0},{24,8},{1,17},{9,25},{17,1},{25,9},{2,18},{10... | collective-permute-start | bytes 393224 | tf_op jit(solution)/shard_map/ppermute | solution.py:285
  107.1 1.5 %collective-permute-start.29 = (bf16[512,128]{1,0:T(8,128)(2,1)}, bf16[512,128]{1,0:T(8,128)(2,1)S(1)}, u32[]{:S(2)}, u32[]{:S(2)}) collective-permute-start(bf16[512,128]{1,0:T(8,128)(2,1)} %get-tuple-element.55), channel_id=1, source_target_pairs={{0,24},{8,0},{16,8},{24,16},{1,25},{9,1},{17,9},{25,17},{2,26},{10... | collective-permute-start | bytes 393224 | tf_op jit(solution)/shard_map/ppermute | solution.py:285
  110.0 2.3 %collective-permute-start.32 = (bf16[512,128]{1,0:T(8,128)(2,1)}, bf16[512,128]{1,0:T(8,128)(2,1)S(1)}, u32[]{:S(2)}, u32[]{:S(2)}) collective-permute-start(bf16[512,128]{1,0:T(8,128)(2,1)} %get-tuple-element.59), channel_id=1, source_target_pairs={{0,24},{8,0},{16,8},{24,16},{1,25},{9,1},{17,9},{25,17},{2,26},{10... | collective-permute-start | bytes 393224 | tf_op jit(solution)/shard_map/ppermute | solution.py:285
  113.7 1.7 %add_convert_fusion.1 = bf16[512,128]{1,0:T(8,128)(2,1)} fusion(bf16[512,128]{1,0:T(8,128)(2,1)S(1)} %collective-permute-done.29, bf16[512,128]{1,0:T(8,128)(2,1)S(1)} %collective-permute-done.28, f32[512,128]{1,0:T(8,128)} %get-tuple-element.52, bf16[512,128]{1,0:T(8,128)(2,1)S(1)} %collective-permute-done.27), kind=kLoop, calls=%fused_computation.3 | loop fusion | flops 458752 | bytes 786432 | tf_op jit(solution)/shard_map/convert_element_type | solution.py:389
  117.2 1.7 %add_convert_fusion = bf16[512,128]{1,0:T(8,128)(2,1)} fusion(bf16[512,128]{1,0:T(8,128)(2,1)S(1)} %collective-permute-done.32, bf16[512,128]{1,0:T(8,128)(2,1)S(1)} %collective-permute-done.31, f32[512,128]{1,0:T(8,128)} %get-tuple-element.56, bf16[512,128]{1,0:T(8,128)(2,1)S(1)} %collective-permute-done.30), kind=kLoop, calls=%fused_computation.2 | loop fusion | flops 458752 | bytes 786432 | tf_op jit(solution)/shard_map/convert_element_type | solution.py:389
  (91 shorter events, 16.3 us)
Async XLA Ops:
  5.1 45.8 %all-to-all-start.1 = ((bf16[8,4,128,128]{3,2,1,0:T(8,128)(2,1)}), bf16[8,4,128,128]{3,2,1,0:T(8,128)(2,1)}, u32[]{:S(2)}, u32[]{:S(2)}) async-start(bf16[8,4,128,128]{3,2,1,0:T(8,128)(2,1)} %get-tuple-element.51), calls=%async_computation.1 | async-start | bytes 2097152 | tf_op jit(solution)/shard_map/all_to_all | solution.py:304
  13.8 14.8 %collective-permute-start.1 = (bf16[1040,256]{1,0:T(8,128)(2,1)}, bf16[1040,256]{1,0:T(8,128)(2,1)}, u32[]{:S(2)}, u32[]{:S(2)}) collective-permute-start(bf16[1040,256]{1,0:T(8,128)(2,1)} %get-tuple-element.32.refs_0_), channel_id=1, source_target_pairs={{0,64},{64,128},{128,192},{192,0},{1,65},{65,129},{129,193},{193,1... | collective-permute-start | bytes 1597448 | tf_op jit(solution)/shard_map/ppermute | solution.py:285
  15.3 13.3 %collective-permute-start = (bf16[1040,256]{1,0:T(8,128)(2,1)}, bf16[1040,256]{1,0:T(8,128)(2,1)}, u32[]{:S(2)}, u32[]{:S(2)}) collective-permute-start(bf16[1040,256]{1,0:T(8,128)(2,1)} %get-tuple-element.32.refs_0_), channel_id=1, source_target_pairs={{0,192},{64,0},{128,64},{192,128},{1,193},{65,1},{129,65},{193,129... | collective-permute-start | bytes 1597448 | tf_op jit(solution)/shard_map/ppermute | solution.py:285
  21.5 12.1 %collective-permute-start.2 = (bf16[896,256]{1,0:T(8,128)(2,1)}, bf16[896,256]{1,0:T(8,128)(2,1)}, u32[]{:S(2)}, u32[]{:S(2)}) collective-permute-start(bf16[896,256]{1,0:T(8,128)(2,1)} %get-tuple-element.45.refs_0_), channel_id=1, source_target_pairs={{0,24},{8,0},{16,8},{24,16},{32,40},{40,48},{48,56},{56,32},{1,25}... | collective-permute-start | bytes 1376264 | tf_op jit(solution)/shard_map/ppermute | solution.py:309
  30.5 10.8 %collective-permute-start.5 = (bf16[528,256]{1,0:T(8,128)(2,1)}, bf16[528,256]{1,0:T(8,128)(2,1)S(1)}, u32[]{:S(2)}, u32[]{:S(2)}) collective-permute-start(bf16[528,256]{1,0:T(8,128)(2,1)} %get-tuple-element.41), channel_id=1, source_target_pairs={{0,192},{64,0},{128,64},{192,128},{1,193},{65,1},{129,65},{193,129... | collective-permute-start | bytes 811016 | tf_op jit(solution)/shard_map/ppermute | solution.py:285
  33.5 7.8 %collective-permute-start.6 = (bf16[512,256]{1,0:T(8,128)(2,1)}, bf16[512,256]{1,0:T(8,128)(2,1)S(1)}, u32[]{:S(2)}, u32[]{:S(2)}) collective-permute-start(bf16[512,256]{1,0:T(8,128)(2,1)} %get-tuple-element.42), channel_id=1, source_target_pairs={{0,64},{64,128},{128,192},{192,0},{1,65},{65,129},{129,193},{193,1... | collective-permute-start | bytes 786440 | tf_op jit(solution)/shard_map/ppermute | solution.py:285
  33.5 8.3 %collective-permute-start.4 = (bf16[896,256]{1,0:T(8,128)(2,1)}, bf16[896,256]{1,0:T(8,128)(2,1)}, u32[]{:S(2)}, u32[]{:S(2)}) collective-permute-start(bf16[896,256]{1,0:T(8,128)(2,1)} %collective-permute-done.2.refs_1_), channel_id=1, source_target_pairs={{0,32},{32,0},{1,33},{33,1},{2,34},{34,2},{3,35},{35,3},{4,36},{36... | collective-permute-start | bytes 1376264 | tf_op jit(solution)/shard_map/ppermute | solution.py:285
  33.5 9.4 %collective-permute-start.3 = (bf16[896,256]{1,0:T(8,128)(2,1)}, bf16[896,256]{1,0:T(8,128)(2,1)}, u32[]{:S(2)}, u32[]{:S(2)}) collective-permute-start(bf16[896,256]{1,0:T(8,128)(2,1)} %collective-permute-done.2.refs_1_), channel_id=1, source_target_pairs={{0,24},{8,0},{16,8},{24,16},{32,40},{40,48},{48,56},{56,32},{1,25}... | collective-permute-start | bytes 1376264 | tf_op jit(solution)/shard_map/ppermute | solution.py:309
  36.6 6.3 %collective-permute-start.7 = (bf16[1040,256]{1,0:T(8,128)(2,1)}, bf16[1040,256]{1,0:T(8,128)(2,1)}, u32[]{:S(2)}, u32[]{:S(2)}) collective-permute-start(bf16[1040,256]{1,0:T(8,128)(2,1)} %get-tuple-element.32.refs_0_), channel_id=1, source_target_pairs={{0,32},{32,0},{1,33},{33,1},{2,34},{34,2},{3,35},{35,3},{4,36},{36... | collective-permute-start | bytes 1597448 | tf_op jit(solution)/shard_map/ppermute | solution.py:285
  50.9 37.1 %all-to-all-start = ((bf16[32,4,32,256]{3,2,1,0:T(8,128)(2,1)}), bf16[32,4,32,256]{3,2,1,0:T(8,128)(2,1)}, u32[]{:S(2)}, u32[]{:S(2)}) async-start(bf16[32,4,32,256]{3,2,1,0:T(8,128)(2,1)} %bitcast.18), calls=%async_computation | async-start | bytes 4194304 | tf_op jit(solution)/shard_map/all_to_all | solution.py:359
  58.8 29.1 %collective-permute-start.26 = (bf16[8,4,128,128]{3,2,1,0:T(8,128)(2,1)}, bf16[8,4,128,128]{3,2,1,0:T(8,128)(2,1)}, u32[]{:S(2)}, u32[]{:S(2)}) collective-permute-start(bf16[8,4,128,128]{3,2,1,0:T(8,128)(2,1)} %all-to-all-done.1.refs_20_), channel_id=1, source_target_pairs={{0,32},{32,0},{1,33},{33,1},{2,34},{34,2},{3,35},{35,3},{4,36},{36... | collective-permute-start | bytes 3145736 | tf_op jit(solution)/shard_map/ppermute | solution.py:285
  59.1 6.3 %collective-permute-start.12 = (bf16[512,128]{1,0:T(8,128)(2,1)S(1)}, bf16[512,128]{1,0:T(8,128)(2,1)S(1)}, u32[]{:S(2)}, u32[]{:S(2)}) collective-permute-start(bf16[512,128]{1,0:T(8,128)(2,1)S(1)} %copy-done.4), channel_id=1, source_target_pairs={{0,7},{1,0},{2,1},{3,2},{4,3},{5,4},{6,5},{7,6},{8,15},{9,8},{10,9... | collective-permute-start | bytes 393224 | tf_op jit(solution)/shard_map/ppermute | solution.py:285
  59.5 8.7 %collective-permute-start.19 = (bf16[512,128]{1,0:T(8,128)(2,1)S(1)}, bf16[512,128]{1,0:T(8,128)(2,1)S(1)}, u32[]{:S(2)}, u32[]{:S(2)}) collective-permute-start(bf16[512,128]{1,0:T(8,128)(2,1)S(1)} %copy-done.5), channel_id=1, source_target_pairs={{0,7},{1,0},{2,1},{3,2},{4,3},{5,4},{6,5},{7,6},{8,15},{9,8},{10,9... | collective-permute-start | bytes 393224 | tf_op jit(solution)/shard_map/ppermute | solution.py:285
  62.3 7.5 %collective-permute-start.16 = (bf16[512,128]{1,0:T(8,128)(2,1)S(1)}, bf16[512,128]{1,0:T(8,128)(2,1)S(1)}, u32[]{:S(2)}, u32[]{:S(2)}) collective-permute-start(bf16[512,128]{1,0:T(8,128)(2,1)S(1)} %copy-done.4), channel_id=1, source_target_pairs={{0,1},{1,2},{2,3},{3,4},{4,5},{5,6},{6,7},{7,0},{8,9},{9,10},{10,1... | collective-permute-start | bytes 393224 | tf_op jit(solution)/shard_map/ppermute | solution.py:285
  62.3 8.0 %collective-permute-start.23 = (bf16[512,128]{1,0:T(8,128)(2,1)S(1)}, bf16[512,128]{1,0:T(8,128)(2,1)S(1)}, u32[]{:S(2)}, u32[]{:S(2)}) collective-permute-start(bf16[512,128]{1,0:T(8,128)(2,1)S(1)} %copy-done.5), channel_id=1, source_target_pairs={{0,1},{1,2},{2,3},{3,4},{4,5},{5,6},{6,7},{7,0},{8,9},{9,10},{10,1... | collective-permute-start | bytes 393224 | tf_op jit(solution)/shard_map/ppermute | solution.py:285
  65.4 6.5 %collective-permute-start.13 = (bf16[512,128]{1,0:T(8,128)(2,1)S(1)}, bf16[512,128]{1,0:T(8,128)(2,1)S(1)}, u32[]{:S(2)}, u32[]{:S(2)}) collective-permute-start(bf16[512,128]{1,0:T(8,128)(2,1)S(1)} %collective-permute-done.12.refs_5_), channel_id=1, source_target_pairs={{0,7},{1,0},{2,1},{3,2},{4,3},{5,4},{6,5},{7,6},{8,15},{9,8},{10,9... | collective-permute-start | bytes 393224 | tf_op jit(solution)/shard_map/ppermute | solution.py:285
  68.2 5.1 %collective-permute-start.20 = (bf16[512,128]{1,0:T(8,128)(2,1)S(1)}, bf16[512,128]{1,0:T(8,128)(2,1)S(1)}, u32[]{:S(2)}, u32[]{:S(2)}) collective-permute-start(bf16[512,128]{1,0:T(8,128)(2,1)S(1)} %collective-permute-done.19.refs_13_), channel_id=1, source_target_pairs={{0,7},{1,0},{2,1},{3,2},{4,3},{5,4},{6,5},{7,6},{8,15},{9,8},{10,9... | collective-permute-start | bytes 393224 | tf_op jit(solution)/shard_map/ppermute | solution.py:285
  69.9 6.8 %collective-permute-start.17 = (bf16[512,128]{1,0:T(8,128)(2,1)S(1)}, bf16[512,128]{1,0:T(8,128)(2,1)S(1)}, u32[]{:S(2)}, u32[]{:S(2)}) collective-permute-start(bf16[512,128]{1,0:T(8,128)(2,1)S(1)} %collective-permute-done.16.refs_11_), channel_id=1, source_target_pairs={{0,1},{1,2},{2,3},{3,4},{4,5},{5,6},{6,7},{7,0},{8,9},{9,10},{10,1... | collective-permute-start | bytes 393224 | tf_op jit(solution)/shard_map/ppermute | solution.py:285
  70.3 7.6 %collective-permute-start.24 = (bf16[512,128]{1,0:T(8,128)(2,1)S(1)}, bf16[512,128]{1,0:T(8,128)(2,1)S(1)}, u32[]{:S(2)}, u32[]{:S(2)}) collective-permute-start(bf16[512,128]{1,0:T(8,128)(2,1)S(1)} %collective-permute-done.23.refs_19_), channel_id=1, source_target_pairs={{0,1},{1,2},{2,3},{3,4},{4,5},{5,6},{6,7},{7,0},{8,9},{9,10},{10,1... | collective-permute-start | bytes 393224 | tf_op jit(solution)/shard_map/ppermute | solution.py:285
  71.9 7.2 %collective-permute-start.14 = (bf16[512,128]{1,0:T(8,128)(2,1)S(1)}, bf16[512,128]{1,0:T(8,128)(2,1)S(1)}, u32[]{:S(2)}, u32[]{:S(2)}) collective-permute-start(bf16[512,128]{1,0:T(8,128)(2,1)S(1)} %collective-permute-done.13.refs_6_), channel_id=1, source_target_pairs={{0,7},{1,0},{2,1},{3,2},{4,3},{5,4},{6,5},{7,6},{8,15},{9,8},{10,9... | collective-permute-start | bytes 393224 | tf_op jit(solution)/shard_map/ppermute | solution.py:285
  73.2 7.9 %collective-permute-start.21 = (bf16[512,128]{1,0:T(8,128)(2,1)S(1)}, bf16[512,128]{1,0:T(8,128)(2,1)S(1)}, u32[]{:S(2)}, u32[]{:S(2)}) collective-permute-start(bf16[512,128]{1,0:T(8,128)(2,1)S(1)} %collective-permute-done.20.refs_14_), channel_id=1, source_target_pairs={{0,7},{1,0},{2,1},{3,2},{4,3},{5,4},{6,5},{7,6},{8,15},{9,8},{10,9... | collective-permute-start | bytes 393224 | tf_op jit(solution)/shard_map/ppermute | solution.py:285
  76.7 7.7 %collective-permute-start.18 = (bf16[512,128]{1,0:T(8,128)(2,1)S(1)}, bf16[512,128]{1,0:T(8,128)(2,1)S(1)}, u32[]{:S(2)}, u32[]{:S(2)}) collective-permute-start(bf16[512,128]{1,0:T(8,128)(2,1)S(1)} %collective-permute-done.17.refs_10_), channel_id=1, source_target_pairs={{0,1},{1,2},{2,3},{3,4},{4,5},{5,6},{6,7},{7,0},{8,9},{9,10},{10,1... | collective-permute-start | bytes 393224 | tf_op jit(solution)/shard_map/ppermute | solution.py:285
  77.9 6.6 %collective-permute-start.25 = (bf16[512,128]{1,0:T(8,128)(2,1)S(1)}, bf16[512,128]{1,0:T(8,128)(2,1)S(1)}, u32[]{:S(2)}, u32[]{:S(2)}) collective-permute-start(bf16[512,128]{1,0:T(8,128)(2,1)S(1)} %collective-permute-done.24.refs_18_), channel_id=1, source_target_pairs={{0,1},{1,2},{2,3},{3,4},{4,5},{5,6},{6,7},{7,0},{8,9},{9,10},{10,1... | collective-permute-start | bytes 393224 | tf_op jit(solution)/shard_map/ppermute | solution.py:285
  79.2 6.7 %collective-permute-start.15 = (bf16[512,128]{1,0:T(8,128)(2,1)S(1)}, bf16[512,128]{1,0:T(8,128)(2,1)S(1)}, u32[]{:S(2)}, u32[]{:S(2)}) collective-permute-start(bf16[512,128]{1,0:T(8,128)(2,1)S(1)} %collective-permute-done.14.refs_7_), channel_id=1, source_target_pairs={{0,7},{1,0},{2,1},{3,2},{4,3},{5,4},{6,5},{7,6},{8,15},{9,8},{10,9... | collective-permute-start | bytes 393224 | tf_op jit(solution)/shard_map/ppermute | solution.py:285
  81.2 6.1 %collective-permute-start.22 = (bf16[512,128]{1,0:T(8,128)(2,1)S(1)}, bf16[512,128]{1,0:T(8,128)(2,1)S(1)}, u32[]{:S(2)}, u32[]{:S(2)}) collective-permute-start(bf16[512,128]{1,0:T(8,128)(2,1)S(1)} %collective-permute-done.21.refs_15_), channel_id=1, source_target_pairs={{0,7},{1,0},{2,1},{3,2},{4,3},{5,4},{6,5},{7,6},{8,15},{9,8},{10,9... | collective-permute-start | bytes 393224 | tf_op jit(solution)/shard_map/ppermute | solution.py:285
  95.7 23.2 %all-to-all-start.2 = ((bf16[8,32,896]{2,1,0:T(8,128)(2,1)}), bf16[8,32,896]{2,1,0:T(8,128)(2,1)S(1)}, u32[]{:S(2)}, u32[]{:S(2)}) async-start(bf16[8,32,896]{2,1,0:T(8,128)(2,1)} %bitcast.20), calls=%async_computation.2 | async-start | bytes 917504 | tf_op jit(solution)/shard_map/all_to_all | solution.py:382
  102.9 7.1 %collective-permute-start.27 = (bf16[512,128]{1,0:T(8,128)(2,1)}, bf16[512,128]{1,0:T(8,128)(2,1)S(1)}, u32[]{:S(2)}, u32[]{:S(2)}) collective-permute-start(bf16[512,128]{1,0:T(8,128)(2,1)} %get-tuple-element.53), channel_id=1, source_target_pairs={{0,8},{8,16},{16,24},{24,0},{1,9},{9,17},{17,25},{25,1},{2,10},{10... | collective-permute-start | bytes 393224 | tf_op jit(solution)/shard_map/ppermute | solution.py:285
  104.4 9.2 %collective-permute-start.28 = (bf16[512,128]{1,0:T(8,128)(2,1)}, bf16[512,128]{1,0:T(8,128)(2,1)S(1)}, u32[]{:S(2)}, u32[]{:S(2)}) collective-permute-start(bf16[512,128]{1,0:T(8,128)(2,1)} %get-tuple-element.54), channel_id=1, source_target_pairs={{0,16},{8,24},{16,0},{24,8},{1,17},{9,25},{17,1},{25,9},{2,18},{10... | collective-permute-start | bytes 393224 | tf_op jit(solution)/shard_map/ppermute | solution.py:285
  107.1 6.6 %collective-permute-start.29 = (bf16[512,128]{1,0:T(8,128)(2,1)}, bf16[512,128]{1,0:T(8,128)(2,1)S(1)}, u32[]{:S(2)}, u32[]{:S(2)}) collective-permute-start(bf16[512,128]{1,0:T(8,128)(2,1)} %get-tuple-element.55), channel_id=1, source_target_pairs={{0,24},{8,0},{16,8},{24,16},{1,25},{9,1},{17,9},{25,17},{2,26},{10... | collective-permute-start | bytes 393224 | tf_op jit(solution)/shard_map/ppermute | solution.py:285
  108.5 6.8 %collective-permute-start.30 = (bf16[512,128]{1,0:T(8,128)(2,1)}, bf16[512,128]{1,0:T(8,128)(2,1)S(1)}, u32[]{:S(2)}, u32[]{:S(2)}) collective-permute-start(bf16[512,128]{1,0:T(8,128)(2,1)} %get-tuple-element.57), channel_id=1, source_target_pairs={{0,8},{8,16},{16,24},{24,0},{1,9},{9,17},{17,25},{25,1},{2,10},{10... | collective-permute-start | bytes 393224 | tf_op jit(solution)/shard_map/ppermute | solution.py:285
  109.1 7.3 %collective-permute-start.31 = (bf16[512,128]{1,0:T(8,128)(2,1)}, bf16[512,128]{1,0:T(8,128)(2,1)S(1)}, u32[]{:S(2)}, u32[]{:S(2)}) collective-permute-start(bf16[512,128]{1,0:T(8,128)(2,1)} %get-tuple-element.58), channel_id=1, source_target_pairs={{0,16},{8,24},{16,0},{24,8},{1,17},{9,25},{17,1},{25,9},{2,18},{10... | collective-permute-start | bytes 393224 | tf_op jit(solution)/shard_map/ppermute | solution.py:285
  110.0 7.2 %collective-permute-start.32 = (bf16[512,128]{1,0:T(8,128)(2,1)}, bf16[512,128]{1,0:T(8,128)(2,1)S(1)}, u32[]{:S(2)}, u32[]{:S(2)}) collective-permute-start(bf16[512,128]{1,0:T(8,128)(2,1)} %get-tuple-element.59), channel_id=1, source_target_pairs={{0,24},{8,0},{16,8},{24,16},{1,25},{9,1},{17,9},{25,17},{2,26},{10... | collective-permute-start | bytes 393224 | tf_op jit(solution)/shard_map/ppermute | solution.py:285
  (25 other events, 122.5 us)
